TPU v7x, 32 devices: a whole 2x2x4 slice. The times are simulated.
32 devices in a mesh: box: 8 (over z, x), angle: 4 (over y, core).
Axes of the slice: x: 2, y: 2, z: 4, core: 2. Of those that a mesh axis runs over, the one named last changes fastest.
Arguments:
- top_patterns: bfloat16 [16, 2, 256, 512], P('box', None, 'angle'), may hold values from -6 to 6
- theta_upper: bfloat16 [128, 256], replicated, may hold values from -0.375 to 0.375
- phi_upper: bfloat16 [256, 512], replicated, may hold values from -0.25 to 0.25
- angles_upper: float32 [8, 128, 256], P(None, 'angle'), may hold values from -3.140625 to 3.140625
- table_upper: bfloat16 [316, 2, 128, 256], P(None, None, 'angle'), may hold values from -0.59765625 to 0.59765625
- outgoing_upper: bfloat16 [128, 2, 128, 256], P('box', None, 'angle'), may hold values from -6 to 6
- list_upper: int32 [128, 16], P('box'), may hold values from 0 to 127, as said below
- offset_upper: int32 [128, 16], P('box'), may hold values from 0 to 315
- theta_lower: bfloat16 [64, 128], replicated, may hold values from -0.5 to 0.5
- phi_lower: bfloat16 [128, 256], replicated, may hold values from -0.375 to 0.375
- angles_lower: float32 [8, 64, 128], P(None, 'angle'), may hold values from -3.140625 to 3.140625
- table_lower: bfloat16 [316, 2, 64, 128], P(None, None, 'angle'), may hold values from -0.59765625 to 0.59765625
- outgoing_lower: bfloat16 [1024, 2, 64, 128], P('box', None, 'angle'), may hold values from -6 to 6
- list_lower: int32 [1024, 16], P('box'), may hold values from 0 to 1023, as said below
- offset_lower: int32 [1024, 16], P('box'), may hold values from 0 to 315
- switch_theta: bfloat16 [64, 64], replicated, may hold values from -0.75 to 0.75
- switch_phi: bfloat16 [2, 128, 128], replicated, may hold values from -0.5 to 0.5
Outputs:
- coefficients: float32 [1024, 2, 8192], P(('box', 'angle'))
Inputs may be any that keep to these rules, and one draw needn't show every extreme that they name: `list_upper`: Upper-level boxes form blocks of 16 consecutive ids, block k being ids k * 16 to (k + 1) * 16 - 1. Every entry of box g lies in g's own block or in the block whose number is g's block number XOR 4; entry 0 is the box at g's position within that other block. `list_lower`: Lower-level boxes form blocks of 128 consecutive ids. Every entry of box h lies in h's own block or in the block whose number is h's block number XOR 1; entry 0 is the box at h's position within that other block.
All inputs are finite; a program needn't handle non-finite values.
Results may differ from a plain program's by a relative error of at most 0.0039.
Values may be sent and summed in bfloat16 or wider, within the bound.
No kernel may reach another device: no remote copies, remote signals or barrier semaphores. Data moves between devices by JAX's collectives and lax.ppermute only.
A program may use at most 128 MiB of HBM per device.

v0:
```python
import jax
import jax.numpy as jnp
from jax import lax
from jax.sharding import PartitionSpec as P


def partner_2(value, axis, apart):
    mask = 2**apart
    pairs = [(source, source ^ mask) for source in range(lax.axis_size(axis))]
    return lax.ppermute(value, axis, pairs)


def shift_children(coarse, angles):
    cosines = jnp.cos(angles)[None]
    sine_part = jnp.sin(angles)[None]
    real_part = coarse[:, 0][:, None] * cosines - coarse[:, 1][:, None] * sine_part
    imag_part = coarse[:, 0][:, None] * sine_part + coarse[:, 1][:, None] * cosines
    stacked = jnp.stack([real_part, imag_part], axis=2)
    return stacked.reshape((stacked.shape[0] * stacked.shape[1],) + stacked.shape[2:])


def translate(outgoing, partner, table_rows, entry_lists, offsets):
    block_size = outgoing.shape[0]
    own_block = lax.axis_index("box")
    local_ids = jnp.where(
        entry_lists // block_size == own_block,
        entry_lists % block_size,
        block_size + entry_lists % block_size,
    )
    source_pool = jnp.concatenate([outgoing, partner], axis=0)
    entries = entry_lists.shape[1]
    group_size = min(8, entries)
    real_sum = jnp.zeros((block_size,) + outgoing.shape[2:], jnp.float32)
    imag_sum = jnp.zeros_like(real_sum)
    for first_entry in range(0, entries, group_size):
        source = jnp.take(source_pool, local_ids[:, first_entry : first_entry + group_size], axis=0)
        factor = jnp.take(table_rows, offsets[:, first_entry : first_entry + group_size], axis=0)
        source_real = source[:, :, 0].astype(jnp.float32)
        source_imag = source[:, :, 1].astype(jnp.float32)
        factor_real = factor[:, :, 0].astype(jnp.float32)
        factor_imag = factor[:, :, 1].astype(jnp.float32)
        real_sum = real_sum + jnp.sum(factor_real * source_real - factor_imag * source_imag, axis=1)
        imag_sum = imag_sum + jnp.sum(factor_real * source_imag + factor_imag * source_real, axis=1)
    return jnp.stack([real_sum, imag_sum], axis=1)


def scattered_pass(patterns, theta_map, phi_map, upper_level):
    held_rows = patterns.shape[2]
    narrowed = jnp.einsum("bctp,qp->bctq", patterns, phi_map, preferred_element_type=jnp.float32)
    columns = lax.dynamic_slice_in_dim(
        theta_map, lax.axis_index("angle") * held_rows, held_rows, 1
    ).astype(jnp.float32)

    def partial_rows():
        return jnp.einsum("ut,bctq->ubcq", columns, narrowed, precision=lax.Precision.HIGHEST)

    if upper_level:
        shared = lax.psum_scatter(partial_rows(), "angle", scatter_dimension=0, tiled=True)
    else:
        shared = lax.psum_scatter(partial_rows(), "angle", scatter_dimension=0, tiled=True)
    return jnp.transpose(shared, (1, 2, 0, 3))


def anterpolate(patterns, theta_map, phi_map, upper_level):
    if upper_level:
        return scattered_pass(patterns, theta_map, phi_map, True)
    return scattered_pass(patterns, theta_map, phi_map, False)


def project(patterns, theta_map, switch_phi):
    theta_pass = jnp.einsum(
        "ut,bctp->bcup", theta_map, patterns, preferred_element_type=jnp.float32
    )
    phi_real = switch_phi[0].astype(jnp.float32)
    phi_imag = switch_phi[1].astype(jnp.float32)
    coeff_real = jnp.einsum(
        "bup,vp->buv", theta_pass[:, 0], phi_real, precision=lax.Precision.HIGHEST
    ) - jnp.einsum("bup,vp->buv", theta_pass[:, 1], phi_imag, precision=lax.Precision.HIGHEST)
    coeff_imag = jnp.einsum(
        "bup,vp->buv", theta_pass[:, 0], phi_imag, precision=lax.Precision.HIGHEST
    ) + jnp.einsum("bup,vp->buv", theta_pass[:, 1], phi_real, precision=lax.Precision.HIGHEST)
    stacked = jnp.stack([coeff_real, coeff_imag], axis=1)
    return stacked.reshape(stacked.shape[0], 2, stacked.shape[2] * stacked.shape[3])


def per_device(
    top_patterns,
    theta_upper,
    phi_upper,
    angles_upper,
    table_upper,
    outgoing_upper,
    list_upper,
    offset_upper,
    theta_lower,
    phi_lower,
    angles_lower,
    table_lower,
    outgoing_lower,
    list_lower,
    offset_lower,
    switch_theta,
    switch_phi,
):
    bit_count = lax.axis_size("box").bit_length() - 1
    coarse = anterpolate(top_patterns, theta_upper, phi_upper, True)
    partner = partner_2(outgoing_upper, "box", bit_count - 1)
    incoming_upper = (
        shift_children(coarse, angles_upper)
        + translate(outgoing_upper, partner, table_upper, list_upper, offset_upper)
    ).astype(jnp.bfloat16)
    lower_partner = partner_2(outgoing_lower, "box", 0)
    translated_lower = translate(
        outgoing_lower, lower_partner, table_lower, list_lower, offset_lower
    )
    coarse = anterpolate(incoming_upper, theta_lower, phi_lower, False)
    incoming_lower = (shift_children(coarse, angles_lower) + translated_lower).astype(jnp.bfloat16)
    whole_rows = lax.all_to_all(incoming_lower, "angle", split_axis=0, concat_axis=2, tiled=True)
    return project(whole_rows, switch_theta, switch_phi)


def solution(mesh):
    return jax.shard_map(
        per_device,
        mesh=mesh,
        in_specs=(
            P("box", None, "angle", None),
            P(),
            P(),
            P(None, "angle", None),
            P(None, None, "angle", None),
            P("box", None, "angle", None),
            P("box", None),
            P("box", None),
            P(),
            P(),
            P(None, "angle", None),
            P(None, None, "angle", None),
            P("box", None, "angle", None),
            P("box", None),
            P("box", None),
            P(),
            P(),
        ),
        out_specs=P(("box", "angle"), None, None),
        check_vma=False,
    )
```

profile of v0, /device:TPU:0, one launch (start us, length us, event | category | flops | bytes accessed | tf_op | source)
XLA Modules:
  0.0 179.0 jit_solution(14348572142065014077)
XLA Ops:
  6.5 4.1 %collective-permute-start = (bf16[16,2,32,256]{3,2,1,0:T(8,128)(2,1)}, bf16[16,2,32,256]{3,2,1,0:T(8,128)(2,1)}, u32[]{:S(2)}, u32[]{:S(2)}) collective-permute-start(bf16[16,2,32,256]{3,2,1,0:T(8,128)(2,1)} %param.30), channel_id=1, source_target_pairs={{0,16},{4,20},{8,24},{12,28},{16,0},{20,4},{24,8},{28,12},{1,17},{... | collective-permute-start | bytes 1572872 | tf_op jit(solution)/shard_map/ppermute | solution.py:10
  10.6 1.3 fusion.22
  11.9 2.0 %fusion.25 = f32[128,2,2,256]{3,0,2,1:T(8,128)} fusion(f32[2,2,64,256]{3,2,1,0:T(8,128)S(1)} %fusion.22, bf16[128,256]{1,0:T(8,128)(2,1)} %param.26, s32[]{:T(128)S(6)} %select_n.66), kind=kOutput, calls=%fused_computation.77 | convolution fusion | flops 100663296 | bytes 819204 | tf_op jit(solution)/shard_map/ut,bctq->ubcq/dot_general | solution.py:55
  14.0 1.6 collective-permute-start.1
  15.6 1.9 %constant_dynamic-update-slice_fusion.1 = bf16[32,2,32,256]{3,2,1,0:T(8,128)(2,1)} fusion(bf16[16,2,32,256]{3,2,1,0:T(8,128)(2,1)} %param.30), kind=kLoop, calls=%fused_computation.115 | loop fusion | bytes 1048576
  17.5 0.7 add_select_fusion.3
  18.3 0.8 compare_select_fusion.1
  19.2 0.9 compare_and_fusion.1
  20.0 2.4 %constant_dynamic-update-slice_fusion.3 = bf16[256,2,16,128]{3,2,1,0:T(8,128)(2,1)} fusion(bf16[128,2,16,128]{3,2,1,0:T(8,128)(2,1)} %param.37), kind=kLoop, calls=%fused_computation.117 | loop fusion | bytes 2097152
  22.9 6.7 %gather_fusion.2 = bf16[128,2,32,256]{3,2,1,0:T(8,128)(2,1)} fusion(bf16[316,2,32,256]{3,2,1,0:T(8,128)(2,1)} %param.29, s32[1024]{0:T(1024)S(1)} %get-tuple-element.47), kind=kCustom, calls=%fused_computation.4.clone | custom fusion | bytes 8389120 | tf_op jit(solution)/shard_map/jit(_take)/gather | solution.py:37
  29.6 6.8 %gather_fusion = bf16[128,2,32,256]{3,2,1,0:T(8,128)(2,1)} fusion(bf16[316,2,32,256]{3,2,1,0:T(8,128)(2,1)} %param.29, s32[1024]{0:T(1024)S(1)} %get-tuple-element.48), kind=kCustom, calls=%fused_computation.clone | custom fusion | bytes 8389120 | tf_op jit(solution)/shard_map/jit(_take)/gather | solution.py:37
  36.4 1.6 fusion.48
  37.9 0.2 fusion.49
  38.2 0.1 copy.31
  38.4 0.1 copy.35
  38.6 0.1 copy.30
  38.7 0.1 copy.29
  38.9 0.1 copy.33
  39.1 0.1 copy.28
  39.2 0.1 copy.34
  39.4 9.9 %gather_fusion.4 = bf16[1024,2,16,128]{3,2,1,0:T(8,128)(2,1)} fusion(bf16[316,2,16,128]{3,2,1,0:T(8,128)(2,1)S(1)} %copy-done, s32[1024]{0:T(1024)S(1)} %get-tuple-element.52), kind=kCustom, calls=%fused_computation.2.clone | custom fusion | bytes 16781312 | tf_op jit(solution)/shard_map/jit(_take)/gather | solution.py:37
  49.3 9.9 %gather_fusion.6 = bf16[1024,2,16,128]{3,2,1,0:T(8,128)(2,1)} fusion(bf16[316,2,16,128]{3,2,1,0:T(8,128)(2,1)S(1)} %copy-done, s32[1024]{0:T(1024)S(1)} %get-tuple-element.51), kind=kCustom, calls=%fused_computation.6.clone | custom fusion | bytes 16781312 | tf_op jit(solution)/shard_map/jit(_take)/gather | solution.py:37
  59.2 0.1 copy.32
  59.3 4.6 %broadcast_select_fusion.5 = bf16[16,8,2,32,256]{4,3,2,1,0:T(8,128)(2,1)} fusion(bf16[16,8,2,32,256]{4,3,2,1,0:T(8,128)(2,1)} %bitcast.98, pred[16,8]{1,0:T(8,128)(4,1)S(1)} %get-tuple-element.37), kind=kLoop, calls=%fused_computation.45 | loop fusion | flops 2097152 | bytes 8388736 | tf_op jit(solution)/shard_map/jit(_take)/select_n | solution.py:37
  63.9 7.9 %broadcast_select_fusion.3 = bf16[128,8,2,16,128]{4,3,2,1,0:T(8,128)(2,1)} fusion(bf16[128,8,2,16,128]{4,3,2,1,0:T(8,128)(2,1)} %bitcast.93, pred[128,8]{1,0:T(8,128)(4,1)S(1)} %copy.28), kind=kLoop, calls=%fused_computation.27 | loop fusion | flops 4194304 | bytes 16778240 | tf_op jit(solution)/shard_map/jit(_take)/select_n | solution.py:37
  71.8 1.1 copy-done.4
  72.8 4.1 %broadcast_select_fusion.1 = bf16[128,8,2,16,128]{4,3,2,1,0:T(8,128)(2,1)} fusion(bf16[128,8,2,16,128]{4,3,2,1,0:T(8,128)(2,1)S(1)} %bitcast.94, pred[128,8]{1,0:T(8,128)(4,1)S(1)} %copy.32), kind=kLoop, calls=%fused_computation.25 | loop fusion | flops 4194304 | bytes 16778240 | tf_op jit(solution)/shard_map/jit(_take)/select_n | solution.py:37
  77.0 0.2 copy-done.6
  77.2 2.4 %broadcast_select_fusion.7 = bf16[16,8,2,32,256]{4,3,2,1,0:T(8,128)(2,1)} fusion(bf16[16,8,2,32,256]{4,3,2,1,0:T(8,128)(2,1)S(1)} %bitcast.97, pred[16,8]{1,0:T(8,128)(4,1)S(1)} %get-tuple-element.38), kind=kLoop, calls=%fused_computation.47 | loop fusion | flops 2097152 | bytes 8388736 | tf_op jit(solution)/shard_map/jit(_take)/select_n | solution.py:37
  79.6 1.1 constant_dynamic-update-slice_fusion
  80.7 2.8 %gather_fusion.3 = bf16[128,2,32,256]{3,2,1,0:T(8,128)(2,1)} fusion(bf16[32,2,32,256]{3,2,1,0:T(8,128)(2,1)S(1)} %constant_dynamic-update-slice_fusion, s32[1024]{0:T(1024)S(1)} %get-tuple-element.45), kind=kCustom, calls=%fused_computation.5.clone | custom fusion | bytes 8389120 | tf_op jit(solution)/shard_map/jit(_take)/gather | solution.py:36
  83.5 2.8 %gather_fusion.1 = bf16[128,2,32,256]{3,2,1,0:T(8,128)(2,1)} fusion(bf16[32,2,32,256]{3,2,1,0:T(8,128)(2,1)S(1)} %constant_dynamic-update-slice_fusion, s32[1024]{0:T(1024)S(1)} %get-tuple-element.46), kind=kCustom, calls=%fused_computation.1.clone | custom fusion | bytes 8389120 | tf_op jit(solution)/shard_map/jit(_take)/gather | solution.py:36
  86.3 2.8 %broadcast_select_fusion.4 = bf16[16,8,2,32,256]{4,3,2,1,0:T(8,128)(2,1)S(1)} fusion(bf16[16,8,2,32,256]{4,3,2,1,0:T(8,128)(2,1)} %bitcast.100, pred[16,8]{1,0:T(8,128)(4,1)S(1)} %get-tuple-element.41), kind=kLoop, calls=%fused_computation.44 | loop fusion | flops 2097152 | bytes 8388736 | tf_op jit(solution)/shard_map/jit(_take)/select_n | solution.py:36
  89.1 0.7 copy-done.8
  89.8 2.1 %fusion.13 = (f32[16,32,256]{2,1,0:T(8,128)S(1)}, f32[16,32,256]{2,1,0:T(8,128)S(1)}) fusion(bf16[16,8,2,32,256]{4,3,2,1,0:T(8,128)(2,1)S(1)} %broadcast_select_fusion.4, bf16[16,8,2,32,256]{4,3,2,1,0:T(8,128)(2,1)S(1)} %copy-done.8), kind=kLoop, calls=%fused_computation.41 | loop fusion | flops 12320768 | bytes 9437184 | tf_op jit(solution)/shard_map/reduce_sum | solution.py:42
  92.0 0.5 broadcast_select_fusion.6
  92.4 1.7 copy-done.9
  94.2 2.1 %fusion.9 = (f32[16,32,256]{2,1,0:T(8,128)S(1)}, f32[16,32,256]{2,1,0:T(8,128)S(1)}) fusion(bf16[16,8,2,32,256]{4,3,2,1,0:T(8,128)(2,1)S(1)} %broadcast_select_fusion.6, bf16[16,8,2,32,256]{4,3,2,1,0:T(8,128)(2,1)S(1)} %copy-done.9), kind=kLoop, calls=%fused_computation.37 | loop fusion | flops 12320768 | bytes 9437184 | tf_op jit(solution)/shard_map/reduce_sum | solution.py:42
  96.4 0.9 add_bitcast_fusion.2
  97.3 0.9 slice_bitcast_fusion.9
  98.2 0.1 multiply_subtract_fusion.1
  98.4 1.3 fusion.20
  99.7 1.6 fusion.36
  101.4 1.4 constant_dynamic-update-slice_fusion.2
  102.8 10.0 %gather_fusion.5 = bf16[1024,2,16,128]{3,2,1,0:T(8,128)(2,1)} fusion(bf16[256,2,16,128]{3,2,1,0:T(8,128)(2,1)S(1)} %constant_dynamic-update-slice_fusion.2, s32[1024]{0:T(1024)S(1)} %get-tuple-element.50), kind=kCustom, calls=%fused_computation.3.clone | custom fusion | bytes 16781312 | tf_op jit(solution)/shard_map/jit(_take)/gather | solution.py:36
  112.8 9.9 %gather_fusion.7 = bf16[1024,2,16,128]{3,2,1,0:T(8,128)(2,1)} fusion(bf16[256,2,16,128]{3,2,1,0:T(8,128)(2,1)S(1)} %constant_dynamic-update-slice_fusion.2, s32[1024]{0:T(1024)S(1)} %get-tuple-element.49), kind=kCustom, calls=%fused_computation.7.clone | custom fusion | bytes 16781312 | tf_op jit(solution)/shard_map/jit(_take)/gather | solution.py:36
  122.6 8.5 %broadcast_select_fusion.2 = bf16[128,8,2,16,128]{4,3,2,1,0:T(8,128)(2,1)} fusion(bf16[128,8,2,16,128]{4,3,2,1,0:T(8,128)(2,1)} %bitcast.95, pred[128,8]{1,0:T(8,128)(4,1)S(1)} %copy.30), kind=kLoop, calls=%fused_computation.26 | loop fusion | flops 4194304 | bytes 16778240 | tf_op jit(solution)/shard_map/jit(_take)/select_n | solution.py:36
  131.2 1.6 broadcast_select_fusion
  132.8 1.3 slice-done.3
  134.2 7.0 %fusion.1 = (f32[128,16,128]{2,1,0:T(8,128)S(1)}, f32[128,16,128]{2,1,0:T(8,128)S(1)}) fusion(bf16[128,8,2,16,128]{4,3,2,1,0:T(8,128)(2,1)} %broadcast_select_fusion.2, bf16[128,8,2,16,128]{4,3,2,1,0:T(8,128)(2,1)S(1)} %bitcast.92), kind=kLoop, calls=%fused_computation.17 | loop fusion | flops 24641536 | bytes 18874368 | tf_op jit(solution)/shard_map/reduce_sum | solution.py:42
  141.2 5.2 %fusion.5 = (f32[128,16,128]{2,1,0:T(8,128)S(1)}, f32[128,16,128]{2,1,0:T(8,128)S(1)}) fusion(bf16[128,8,2,16,128]{4,3,2,1,0:T(8,128)(2,1)S(1)} %broadcast_select_fusion, bf16[128,8,2,16,128]{4,3,2,1,0:T(8,128)(2,1)S(1)} %bitcast.90), kind=kLoop, calls=%fused_computation.21 | loop fusion | flops 24641536 | bytes 18874368 | tf_op jit(solution)/shard_map/reduce_sum | solution.py:42
  146.4 0.1 add_bitcast_fusion
  146.5 0.1 add_bitcast_fusion.1
  146.7 1.0 slice_bitcast_fusion.7
  147.7 0.3 multiply_subtract_fusion
  148.0 0.4 fusion.16
  148.4 17.2 %all_to_all.18 = bf16[128,2,16,128]{3,2,1,0:T(8,128)(2,1)S(1)} all-to-all(bf16[128,2,16,128]{3,2,1,0:T(8,128)(2,1)S(1)} %fusion.16), channel_id=1, replica_groups=mesh['box'=8,'angle'=4] {'angle'}, dimensions={0} | all-to-all | bytes 2097152 | tf_op jit(solution)/shard_map/all_to_all | solution.py:118
  165.6 0.3 copy.36
  165.9 0.4 convolution_bitcast_fusion
  166.4 0.6 fusion.19
  167.0 0.6 fusion.18
  167.6 0.6 convolution_subtract_fusion
  168.2 0.6 convolution_add_fusion
  168.8 3.4 %pad_maximum_fusion = f32[32,2,8192]{2,1,0:T(2,128)} fusion(f32[32,1,8192]{2,1,0:T(1,128)S(1)} %bitcast.105, f32[32,1,8192]{2,1,0:T(1,128)S(1)} %bitcast.104), kind=kLoop, calls=%fused_computation.50 | loop fusion | flops 524288 | bytes 4194304 | tf_op jit(solution)/shard_map/stack | solution.py:82
  (71 shorter events, 1.3 us)
Async XLA Ops:
  6.5 32.8 %copy-start = (bf16[316,2,16,128]{3,2,1,0:T(8,128)(2,1)S(1)}, bf16[316,2,16,128]{3,2,1,0:T(8,128)(2,1)}, u32[]{:S(2)}) copy-start(bf16[316,2,16,128]{3,2,1,0:T(8,128)(2,1)} %param.36) | copy-start | bytes 7766020
  6.5 15.9 %copy-start.18 = (s32[128,16]{0,1:T(8,128)S(1)}, s32[128,16]{0,1:T(8,128)}, u32[]{:S(2)}) copy-start(s32[128,16]{0,1:T(8,128)} %param.38) | copy-start | bytes 24580
  6.5 15.9 %copy-start.15 = (s32[128,16]{0,1:T(8,128)S(1)}, s32[128,16]{0,1:T(8,128)}, u32[]{:S(2)}) copy-start(s32[128,16]{0,1:T(8,128)} %param.39) | copy-start | bytes 24580
  6.5 90.8 %reduce-scatter.3.cloned.1.call-start = ((), (), s32[]{:S(2)}) async-start(), calls=%async_computation.3 | async-start | bytes 655360 | tf_op jit(solution)/shard_map/reduce_scatter | solution.py:58
  6.5 73.1 %collective-permute-start = (bf16[16,2,32,256]{3,2,1,0:T(8,128)(2,1)}, bf16[16,2,32,256]{3,2,1,0:T(8,128)(2,1)}, u32[]{:S(2)}, u32[]{:S(2)}) collective-permute-start(bf16[16,2,32,256]{3,2,1,0:T(8,128)(2,1)} %param.30), channel_id=1, source_target_pairs={{0,16},{4,20},{8,24},{12,28},{16,0},{20,4},{24,8},{28,12},{1,17},{... | collective-permute-start | bytes 1572872 | tf_op jit(solution)/shard_map/ppermute | solution.py:10
  14.0 132.8 %reduce-scatter.5.cloned.1.call-start = ((), (), s32[]{:S(2)}) async-start(), calls=%async_computation.4 | async-start | bytes 1310720 | tf_op jit(solution)/shard_map/reduce_scatter | solution.py:60
  14.0 87.4 %collective-permute-start.1 = (bf16[128,2,16,128]{3,2,1,0:T(8,128)(2,1)}, bf16[128,2,16,128]{3,2,1,0:T(8,128)(2,1)}, u32[]{:S(2)}, u32[]{:S(2)}) collective-permute-start(bf16[128,2,16,128]{3,2,1,0:T(8,128)(2,1)} %param.37), channel_id=1, source_target_pairs={{0,4},{4,0},{8,12},{12,8},{16,20},{20,16},{24,28},{28,24},{1,5},{5... | collective-permute-start | bytes 3145736 | tf_op jit(solution)/shard_map/ppermute | solution.py:10
  29.6 6.8 %copy-start.12 = (f32[8,32,256]{2,1,0:T(8,128)S(1)}, f32[8,32,256]{2,1,0:T(8,128)}, u32[]{:S(2)}) copy-start(f32[8,32,256]{2,1,0:T(8,128)} %param.28) | copy-start | bytes 786436
  29.6 8.4 %copy-start.13 = (f32[8,16,128]{2,1,0:T(8,128)S(1)}, f32[8,16,128]{2,1,0:T(8,128)}, u32[]{:S(2)}) copy-start(f32[8,16,128]{2,1,0:T(8,128)} %param.35) | copy-start | bytes 196612
  63.9 8.9 %copy-start.4 = (bf16[1024,2,16,128]{3,2,1,0:T(8,128)(2,1)S(1)}, bf16[1024,2,16,128]{3,2,1,0:T(8,128)(2,1)}, u32[]{:S(2)}) copy-start(bf16[1024,2,16,128]{3,2,1,0:T(8,128)(2,1)} %gather_fusion.6) | copy-start | bytes 25165828
  72.8 4.4 %copy-start.6 = (bf16[128,2,32,256]{3,2,1,0:T(8,128)(2,1)S(1)}, bf16[128,2,32,256]{3,2,1,0:T(8,128)(2,1)}, u32[]{:S(2)}) copy-start(bf16[128,2,32,256]{3,2,1,0:T(8,128)(2,1)} %gather_fusion) | copy-start | bytes 12582916
  77.2 2.4 %copy-start.3 = (bf16[32,2,32,256]{3,2,1,0:T(8,128)(2,1)S(1)}, bf16[32,2,32,256]{3,2,1,0:T(8,128)(2,1)}, u32[]{:S(2)}) copy-start(bf16[32,2,32,256]{3,2,1,0:T(8,128)(2,1)} %constant_dynamic-update-slice_fusion.1) | copy-start | bytes 3145732
  86.3 3.4 %copy-start.8 = (bf16[16,8,2,32,256]{4,3,2,1,0:T(8,128)(2,1)S(1)}, bf16[16,8,2,32,256]{4,3,2,1,0:T(8,128)(2,1)}, u32[]{:S(2)}) copy-start(bf16[16,8,2,32,256]{4,3,2,1,0:T(8,128)(2,1)} %broadcast_select_fusion.5) | copy-start | bytes 12582916
  89.8 2.2 %copy-start.7 = (bf16[128,2,32,256]{3,2,1,0:T(8,128)(2,1)S(1)}, bf16[128,2,32,256]{3,2,1,0:T(8,128)(2,1)}, u32[]{:S(2)}) copy-start(bf16[128,2,32,256]{3,2,1,0:T(8,128)(2,1)} %gather_fusion.1) | copy-start | bytes 12582916
  92.0 2.2 %copy-start.9 = (bf16[16,8,2,32,256]{4,3,2,1,0:T(8,128)(2,1)S(1)}, bf16[16,8,2,32,256]{4,3,2,1,0:T(8,128)(2,1)}, u32[]{:S(2)}) copy-start(bf16[16,8,2,32,256]{4,3,2,1,0:T(8,128)(2,1)} %broadcast_select_fusion.7) | copy-start | bytes 12582916
  94.2 4.0 %copy-start.10 = (f32[8,32,256]{2,1,0:T(8,128)S(1)}, f32[8,32,256]{2,1,0:T(8,128)}, u32[]{:S(2)}) copy-start(f32[8,32,256]{2,1,0:T(8,128)} %get-tuple-element.24) | copy-start | bytes 786436
  96.3 2.1 %copy-start.14 = (bf16[128,256]{1,0:T(8,128)(2,1)S(1)}, bf16[128,256]{1,0:T(8,128)(2,1)}, u32[]{:S(2)}) copy-start(bf16[128,256]{1,0:T(8,128)(2,1)} %param.34) | copy-start | bytes 196612
  96.3 3.4 %copy-start.16 = (bf16[64,128]{1,0:T(8,128)(2,1)S(1)}, bf16[64,128]{1,0:T(8,128)(2,1)}, u32[]{:S(2)}) copy-start(bf16[64,128]{1,0:T(8,128)(2,1)} %param.33) | copy-start | bytes 49156
  96.4 5.0 %copy-start.2 = (bf16[256,2,16,128]{3,2,1,0:T(8,128)(2,1)S(1)}, bf16[256,2,16,128]{3,2,1,0:T(8,128)(2,1)}, u32[]{:S(2)}) copy-start(bf16[256,2,16,128]{3,2,1,0:T(8,128)(2,1)} %constant_dynamic-update-slice_fusion.3) | copy-start | bytes 6291460
  122.6 8.6 %copy-start.5 = (bf16[1024,2,16,128]{3,2,1,0:T(8,128)(2,1)S(1)}, bf16[1024,2,16,128]{3,2,1,0:T(8,128)(2,1)}, u32[]{:S(2)}) copy-start(bf16[1024,2,16,128]{3,2,1,0:T(8,128)(2,1)} %gather_fusion.7) | copy-start | bytes 25165828
  122.6 10.2 %slice-start.2 = ((s8[8388608]{0:T(1024)(128)(4,1)}), s8[4194304]{0:T(1024)(128)(4,1)S(1)}, s32[]{:S(2)}) async-start(s8[8388608]{0:T(1024)(128)(4,1)} %bitcast.91), calls=%async_computation.7 | async-start | bytes 8388608
  131.2 3.0 %slice-start.3 = ((s8[8388608]{0:T(1024)(128)(4,1)}), s8[4194304]{0:T(1024)(128)(4,1)S(1)}, s32[]{:S(2)}) async-start(s8[8388608]{0:T(1024)(128)(4,1)} %bitcast.91), calls=%async_computation.8 | async-start | bytes 8388608
  131.2 10.0 %slice-start = ((s8[8388608]{0:T(1024)(128)(4,1)}), s8[4194304]{0:T(1024)(128)(4,1)S(1)}, s32[]{:S(2)}) async-start(s8[8388608]{0:T(1024)(128)(4,1)} %bitcast.89), calls=%async_computation.5 | async-start | bytes 8388608
  134.2 7.0 %slice-start.1 = ((s8[8388608]{0:T(1024)(128)(4,1)}), s8[4194304]{0:T(1024)(128)(4,1)S(1)}, s32[]{:S(2)}) async-start(s8[8388608]{0:T(1024)(128)(4,1)} %bitcast.89), calls=%async_computation.6 | async-start | bytes 8388608
  148.0 17.9 %copy-start.17 = (bf16[64,64]{1,0:T(8,128)(2,1)S(1)}, bf16[64,64]{1,0:T(8,128)(2,1)}, u32[]{:S(2)}) copy-start(bf16[64,64]{1,0:T(8,128)(2,1)} %param.40) | copy-start | bytes 24580
  148.4 18.0 %copy-start.11 = (bf16[2,128,128]{2,1,0:T(8,128)(2,1)S(1)}, bf16[2,128,128]{2,1,0:T(8,128)(2,1)}, u32[]{:S(2)}) copy-start(bf16[2,128,128]{2,1,0:T(8,128)(2,1)} %param.41) | copy-start | bytes 196612
  167.6 4.6 %copy-start.1 = (bf16[316,2,16,128]{3,2,1,0:T(8,128)(2,1)S(1)}, bf16[316,2,16,128]{3,2,1,0:T(8,128)(2,1)}, u32[]{:S(2)}) copy-start(bf16[316,2,16,128]{3,2,1,0:T(8,128)(2,1)} %param.36) | copy-start | bytes 7766020
Sparse Core Ops, SparseCore 0:
  14.1 20.9 reduce-scatter.2
  101.5 23.2 reduce-scatter.4
where the time goes:
time: 180 us; the launch traced here: 179 us
  local copies, waits for them, and re-layouts  76.3 us (42%)
  other arithmetic  56.9 us (32%)
  blocking collectives  17.2 us (10%)
  between operations  13.8 us (8%)
  matrix products  9.05 us (5%)
  starting transfers between devices  5.7 us (3%)
    gather x4, local copies, waits for them, and re-layouts, translate(): jnp.take(table_rows, offsets[:, first_entry:first_entry + group_size], ax...  33.3 us
    gather x4, local copies, waits for them, and re-layouts, translate(): jnp.take(source_pool, local_ids[:, first_entry:first_entry + group_size],...  25.5 us
    select_n x6, other arithmetic, translate(): jnp.take(table_rows, offsets[:, first_entry:first_entry + group_size], ax...  19.9 us
    all_to_all x1, blocking collectives, per_device(): lax.all_to_all(incoming_lower, 'angle', split_axis=0, concat_axis=2, tile...  17.2 us
    reduce_sum x4, other arithmetic, translate(): jnp.sum(factor_real * source_real - factor_imag * source_imag, axis=1)  16.4 us
    select_n x6, other arithmetic, translate(): jnp.take(source_pool, local_ids[:, first_entry:first_entry + group_size],...  13.4 us
    unnamed x48, local copies, waits for them, and re-layouts  9.46 us
    ppermute x2, starting transfers between devices, partner_2(): return lax.ppermute(value, axis, pairs)  5.66 us
  transfers between devices with their start and end apart: 4, of which 0 were waited for; matrix products, arithmetic and copies ran while one was open for 72% of the time, Pallas kernels for 0%

commit v1 on v0

v1 whole, which is shorter than its diff:
```python
import functools

import jax
import jax.numpy as jnp
from jax import lax
from jax.experimental import pallas as pl
from jax.experimental.pallas import tpu as pltpu
from jax.sharding import PartitionSpec as P

F32, BF16 = jnp.float32, jnp.bfloat16
VM = pl.BlockSpec(memory_space=pltpu.VMEM)
SM = pl.BlockSpec(memory_space=pltpu.SMEM)
SHIFT = 9
NT = (((1,), (1,)), ((), ()))


def swap(value, axis, mask):
    pairs = [(source, source ^ mask) for source in range(lax.axis_size(axis))]
    return lax.ppermute(value, axis, pairs)


def kernel_call(body, outs, scalars, arrays, name, scratch=(), vmem=16 << 20, flops=0):
    moved = sum(a.size * a.dtype.itemsize for a in arrays)
    return pl.pallas_call(
        body,
        out_shape=outs,
        in_specs=[SM] * len(scalars) + [VM] * len(arrays),
        out_specs=[VM] * len(outs),
        scratch_shapes=list(scratch),
        compiler_params=pltpu.CompilerParams(vmem_limit_bytes=vmem),
        cost_estimate=pl.CostEstimate(flops=flops, bytes_accessed=moved, transcendentals=0),
        name=name,
    )(*scalars, *arrays)


def split_dot(left, value, dims):
    high = value.astype(BF16)
    low = (value - high.astype(F32)).astype(BF16)
    return lax.dot_general(left, high, dims, preferred_element_type=F32) + lax.dot_general(
        left, low, dims, preferred_element_type=F32
    )


def widen_body(table, source, table_out, source_out):
    count = source.shape[0]
    table_out[...] = table[...].astype(F32)
    source_out[0:count] = source[...].astype(F32)
    source_out[count] = jnp.zeros(source.shape[1:], F32)


def box_sum(box, entries, code, table, source):
    rows = table.shape[1] // 2
    real = imag = None
    for entry in range(entries):
        word = code[box * entries + entry]
        factor = table[word & ((1 << SHIFT) - 1)]
        value = source[word >> SHIFT]
        fr, fi, sr, si = factor[:rows], factor[rows:], value[:rows], value[rows:]
        re, im = fr * sr - fi * si, fr * si + fi * sr
        real = re if real is None else real + re
        imag = im if imag is None else imag + im
    return real, imag


def sums_body(groups, per, entries, me, *refs):
    codes = max(which for _, which in groups) + 1
    code_refs, (table, source), outs = refs[:codes], refs[codes : codes + 2], refs[codes + 2 :]
    rows = table.shape[1] // 2
    for (masks, which), out in zip(groups, outs, strict=True):
        for place, mask in enumerate(masks):
            first = jnp.bitwise_xor(me[0], mask) * per

            def one(i, carry, first=first, place=place, which=which, out=out):
                real, imag = box_sum(first + i, entries, code_refs[which], table, source)
                out[place * per + i, 0:rows] = real.astype(out.dtype)
                out[place * per + i, rows:] = imag.astype(out.dtype)
                return carry

            lax.fori_loop(0, per, one, 0, unroll=2)


def early_body(peers, rows, me, top, theta, phi, angles, *refs):
    outs, (padded, summed) = refs[:peers], refs[peers:]
    held = top.shape[0] // 4
    narrowed = lax.dot_general(top[...], phi[...], NT, preferred_element_type=F32)
    padded[...] = jnp.zeros(padded.shape, F32)
    for k in range(4):
        padded[k, me[0]] = narrowed[k * held : (k + 1) * held]
    for k in range(4):
        full = padded[k].reshape(peers * held, narrowed.shape[1])
        part = split_dot(theta[...], full, (((1,), (0,)), ((), ())))
        summed[k] = part.reshape(peers, rows, narrowed.shape[1])
    low = angles.shape[1]
    half = angles.shape[0] // 2
    for mask, out in enumerate(outs):
        for k in range(4):
            out[k * rows : (k + 1) * rows] = summed[k, jnp.bitwise_xor(me[0], mask)]
        for c in range(half):
            start = 4 * rows + c * low
            out[start : start + low, 0:128] = angles[c]
            out[start : start + low, 128:256] = angles[half + c]


def shift_body(peers, rows, low, me, angles, *refs):
    parts, (shifted, trig) = refs[:peers], refs[peers:]
    children = angles.shape[0]
    half = children // 2
    for c in range(children):
        cosine, sine = jnp.cos(angles[c]), jnp.sin(angles[c])
        for b in range(2):
            re = parts[0][2 * b * rows : (2 * b + 1) * rows]
            im = parts[0][(2 * b + 1) * rows : (2 * b + 2) * rows]
            for part in parts[1:]:
                re = re + part[2 * b * rows : (2 * b + 1) * rows]
                im = im + part[(2 * b + 1) * rows : (2 * b + 2) * rows]
            shifted[b * children + c, 0] = re * cosine - im * sine
            shifted[b * children + c, 1] = re * sine + im * cosine
    for mask, part in enumerate(parts):
        for c in range(half):
            start = 4 * rows + c * low
            for side in range(2):
                angle = part[start : start + low, side * 128 : side * 128 + 128]
                place = jnp.bitwise_xor(me[0], mask)
                trig[0, side * half + c, place] = jnp.cos(angle)
                trig[1, side * half + c, place] = jnp.sin(angle)


def upper_body(peers, entries, me, code, own, far, table, shifted, phi, *refs):
    outs, (pool, whole) = refs[:peers], refs[peers:]
    boxes, _, rows, _ = own.shape
    pool[0:boxes] = own[...].astype(F32)
    pool[boxes:] = far[...].astype(F32)
    step = min(16, rows)
    per = boxes // peers

    def one(box, carry):
        for r in range(0, rows, step):
            span = slice(r, r + step)
            real, imag = shifted[box, 0, span], shifted[box, 1, span]
            for entry in range(entries):
                word = code[box * entries + entry]
                offset, place = word & ((1 << SHIFT) - 1), word >> SHIFT
                fr, fi = table[offset, 0, span].astype(F32), table[offset, 1, span].astype(F32)
                sr, si = pool[place, 0, span], pool[place, 1, span]
                real = real + (fr * sr - fi * si)
                imag = imag + (fr * si + fi * sr)
            whole[box, 0, span] = real
            whole[box, 1, span] = imag
        return carry

    lax.fori_loop(0, boxes, one, 0)
    for mask in range(peers):
        first = jnp.bitwise_xor(me[0], mask) * per
        for i in range(per):
            for c in range(2):
                incoming = whole[first + i, c].astype(BF16)
                narrow = lax.dot_general(incoming, phi[...], NT, preferred_element_type=F32)
                outs[mask][i, c * rows : (c + 1) * rows] = narrow.astype(BF16)


def final_body(peers, me, *refs):
    ups, lows = refs[:peers], refs[peers : 2 * peers]
    trig, theta, mix, expand, out, rows_up, rows_low, pattern = refs[2 * peers :]
    children, rows = trig.shape[1], trig.shape[2]
    high_rows, low_rows = rows_up.shape[2], rows_low.shape[3]
    for mask in range(peers):
        place = jnp.bitwise_xor(me[0], mask)
        for c in range(2):
            rows_up[c, place] = ups[mask][0, c * high_rows : (c + 1) * high_rows].astype(F32)
            for k in range(children):
                piece = lows[mask][k, c * low_rows : (c + 1) * low_rows]
                rows_low[k, c, place] = piece.astype(F32)
    coarse = []
    for c in range(2):
        full = rows_up[c].reshape(peers * high_rows, 128).astype(BF16)
        coarse.append(jnp.dot(theta[...], full, preferred_element_type=F32))
    for k in range(children):
        cosine, sine = trig[0, k], trig[1, k]
        real = coarse[0] * cosine - coarse[1] * sine + rows_low[k, 0].reshape(rows, 128)
        imag = coarse[0] * sine + coarse[1] * cosine + rows_low[k, 1].reshape(rows, 128)
        pattern[k * rows : (k + 1) * rows, 0:128] = real.astype(BF16)
        pattern[k * rows : (k + 1) * rows, 128:256] = imag.astype(BF16)
    for k in range(0, children, 2):
        block = pattern[k * rows : (k + 2) * rows]
        turned = lax.dot_general(block, mix[...], NT, preferred_element_type=F32)
        one, two = turned[:rows], turned[rows:]
        stacked = jnp.concatenate(
            [
                jnp.concatenate([one[:, :128], two[:, :128]], axis=1),
                jnp.concatenate([one[:, 128:], two[:, 128:]], axis=1),
            ],
            axis=0,
        )
        result = split_dot(expand[...], stacked, (((1,), (0,)), ((), ())))
        size = expand.shape[0]
        out[k * size : (k + 1) * size] = result[:, :128]
        out[(k + 1) * size : (k + 2) * size] = result[:, 128:]


def struct(shape, dtype):
    return jax.ShapeDtypeStruct(shape, dtype)


def per_device(
    top_patterns,
    theta_upper,
    phi_upper,
    angles_upper,
    table_upper,
    outgoing_upper,
    list_upper,
    offset_upper,
    theta_lower,
    phi_lower,
    angles_lower,
    table_lower,
    outgoing_lower,
    list_lower,
    offset_lower,
    switch_theta,
    switch_phi,
):
    peers = lax.axis_size("angle")
    home = lax.axis_index("box")
    me = lax.axis_index("angle").astype(jnp.int32).reshape(1)
    far_mask = lax.axis_size("box") // 2
    boxes, _, low, lanes = outgoing_lower.shape
    per = boxes // peers
    entries = list_lower.shape[1]
    upper_boxes, _, rows, wide = outgoing_upper.shape
    upper_per = upper_boxes // peers

    other = list_lower // boxes != home
    spot = list_lower % boxes
    ask_code = ((jnp.where(other, spot, boxes) << SHIFT) + offset_lower).reshape(-1)
    own_code = ((jnp.where(other, boxes, spot) << SHIFT) + offset_lower).reshape(-1)
    far_code = swap(ask_code, "box", 1)
    far_upper = swap(outgoing_upper, "box", far_mask)
    upper_spot = list_upper % upper_boxes + jnp.where(list_upper // upper_boxes != home, upper_boxes, 0)
    upper_code = ((upper_spot << SHIFT) + offset_upper).reshape(-1)

    children = angles_lower.shape[0]
    part_rows = 4 * rows + children * low // 2
    held = top_patterns.shape[2]
    parts = kernel_call(
        functools.partial(early_body, peers, rows),
        [struct((part_rows, wide), F32)] * peers,
        [me],
        [top_patterns.reshape(4 * held, -1), theta_upper, phi_upper, angles_lower],
        "early",
        scratch=[pltpu.VMEM((4, peers, held, wide), F32), pltpu.VMEM((4, peers, rows, wide), F32)],
        flops=4 * held * wide * 512 * 2,
    )
    parts = [swap(part, "angle", mask) if mask else part for mask, part in enumerate(parts)]
    shifted, trig = kernel_call(
        functools.partial(shift_body, peers, rows, low),
        [
            struct((upper_boxes, 2, rows, wide), F32),
            struct((2, children, peers, low, lanes), F32),
        ],
        [me],
        [angles_upper, *parts],
        "shift",
    )
    trig = trig.reshape(2, children, peers * low, lanes)

    table, source = kernel_call(
        widen_body,
        [
            struct((table_lower.shape[0], 2 * low, lanes), F32),
            struct((boxes + 1, 2 * low, lanes), F32),
        ],
        [],
        [table_lower.reshape(-1, 2 * low, lanes), outgoing_lower.reshape(-1, 2 * low, lanes)],
        "widen",
    )
    outer, inner = list(range(peers - 1, peers // 2 - 1, -1)), list(range(peers // 2 - 1, -1, -1))
    first = kernel_call(
        functools.partial(sums_body, [((mask,), 0) for mask in outer], per, entries),
        [struct((per, 2 * low, lanes), BF16)] * len(outer),
        [me, far_code],
        [table, source],
        "sums_first",
    )
    rest = kernel_call(
        functools.partial(
            sums_body,
            [(tuple(inner), 0)] + [((mask,), 1) for mask in outer + inner],
            per,
            entries,
        ),
        [struct((len(inner) * per, 2 * low, lanes), BF16)]
        + [struct((per, 2 * low, lanes), F32)] * peers,
        [me, far_code, own_code],
        [table, source],
        "sums_rest",
    )
    own = dict(zip(outer + inner, rest[1:], strict=True))
    got = {mask: swap(value, "box", 1) for mask, value in zip(outer, first, strict=True)}
    last = swap(rest[0], "box", 1)
    for place, mask in enumerate(inner):
        got[mask] = last[place * per : (place + 1) * per]
    lows = []
    for mask in outer + inner:
        total = (own[mask] + got[mask].astype(F32)).astype(BF16)
        lows.append((mask, swap(total, "angle", mask) if mask else total))
    lows = [value for _, value in sorted(lows, key=lambda item: item[0])]

    ups = kernel_call(
        functools.partial(upper_body, peers, entries),
        [struct((upper_per, 2 * rows, lanes), BF16)] * peers,
        [me, upper_code],
        [outgoing_upper, far_upper, table_upper, shifted, phi_lower],
        "upper",
        scratch=[
            pltpu.VMEM((2 * upper_boxes, 2, rows, wide), F32),
            pltpu.VMEM((upper_boxes, 2, rows, wide), F32),
        ],
    )
    ups = [swap(value, "angle", mask) if mask else value for mask, value in enumerate(ups)]

    orders, angles = switch_theta.shape
    pair = jnp.eye(2, dtype=BF16)
    expand = (switch_theta[:, None, None, :] * pair[None, :, :, None]).reshape(2 * orders, 2 * angles)
    mix = jnp.concatenate(
        [
            jnp.concatenate([switch_phi[0], -switch_phi[1]], axis=1),
            jnp.concatenate([switch_phi[1], switch_phi[0]], axis=1),
        ],
        axis=0,
    )
    azimuths = switch_phi.shape[1]
    whole = lambda shape: pl.BlockSpec(shape, lambda b: (0,) * len(shape))
    out = pl.pallas_call(
        functools.partial(final_body, peers),
        out_shape=struct((per * 2 * orders, azimuths), F32),
        grid=(upper_per,),
        in_specs=[SM]
        + [pl.BlockSpec((1, 2 * rows, lanes), lambda b: (b, 0, 0))] * peers
        + [pl.BlockSpec((children, 2 * low, lanes), lambda b: (b, 0, 0))] * peers
        + [whole(trig.shape), whole(theta_lower.shape), whole(mix.shape), whole(expand.shape)],
        out_specs=pl.BlockSpec((children * 2 * orders, azimuths), lambda b: (b, 0)),
        scratch_shapes=[
            pltpu.VMEM((2, peers, rows, lanes), F32),
            pltpu.VMEM((children, 2, peers, low, lanes), F32),
            pltpu.VMEM((children * peers * low, 2 * lanes), BF16),
        ],
        compiler_params=pltpu.CompilerParams(vmem_limit_bytes=16 << 20),
        name="expand",
    )(me, *ups, *lows, trig, theta_lower, mix, expand)
    out = out.reshape(per, orders, 2, azimuths)
    return jnp.transpose(out, (0, 2, 1, 3)).reshape(per, 2, orders * azimuths)


def solution(mesh):
    return jax.shard_map(
        per_device,
        mesh=mesh,
        in_specs=(
            P("box", None, "angle", None),
            P(),
            P(),
            P(None, "angle", None),
            P(None, None, "angle", None),
            P("box", None, "angle", None),
            P("box", None),
            P("box", None),
            P(),
            P(),
            P(None, "angle", None),
            P(None, None, "angle", None),
            P("box", None, "angle", None),
            P("box", None),
            P("box", None),
            P(),
            P(),
        ),
        out_specs=P(("box", "angle"), None, None),
        check_vma=False,
    )
```

time: 180 us -> 103 us (0.57)
  local copies, waits for them, and re-layouts: 76.3 us -> 20.8 us
  other arithmetic: 56.9 us -> 2.93 us
  waiting for transfers between devices: 0.06 us -> 35.4 us
  Pallas kernels: 0 us -> 29.6 us
  blocking collectives: 17.2 us -> 0 us
  between operations: 13.8 us -> 0.21 us
  matrix products: 9.05 us -> 0 us
  starting transfers between devices: 5.7 us -> 13.5 us
    gather x8 -> x0, local copies, waits for them, and re-layouts: 58.7 us -> none  [the longest x4 33.3 us: translate(): jnp.take(table_rows, offsets[:, first_entry:first_entry + group_size], ax...]
    ppermute x2 -> x14, waiting for transfers between devices: 0.01 us -> 35.4 us  [swap(): return lax.ppermute(value, axis, pairs)]
    select_n x14 -> x0, other arithmetic: 34 us -> none  [the longest x6 19.9 us: translate(): jnp.take(table_rows, offsets[:, first_entry:first_entry + group_size], ax...]
    pallas_call x0 -> x7, Pallas kernels: none -> 29.6 us  [the longest x6 25.1 us: kernel_call(): pl.pallas_call(body, out_shape=outs, in_specs=[SM] * len(scalars) + [VM]...]
    all_to_all x1 -> x0, blocking collectives: 17.2 us -> none  [per_device(): lax.all_to_all(incoming_lower, 'angle', split_axis=0, concat_axis=2, tile...]
    reduce_sum x4 -> x0, other arithmetic: 16.4 us -> none  [translate(): jnp.sum(factor_real * source_real - factor_imag * source_imag, axis=1)]
    dot_general x9 -> x0, matrix products: 9.05 us -> none  [the longest x2 3.59 us: partial_rows(): jnp.einsum('ut,bctq->ubcq', columns, narrowed, precision=lax.Precision.HI...]
    ppermute x2 -> x14, starting transfers between devices: 5.66 us -> 13.5 us  [swap(): return lax.ppermute(value, axis, pairs)]
  transfers between devices with their start and end apart: 4 -> 14, of which waited for: 0 -> 4; matrix products, arithmetic and copies ran while one was open for 72% -> 6% of each run, Pallas kernels for 0% -> 24%
where the time goes in v1:
time: 103 us
  waiting for transfers between devices  35.4 us (34%)
  Pallas kernels  29.6 us (29%)
  local copies, waits for them, and re-layouts  20.8 us (20%)
  starting transfers between devices  13.5 us (13%)
  other arithmetic  2.93 us (3%)
    ppermute x14, waiting for transfers between devices, swap(): return lax.ppermute(value, axis, pairs)  35.4 us
    pallas_call x6, Pallas kernels, kernel_call(): pl.pallas_call(body, out_shape=outs, in_specs=[SM] * len(scalars) + [VM]...  25.1 us
    unnamed x58, local copies, waits for them, and re-layouts  16.8 us
    ppermute x14, starting transfers between devices, swap(): return lax.ppermute(value, axis, pairs)  13.5 us
    pallas_call x1, Pallas kernels, per_device(): pl.pallas_call(functools.partial(final_body, peers), out_shape=struct((pe...  4.5 us
  transfers between devices with their start and end apart: 14, of which 4 were waited for; matrix products, arithmetic and copies ran while one was open for 6% of the time, Pallas kernels for 24%

profile of v1, /device:TPU:0, one launch (start us, length us, event | category | flops | bytes accessed | tf_op | source)
XLA Modules:
  0.0 102.6 jit_solution(4420607991229418669)
XLA Ops:
  0.0 0.7 shift-left_add_fusion
  0.7 0.1 copy.19
  0.8 0.1 reshape.46
  0.9 3.0 %collective-permute-start.7 = (s32[2048]{0:T(1024)S(1)}, s32[2048]{0:T(1024)S(1)}, u32[]{:S(2)}, u32[]{:S(2)}) collective-permute-start(s32[2048]{0:T(1024)S(1)} %reshape.46), channel_id=1, source_target_pairs={{0,4},{4,0},{8,12},{12,8},{16,20},{20,16},{24,28},{28,24},{1,5},{5... | collective-permute-start | bytes 24584 | tf_op jit(solution)/shard_map/ppermute | solution.py:19
  3.9 0.9 copy-done.11
  4.8 0.9 copy-done.12
  5.8 0.8 copy-done.16
  6.6 0.8 copy-done.17
  7.5 1.5 %early.1 = (f32[192,256]{1,0:T(8,128)S(1)}, f32[192,256]{1,0:T(8,128)}, f32[192,256]{1,0:T(8,128)}, f32[192,256]{1,0:T(8,128)S(1)}) custom-call(s32[1]{0:T(128)} %bitcast.me, bf16[256,512]{1,0:T(8,128)(2,1)S(1)} %bitcast.19, bf16[128,256]{1,0:T(8,128)(2,1)S(1)} %copy-done.16, bf16[256,512]{1,0:T(8,128)(2,1)S(1)} %copy-done.12, f32[8,16,128]{2,1,0:T(8,128)S(1)} %copy-done.17), custom_call_target="tpu_custom_call" | custom-call | flops 67108864 | bytes 655360 | tf_op jit(solution)/shard_map/early/pallas_call | solution.py:24
  9.0 0.0 collective-permute-start.1
  9.0 1.5 %collective-permute-start.2 = (f32[192,256]{1,0:T(8,128)}, f32[192,256]{1,0:T(8,128)}, u32[]{:S(2)}, u32[]{:S(2)}) collective-permute-start(f32[192,256]{1,0:T(8,128)} %get-tuple-element.26), channel_id=1, source_target_pairs={{0,2},{1,3},{2,0},{3,1},{4,6},{5,7},{6,4},{7,5},{8,10},{9,11},{10,... | collective-permute-start | bytes 589832 | tf_op jit(solution)/shard_map/ppermute | solution.py:19
  10.5 1.4 %slice_bitcast_fusion = (bf16[128,128]{1,0:T(8,128)(2,1)}, bf16[128,128]{1,0:T(8,128)(2,1)}) fusion(bf16[2,128,128]{2,1,0:T(8,128)(2,1)} %param.33), kind=kLoop, calls=%fused_computation.6 | loop fusion | bytes 131072 | tf_op jit(solution)/shard_map/squeeze | solution.py:327
  11.9 0.0 copy-start.3
  11.9 1.7 %copy-done.3 = bf16[316,2,16,128]{3,2,1,0:T(8,128)(2,1)S(1)} copy-done((bf16[316,2,16,128]{3,2,1,0:T(8,128)(2,1)S(1)}, bf16[316,2,16,128]{3,2,1,0:T(8,128)(2,1)}, u32[]{:S(2)}) %copy-start.3) | copy-done | bytes 2588696
  13.6 1.2 %copy-done.4 = bf16[128,2,16,128]{3,2,1,0:T(8,128)(2,1)S(1)} copy-done((bf16[128,2,16,128]{3,2,1,0:T(8,128)(2,1)S(1)}, bf16[128,2,16,128]{3,2,1,0:T(8,128)(2,1)}, u32[]{:S(2)}) %copy-start.4) | copy-done | bytes 1048600
  14.9 0.5 widen.1
  15.3 0.0 collective-permute-done.7.refs_0_
  15.3 0.0 copy-start.18
  15.4 0.0 copy-start.26
  15.4 4.0 %sums_first.1 = (bf16[32,32,128]{2,1,0:T(8,128)(2,1)}, bf16[32,32,128]{2,1,0:T(8,128)(2,1)}) custom-call(s32[1]{0:T(128)} %bitcast.me, s32[2048]{0:T(1024)S(1)} %collective-permute-done.7.refs_0_, f32[316,32,128]{2,1,0:T(8,128)S(1)} %get-tuple-element.33.refs_2_.refs_1_, f32[129,32,128]{2,1,0:T(8,128)S(1)} %get-tuple-element.34.refs_3_.refs_2_), custom_call_target="tpu_custom_call" | custom-call | bytes 7290880 | tf_op jit(solution)/shard_map/sums_first/pallas_call | solution.py:24
  19.4 0.5 collective-permute-start.12
  19.9 0.7 broadcast_multiply_fusion
  20.6 0.1 copy.20
  20.7 0.7 reshape.47.refs_1_
  21.4 2.5 %copy-done.1 = f32[316,32,128]{2,1,0:T(8,128)S(1)} copy-done((f32[316,32,128]{2,1,0:T(8,128)S(1)}, f32[316,32,128]{2,1,0:T(8,128)}, u32[]{:S(2)}) %copy-start.1) | copy-done | bytes 5177368
  23.9 0.7 copy-done.19
  24.6 0.7 copy-done.20
  25.3 10.4 %sums_rest.1 = (bf16[64,32,128]{2,1,0:T(8,128)(2,1)}, f32[32,32,128]{2,1,0:T(8,128)S(1)}, f32[32,32,128]{2,1,0:T(8,128)S(1)}, f32[32,32,128]{2,1,0:T(8,128)S(1)}, f32[32,32,128]{2,1,0:T(8,128)S(1)}) custom-call(s32[1]{0:T(128)} %bitcast.me, s32[2048]{0:T(1024)S(1)} %copy-done.19, s32[2048]{0:T(1024)S(1)} %copy-done.20, f32[316,32,128]{2,1,0:T(8,128)S(1)} %copy-done.1, ...), custom_call_target="tpu_custom_call" | custom-call | bytes 7290880 | tf_op jit(solution)/shard_map/sums_rest/pallas_call | solution.py:24
  35.7 0.8 copy-done.6
  36.5 0.8 copy-done.7
  37.3 0.8 copy-done.9
  38.2 1.5 %collective-permute-start.8 = (bf16[64,32,128]{2,1,0:T(8,128)(2,1)}, bf16[64,32,128]{2,1,0:T(8,128)(2,1)S(1)}, u32[]{:S(2)}, u32[]{:S(2)}) collective-permute-start(bf16[64,32,128]{2,1,0:T(8,128)(2,1)} %get-tuple-element.36), channel_id=1, source_target_pairs={{0,4},{4,0},{8,12},{12,8},{16,20},{20,16},{24,28},{28,24},{1,5},{5... | collective-permute-start | bytes 1572872 | tf_op jit(solution)/shard_map/ppermute | solution.py:19
  39.6 0.5 collective-permute-start.10
  40.2 0.1 reshape.44.code
  40.3 1.5 %mul.20.refs_11_ = bf16[128,128]{1,0:T(8,128)(2,1)} reshape(bf16[64,2,2,64]{3,2,1,0:T(2,128)(2,1)} %broadcast_multiply_fusion) | data formatting | bytes 65536 | tf_op jit(solution)/shard_map/mul | solution.py:324
  41.8 0.0 collective-permute-done.12
  41.8 0.0 collective-permute-start.3
  41.8 0.0 copy-start.15
  41.9 1.2 %add_convert_fusion = bf16[32,32,128]{2,1,0:T(8,128)(2,1)S(1)} fusion(f32[32,32,128]{2,1,0:T(8,128)} %copy-done.6, bf16[32,32,128]{2,1,0:T(8,128)(2,1)} %collective-permute-done.12), kind=kLoop, calls=%fused_computation | loop fusion | flops 393216 | bytes 1048576 | tf_op jit(solution)/shard_map/convert_element_type | solution.py:305
  43.1 14.7 %collective-permute-done.10 = bf16[32,32,128]{2,1,0:T(8,128)(2,1)S(1)} collective-permute-done((bf16[32,32,128]{2,1,0:T(8,128)(2,1)}, bf16[32,32,128]{2,1,0:T(8,128)(2,1)S(1)}, u32[]{:S(2)}, u32[]{:S(2)}) %collective-permute-start.10) | collective-permute-done | bytes 262176 | tf_op jit(solution)/shard_map/ppermute | solution.py:19
  57.8 2.6 %collective-permute-start = (bf16[16,2,32,256]{3,2,1,0:T(8,128)(2,1)S(1)}, bf16[16,2,32,256]{3,2,1,0:T(8,128)(2,1)S(1)}, u32[]{:S(2)}, u32[]{:S(2)}) collective-permute-start(bf16[16,2,32,256]{3,2,1,0:T(8,128)(2,1)S(1)} %copy-done.5), channel_id=1, source_target_pairs={{0,16},{4,20},{8,24},{12,28},{16,0},{20,4},{24,8},{28,12},{1,17},{... | collective-permute-start | bytes 1572872 | tf_op jit(solution)/shard_map/ppermute | solution.py:19
  60.4 0.1 add_convert_fusion.1
  60.4 0.0 collective-permute-done.8
  60.4 0.1 collective-permute-start.13
  60.5 0.2 add_convert_fusion.2
  60.7 0.0 collective-permute-done.1.refs_1_
  60.7 0.6 collective-permute-start.11
  61.3 0.0 collective-permute-done.2.refs_2_
  61.3 1.3 %collective-permute-start.9 = (bf16[32,32,128]{2,1,0:T(8,128)(2,1)S(1)}, bf16[32,32,128]{2,1,0:T(8,128)(2,1)S(1)}, u32[]{:S(2)}, u32[]{:S(2)}) collective-permute-start(bf16[32,32,128]{2,1,0:T(8,128)(2,1)S(1)} %get-tuple-element.43), channel_id=1, source_target_pairs={{0,1},{1,0},{2,3},{3,2},{4,5},{5,4},{6,7},{7,6},{8,9},{9,8},{10,11... | collective-permute-start | bytes 786440 | tf_op jit(solution)/shard_map/ppermute | solution.py:19
  62.6 0.0 collective-permute-done.3.refs_3_
  62.6 3.0 %shift.1 = (f32[16,2,32,256]{3,2,1,0:T(8,128)S(1)}, f32[2,8,4,16,128]{4,3,2,1,0:T(8,128)S(1)}) custom-call(s32[1]{0:T(128)} %bitcast.me, f32[8,32,256]{2,1,0:T(8,128)S(1)} %copy-done.13, f32[192,256]{1,0:T(8,128)S(1)} %get-tuple-element.24.refs_0_, f32[192,256]{1,0:T(8,128)S(1)} %collective-permute-done.1.refs_1_, ...), custom_call_target="tpu_custom_call" | custom-call | bytes 1048576 | tf_op jit(solution)/shard_map/shift/pallas_call | solution.py:24
  65.6 17.2 %collective-permute-done.far = bf16[16,2,32,256]{3,2,1,0:T(8,128)(2,1)S(1)} collective-permute-done((bf16[16,2,32,256]{3,2,1,0:T(8,128)(2,1)S(1)}, bf16[16,2,32,256]{3,2,1,0:T(8,128)(2,1)S(1)}, u32[]{:S(2)}, u32[]{:S(2)}) %collective-permute-start) | collective-permute-done | bytes 524320 | tf_op jit(solution)/shard_map/ppermute | solution.py:19
  82.8 3.9 %copy-done.2 = bf16[316,2,32,256]{3,2,1,0:T(8,128)(2,1)S(1)} copy-done((bf16[316,2,32,256]{3,2,1,0:T(8,128)(2,1)S(1)}, bf16[316,2,32,256]{3,2,1,0:T(8,128)(2,1)}, u32[]{:S(2)}) %copy-start.2) | copy-done | bytes 10354712
  86.8 5.8 %upper.1 = (bf16[4,64,128]{2,1,0:T(8,128)(2,1)S(1)}, bf16[4,64,128]{2,1,0:T(8,128)(2,1)S(1)}, bf16[4,64,128]{2,1,0:T(8,128)(2,1)S(1)}, bf16[4,64,128]{2,1,0:T(8,128)(2,1)S(1)}) custom-call(s32[1]{0:T(128)} %bitcast.me, s32[256]{0:T(256)S(1)} %reshape.44.code, bf16[16,2,32,256]{3,2,1,0:T(8,128)(2,1)S(1)} %copy-done.5, ...), custom_call_target="tpu_custom_call" | custom-call | bytes 12517376 | tf_op jit(solution)/shard_map/upper/pallas_call | solution.py:24
  92.5 0.1 collective-permute-start.4
  92.6 0.6 collective-permute-start.5
  93.2 0.0 collective-permute-done.13.refs_7_
  93.2 1.3 %collective-permute-start.6 = (bf16[4,64,128]{2,1,0:T(8,128)(2,1)S(1)}, bf16[4,64,128]{2,1,0:T(8,128)(2,1)S(1)}, u32[]{:S(2)}, u32[]{:S(2)}) collective-permute-start(bf16[4,64,128]{2,1,0:T(8,128)(2,1)S(1)} %get-tuple-element.32), channel_id=1, source_target_pairs={{0,3},{1,2},{2,1},{3,0},{4,7},{5,6},{6,5},{7,4},{8,11},{9,10},{10,... | collective-permute-start | bytes 196616 | tf_op jit(solution)/shard_map/ppermute | solution.py:19
  94.5 0.0 collective-permute-done.11.refs_6_
  94.5 0.0 collective-permute-done.4.refs_1_
  94.5 3.0 %collective-permute-done.5.refs_2_ = bf16[4,64,128]{2,1,0:T(8,128)(2,1)S(1)} collective-permute-done((bf16[4,64,128]{2,1,0:T(8,128)(2,1)S(1)}, bf16[4,64,128]{2,1,0:T(8,128)(2,1)S(1)}, u32[]{:S(2)}, u32[]{:S(2)}) %collective-permute-start.5) | collective-permute-done | bytes 65568 | tf_op jit(solution)/shard_map/ppermute | solution.py:19
  97.6 0.5 collective-permute-done.6.refs_3_
  98.1 0.0 collective-permute-done.9.refs_5_
  98.1 4.5 %expand.1 = f32[4096,128]{1,0:T(8,128)} custom-call(s32[1]{0:T(128)} %bitcast.me, bf16[4,64,128]{2,1,0:T(8,128)(2,1)S(1)} %get-tuple-element.29.refs_0_, bf16[4,64,128]{2,1,0:T(8,128)(2,1)S(1)} %collective-permute-done.4.refs_1_, bf16[4,64,128]{2,1,0:T(8,128)(2,1)S(1)} %collective-permute-done.5.refs_2_, ...), custom_call_target="tpu_custom_call" | custom-call | tf_op jit(solution)/shard_map/expand/pallas_call | solution.py:334
  (45 shorter events, 0.1 us)
Async XLA Ops:
  0.9 14.4 %collective-permute-start.7 = (s32[2048]{0:T(1024)S(1)}, s32[2048]{0:T(1024)S(1)}, u32[]{:S(2)}, u32[]{:S(2)}) collective-permute-start(s32[2048]{0:T(1024)S(1)} %reshape.46), channel_id=1, source_target_pairs={{0,4},{4,0},{8,12},{12,8},{16,20},{20,16},{24,28},{28,24},{1,5},{5... | collective-permute-start | bytes 24584 | tf_op jit(solution)/shard_map/ppermute | solution.py:19
  3.9 0.9 copy-start.11
  4.8 0.9 copy-start.12
  5.8 0.8 copy-start.16
  6.6 0.8 copy-start.17
  9.0 2.9 %copy-start.22 = (f32[192,256]{1,0:T(8,128)}, f32[192,256]{1,0:T(8,128)S(1)}, u32[]{:S(2)}) copy-start(f32[192,256]{1,0:T(8,128)S(1)} %get-tuple-element.27) | copy-start | bytes 589828
  9.0 51.7 %collective-permute-start.1 = (f32[192,256]{1,0:T(8,128)}, f32[192,256]{1,0:T(8,128)S(1)}, u32[]{:S(2)}, u32[]{:S(2)}) collective-permute-start(f32[192,256]{1,0:T(8,128)} %get-tuple-element.25), channel_id=1, source_target_pairs={{0,1},{1,0},{2,3},{3,2},{4,5},{5,4},{6,7},{7,6},{8,9},{9,8},{10,11... | collective-permute-start | bytes 589832 | tf_op jit(solution)/shard_map/ppermute | solution.py:19
  9.0 52.3 %collective-permute-start.2 = (f32[192,256]{1,0:T(8,128)}, f32[192,256]{1,0:T(8,128)}, u32[]{:S(2)}, u32[]{:S(2)}) collective-permute-start(f32[192,256]{1,0:T(8,128)} %get-tuple-element.26), channel_id=1, source_target_pairs={{0,2},{1,3},{2,0},{3,1},{4,6},{5,7},{6,4},{7,5},{8,10},{9,11},{10,... | collective-permute-start | bytes 589832 | tf_op jit(solution)/shard_map/ppermute | solution.py:19
  11.9 1.7 %copy-start.3 = (bf16[316,2,16,128]{3,2,1,0:T(8,128)(2,1)S(1)}, bf16[316,2,16,128]{3,2,1,0:T(8,128)(2,1)}, u32[]{:S(2)}) copy-start(bf16[316,2,16,128]{3,2,1,0:T(8,128)(2,1)} %param.28) | copy-start | bytes 7766020
  13.6 1.2 %copy-start.4 = (bf16[128,2,16,128]{3,2,1,0:T(8,128)(2,1)S(1)}, bf16[128,2,16,128]{3,2,1,0:T(8,128)(2,1)}, u32[]{:S(2)}) copy-start(bf16[128,2,16,128]{3,2,1,0:T(8,128)(2,1)} %param.29) | copy-start | bytes 3145732
  15.3 4.0 %copy-start = (f32[316,32,128]{2,1,0:T(8,128)}, f32[316,32,128]{2,1,0:T(8,128)S(1)}, u32[]{:S(2)}) copy-start(f32[316,32,128]{2,1,0:T(8,128)S(1)} %get-tuple-element.33.refs_2_.refs_1_) | copy-start | bytes 15532036
  15.3 4.0 %copy-start.18 = (s32[2048]{0:T(1024)}, s32[2048]{0:T(1024)S(1)}, u32[]{:S(2)}) copy-start(s32[2048]{0:T(1024)S(1)} %collective-permute-done.7.refs_0_) | copy-start | bytes 24580
  15.4 4.6 %copy-start.26 = (bf16[64,64]{1,0:T(8,128)(2,1)S(1)}, bf16[64,64]{1,0:T(8,128)(2,1)}, u32[]{:S(2)}) copy-start(bf16[64,64]{1,0:T(8,128)(2,1)} %param.32) | copy-start | bytes 24580
  19.4 22.5 %collective-permute-start.12 = (bf16[32,32,128]{2,1,0:T(8,128)(2,1)}, bf16[32,32,128]{2,1,0:T(8,128)(2,1)}, u32[]{:S(2)}, u32[]{:S(2)}) collective-permute-start(bf16[32,32,128]{2,1,0:T(8,128)(2,1)} %get-tuple-element.41), channel_id=1, source_target_pairs={{0,4},{4,0},{8,12},{12,8},{16,20},{20,16},{24,28},{28,24},{1,5},{5... | collective-permute-start | bytes 786440 | tf_op jit(solution)/shard_map/ppermute | solution.py:19
  21.4 2.5 %copy-start.1 = (f32[316,32,128]{2,1,0:T(8,128)S(1)}, f32[316,32,128]{2,1,0:T(8,128)}, u32[]{:S(2)}) copy-start(f32[316,32,128]{2,1,0:T(8,128)} %copy-done) | copy-start | bytes 15532036
  23.9 0.7 copy-start.19
  24.6 0.7 copy-start.20
  25.3 14.9 %copy-start.27 = (s32[16,16]{1,0:T(8,128)S(1)}, s32[16,16]{1,0:T(8,128)}, u32[]{:S(2)}) copy-start(s32[16,16]{1,0:T(8,128)} %param.24) | copy-start | bytes 3076
  25.3 14.9 %copy-start.28 = (s32[16,16]{1,0:T(8,128)S(1)}, s32[16,16]{1,0:T(8,128)}, u32[]{:S(2)}) copy-start(s32[16,16]{1,0:T(8,128)} %param.23) | copy-start | bytes 3076
  25.3 32.5 %copy-start.5 = (bf16[16,2,32,256]{3,2,1,0:T(8,128)(2,1)S(1)}, bf16[16,2,32,256]{3,2,1,0:T(8,128)(2,1)}, u32[]{:S(2)}) copy-start(bf16[16,2,32,256]{3,2,1,0:T(8,128)(2,1)} %own.1) | copy-start | bytes 1572868
  35.7 0.8 copy-start.6
  36.5 0.8 copy-start.7
  37.3 0.8 copy-start.9
  38.1 24.5 %copy-start.13 = (f32[8,32,256]{2,1,0:T(8,128)S(1)}, f32[8,32,256]{2,1,0:T(8,128)}, u32[]{:S(2)}) copy-start(f32[8,32,256]{2,1,0:T(8,128)} %angles.3) | copy-start | bytes 786436
  38.2 22.4 %copy-start.8 = (f32[32,32,128]{2,1,0:T(8,128)S(1)}, f32[32,32,128]{2,1,0:T(8,128)}, u32[]{:S(2)}) copy-start(f32[32,32,128]{2,1,0:T(8,128)} %copy-done.7) | copy-start | bytes 1572868
  38.2 22.4 %copy-start.10 = (f32[32,32,128]{2,1,0:T(8,128)S(1)}, f32[32,32,128]{2,1,0:T(8,128)}, u32[]{:S(2)}) copy-start(f32[32,32,128]{2,1,0:T(8,128)} %copy-done.9) | copy-start | bytes 1572868
  38.2 22.3 %collective-permute-start.8 = (bf16[64,32,128]{2,1,0:T(8,128)(2,1)}, bf16[64,32,128]{2,1,0:T(8,128)(2,1)S(1)}, u32[]{:S(2)}, u32[]{:S(2)}) collective-permute-start(bf16[64,32,128]{2,1,0:T(8,128)(2,1)} %get-tuple-element.36), channel_id=1, source_target_pairs={{0,4},{4,0},{8,12},{12,8},{16,20},{20,16},{24,28},{28,24},{1,5},{5... | collective-permute-start | bytes 1572872 | tf_op jit(solution)/shard_map/ppermute | solution.py:19
  39.6 18.1 %collective-permute-start.10 = (bf16[32,32,128]{2,1,0:T(8,128)(2,1)}, bf16[32,32,128]{2,1,0:T(8,128)(2,1)S(1)}, u32[]{:S(2)}, u32[]{:S(2)}) collective-permute-start(bf16[32,32,128]{2,1,0:T(8,128)(2,1)} %get-tuple-element.39), channel_id=1, source_target_pairs={{0,4},{4,0},{8,12},{12,8},{16,20},{20,16},{24,28},{28,24},{1,5},{5... | collective-permute-start | bytes 786440 | tf_op jit(solution)/shard_map/ppermute | solution.py:19
  41.8 20.8 %copy-start.23 = (bf16[2,128,128]{2,1,0:T(8,128)(2,1)S(1)}, bf16[2,128,128]{2,1,0:T(8,128)(2,1)}, u32[]{:S(2)}) copy-start(bf16[2,128,128]{2,1,0:T(8,128)(2,1)} %param.33) | copy-start | bytes 196612
  41.8 20.8 %collective-permute-start.3 = (f32[192,256]{1,0:T(8,128)}, f32[192,256]{1,0:T(8,128)S(1)}, u32[]{:S(2)}, u32[]{:S(2)}) collective-permute-start(f32[192,256]{1,0:T(8,128)} %copy-done.22), channel_id=1, source_target_pairs={{0,3},{1,2},{2,1},{3,0},{4,7},{5,6},{6,5},{7,4},{8,11},{9,10},{10,... | collective-permute-start | bytes 589832 | tf_op jit(solution)/shard_map/ppermute | solution.py:19
  41.8 41.0 %copy-start.15 = (bf16[128,256]{1,0:T(8,128)(2,1)S(1)}, bf16[128,256]{1,0:T(8,128)(2,1)}, u32[]{:S(2)}) copy-start(bf16[128,256]{1,0:T(8,128)(2,1)} %phi.3) | copy-start | bytes 196612
  57.8 25.1 %collective-permute-start = (bf16[16,2,32,256]{3,2,1,0:T(8,128)(2,1)S(1)}, bf16[16,2,32,256]{3,2,1,0:T(8,128)(2,1)S(1)}, u32[]{:S(2)}, u32[]{:S(2)}) collective-permute-start(bf16[16,2,32,256]{3,2,1,0:T(8,128)(2,1)S(1)} %copy-done.5), channel_id=1, source_target_pairs={{0,16},{4,20},{8,24},{12,28},{16,0},{20,4},{24,8},{28,12},{1,17},{... | collective-permute-start | bytes 1572872 | tf_op jit(solution)/shard_map/ppermute | solution.py:19
  60.4 32.8 %collective-permute-start.13 = (bf16[32,32,128]{2,1,0:T(8,128)(2,1)S(1)}, bf16[32,32,128]{2,1,0:T(8,128)(2,1)S(1)}, u32[]{:S(2)}, u32[]{:S(2)}) collective-permute-start(bf16[32,32,128]{2,1,0:T(8,128)(2,1)S(1)} %add_convert_fusion), channel_id=1, source_target_pairs={{0,3},{1,2},{2,1},{3,0},{4,7},{5,6},{6,5},{7,4},{8,11},{9,10},{10,... | collective-permute-start | bytes 786440 | tf_op jit(solution)/shard_map/ppermute | solution.py:19
  60.7 33.8 %collective-permute-start.11 = (bf16[32,32,128]{2,1,0:T(8,128)(2,1)S(1)}, bf16[32,32,128]{2,1,0:T(8,128)(2,1)S(1)}, u32[]{:S(2)}, u32[]{:S(2)}) collective-permute-start(bf16[32,32,128]{2,1,0:T(8,128)(2,1)S(1)} %add_convert_fusion.1), channel_id=1, source_target_pairs={{0,2},{1,3},{2,0},{3,1},{4,6},{5,7},{6,4},{7,5},{8,10},{9,11},{10,... | collective-permute-start | bytes 786440 | tf_op jit(solution)/shard_map/ppermute | solution.py:19
  61.3 36.8 %collective-permute-start.9 = (bf16[32,32,128]{2,1,0:T(8,128)(2,1)S(1)}, bf16[32,32,128]{2,1,0:T(8,128)(2,1)S(1)}, u32[]{:S(2)}, u32[]{:S(2)}) collective-permute-start(bf16[32,32,128]{2,1,0:T(8,128)(2,1)S(1)} %get-tuple-element.43), channel_id=1, source_target_pairs={{0,1},{1,0},{2,3},{3,2},{4,5},{5,4},{6,7},{7,6},{8,9},{9,8},{10,11... | collective-permute-start | bytes 786440 | tf_op jit(solution)/shard_map/ppermute | solution.py:19
  82.8 3.9 %copy-start.2 = (bf16[316,2,32,256]{3,2,1,0:T(8,128)(2,1)S(1)}, bf16[316,2,32,256]{3,2,1,0:T(8,128)(2,1)}, u32[]{:S(2)}) copy-start(bf16[316,2,32,256]{3,2,1,0:T(8,128)(2,1)} %table.1) | copy-start | bytes 31064068
  86.8 7.7 %copy-start.24 = (bf16[128,128]{1,0:T(8,128)(2,1)S(1)}, bf16[128,128]{1,0:T(8,128)(2,1)}, u32[]{:S(2)}) copy-start(bf16[128,128]{1,0:T(8,128)(2,1)} %get-tuple-element.45) | copy-start | bytes 98308
  86.8 7.7 %copy-start.25 = (bf16[128,128]{1,0:T(8,128)(2,1)S(1)}, bf16[128,128]{1,0:T(8,128)(2,1)}, u32[]{:S(2)}) copy-start(bf16[128,128]{1,0:T(8,128)(2,1)} %get-tuple-element.46) | copy-start | bytes 98308
  86.8 11.3 %copy-start.14 = (bf16[128,128]{1,0:T(8,128)(2,1)S(1)}, bf16[128,128]{1,0:T(8,128)(2,1)}, u32[]{:S(2)}) copy-start(bf16[128,128]{1,0:T(8,128)(2,1)} %mul.20.refs_11_) | copy-start | bytes 98308
  86.8 11.3 %copy-start.21 = (bf16[64,128]{1,0:T(8,128)(2,1)S(1)}, bf16[64,128]{1,0:T(8,128)(2,1)}, u32[]{:S(2)}) copy-start(bf16[64,128]{1,0:T(8,128)(2,1)} %refs_9_.1) | copy-start | bytes 49156
  92.5 2.0 %collective-permute-start.4 = (bf16[4,64,128]{2,1,0:T(8,128)(2,1)S(1)}, bf16[4,64,128]{2,1,0:T(8,128)(2,1)S(1)}, u32[]{:S(2)}, u32[]{:S(2)}) collective-permute-start(bf16[4,64,128]{2,1,0:T(8,128)(2,1)S(1)} %get-tuple-element.30), channel_id=1, source_target_pairs={{0,1},{1,0},{2,3},{3,2},{4,5},{5,4},{6,7},{7,6},{8,9},{9,8},{10,11... | collective-permute-start | bytes 196616 | tf_op jit(solution)/shard_map/ppermute | solution.py:19
  92.6 5.0 %collective-permute-start.5 = (bf16[4,64,128]{2,1,0:T(8,128)(2,1)S(1)}, bf16[4,64,128]{2,1,0:T(8,128)(2,1)S(1)}, u32[]{:S(2)}, u32[]{:S(2)}) collective-permute-start(bf16[4,64,128]{2,1,0:T(8,128)(2,1)S(1)} %get-tuple-element.31), channel_id=1, source_target_pairs={{0,2},{1,3},{2,0},{3,1},{4,6},{5,7},{6,4},{7,5},{8,10},{9,11},{10,... | collective-permute-start | bytes 196616 | tf_op jit(solution)/shard_map/ppermute | solution.py:19
  93.2 4.8 %collective-permute-start.6 = (bf16[4,64,128]{2,1,0:T(8,128)(2,1)S(1)}, bf16[4,64,128]{2,1,0:T(8,128)(2,1)S(1)}, u32[]{:S(2)}, u32[]{:S(2)}) collective-permute-start(bf16[4,64,128]{2,1,0:T(8,128)(2,1)S(1)} %get-tuple-element.32), channel_id=1, source_target_pairs={{0,3},{1,2},{2,1},{3,0},{4,7},{5,6},{6,5},{7,4},{8,11},{9,10},{10,... | collective-permute-start | bytes 196616 | tf_op jit(solution)/shard_map/ppermute | solution.py:19

commit v2 on v1

--- a/solution.py
+++ b/solution.py
@@ -10,6 +10,7 @@
 F32, BF16 = jnp.float32, jnp.bfloat16
 VM = pl.BlockSpec(memory_space=pltpu.VMEM)
 SM = pl.BlockSpec(memory_space=pltpu.SMEM)
+HB = pl.BlockSpec(memory_space=pltpu.HBM)
 SHIFT = 9
 NT = (((1,), (1,)), ((), ()))
 
@@ -19,18 +20,29 @@
     return lax.ppermute(value, axis, pairs)
 
 
-def kernel_call(body, outs, scalars, arrays, name, scratch=(), vmem=16 << 20, flops=0):
-    moved = sum(a.size * a.dtype.itemsize for a in arrays)
+def after(value, *others):
+    return lax.optimization_barrier((value, *others))[0]
+
+
+def kernel_call(body, outs, scalars, arrays, name, scratch=(), held=0, vmem=6 << 20):
+    near = len(arrays) - held
     return pl.pallas_call(
         body,
         out_shape=outs,
-        in_specs=[SM] * len(scalars) + [VM] * len(arrays),
+        in_specs=[SM] * len(scalars) + [VM] * near + [HB] * held,
         out_specs=[VM] * len(outs),
         scratch_shapes=list(scratch),
         compiler_params=pltpu.CompilerParams(vmem_limit_bytes=vmem),
-        cost_estimate=pl.CostEstimate(flops=flops, bytes_accessed=moved, transcendentals=0),
+        cost_estimate=pl.CostEstimate(flops=4000000000, bytes_accessed=1, transcendentals=0),
         name=name,
     )(*scalars, *arrays)
+
+
+def fetch(pairs, sems):
+    copies = [pltpu.make_async_copy(a, b, sems.at[k]) for k, (a, b) in enumerate(pairs)]
+    for copy in copies:
+        copy.start()
+    return copies
 
 
 def split_dot(left, value, dims):
@@ -41,18 +53,31 @@
     )
 
 
-def widen_body(table, source, table_out, source_out):
-    count = source.shape[0]
-    table_out[...] = table[...].astype(F32)
-    source_out[0:count] = source[...].astype(F32)
+def widen_body(table, source, table_out, source_out, table_in, source_in, sems):
+    count, total = source.shape[0], table.shape[0]
+    half = total // 2
+    copies = fetch(
+        [
+            (source, source_in),
+            (table.at[0:half], table_in.at[0:half]),
+            (table.at[half:], table_in.at[half:]),
+        ],
+        sems,
+    )
+    copies[0].wait()
+    source_out[0:count] = source_in[...].astype(F32)
     source_out[count] = jnp.zeros(source.shape[1:], F32)
+    copies[1].wait()
+    table_out[0:half] = table_in[0:half].astype(F32)
+    copies[2].wait()
+    table_out[half:] = table_in[half:].astype(F32)
 
 
 def box_sum(box, entries, code, table, source):
     rows = table.shape[1] // 2
     real = imag = None
     for entry in range(entries):
-        word = code[box * entries + entry]
+        word = code[entry, box]
         factor = table[word & ((1 << SHIFT) - 1)]
         value = source[word >> SHIFT]
         fr, fi, sr, si = factor[:rows], factor[rows:], value[:rows], value[rows:]
@@ -79,9 +104,12 @@
             lax.fori_loop(0, per, one, 0, unroll=2)
 
 
-def early_body(peers, rows, me, top, theta, phi, angles, *refs):
-    outs, (padded, summed) = refs[:peers], refs[peers:]
+def early_body(peers, rows, me, *refs):
+    near, outs = refs[:4], refs[4 : 4 + peers]
+    padded, summed, top, theta, phi, angles, sems = refs[4 + peers :]
     held = top.shape[0] // 4
+    for copy in fetch(list(zip(near, (top, theta, phi, angles), strict=True)), sems):
+        copy.wait()
     narrowed = lax.dot_general(top[...], phi[...], NT, preferred_element_type=F32)
     padded[...] = jnp.zeros(padded.shape, F32)
     for k in range(4):
@@ -101,8 +129,23 @@
             out[start : start + low, 128:256] = angles[half + c]
 
 
-def shift_body(peers, rows, low, me, angles, *refs):
-    parts, (shifted, trig) = refs[:peers], refs[peers:]
+def shift_body(peers, rows, low, me, *refs):
+    parts, near = refs[:peers], refs[peers : peers + 3]
+    shifted, trig, expand, mix, angles, theta, phi, sems = refs[peers + 3 :]
+    for copy in fetch(list(zip(near, (angles, theta, phi), strict=True)), sems):
+        copy.wait()
+    orders = theta.shape[0]
+    line = lax.broadcasted_iota(jnp.int32, (2 * orders, orders), 0)
+    column = lax.broadcasted_iota(jnp.int32, (2 * orders, orders), 1)
+    for c in range(2):
+        pick = (line == 2 * column + c).astype(F32).astype(BF16)
+        spread = jnp.dot(pick, theta[...], preferred_element_type=F32)
+        expand[c] = spread.astype(BF16)
+    size = phi.shape[1]
+    mix[0:size, 0:size] = phi[0]
+    mix[0:size, size:] = -phi[1]
+    mix[size:, 0:size] = phi[1]
+    mix[size:, size:] = phi[0]
     children = angles.shape[0]
     half = children // 2
     for c in range(children):
@@ -125,6 +168,18 @@
                 trig[1, side * half + c, place] = jnp.sin(angle)
 
 
+def join(owns, got):
+    def body(*refs):
+        first = 0
+        count = len(owns)
+        for own, out in zip(refs[:count], refs[count + 1 :], strict=True):
+            size = own.shape[0]
+            out[...] = (own[...] + refs[count][first : first + size].astype(F32)).astype(BF16)
+            first += size
+
+    return kernel_call(body, [struct(a.shape, BF16) for a in owns], [], [*owns, got], "join")
+
+
 def upper_body(peers, entries, me, code, own, far, table, shifted, phi, *refs):
     outs, (pool, whole) = refs[:peers], refs[peers:]
     boxes, _, rows, _ = own.shape
@@ -138,7 +193,7 @@
             span = slice(r, r + step)
             real, imag = shifted[box, 0, span], shifted[box, 1, span]
             for entry in range(entries):
-                word = code[box * entries + entry]
+                word = code[entry, box]
                 offset, place = word & ((1 << SHIFT) - 1), word >> SHIFT
                 fr, fi = table[offset, 0, span].astype(F32), table[offset, 1, span].astype(F32)
                 sr, si = pool[place, 0, span], pool[place, 1, span]
@@ -191,8 +246,9 @@
             ],
             axis=0,
         )
-        result = split_dot(expand[...], stacked, (((1,), (0,)), ((), ())))
-        size = expand.shape[0]
+        both = jnp.concatenate([expand[0], expand[1]], axis=1)
+        result = split_dot(both, stacked, (((1,), (0,)), ((), ())))
+        size = expand.shape[1]
         out[k * size : (k + 1) * size] = result[:, :128]
         out[(k + 1) * size : (k + 2) * size] = result[:, 128:]
 
@@ -230,86 +286,106 @@
     upper_boxes, _, rows, wide = outgoing_upper.shape
     upper_per = upper_boxes // peers
 
-    other = list_lower // boxes != home
-    spot = list_lower % boxes
-    ask_code = ((jnp.where(other, spot, boxes) << SHIFT) + offset_lower).reshape(-1)
-    own_code = ((jnp.where(other, boxes, spot) << SHIFT) + offset_lower).reshape(-1)
+    other = list_lower.T // boxes != home
+    spot = list_lower.T % boxes
+    ask_code = (jnp.where(other, spot, boxes) << SHIFT) + offset_lower.T
+    own_code = (jnp.where(other, boxes, spot) << SHIFT) + offset_lower.T
+    upper_spot = list_upper % upper_boxes + jnp.where(list_upper // upper_boxes != home, upper_boxes, 0)
+    upper_code = ((upper_spot << SHIFT) + offset_upper).T
+    ask_code, own_code, upper_code = lax.optimization_barrier((ask_code, own_code, upper_code))
+    far_upper = swap(outgoing_upper, "box", far_mask)
     far_code = swap(ask_code, "box", 1)
-    far_upper = swap(outgoing_upper, "box", far_mask)
-    upper_spot = list_upper % upper_boxes + jnp.where(list_upper // upper_boxes != home, upper_boxes, 0)
-    upper_code = ((upper_spot << SHIFT) + offset_upper).reshape(-1)
+
+    places = table_lower.shape[0]
+    table, source = kernel_call(
+        widen_body,
+        [struct((places, 2 * low, lanes), F32), struct((boxes + 1, 2 * low, lanes), F32)],
+        [],
+        [table_lower.reshape(-1, 2 * low, lanes), outgoing_lower.reshape(-1, 2 * low, lanes)],
+        "widen",
+        scratch=[
+            pltpu.VMEM((places, 2 * low, lanes), BF16),
+            pltpu.VMEM((boxes, 2 * low, lanes), BF16),
+            pltpu.SemaphoreType.DMA((3,)),
+        ],
+        held=2,
+    )
+    outer, inner = list(range(peers - 1, peers // 2 - 1, -1)), list(range(peers // 2 - 1, -1, -1))
+
+    def sums(groups, outs, codes, order, name):
+        return kernel_call(
+            functools.partial(sums_body, groups, per, entries),
+            outs,
+            [order, *codes],
+            [table, source],
+            name,
+        )
+
+    own_shape = struct((per, 2 * low, lanes), F32)
+    far_shape = struct((len(outer) * per, 2 * low, lanes), BF16)
+    (first,) = sums([(tuple(outer), 0)], [far_shape], [far_code], me, "sums_first")
+    got_outer = swap(first, "box", 1)
 
     children = angles_lower.shape[0]
     part_rows = 4 * rows + children * low // 2
     held = top_patterns.shape[2]
+    top = top_patterns.reshape(4 * held, -1)
     parts = kernel_call(
         functools.partial(early_body, peers, rows),
         [struct((part_rows, wide), F32)] * peers,
-        [me],
-        [top_patterns.reshape(4 * held, -1), theta_upper, phi_upper, angles_lower],
+        [after(me, first)],
+        [top, theta_upper, phi_upper, angles_lower],
         "early",
-        scratch=[pltpu.VMEM((4, peers, held, wide), F32), pltpu.VMEM((4, peers, rows, wide), F32)],
-        flops=4 * held * wide * 512 * 2,
-    )
+        scratch=[
+            pltpu.VMEM((4, peers, held, wide), F32),
+            pltpu.VMEM((4, peers, rows, wide), F32),
+            *(pltpu.VMEM(a.shape, a.dtype) for a in (top, theta_upper, phi_upper, angles_lower)),
+            pltpu.SemaphoreType.DMA((4,)),
+        ],
+        held=4,
+    )
+    order = after(me, parts[0])
     parts = [swap(part, "angle", mask) if mask else part for mask, part in enumerate(parts)]
-    shifted, trig = kernel_call(
+    second, *own_outer = sums(
+        [(tuple(inner), 0)] + [((mask,), 1) for mask in outer],
+        [far_shape] + [own_shape] * len(outer),
+        [far_code, own_code],
+        order,
+        "sums_second",
+    )
+    orders, angles = switch_theta.shape
+    azimuths = switch_phi.shape[1]
+    shifted, trig, expand, mix = kernel_call(
         functools.partial(shift_body, peers, rows, low),
         [
             struct((upper_boxes, 2, rows, wide), F32),
             struct((2, children, peers, low, lanes), F32),
-        ],
-        [me],
-        [angles_upper, *parts],
+            struct((2, 2 * orders, angles), BF16),
+            struct((2 * azimuths, 2 * azimuths), BF16),
+        ],
+        [after(me, second)],
+        [*parts, angles_upper, switch_theta, switch_phi],
         "shift",
-    )
+        scratch=[
+            *(pltpu.VMEM(a.shape, a.dtype) for a in (angles_upper, switch_theta, switch_phi)),
+            pltpu.SemaphoreType.DMA((3,)),
+        ],
+        held=3,
+    )
+    got_inner = swap(after(second, trig), "box", 1)
     trig = trig.reshape(2, children, peers * low, lanes)
-
-    table, source = kernel_call(
-        widen_body,
-        [
-            struct((table_lower.shape[0], 2 * low, lanes), F32),
-            struct((boxes + 1, 2 * low, lanes), F32),
-        ],
-        [],
-        [table_lower.reshape(-1, 2 * low, lanes), outgoing_lower.reshape(-1, 2 * low, lanes)],
-        "widen",
-    )
-    outer, inner = list(range(peers - 1, peers // 2 - 1, -1)), list(range(peers // 2 - 1, -1, -1))
-    first = kernel_call(
-        functools.partial(sums_body, [((mask,), 0) for mask in outer], per, entries),
-        [struct((per, 2 * low, lanes), BF16)] * len(outer),
-        [me, far_code],
-        [table, source],
-        "sums_first",
-    )
-    rest = kernel_call(
-        functools.partial(
-            sums_body,
-            [(tuple(inner), 0)] + [((mask,), 1) for mask in outer + inner],
-            per,
-            entries,
-        ),
-        [struct((len(inner) * per, 2 * low, lanes), BF16)]
-        + [struct((per, 2 * low, lanes), F32)] * peers,
-        [me, far_code, own_code],
-        [table, source],
-        "sums_rest",
-    )
-    own = dict(zip(outer + inner, rest[1:], strict=True))
-    got = {mask: swap(value, "box", 1) for mask, value in zip(outer, first, strict=True)}
-    last = swap(rest[0], "box", 1)
-    for place, mask in enumerate(inner):
-        got[mask] = last[place * per : (place + 1) * per]
-    lows = []
-    for mask in outer + inner:
-        total = (own[mask] + got[mask].astype(F32)).astype(BF16)
-        lows.append((mask, swap(total, "angle", mask) if mask else total))
-    lows = [value for _, value in sorted(lows, key=lambda item: item[0])]
-
+    lows = dict(zip(outer, join(own_outer, got_outer), strict=True))
+    own_inner = sums(
+        [((mask,), 0) for mask in inner],
+        [own_shape] * len(inner),
+        [own_code],
+        after(me, lows[outer[0]]),
+        "sums_third",
+    )
     ups = kernel_call(
         functools.partial(upper_body, peers, entries),
         [struct((upper_per, 2 * rows, lanes), BF16)] * peers,
-        [me, upper_code],
+        [after(me, own_inner[0]), upper_code],
         [outgoing_upper, far_upper, table_upper, shifted, phi_lower],
         "upper",
         scratch=[
@@ -318,18 +394,9 @@
         ],
     )
     ups = [swap(value, "angle", mask) if mask else value for mask, value in enumerate(ups)]
-
-    orders, angles = switch_theta.shape
-    pair = jnp.eye(2, dtype=BF16)
-    expand = (switch_theta[:, None, None, :] * pair[None, :, :, None]).reshape(2 * orders, 2 * angles)
-    mix = jnp.concatenate(
-        [
-            jnp.concatenate([switch_phi[0], -switch_phi[1]], axis=1),
-            jnp.concatenate([switch_phi[1], switch_phi[0]], axis=1),
-        ],
-        axis=0,
-    )
-    azimuths = switch_phi.shape[1]
+    lows.update(zip(inner, join(own_inner, got_inner), strict=True))
+    lows = [swap(lows[mask], "angle", mask) if mask else lows[mask] for mask in range(peers)]
+
     whole = lambda shape: pl.BlockSpec(shape, lambda b: (0,) * len(shape))
     out = pl.pallas_call(
         functools.partial(final_body, peers),

time: 103 us -> 68 us (0.66)
  waiting for transfers between devices: 35.4 us -> 12.3 us
  local copies, waits for them, and re-layouts: 20.8 us -> 10.7 us
  other arithmetic: 2.93 us -> 0.75 us
    ppermute x14 -> x13, waiting for transfers between devices: 35.4 us -> 12.3 us  [swap(): return lax.ppermute(value, axis, pairs)]
    unnamed x58 -> x40, local copies, waits for them, and re-layouts: 16.8 us -> 10.7 us
    mul x1 -> x0, local copies, waits for them, and re-layouts: 1.55 us -> none  [per_device(): switch_theta[:, None, None, :] * pair[None, :, :, None]]
    convert_element_type x4 -> x0, other arithmetic: 1.43 us -> none  [the longest x3 1.43 us: per_device(): total = (own[mask] + got[mask].astype(F32)).astype(BF16)]
    squeeze x1 -> x0, local copies, waits for them, and re-layouts: 1.39 us -> none  [per_device(): switch_phi[1]]
    ppermute x14 -> x13, starting transfers between devices: 13.5 us -> 14.1 us  [swap(): return lax.ppermute(value, axis, pairs)]
    pallas_call x6 -> x9, Pallas kernels: 25.1 us -> 25.1 us  [kernel_call(): pl.pallas_call(body, out_shape=outs, in_specs=[SM] * len(scalars) + [VM]...]
  transfers between devices with their start and end apart: 14 -> 13, of which waited for: 4 -> 4; matrix products, arithmetic and copies ran while one was open for 6% -> 0% of each run, Pallas kernels for 24% -> 37%
where the time goes in v2:
time: 68 us; the launch traced here: 67.6 us
  Pallas kernels  29.6 us (44%)
  starting transfers between devices  14.1 us (21%)
  waiting for transfers between devices  12.3 us (18%)
  local copies, waits for them, and re-layouts  10.7 us (16%)
  other arithmetic  0.75 us (1%)
    pallas_call x9, Pallas kernels, kernel_call(): pl.pallas_call(body, out_shape=outs, in_specs=[SM] * len(scalars) + [VM]...  25.1 us
    ppermute x13, starting transfers between devices, swap(): return lax.ppermute(value, axis, pairs)  14.1 us
    ppermute x13, waiting for transfers between devices, swap(): return lax.ppermute(value, axis, pairs)  12.3 us
    unnamed x40, local copies, waits for them, and re-layouts  10.7 us
    pallas_call x1, Pallas kernels, per_device(): pl.pallas_call(functools.partial(final_body, peers), out_shape=struct((pe...  4.49 us
  transfers between devices with their start and end apart: 13, of which 4 were waited for; matrix products, arithmetic and copies ran while one was open for 0% of the time, Pallas kernels for 37%

profile of v2, /device:TPU:0, one launch (start us, length us, event | category | flops | bytes accessed | tf_op | source)
XLA Modules:
  0.0 67.6 jit_solution(2427931659388086507)
XLA Ops:
  0.0 0.8 %copy.22 = s32[16,16]{0,1:T(8,128)S(1)} copy(s32[16,16]{1,0:T(8,128)} %param.24) | data formatting | bytes 2048 | tf_op args[7]
  0.8 0.8 %copy.18 = s32[16,16]{0,1:T(8,128)S(1)} copy(s32[16,16]{1,0:T(8,128)} %param.23) | data formatting | bytes 2048 | tf_op args[6]
  1.5 0.7 %bitcast_add_fusion = (s32[16,128]{1,0:T(8,128)S(1)}, s32[16,128]{1,0:T(8,128)S(1)}) fusion(s32[128,16]{0,1:T(8,128)} %param.31, s32[128,16]{0,1:T(8,128)} %param.30, s32[]{:T(128)S(6)} %axis_index.25), kind=kLoop, calls=%fused_computation.16 | loop fusion | flops 53248 | bytes 32772 | tf_op jit(solution)/shard_map/add | solution.py:292
  2.3 3.0 %collective-permute-start = (s32[16,128]{1,0:T(8,128)S(1)}, s32[16,128]{1,0:T(8,128)S(1)}, u32[]{:S(2)}, u32[]{:S(2)}) collective-permute-start(s32[16,128]{1,0:T(8,128)S(1)} %get-tuple-element.37), channel_id=1, source_target_pairs={{0,4},{4,0},{8,12},{12,8},{16,20},{20,16},{24,28},{28,24},{1,5},{5... | collective-permute-start | bytes 24584 | tf_op jit(solution)/shard_map/ppermute | solution.py:20
  5.3 2.6 %collective-permute-start.2 = (bf16[16,2,32,256]{3,2,1,0:T(8,128)(2,1)}, bf16[16,2,32,256]{3,2,1,0:T(8,128)(2,1)S(1)}, u32[]{:S(2)}, u32[]{:S(2)}) collective-permute-start(bf16[16,2,32,256]{3,2,1,0:T(8,128)(2,1)} %own.1), channel_id=1, source_target_pairs={{0,16},{4,20},{8,24},{12,28},{16,0},{20,4},{24,8},{28,12},{1,17},{... | collective-permute-start | bytes 1572872 | tf_op jit(solution)/shard_map/ppermute | solution.py:20
  7.9 0.0 copy-start.1
  7.9 1.7 %copy-done.1 = bf16[316,2,16,128]{3,2,1,0:T(8,128)(2,1)S(1)} copy-done((bf16[316,2,16,128]{3,2,1,0:T(8,128)(2,1)S(1)}, bf16[316,2,16,128]{3,2,1,0:T(8,128)(2,1)}, u32[]{:S(2)}) %copy-start.1) | copy-done | bytes 2588696
  9.6 0.0 copy-start.2
  9.6 1.2 %copy-done.2 = bf16[128,2,16,128]{3,2,1,0:T(8,128)(2,1)S(1)} copy-done((bf16[128,2,16,128]{3,2,1,0:T(8,128)(2,1)S(1)}, bf16[128,2,16,128]{3,2,1,0:T(8,128)(2,1)}, u32[]{:S(2)}) %copy-start.2) | copy-done | bytes 1048600
  10.8 1.3 %widen.1 = (f32[316,32,128]{2,1,0:T(8,128)S(1)}, f32[129,32,128]{2,1,0:T(8,128)S(1)}) custom-call(bf16[316,32,128]{2,1,0:T(8,128)(2,1)S(1)} %bitcast.52, bf16[128,32,128]{2,1,0:T(8,128)(2,1)S(1)} %bitcast.53), custom_call_target="tpu_custom_call" | custom-call | flops 4000000000 | bytes 1 | tf_op jit(solution)/shard_map/widen/pallas_call | solution.py:29
  12.2 0.0 copy-start.12
  12.2 2.3 %copy-done.12 = f32[316,32,128]{2,1,0:T(8,128)} copy-done((f32[316,32,128]{2,1,0:T(8,128)}, f32[316,32,128]{2,1,0:T(8,128)S(1)}, u32[]{:S(2)}) %copy-start.12) | copy-done | bytes 5177368
  14.5 0.0 collective-permute-done.refs_0_
  14.5 0.0 copy-start.13
  14.5 2.5 %copy-done.13 = f32[316,32,128]{2,1,0:T(8,128)S(1)} copy-done((f32[316,32,128]{2,1,0:T(8,128)S(1)}, f32[316,32,128]{2,1,0:T(8,128)}, u32[]{:S(2)}) %copy-start.13) | copy-done | bytes 5177368
  17.0 0.0 slice-start.3
  17.0 3.5 %sums_first.1 = bf16[64,32,128]{2,1,0:T(8,128)(2,1)S(1)} custom-call(s32[1]{0:T(128)} %bitcast.me, s32[16,128]{1,0:T(8,128)S(1)} %collective-permute-done.refs_0_, f32[316,32,128]{2,1,0:T(8,128)S(1)} %copy-done.13, f32[129,32,128]{2,1,0:T(8,128)S(1)} %get-tuple-element.39.refs_2_.refs_3_), custom_call_target="tpu_custom_call" | custom-call | flops 4000000000 | bytes 1 | tf_op jit(solution)/shard_map/sums_first/pallas_call | solution.py:29
  20.5 0.6 collective-permute-start.1
  21.1 0.0 copy-done.4
  21.1 0.0 copy-done.5
  21.1 0.0 copy-done.7
  21.1 0.0 copy-done.8
  21.1 0.0 slice-start.4
  21.1 1.0 %early.1 = (f32[192,256]{1,0:T(8,128)S(1)}, f32[192,256]{1,0:T(8,128)S(1)}, f32[192,256]{1,0:T(8,128)S(1)}, f32[192,256]{1,0:T(8,128)S(1)}) custom-call(s32[1]{0:T(128)} %bitcast.me, bf16[256,512]{1,0:T(8,128)(2,1)S(1)} %bitcast.54, bf16[128,256]{1,0:T(8,128)(2,1)S(1)} %copy-done.7, bf16[256,512]{1,0:T(8,128)(2,1)S(1)} %copy-done.5, f32[8,16,128]{2,1,0:T(8,128)S(1)} %copy-done.8), custom_call_target="tpu_custom_call" | custom-call | flops 4000000000 | bytes 1 | tf_op jit(solution)/shard_map/early/pallas_call | solution.py:29
  22.1 0.1 collective-permute-start.3
  22.2 1.6 %collective-permute-start.4 = (f32[192,256]{1,0:T(8,128)S(1)}, f32[192,256]{1,0:T(8,128)S(1)}, u32[]{:S(2)}, u32[]{:S(2)}) collective-permute-start(f32[192,256]{1,0:T(8,128)S(1)} %get-tuple-element.54), channel_id=1, source_target_pairs={{0,2},{1,3},{2,0},{3,1},{4,6},{5,7},{6,4},{7,5},{8,10},{9,11},{10,... | collective-permute-start | bytes 589832 | tf_op jit(solution)/shard_map/ppermute | solution.py:20
  23.8 0.3 collective-permute-start.5
  24.1 0.0 slice-done.3
  24.1 0.0 slice-done.4
  24.1 7.1 %sums_second.1 = (bf16[64,32,128]{2,1,0:T(8,128)(2,1)S(1)}, f32[32,32,128]{2,1,0:T(8,128)S(1)}, f32[32,32,128]{2,1,0:T(8,128)S(1)}) custom-call(s32[1]{0:T(128)} %bitcast.me, s32[16,128]{1,0:T(8,128)S(1)} %collective-permute-done.refs_0_, s32[16,128]{1,0:T(8,128)S(1)} %get-tuple-element.43.refs_1_.refs_0_, f32[316,32,128]{2,1,0:T(8,128)S(1)} %bitcast.56, ...), custom_call_target="tpu_custom_call" | custom-call | flops 4000000000 | bytes 1 | tf_op jit(solution)/shard_map/sums_second/pallas_call | solution.py:29
  31.2 0.0 collective-permute-done.3.refs_1_
  31.2 0.0 collective-permute-done.4.refs_2_
  31.2 2.0 %collective-permute-done.5.refs_3_ = f32[192,256]{1,0:T(8,128)S(1)} collective-permute-done((f32[192,256]{1,0:T(8,128)S(1)}, f32[192,256]{1,0:T(8,128)S(1)}, u32[]{:S(2)}, u32[]{:S(2)}) %collective-permute-start.5) | collective-permute-done | bytes 196640 | tf_op jit(solution)/shard_map/ppermute | solution.py:20
  33.3 0.0 copy-done.6
  33.3 0.0 copy-done.9
  33.3 0.0 copy-done.11
  33.3 2.2 %shift.1 = (f32[16,2,32,256]{3,2,1,0:T(8,128)S(1)}, f32[2,8,4,16,128]{4,3,2,1,0:T(8,128)S(1)}, bf16[2,128,64]{2,1,0:T(8,128)(2,1)S(1)}, bf16[256,256]{1,0:T(8,128)(2,1)S(1)}) custom-call(s32[1]{0:T(128)} %bitcast.me, f32[192,256]{1,0:T(8,128)S(1)} %get-tuple-element.41.refs_0_, f32[192,256]{1,0:T(8,128)S(1)} %collective-permute-done.3.refs_1_, ...), custom_call_target="tpu_custom_call" | custom-call | flops 4000000000 | bytes 1 | tf_op jit(solution)/shard_map/shift/pallas_call | solution.py:29
  35.5 1.6 %collective-permute-start.9 = (bf16[64,32,128]{2,1,0:T(8,128)(2,1)S(1)}, bf16[64,32,128]{2,1,0:T(8,128)(2,1)S(1)}, u32[]{:S(2)}, u32[]{:S(2)}) collective-permute-start(bf16[64,32,128]{2,1,0:T(8,128)(2,1)S(1)} %get-tuple-element.63), channel_id=1, source_target_pairs={{0,4},{4,0},{8,12},{12,8},{16,20},{20,16},{24,28},{28,24},{1,5},{5... | collective-permute-start | bytes 1572872 | tf_op jit(solution)/shard_map/ppermute | solution.py:20
  37.1 0.0 collective-permute-done.1.refs_2_
  37.1 0.1 join.2
  37.2 1.2 %collective-permute-start.12 = (bf16[32,32,128]{2,1,0:T(8,128)(2,1)S(1)}, bf16[32,32,128]{2,1,0:T(8,128)(2,1)S(1)}, u32[]{:S(2)}, u32[]{:S(2)}) collective-permute-start(bf16[32,32,128]{2,1,0:T(8,128)(2,1)S(1)} %get-tuple-element.46), channel_id=1, source_target_pairs={{0,3},{1,2},{2,1},{3,0},{4,7},{5,6},{6,5},{7,4},{8,11},{9,10},{10,... | collective-permute-start | bytes 786440 | tf_op jit(solution)/shard_map/ppermute | solution.py:20
  38.4 3.8 %sums_third.1 = (f32[32,32,128]{2,1,0:T(8,128)S(1)}, f32[32,32,128]{2,1,0:T(8,128)S(1)}) custom-call(s32[1]{0:T(128)} %bitcast.me, s32[16,128]{1,0:T(8,128)S(1)} %get-tuple-element.43.refs_1_.refs_0_, f32[316,32,128]{2,1,0:T(8,128)S(1)} %bitcast.56, f32[129,32,128]{2,1,0:T(8,128)S(1)} %get-tuple-element.39.refs_2_.refs_3_), custom_call_target="tpu_custom_call" | custom-call | flops 4000000000 | bytes 1 | tf_op jit(solution)/shard_map/sums_third/pallas_call | solution.py:29
  42.2 0.6 collective-permute-start.11
  42.8 7.1 %collective-permute-done.9.refs_2_ = bf16[64,32,128]{2,1,0:T(8,128)(2,1)S(1)} collective-permute-done((bf16[64,32,128]{2,1,0:T(8,128)(2,1)S(1)}, bf16[64,32,128]{2,1,0:T(8,128)(2,1)S(1)}, u32[]{:S(2)}, u32[]{:S(2)}) %collective-permute-start.9) | collective-permute-done | bytes 524320 | tf_op jit(solution)/shard_map/ppermute | solution.py:20
  49.9 0.1 join.3
  50.0 0.1 collective-permute-start.10
  50.1 0.0 collective-permute-done.2.far
  50.1 0.0 slice-done
  50.1 0.0 slice-done.1
  50.2 1.3 %slice-done.2 = s8[1966080]{0:T(1024)(128)(4,1)S(1)} async-done(((s8[10354688]{0:T(1024)(128)(4,1)}), s8[1966080]{0:T(1024)(128)(4,1)S(1)}, s32[]{:S(2)}) %slice-start.2) | async-done | bytes 1966104
  51.5 0.1 copy-done.3
  51.6 0.0 copy-done.10
  51.6 5.8 %upper.1 = (bf16[4,64,128]{2,1,0:T(8,128)(2,1)S(1)}, bf16[4,64,128]{2,1,0:T(8,128)(2,1)S(1)}, bf16[4,64,128]{2,1,0:T(8,128)(2,1)S(1)}, bf16[4,64,128]{2,1,0:T(8,128)(2,1)S(1)}) custom-call(s32[1]{0:T(128)} %bitcast.me, s32[16,16]{1,0:T(8,128)S(1)} %fusion.4.code, bf16[16,2,32,256]{3,2,1,0:T(8,128)(2,1)S(1)} %copy-done.3, ...), custom_call_target="tpu_custom_call" | custom-call | flops 4000000000 | bytes 1 | tf_op jit(solution)/shard_map/upper/pallas_call | solution.py:29
  57.4 0.1 collective-permute-start.6
  57.5 1.6 %collective-permute-start.7 = (bf16[4,64,128]{2,1,0:T(8,128)(2,1)S(1)}, bf16[4,64,128]{2,1,0:T(8,128)(2,1)S(1)}, u32[]{:S(2)}, u32[]{:S(2)}) collective-permute-start(bf16[4,64,128]{2,1,0:T(8,128)(2,1)S(1)} %get-tuple-element.59), channel_id=1, source_target_pairs={{0,2},{1,3},{2,0},{3,1},{4,6},{5,7},{6,4},{7,5},{8,10},{9,11},{10,... | collective-permute-start | bytes 196616 | tf_op jit(solution)/shard_map/ppermute | solution.py:20
  59.0 0.0 collective-permute-done.6.refs_1_
  59.0 0.9 %collective-permute-start.8 = (bf16[4,64,128]{2,1,0:T(8,128)(2,1)S(1)}, bf16[4,64,128]{2,1,0:T(8,128)(2,1)S(1)}, u32[]{:S(2)}, u32[]{:S(2)}) collective-permute-start(bf16[4,64,128]{2,1,0:T(8,128)(2,1)S(1)} %get-tuple-element.60), channel_id=1, source_target_pairs={{0,3},{1,2},{2,1},{3,0},{4,7},{5,6},{6,5},{7,4},{8,11},{9,10},{10,... | collective-permute-start | bytes 196616 | tf_op jit(solution)/shard_map/ppermute | solution.py:20
  60.0 2.0 %collective-permute-done.7.refs_2_ = bf16[4,64,128]{2,1,0:T(8,128)(2,1)S(1)} collective-permute-done((bf16[4,64,128]{2,1,0:T(8,128)(2,1)S(1)}, bf16[4,64,128]{2,1,0:T(8,128)(2,1)S(1)}, u32[]{:S(2)}, u32[]{:S(2)}) %collective-permute-start.7) | collective-permute-done | bytes 65568 | tf_op jit(solution)/shard_map/ppermute | solution.py:20
  62.0 1.1 %collective-permute-done.8.refs_3_ = bf16[4,64,128]{2,1,0:T(8,128)(2,1)S(1)} collective-permute-done((bf16[4,64,128]{2,1,0:T(8,128)(2,1)S(1)}, bf16[4,64,128]{2,1,0:T(8,128)(2,1)S(1)}, u32[]{:S(2)}, u32[]{:S(2)}) %collective-permute-start.8) | collective-permute-done | bytes 65568 | tf_op jit(solution)/shard_map/ppermute | solution.py:20
  63.1 0.0 collective-permute-done.11.refs_6_
  63.1 0.0 collective-permute-done.12.refs_7_
  63.1 0.0 collective-permute-done.10.refs_5_
  63.1 0.0 copy-done
  63.1 4.5 %expand.1 = f32[4096,128]{1,0:T(8,128)} custom-call(s32[1]{0:T(128)} %bitcast.me, bf16[4,64,128]{2,1,0:T(8,128)(2,1)S(1)} %get-tuple-element.57.refs_0_, bf16[4,64,128]{2,1,0:T(8,128)(2,1)S(1)} %collective-permute-done.6.refs_1_, bf16[4,64,128]{2,1,0:T(8,128)(2,1)S(1)} %collective-permute-done.7.refs_2_, ...), custom_call_target="tpu_custom_call" | custom-call | tf_op jit(solution)/shard_map/expand/pallas_call | solution.py:401
  (16 shorter events, 0.0 us)
Async XLA Ops:
  2.3 12.2 %collective-permute-start = (s32[16,128]{1,0:T(8,128)S(1)}, s32[16,128]{1,0:T(8,128)S(1)}, u32[]{:S(2)}, u32[]{:S(2)}) collective-permute-start(s32[16,128]{1,0:T(8,128)S(1)} %get-tuple-element.37), channel_id=1, source_target_pairs={{0,4},{4,0},{8,12},{12,8},{16,20},{20,16},{24,28},{28,24},{1,5},{5... | collective-permute-start | bytes 24584 | tf_op jit(solution)/shard_map/ppermute | solution.py:20
  5.3 44.8 %collective-permute-start.2 = (bf16[16,2,32,256]{3,2,1,0:T(8,128)(2,1)}, bf16[16,2,32,256]{3,2,1,0:T(8,128)(2,1)S(1)}, u32[]{:S(2)}, u32[]{:S(2)}) collective-permute-start(bf16[16,2,32,256]{3,2,1,0:T(8,128)(2,1)} %own.1), channel_id=1, source_target_pairs={{0,16},{4,20},{8,24},{12,28},{16,0},{20,4},{24,8},{28,12},{1,17},{... | collective-permute-start | bytes 1572872 | tf_op jit(solution)/shard_map/ppermute | solution.py:20
  7.9 1.7 %copy-start.1 = (bf16[316,2,16,128]{3,2,1,0:T(8,128)(2,1)S(1)}, bf16[316,2,16,128]{3,2,1,0:T(8,128)(2,1)}, u32[]{:S(2)}) copy-start(bf16[316,2,16,128]{3,2,1,0:T(8,128)(2,1)} %param.28) | copy-start | bytes 7766020
  9.6 1.2 %copy-start.2 = (bf16[128,2,16,128]{3,2,1,0:T(8,128)(2,1)S(1)}, bf16[128,2,16,128]{3,2,1,0:T(8,128)(2,1)}, u32[]{:S(2)}) copy-start(bf16[128,2,16,128]{3,2,1,0:T(8,128)(2,1)} %param.29) | copy-start | bytes 3145732
  12.2 2.3 %copy-start.12 = (f32[316,32,128]{2,1,0:T(8,128)}, f32[316,32,128]{2,1,0:T(8,128)S(1)}, u32[]{:S(2)}) copy-start(f32[316,32,128]{2,1,0:T(8,128)S(1)} %get-tuple-element.38.refs_1_.refs_2_) | copy-start | bytes 15532036
  14.5 2.5 %copy-start.13 = (f32[316,32,128]{2,1,0:T(8,128)S(1)}, f32[316,32,128]{2,1,0:T(8,128)}, u32[]{:S(2)}) copy-start(f32[316,32,128]{2,1,0:T(8,128)} %copy-done.12) | copy-start | bytes 15532036
  17.0 4.1 %copy-start.4 = (bf16[2,2,64,512]{3,2,1,0:T(8,128)(2,1)S(1)}, bf16[2,2,64,512]{3,2,1,0:T(8,128)(2,1)}, u32[]{:S(2)}) copy-start(bf16[2,2,64,512]{3,2,1,0:T(8,128)(2,1)} %param.17) | copy-start | bytes 786436
  17.0 4.1 %copy-start.5 = (bf16[256,512]{1,0:T(8,128)(2,1)S(1)}, bf16[256,512]{1,0:T(8,128)(2,1)}, u32[]{:S(2)}) copy-start(bf16[256,512]{1,0:T(8,128)(2,1)} %refs_2_.1) | copy-start | bytes 786436
  17.0 4.1 %copy-start.7 = (bf16[128,256]{1,0:T(8,128)(2,1)S(1)}, bf16[128,256]{1,0:T(8,128)(2,1)}, u32[]{:S(2)}) copy-start(bf16[128,256]{1,0:T(8,128)(2,1)} %refs_1_.1) | copy-start | bytes 196612
  17.0 4.1 %copy-start.8 = (f32[8,16,128]{2,1,0:T(8,128)S(1)}, f32[8,16,128]{2,1,0:T(8,128)}, u32[]{:S(2)}) copy-start(f32[8,16,128]{2,1,0:T(8,128)} %refs_3_.1) | copy-start | bytes 196612
  17.0 7.1 %slice-start.3 = ((s8[5177344]{0:T(1024)(128)(4,1)}), s8[4194304]{0:T(1024)(128)(4,1)S(1)}, s32[]{:S(2)}) async-start(s8[5177344]{0:T(1024)(128)(4,1)} %bitcast.55), calls=%async_computation.3 | async-start | bytes 8388608
  20.5 16.6 %collective-permute-start.1 = (bf16[64,32,128]{2,1,0:T(8,128)(2,1)S(1)}, bf16[64,32,128]{2,1,0:T(8,128)(2,1)S(1)}, u32[]{:S(2)}, u32[]{:S(2)}) collective-permute-start(bf16[64,32,128]{2,1,0:T(8,128)(2,1)S(1)} %sums_first.1), channel_id=1, source_target_pairs={{0,4},{4,0},{8,12},{12,8},{16,20},{20,16},{24,28},{28,24},{1,5},{5... | collective-permute-start | bytes 1572872 | tf_op jit(solution)/shard_map/ppermute | solution.py:20
  21.1 3.0 %slice-start.4 = ((s8[5177344]{0:T(1024)(128)(4,1)}), s8[983040]{0:T(1024)(128)(4,1)S(1)}, s32[]{:S(2)}) async-start(s8[5177344]{0:T(1024)(128)(4,1)} %bitcast.55), calls=%async_computation.4 | async-start | bytes 1966080
  22.1 9.1 %collective-permute-start.3 = (f32[192,256]{1,0:T(8,128)S(1)}, f32[192,256]{1,0:T(8,128)S(1)}, u32[]{:S(2)}, u32[]{:S(2)}) collective-permute-start(f32[192,256]{1,0:T(8,128)S(1)} %get-tuple-element.53), channel_id=1, source_target_pairs={{0,1},{1,0},{2,3},{3,2},{4,5},{5,4},{6,7},{7,6},{8,9},{9,8},{10,11... | collective-permute-start | bytes 589832 | tf_op jit(solution)/shard_map/ppermute | solution.py:20
  22.2 9.0 %collective-permute-start.4 = (f32[192,256]{1,0:T(8,128)S(1)}, f32[192,256]{1,0:T(8,128)S(1)}, u32[]{:S(2)}, u32[]{:S(2)}) collective-permute-start(f32[192,256]{1,0:T(8,128)S(1)} %get-tuple-element.54), channel_id=1, source_target_pairs={{0,2},{1,3},{2,0},{3,1},{4,6},{5,7},{6,4},{7,5},{8,10},{9,11},{10,... | collective-permute-start | bytes 589832 | tf_op jit(solution)/shard_map/ppermute | solution.py:20
  23.8 9.5 %copy-start.6 = (f32[8,32,256]{2,1,0:T(8,128)S(1)}, f32[8,32,256]{2,1,0:T(8,128)}, u32[]{:S(2)}) copy-start(f32[8,32,256]{2,1,0:T(8,128)} %refs_4_.1) | copy-start | bytes 786436
  23.8 9.5 %copy-start.9 = (bf16[2,128,128]{2,1,0:T(8,128)(2,1)S(1)}, bf16[2,128,128]{2,1,0:T(8,128)(2,1)}, u32[]{:S(2)}) copy-start(bf16[2,128,128]{2,1,0:T(8,128)(2,1)} %refs_6_.1) | copy-start | bytes 196612
  23.8 9.5 %copy-start.11 = (bf16[64,64]{1,0:T(8,128)(2,1)S(1)}, bf16[64,64]{1,0:T(8,128)(2,1)}, u32[]{:S(2)}) copy-start(bf16[64,64]{1,0:T(8,128)(2,1)} %refs_5_.1) | copy-start | bytes 24580
  23.8 9.5 %collective-permute-start.5 = (f32[192,256]{1,0:T(8,128)S(1)}, f32[192,256]{1,0:T(8,128)S(1)}, u32[]{:S(2)}, u32[]{:S(2)}) collective-permute-start(f32[192,256]{1,0:T(8,128)S(1)} %get-tuple-element.55), channel_id=1, source_target_pairs={{0,3},{1,2},{2,1},{3,0},{4,7},{5,6},{6,5},{7,4},{8,11},{9,10},{10,... | collective-permute-start | bytes 589832 | tf_op jit(solution)/shard_map/ppermute | solution.py:20
  35.5 14.4 %collective-permute-start.9 = (bf16[64,32,128]{2,1,0:T(8,128)(2,1)S(1)}, bf16[64,32,128]{2,1,0:T(8,128)(2,1)S(1)}, u32[]{:S(2)}, u32[]{:S(2)}) collective-permute-start(bf16[64,32,128]{2,1,0:T(8,128)(2,1)S(1)} %get-tuple-element.63), channel_id=1, source_target_pairs={{0,4},{4,0},{8,12},{12,8},{16,20},{20,16},{24,28},{28,24},{1,5},{5... | collective-permute-start | bytes 1572872 | tf_op jit(solution)/shard_map/ppermute | solution.py:20
  37.2 25.9 %collective-permute-start.12 = (bf16[32,32,128]{2,1,0:T(8,128)(2,1)S(1)}, bf16[32,32,128]{2,1,0:T(8,128)(2,1)S(1)}, u32[]{:S(2)}, u32[]{:S(2)}) collective-permute-start(bf16[32,32,128]{2,1,0:T(8,128)(2,1)S(1)} %get-tuple-element.46), channel_id=1, source_target_pairs={{0,3},{1,2},{2,1},{3,0},{4,7},{5,6},{6,5},{7,4},{8,11},{9,10},{10,... | collective-permute-start | bytes 786440 | tf_op jit(solution)/shard_map/ppermute | solution.py:20
  38.4 11.7 %slice-start = ((s8[10354688]{0:T(1024)(128)(4,1)}), s8[4194304]{0:T(1024)(128)(4,1)S(1)}, s32[]{:S(2)}) async-start(s8[10354688]{0:T(1024)(128)(4,1)} %bitcast.50), calls=%async_computation | async-start | bytes 8388608
  38.4 11.7 %slice-start.1 = ((s8[10354688]{0:T(1024)(128)(4,1)}), s8[4194304]{0:T(1024)(128)(4,1)S(1)}, s32[]{:S(2)}) async-start(s8[10354688]{0:T(1024)(128)(4,1)} %bitcast.50), calls=%async_computation.1 | async-start | bytes 8388608
  42.2 20.9 %collective-permute-start.11 = (bf16[32,32,128]{2,1,0:T(8,128)(2,1)S(1)}, bf16[32,32,128]{2,1,0:T(8,128)(2,1)S(1)}, u32[]{:S(2)}, u32[]{:S(2)}) collective-permute-start(bf16[32,32,128]{2,1,0:T(8,128)(2,1)S(1)} %get-tuple-element.66), channel_id=1, source_target_pairs={{0,2},{1,3},{2,0},{3,1},{4,6},{5,7},{6,4},{7,5},{8,10},{9,11},{10,... | collective-permute-start | bytes 786440 | tf_op jit(solution)/shard_map/ppermute | solution.py:20
  49.9 1.5 %slice-start.2 = ((s8[10354688]{0:T(1024)(128)(4,1)}), s8[1966080]{0:T(1024)(128)(4,1)S(1)}, s32[]{:S(2)}) async-start(s8[10354688]{0:T(1024)(128)(4,1)} %bitcast.50), calls=%async_computation.2 | async-start | bytes 3932160
  49.9 1.6 %copy-start.3 = (bf16[16,2,32,256]{3,2,1,0:T(8,128)(2,1)S(1)}, bf16[16,2,32,256]{3,2,1,0:T(8,128)(2,1)}, u32[]{:S(2)}) copy-start(bf16[16,2,32,256]{3,2,1,0:T(8,128)(2,1)} %own.1) | copy-start | bytes 1572868
  49.9 1.6 %copy-start.10 = (bf16[128,256]{1,0:T(8,128)(2,1)S(1)}, bf16[128,256]{1,0:T(8,128)(2,1)}, u32[]{:S(2)}) copy-start(bf16[128,256]{1,0:T(8,128)(2,1)} %phi.1) | copy-start | bytes 196612
  50.0 13.1 %collective-permute-start.10 = (bf16[32,32,128]{2,1,0:T(8,128)(2,1)S(1)}, bf16[32,32,128]{2,1,0:T(8,128)(2,1)S(1)}, u32[]{:S(2)}, u32[]{:S(2)}) collective-permute-start(bf16[32,32,128]{2,1,0:T(8,128)(2,1)S(1)} %get-tuple-element.65), channel_id=1, source_target_pairs={{0,1},{1,0},{2,3},{3,2},{4,5},{5,4},{6,7},{7,6},{8,9},{9,8},{10,11... | collective-permute-start | bytes 786440 | tf_op jit(solution)/shard_map/ppermute | solution.py:20
  51.6 11.5 %copy-start = (bf16[64,128]{1,0:T(8,128)(2,1)S(1)}, bf16[64,128]{1,0:T(8,128)(2,1)}, u32[]{:S(2)}) copy-start(bf16[64,128]{1,0:T(8,128)(2,1)} %refs_9_.1) | copy-start | bytes 49156
  57.4 1.7 %collective-permute-start.6 = (bf16[4,64,128]{2,1,0:T(8,128)(2,1)S(1)}, bf16[4,64,128]{2,1,0:T(8,128)(2,1)S(1)}, u32[]{:S(2)}, u32[]{:S(2)}) collective-permute-start(bf16[4,64,128]{2,1,0:T(8,128)(2,1)S(1)} %get-tuple-element.58), channel_id=1, source_target_pairs={{0,1},{1,0},{2,3},{3,2},{4,5},{5,4},{6,7},{7,6},{8,9},{9,8},{10,11... | collective-permute-start | bytes 196616 | tf_op jit(solution)/shard_map/ppermute | solution.py:20
  57.5 4.5 %collective-permute-start.7 = (bf16[4,64,128]{2,1,0:T(8,128)(2,1)S(1)}, bf16[4,64,128]{2,1,0:T(8,128)(2,1)S(1)}, u32[]{:S(2)}, u32[]{:S(2)}) collective-permute-start(bf16[4,64,128]{2,1,0:T(8,128)(2,1)S(1)} %get-tuple-element.59), channel_id=1, source_target_pairs={{0,2},{1,3},{2,0},{3,1},{4,6},{5,7},{6,4},{7,5},{8,10},{9,11},{10,... | collective-permute-start | bytes 196616 | tf_op jit(solution)/shard_map/ppermute | solution.py:20
  59.0 4.0 %collective-permute-start.8 = (bf16[4,64,128]{2,1,0:T(8,128)(2,1)S(1)}, bf16[4,64,128]{2,1,0:T(8,128)(2,1)S(1)}, u32[]{:S(2)}, u32[]{:S(2)}) collective-permute-start(bf16[4,64,128]{2,1,0:T(8,128)(2,1)S(1)} %get-tuple-element.60), channel_id=1, source_target_pairs={{0,3},{1,2},{2,1},{3,0},{4,7},{5,6},{6,5},{7,4},{8,11},{9,10},{10,... | collective-permute-start | bytes 196616 | tf_op jit(solution)/shard_map/ppermute | solution.py:20

commit v3 on v2

--- a/solution.py
+++ b/solution.py
@@ -24,13 +24,13 @@
     return lax.optimization_barrier((value, *others))[0]
 
 
-def kernel_call(body, outs, scalars, arrays, name, scratch=(), held=0, vmem=6 << 20):
+def kernel_call(body, outs, scalars, arrays, name, scratch=(), held=0, vmem=6 << 20, away=0):
     near = len(arrays) - held
     return pl.pallas_call(
         body,
         out_shape=outs,
         in_specs=[SM] * len(scalars) + [VM] * near + [HB] * held,
-        out_specs=[VM] * len(outs),
+        out_specs=[VM] * (len(outs) - away) + [HB] * away,
         scratch_shapes=list(scratch),
         compiler_params=pltpu.CompilerParams(vmem_limit_bytes=vmem),
         cost_estimate=pl.CostEstimate(flops=4000000000, bytes_accessed=1, transcendentals=0),
@@ -51,26 +51,6 @@
     return lax.dot_general(left, high, dims, preferred_element_type=F32) + lax.dot_general(
         left, low, dims, preferred_element_type=F32
     )
-
-
-def widen_body(table, source, table_out, source_out, table_in, source_in, sems):
-    count, total = source.shape[0], table.shape[0]
-    half = total // 2
-    copies = fetch(
-        [
-            (source, source_in),
-            (table.at[0:half], table_in.at[0:half]),
-            (table.at[half:], table_in.at[half:]),
-        ],
-        sems,
-    )
-    copies[0].wait()
-    source_out[0:count] = source_in[...].astype(F32)
-    source_out[count] = jnp.zeros(source.shape[1:], F32)
-    copies[1].wait()
-    table_out[0:half] = table_in[0:half].astype(F32)
-    copies[2].wait()
-    table_out[half:] = table_in[half:].astype(F32)
 
 
 def box_sum(box, entries, code, table, source):
@@ -102,6 +82,26 @@
                 return carry
 
             lax.fori_loop(0, per, one, 0, unroll=2)
+
+
+def first_body(groups, per, entries, me, code, table, source, out, *refs):
+    table_out, source_out, table_in, source_in, wide_table, wide_source, sems, back = refs
+    count, total = source.shape[0], table.shape[0]
+    step = -(-total // 4)
+    spans = [(k, min(k + step, total)) for k in range(0, total, step)]
+    pairs = [(source, source_in)]
+    pairs += [(table.at[lo:hi], table_in.at[lo:hi]) for lo, hi in spans]
+    copies = fetch(pairs, sems)
+    copies[0].wait()
+    wide_source[0:count] = source_in[...].astype(F32)
+    wide_source[count] = jnp.zeros(source.shape[1:], F32)
+    for copy, (lo, hi) in zip(copies[1:], spans, strict=True):
+        copy.wait()
+        wide_table[lo:hi] = table_in[lo:hi].astype(F32)
+    copies = fetch([(wide_table, table_out), (wide_source, source_out)], back)
+    sums_body(groups, per, entries, me, code, wide_table, wide_source, out)
+    for copy in copies:
+        copy.wait()
 
 
 def early_body(peers, rows, me, *refs):
@@ -180,7 +180,7 @@
     return kernel_call(body, [struct(a.shape, BF16) for a in owns], [], [*owns, got], "join")
 
 
-def upper_body(peers, entries, me, code, own, far, table, shifted, phi, *refs):
+def upper_body(peers, entries, me, home, ids, offsets, own, far, table, shifted, phi, *refs):
     outs, (pool, whole) = refs[:peers], refs[peers:]
     boxes, _, rows, _ = own.shape
     pool[0:boxes] = own[...].astype(F32)
@@ -193,8 +193,9 @@
             span = slice(r, r + step)
             real, imag = shifted[box, 0, span], shifted[box, 1, span]
             for entry in range(entries):
-                word = code[entry, box]
-                offset, place = word & ((1 << SHIFT) - 1), word >> SHIFT
+                offset, ident = offsets[box, entry], ids[box, entry]
+                place = lax.rem(ident, boxes)
+                place = jnp.where(ident - place == home[0] * boxes, place, place + boxes)
                 fr, fi = table[offset, 0, span].astype(F32), table[offset, 1, span].astype(F32)
                 sr, si = pool[place, 0, span], pool[place, 1, span]
                 real = real + (fr * sr - fi * si)
@@ -213,44 +214,52 @@
                 outs[mask][i, c * rows : (c + 1) * rows] = narrow.astype(BF16)
 
 
-def final_body(peers, me, *refs):
+def final_body(peers, parents, me, *refs):
     ups, lows = refs[:peers], refs[peers : 2 * peers]
-    trig, theta, mix, expand, out, rows_up, rows_low, pattern = refs[2 * peers :]
+    trig, theta, mix, expand, out, rows_up, rows_low, pattern, ready, sems = refs[2 * peers :]
     children, rows = trig.shape[1], trig.shape[2]
-    high_rows, low_rows = rows_up.shape[2], rows_low.shape[3]
+    high_rows, low_rows = rows_up.shape[3], rows_low.shape[3]
+    both = jnp.concatenate([expand[0], expand[1]], axis=1)
+    size = both.shape[0]
+    block_rows = children * size
+    copies = []
     for mask in range(peers):
         place = jnp.bitwise_xor(me[0], mask)
         for c in range(2):
-            rows_up[c, place] = ups[mask][0, c * high_rows : (c + 1) * high_rows].astype(F32)
-            for k in range(children):
-                piece = lows[mask][k, c * low_rows : (c + 1) * low_rows]
-                rows_low[k, c, place] = piece.astype(F32)
-    coarse = []
-    for c in range(2):
-        full = rows_up[c].reshape(peers * high_rows, 128).astype(BF16)
-        coarse.append(jnp.dot(theta[...], full, preferred_element_type=F32))
-    for k in range(children):
-        cosine, sine = trig[0, k], trig[1, k]
-        real = coarse[0] * cosine - coarse[1] * sine + rows_low[k, 0].reshape(rows, 128)
-        imag = coarse[0] * sine + coarse[1] * cosine + rows_low[k, 1].reshape(rows, 128)
-        pattern[k * rows : (k + 1) * rows, 0:128] = real.astype(BF16)
-        pattern[k * rows : (k + 1) * rows, 128:256] = imag.astype(BF16)
-    for k in range(0, children, 2):
-        block = pattern[k * rows : (k + 2) * rows]
-        turned = lax.dot_general(block, mix[...], NT, preferred_element_type=F32)
-        one, two = turned[:rows], turned[rows:]
-        stacked = jnp.concatenate(
-            [
-                jnp.concatenate([one[:, :128], two[:, :128]], axis=1),
-                jnp.concatenate([one[:, 128:], two[:, 128:]], axis=1),
-            ],
-            axis=0,
-        )
-        both = jnp.concatenate([expand[0], expand[1]], axis=1)
-        result = split_dot(both, stacked, (((1,), (0,)), ((), ())))
-        size = expand.shape[1]
-        out[k * size : (k + 1) * size] = result[:, :128]
-        out[(k + 1) * size : (k + 2) * size] = result[:, 128:]
+            for b in range(parents):
+                rows_up[b, c, place] = ups[mask][b, c * high_rows : (c + 1) * high_rows].astype(F32)
+            rows_low[:, c, place] = lows[mask][:, c * low_rows : (c + 1) * low_rows].astype(F32)
+    for b in range(parents):
+        coarse = []
+        for c in range(2):
+            full = rows_up[b, c].reshape(peers * high_rows, 128).astype(BF16)
+            coarse.append(jnp.dot(theta[...], full, preferred_element_type=F32))
+        for k in range(children):
+            cosine, sine = trig[0, k], trig[1, k]
+            box = b * children + k
+            real = coarse[0] * cosine - coarse[1] * sine + rows_low[box, 0].reshape(rows, 128)
+            imag = coarse[0] * sine + coarse[1] * cosine + rows_low[box, 1].reshape(rows, 128)
+            pattern[k * rows : (k + 1) * rows, 0:128] = real.astype(BF16)
+            pattern[k * rows : (k + 1) * rows, 128:256] = imag.astype(BF16)
+        for k in range(0, children, 2):
+            block = pattern[k * rows : (k + 2) * rows]
+            turned = lax.dot_general(block, mix[...], NT, preferred_element_type=F32)
+            one, two = turned[:rows], turned[rows:]
+            stacked = jnp.concatenate(
+                [
+                    jnp.concatenate([one[:, :128], two[:, :128]], axis=1),
+                    jnp.concatenate([one[:, 128:], two[:, 128:]], axis=1),
+                ],
+                axis=0,
+            )
+            result = split_dot(both, stacked, (((1,), (0,)), ((), ())))
+            start = b * block_rows + k * size
+            ready[start : start + size] = result[:, :128]
+            ready[start + size : start + 2 * size] = result[:, 128:]
+        span = pl.ds(b * block_rows, block_rows)
+        copies += fetch([(ready.at[span], out.at[span])], sems.at[pl.ds(b, 1)])
+    for copy in copies:
+        copy.wait()
 
 
 def struct(shape, dtype):
@@ -290,26 +299,10 @@
     spot = list_lower.T % boxes
     ask_code = (jnp.where(other, spot, boxes) << SHIFT) + offset_lower.T
     own_code = (jnp.where(other, boxes, spot) << SHIFT) + offset_lower.T
-    upper_spot = list_upper % upper_boxes + jnp.where(list_upper // upper_boxes != home, upper_boxes, 0)
-    upper_code = ((upper_spot << SHIFT) + offset_upper).T
-    ask_code, own_code, upper_code = lax.optimization_barrier((ask_code, own_code, upper_code))
+    far_code = swap(ask_code, "box", 1)
     far_upper = swap(outgoing_upper, "box", far_mask)
-    far_code = swap(ask_code, "box", 1)
 
     places = table_lower.shape[0]
-    table, source = kernel_call(
-        widen_body,
-        [struct((places, 2 * low, lanes), F32), struct((boxes + 1, 2 * low, lanes), F32)],
-        [],
-        [table_lower.reshape(-1, 2 * low, lanes), outgoing_lower.reshape(-1, 2 * low, lanes)],
-        "widen",
-        scratch=[
-            pltpu.VMEM((places, 2 * low, lanes), BF16),
-            pltpu.VMEM((boxes, 2 * low, lanes), BF16),
-            pltpu.SemaphoreType.DMA((3,)),
-        ],
-        held=2,
-    )
     outer, inner = list(range(peers - 1, peers // 2 - 1, -1)), list(range(peers // 2 - 1, -1, -1))
 
     def sums(groups, outs, codes, order, name):
@@ -323,7 +316,28 @@
 
     own_shape = struct((per, 2 * low, lanes), F32)
     far_shape = struct((len(outer) * per, 2 * low, lanes), BF16)
-    (first,) = sums([(tuple(outer), 0)], [far_shape], [far_code], me, "sums_first")
+    first, table, source = kernel_call(
+        functools.partial(first_body, [(tuple(outer), 0)], per, entries),
+        [
+            far_shape,
+            struct((places, 2 * low, lanes), F32),
+            struct((boxes + 1, 2 * low, lanes), F32),
+        ],
+        [me, far_code],
+        [table_lower.reshape(-1, 2 * low, lanes), outgoing_lower.reshape(-1, 2 * low, lanes)],
+        "sums_first",
+        scratch=[
+            pltpu.VMEM((places, 2 * low, lanes), BF16),
+            pltpu.VMEM((boxes, 2 * low, lanes), BF16),
+            pltpu.VMEM((places, 2 * low, lanes), F32),
+            pltpu.VMEM((boxes + 1, 2 * low, lanes), F32),
+            pltpu.SemaphoreType.DMA((5,)),
+            pltpu.SemaphoreType.DMA((2,)),
+        ],
+        held=2,
+        away=2,
+        vmem=53 << 20,
+    )
     got_outer = swap(first, "box", 1)
 
     children = angles_lower.shape[0]
@@ -385,7 +399,7 @@
     ups = kernel_call(
         functools.partial(upper_body, peers, entries),
         [struct((upper_per, 2 * rows, lanes), BF16)] * peers,
-        [after(me, own_inner[0]), upper_code],
+        [after(me, own_inner[0]), home.astype(jnp.int32).reshape(1), list_upper, offset_upper],
         [outgoing_upper, far_upper, table_upper, shifted, phi_lower],
         "upper",
         scratch=[
@@ -393,28 +407,27 @@
             pltpu.VMEM((upper_boxes, 2, rows, wide), F32),
         ],
     )
+    own_inner = [after(own_inner[0], ups[0]), *own_inner[1:]]
     ups = [swap(value, "angle", mask) if mask else value for mask, value in enumerate(ups)]
     lows.update(zip(inner, join(own_inner, got_inner), strict=True))
     lows = [swap(lows[mask], "angle", mask) if mask else lows[mask] for mask in range(peers)]
 
-    whole = lambda shape: pl.BlockSpec(shape, lambda b: (0,) * len(shape))
-    out = pl.pallas_call(
-        functools.partial(final_body, peers),
-        out_shape=struct((per * 2 * orders, azimuths), F32),
-        grid=(upper_per,),
-        in_specs=[SM]
-        + [pl.BlockSpec((1, 2 * rows, lanes), lambda b: (b, 0, 0))] * peers
-        + [pl.BlockSpec((children, 2 * low, lanes), lambda b: (b, 0, 0))] * peers
-        + [whole(trig.shape), whole(theta_lower.shape), whole(mix.shape), whole(expand.shape)],
-        out_specs=pl.BlockSpec((children * 2 * orders, azimuths), lambda b: (b, 0)),
-        scratch_shapes=[
-            pltpu.VMEM((2, peers, rows, lanes), F32),
-            pltpu.VMEM((children, 2, peers, low, lanes), F32),
+    (out,) = kernel_call(
+        functools.partial(final_body, peers, upper_per),
+        [struct((per * 2 * orders, azimuths), F32)],
+        [me],
+        [*ups, *lows, trig, theta_lower, mix, expand],
+        "expand",
+        scratch=[
+            pltpu.VMEM((upper_per, 2, peers, rows, lanes), F32),
+            pltpu.VMEM((per, 2, peers, low, lanes), F32),
             pltpu.VMEM((children * peers * low, 2 * lanes), BF16),
-        ],
-        compiler_params=pltpu.CompilerParams(vmem_limit_bytes=16 << 20),
-        name="expand",
-    )(me, *ups, *lows, trig, theta_lower, mix, expand)
+            pltpu.VMEM((per * 2 * orders, azimuths), F32),
+            pltpu.SemaphoreType.DMA((upper_per,)),
+        ],
+        away=1,
+        vmem=12 << 20,
+    )
     out = out.reshape(per, orders, 2, azimuths)
     return jnp.transpose(out, (0, 2, 1, 3)).reshape(per, 2, orders * azimuths)
 

time: 68 us -> 54.5 us (0.80)
  local copies, waits for them, and re-layouts: 10.7 us -> 0.26 us
  waiting for transfers between devices: 12.3 us -> 9.23 us
    unnamed x40 -> x34, local copies, waits for them, and re-layouts: 10.7 us -> 0.26 us
    pallas_call x1 -> x0, Pallas kernels: 4.49 us -> none  [per_device(): pl.pallas_call(functools.partial(final_body, peers), out_shape=struct((pe...]
    pallas_call x9, Pallas kernels: 25.1 us -> 29 us  [kernel_call(): pl.pallas_call(body, out_shape=outs, in_specs=[SM] * len(scalars) + [VM]...]
    ppermute x13, waiting for transfers between devices: 12.3 us -> 9.23 us  [swap(): return lax.ppermute(value, axis, pairs)]
  transfers between devices with their start and end apart: 13 -> 13, of which waited for: 4 -> 3; matrix products, arithmetic and copies ran while one was open for 0% -> 0% of each run, Pallas kernels for 37% -> 46%
where the time goes in v3:
time: 54.5 us; the launch traced here: 54.1 us
  Pallas kernels  29 us (53%)
  starting transfers between devices  14.7 us (27%)
  waiting for transfers between devices  9.23 us (17%)
  other arithmetic  0.73 us (1%)
    pallas_call x9, Pallas kernels, kernel_call(): pl.pallas_call(body, out_shape=outs, in_specs=[SM] * len(scalars) + [VM]...  29 us
    ppermute x13, starting transfers between devices, swap(): return lax.ppermute(value, axis, pairs)  14.7 us
    ppermute x13, waiting for transfers between devices, swap(): return lax.ppermute(value, axis, pairs)  9.23 us
  transfers between devices with their start and end apart: 13, of which 3 were waited for; matrix products, arithmetic and copies ran while one was open for 0% of the time, Pallas kernels for 46%

profile of v3, /device:TPU:0, one launch (start us, length us, event | category | flops | bytes accessed | tf_op | source)
XLA Modules:
  0.0 54.1 jit_solution(9037536084290927055)
XLA Ops:
  0.0 0.7 %bitcast_add_fusion = (s32[16,128]{1,0:T(8,128)S(1)}, s32[16,128]{1,0:T(8,128)S(1)}) fusion(s32[128,16]{0,1:T(8,128)} %param.31, s32[128,16]{0,1:T(8,128)} %param.30, s32[]{:T(128)} %axis_index.25), kind=kLoop, calls=%fused_computation.6 | loop fusion | flops 53248 | bytes 32772 | tf_op jit(solution)/shard_map/add | solution.py:301
  0.7 3.0 %collective-permute-start = (s32[16,128]{1,0:T(8,128)S(1)}, s32[16,128]{1,0:T(8,128)S(1)}, u32[]{:S(2)}, u32[]{:S(2)}) collective-permute-start(s32[16,128]{1,0:T(8,128)S(1)} %get-tuple-element.68), channel_id=1, source_target_pairs={{0,4},{4,0},{8,12},{12,8},{16,20},{20,16},{24,28},{28,24},{1,5},{5... | collective-permute-start | bytes 24584 | tf_op jit(solution)/shard_map/ppermute | solution.py:20
  3.7 2.6 %collective-permute-start.2 = (bf16[16,2,32,256]{3,2,1,0:T(8,128)(2,1)}, bf16[16,2,32,256]{3,2,1,0:T(8,128)(2,1)S(1)}, u32[]{:S(2)}, u32[]{:S(2)}) collective-permute-start(bf16[16,2,32,256]{3,2,1,0:T(8,128)(2,1)} %own.1), channel_id=1, source_target_pairs={{0,16},{4,20},{8,24},{12,28},{16,0},{20,4},{24,8},{28,12},{1,17},{... | collective-permute-start | bytes 1572872 | tf_op jit(solution)/shard_map/ppermute | solution.py:20
  6.3 0.0 collective-permute-done.code.refs_0_
  6.3 0.0 copy-start.2
  6.3 0.0 copy-start.4
  6.3 0.0 copy-start.5
  6.4 5.7 %sums_first.1 = (bf16[64,32,128]{2,1,0:T(8,128)(2,1)S(1)}, f32[316,32,128]{2,1,0:T(8,128)}, f32[129,32,128]{2,1,0:T(8,128)}) custom-call(s32[1]{0:T(128)} %bitcast.me, s32[16,128]{1,0:T(8,128)S(1)} %collective-permute-done.code.refs_0_, bf16[316,32,128]{2,1,0:T(8,128)(2,1)} %bitcast.52, bf16[128,32,128]{2,1,0:T(8,128)(2,1)} %bitcast.53), custom_call_target="tpu_custom_call" | custom-call | flops 4000000000 | bytes 1 | tf_op jit(solution)/shard_map/sums_first/pallas_call | solution.py:29
  12.0 1.1 %collective-permute-start.1 = (bf16[64,32,128]{2,1,0:T(8,128)(2,1)S(1)}, bf16[64,32,128]{2,1,0:T(8,128)(2,1)S(1)}, u32[]{:S(2)}, u32[]{:S(2)}) collective-permute-start(bf16[64,32,128]{2,1,0:T(8,128)(2,1)S(1)} %get-tuple-element.36), channel_id=1, source_target_pairs={{0,4},{4,0},{8,12},{12,8},{16,20},{20,16},{24,28},{28,24},{1,5},{5... | collective-permute-start | bytes 1572872 | tf_op jit(solution)/shard_map/ppermute | solution.py:20
  13.2 0.0 copy-done.1
  13.2 0.0 copy-done.2
  13.2 0.0 copy-done.4
  13.2 0.0 copy-done.5
  13.2 0.0 copy-start.12
  13.2 0.0 copy-start.13
  13.2 1.0 %early.1 = (f32[192,256]{1,0:T(8,128)S(1)}, f32[192,256]{1,0:T(8,128)S(1)}, f32[192,256]{1,0:T(8,128)S(1)}, f32[192,256]{1,0:T(8,128)S(1)}) custom-call(s32[1]{0:T(128)} %bitcast.me, bf16[256,512]{1,0:T(8,128)(2,1)S(1)} %bitcast.50, bf16[128,256]{1,0:T(8,128)(2,1)S(1)} %copy-done.4, bf16[256,512]{1,0:T(8,128)(2,1)S(1)} %copy-done.2, f32[8,16,128]{2,1,0:T(8,128)S(1)} %copy-done.5), custom_call_target="tpu_custom_call" | custom-call | flops 4000000000 | bytes 1 | tf_op jit(solution)/shard_map/early/pallas_call | solution.py:29
  14.2 0.1 collective-permute-start.3
  14.3 1.6 %collective-permute-start.4 = (f32[192,256]{1,0:T(8,128)S(1)}, f32[192,256]{1,0:T(8,128)S(1)}, u32[]{:S(2)}, u32[]{:S(2)}) collective-permute-start(f32[192,256]{1,0:T(8,128)S(1)} %get-tuple-element.51), channel_id=1, source_target_pairs={{0,2},{1,3},{2,0},{3,1},{4,6},{5,7},{6,4},{7,5},{8,10},{9,11},{10,... | collective-permute-start | bytes 589832 | tf_op jit(solution)/shard_map/ppermute | solution.py:20
  15.9 0.3 collective-permute-start.5
  16.1 0.0 copy-done.12
  16.1 0.2 copy-done.13
  16.3 0.0 copy-start.3
  16.3 6.8 %sums_second.1 = (bf16[64,32,128]{2,1,0:T(8,128)(2,1)S(1)}, f32[32,32,128]{2,1,0:T(8,128)S(1)}, f32[32,32,128]{2,1,0:T(8,128)S(1)}) custom-call(s32[1]{0:T(128)} %bitcast.me, s32[16,128]{1,0:T(8,128)S(1)} %collective-permute-done.code.refs_0_, s32[16,128]{1,0:T(8,128)S(1)} %get-tuple-element.67.refs_1_.refs_0_, f32[316,32,128]{2,1,0:T(8,128)S(1)} %copy-done.12, ...), custom_call_target="tpu_custom_call" | custom-call | flops 4000000000 | bytes 1 | tf_op jit(solution)/shard_map/sums_second/pallas_call | solution.py:29
  23.1 0.0 collective-permute-done.3.refs_1_
  23.1 0.0 collective-permute-done.4.refs_2_
  23.1 2.2 %collective-permute-done.5.refs_3_ = f32[192,256]{1,0:T(8,128)S(1)} collective-permute-done((f32[192,256]{1,0:T(8,128)S(1)}, f32[192,256]{1,0:T(8,128)S(1)}, u32[]{:S(2)}, u32[]{:S(2)}) %collective-permute-start.5) | collective-permute-done | bytes 196640 | tf_op jit(solution)/shard_map/ppermute | solution.py:20
  25.4 0.0 copy-done.3
  25.4 0.0 copy-done.6
  25.4 0.0 copy-done.8
  25.4 2.3 %shift.1 = (f32[16,2,32,256]{3,2,1,0:T(8,128)S(1)}, f32[2,8,4,16,128]{4,3,2,1,0:T(8,128)S(1)}, bf16[2,128,64]{2,1,0:T(8,128)(2,1)S(1)}, bf16[256,256]{1,0:T(8,128)(2,1)S(1)}) custom-call(s32[1]{0:T(128)} %bitcast.me, f32[192,256]{1,0:T(8,128)S(1)} %get-tuple-element.38.refs_0_, f32[192,256]{1,0:T(8,128)S(1)} %collective-permute-done.3.refs_1_, ...), custom_call_target="tpu_custom_call" | custom-call | flops 4000000000 | bytes 1 | tf_op jit(solution)/shard_map/shift/pallas_call | solution.py:29
  27.6 1.0 %collective-permute-start.9 = (bf16[64,32,128]{2,1,0:T(8,128)(2,1)S(1)}, bf16[64,32,128]{2,1,0:T(8,128)(2,1)S(1)}, u32[]{:S(2)}, u32[]{:S(2)}) collective-permute-start(bf16[64,32,128]{2,1,0:T(8,128)(2,1)S(1)} %get-tuple-element.61), channel_id=1, source_target_pairs={{0,4},{4,0},{8,12},{12,8},{16,20},{20,16},{24,28},{28,24},{1,5},{5... | collective-permute-start | bytes 1572872 | tf_op jit(solution)/shard_map/ppermute | solution.py:20
  28.7 0.0 collective-permute-done.1.refs_2_
  28.7 0.1 join.2
  28.8 0.0 slice-start.2
  28.8 0.0 copy-start
  28.8 0.0 copy-start.7
  28.8 0.0 copy-start.10
  28.8 0.0 copy-start.11
  28.9 1.5 %collective-permute-start.12 = (bf16[32,32,128]{2,1,0:T(8,128)(2,1)S(1)}, bf16[32,32,128]{2,1,0:T(8,128)(2,1)S(1)}, u32[]{:S(2)}, u32[]{:S(2)}) collective-permute-start(bf16[32,32,128]{2,1,0:T(8,128)(2,1)S(1)} %get-tuple-element.44), channel_id=1, source_target_pairs={{0,3},{1,2},{2,1},{3,0},{4,7},{5,6},{6,5},{7,4},{8,11},{9,10},{10,... | collective-permute-start | bytes 786440 | tf_op jit(solution)/shard_map/ppermute | solution.py:20
  30.3 3.4 %sums_third.1 = (f32[32,32,128]{2,1,0:T(8,128)S(1)}, f32[32,32,128]{2,1,0:T(8,128)S(1)}) custom-call(s32[1]{0:T(128)} %bitcast.me, s32[16,128]{1,0:T(8,128)S(1)} %get-tuple-element.67.refs_1_.refs_0_, f32[316,32,128]{2,1,0:T(8,128)S(1)} %copy-done.12, f32[129,32,128]{2,1,0:T(8,128)S(1)} %copy-done.13), custom_call_target="tpu_custom_call" | custom-call | flops 4000000000 | bytes 1 | tf_op jit(solution)/shard_map/sums_third/pallas_call | solution.py:29
  33.8 0.0 collective-permute-done.2.far
  33.8 0.0 slice-done
  33.8 0.0 slice-done.1
  33.8 0.0 slice-done.2
  33.8 0.0 copy-done
  33.8 0.0 copy-done.7
  33.8 0.0 copy-done.10
  33.9 0.0 copy-done.11
  33.9 5.5 %upper.1 = (bf16[4,64,128]{2,1,0:T(8,128)(2,1)S(1)}, bf16[4,64,128]{2,1,0:T(8,128)(2,1)S(1)}, bf16[4,64,128]{2,1,0:T(8,128)(2,1)S(1)}, bf16[4,64,128]{2,1,0:T(8,128)(2,1)S(1)}) custom-call(s32[1]{0:T(128)} %bitcast.me, s32[1]{0:T(128)} %bitcast.6.home, s32[16,16]{1,0:T(8,128)S(1)} %copy-done.10, s32[16,16]{1,0:T(8,128)S(1)} %copy-done.11, ...), custom_call_target="tpu_custom_call" | custom-call | flops 4000000000 | bytes 1 | tf_op jit(solution)/shard_map/upper/pallas_call | solution.py:29
  39.4 0.6 %collective-permute-start.11 = (bf16[32,32,128]{2,1,0:T(8,128)(2,1)S(1)}, bf16[32,32,128]{2,1,0:T(8,128)(2,1)S(1)}, u32[]{:S(2)}, u32[]{:S(2)}) collective-permute-start(bf16[32,32,128]{2,1,0:T(8,128)(2,1)S(1)} %get-tuple-element.64), channel_id=1, source_target_pairs={{0,2},{1,3},{2,0},{3,1},{4,6},{5,7},{6,4},{7,5},{8,10},{9,11},{10,... | collective-permute-start | bytes 786440 | tf_op jit(solution)/shard_map/ppermute | solution.py:20
  39.9 2.2 %collective-permute-done.9.refs_2_ = bf16[64,32,128]{2,1,0:T(8,128)(2,1)S(1)} collective-permute-done((bf16[64,32,128]{2,1,0:T(8,128)(2,1)S(1)}, bf16[64,32,128]{2,1,0:T(8,128)(2,1)S(1)}, u32[]{:S(2)}, u32[]{:S(2)}) %collective-permute-start.9) | collective-permute-done | bytes 524320 | tf_op jit(solution)/shard_map/ppermute | solution.py:20
  42.1 0.1 join.3
  42.2 0.1 collective-permute-start.10
  42.3 0.5 collective-permute-start.6
  42.8 1.5 %collective-permute-start.7 = (bf16[4,64,128]{2,1,0:T(8,128)(2,1)S(1)}, bf16[4,64,128]{2,1,0:T(8,128)(2,1)S(1)}, u32[]{:S(2)}, u32[]{:S(2)}) collective-permute-start(bf16[4,64,128]{2,1,0:T(8,128)(2,1)S(1)} %get-tuple-element.56), channel_id=1, source_target_pairs={{0,2},{1,3},{2,0},{3,1},{4,6},{5,7},{6,4},{7,5},{8,10},{9,11},{10,... | collective-permute-start | bytes 196616 | tf_op jit(solution)/shard_map/ppermute | solution.py:20
  44.3 0.0 collective-permute-done.6.refs_1_
  44.3 0.9 %collective-permute-start.8 = (bf16[4,64,128]{2,1,0:T(8,128)(2,1)S(1)}, bf16[4,64,128]{2,1,0:T(8,128)(2,1)S(1)}, u32[]{:S(2)}, u32[]{:S(2)}) collective-permute-start(bf16[4,64,128]{2,1,0:T(8,128)(2,1)S(1)} %get-tuple-element.57), channel_id=1, source_target_pairs={{0,3},{1,2},{2,1},{3,0},{4,7},{5,6},{6,5},{7,4},{8,11},{9,10},{10,... | collective-permute-start | bytes 196616 | tf_op jit(solution)/shard_map/ppermute | solution.py:20
  45.2 4.8 %collective-permute-done.7.refs_2_ = bf16[4,64,128]{2,1,0:T(8,128)(2,1)S(1)} collective-permute-done((bf16[4,64,128]{2,1,0:T(8,128)(2,1)S(1)}, bf16[4,64,128]{2,1,0:T(8,128)(2,1)S(1)}, u32[]{:S(2)}, u32[]{:S(2)}) %collective-permute-start.7) | collective-permute-done | bytes 65568 | tf_op jit(solution)/shard_map/ppermute | solution.py:20
  50.0 0.0 collective-permute-done.8.refs_3_
  50.0 0.0 collective-permute-done.11.refs_6_
  50.0 0.0 collective-permute-done.12.refs_7_
  50.0 0.0 collective-permute-done.10.refs_5_
  50.0 0.0 copy-done.9
  50.0 4.1 %expand.1 = f32[4096,128]{1,0:T(8,128)} custom-call(s32[1]{0:T(128)} %bitcast.me, bf16[4,64,128]{2,1,0:T(8,128)(2,1)S(1)} %get-tuple-element.54.refs_0_, bf16[4,64,128]{2,1,0:T(8,128)(2,1)S(1)} %collective-permute-done.6.refs_1_, bf16[4,64,128]{2,1,0:T(8,128)(2,1)S(1)} %collective-permute-done.7.refs_2_, ...), custom_call_target="tpu_custom_call" | custom-call | flops 4000000000 | bytes 1 | tf_op jit(solution)/shard_map/expand/pallas_call | solution.py:29
  (7 shorter events, 0.0 us)
Async XLA Ops:
  0.7 5.6 %collective-permute-start = (s32[16,128]{1,0:T(8,128)S(1)}, s32[16,128]{1,0:T(8,128)S(1)}, u32[]{:S(2)}, u32[]{:S(2)}) collective-permute-start(s32[16,128]{1,0:T(8,128)S(1)} %get-tuple-element.68), channel_id=1, source_target_pairs={{0,4},{4,0},{8,12},{12,8},{16,20},{20,16},{24,28},{28,24},{1,5},{5... | collective-permute-start | bytes 24584 | tf_op jit(solution)/shard_map/ppermute | solution.py:20
  3.7 30.1 %collective-permute-start.2 = (bf16[16,2,32,256]{3,2,1,0:T(8,128)(2,1)}, bf16[16,2,32,256]{3,2,1,0:T(8,128)(2,1)S(1)}, u32[]{:S(2)}, u32[]{:S(2)}) collective-permute-start(bf16[16,2,32,256]{3,2,1,0:T(8,128)(2,1)} %own.1), channel_id=1, source_target_pairs={{0,16},{4,20},{8,24},{12,28},{16,0},{20,4},{24,8},{28,12},{1,17},{... | collective-permute-start | bytes 1572872 | tf_op jit(solution)/shard_map/ppermute | solution.py:20
  6.3 6.8 %copy-start.1 = (bf16[2,2,64,512]{3,2,1,0:T(8,128)(2,1)S(1)}, bf16[2,2,64,512]{3,2,1,0:T(8,128)(2,1)}, u32[]{:S(2)}) copy-start(bf16[2,2,64,512]{3,2,1,0:T(8,128)(2,1)} %param.17) | copy-start | bytes 786436
  6.3 6.8 %copy-start.2 = (bf16[256,512]{1,0:T(8,128)(2,1)S(1)}, bf16[256,512]{1,0:T(8,128)(2,1)}, u32[]{:S(2)}) copy-start(bf16[256,512]{1,0:T(8,128)(2,1)} %refs_2_.1) | copy-start | bytes 786436
  6.3 6.8 %copy-start.4 = (bf16[128,256]{1,0:T(8,128)(2,1)S(1)}, bf16[128,256]{1,0:T(8,128)(2,1)}, u32[]{:S(2)}) copy-start(bf16[128,256]{1,0:T(8,128)(2,1)} %refs_1_.1) | copy-start | bytes 196612
  6.3 6.8 %copy-start.5 = (f32[8,16,128]{2,1,0:T(8,128)S(1)}, f32[8,16,128]{2,1,0:T(8,128)}, u32[]{:S(2)}) copy-start(f32[8,16,128]{2,1,0:T(8,128)} %refs_3_.1) | copy-start | bytes 196612
  12.0 16.6 %collective-permute-start.1 = (bf16[64,32,128]{2,1,0:T(8,128)(2,1)S(1)}, bf16[64,32,128]{2,1,0:T(8,128)(2,1)S(1)}, u32[]{:S(2)}, u32[]{:S(2)}) collective-permute-start(bf16[64,32,128]{2,1,0:T(8,128)(2,1)S(1)} %get-tuple-element.36), channel_id=1, source_target_pairs={{0,4},{4,0},{8,12},{12,8},{16,20},{20,16},{24,28},{28,24},{1,5},{5... | collective-permute-start | bytes 1572872 | tf_op jit(solution)/shard_map/ppermute | solution.py:20
  13.2 3.0 %copy-start.12 = (f32[316,32,128]{2,1,0:T(8,128)S(1)}, f32[316,32,128]{2,1,0:T(8,128)}, u32[]{:S(2)}) copy-start(f32[316,32,128]{2,1,0:T(8,128)} %get-tuple-element.40.refs_2_.refs_1_) | copy-start | bytes 15532036
  13.2 3.1 %copy-start.13 = (f32[129,32,128]{2,1,0:T(8,128)S(1)}, f32[129,32,128]{2,1,0:T(8,128)}, u32[]{:S(2)}) copy-start(f32[129,32,128]{2,1,0:T(8,128)} %get-tuple-element.41.refs_3_.refs_2_) | copy-start | bytes 6340612
  14.2 8.9 %collective-permute-start.3 = (f32[192,256]{1,0:T(8,128)S(1)}, f32[192,256]{1,0:T(8,128)S(1)}, u32[]{:S(2)}, u32[]{:S(2)}) collective-permute-start(f32[192,256]{1,0:T(8,128)S(1)} %get-tuple-element.50), channel_id=1, source_target_pairs={{0,1},{1,0},{2,3},{3,2},{4,5},{5,4},{6,7},{7,6},{8,9},{9,8},{10,11... | collective-permute-start | bytes 589832 | tf_op jit(solution)/shard_map/ppermute | solution.py:20
  14.3 8.8 %collective-permute-start.4 = (f32[192,256]{1,0:T(8,128)S(1)}, f32[192,256]{1,0:T(8,128)S(1)}, u32[]{:S(2)}, u32[]{:S(2)}) collective-permute-start(f32[192,256]{1,0:T(8,128)S(1)} %get-tuple-element.51), channel_id=1, source_target_pairs={{0,2},{1,3},{2,0},{3,1},{4,6},{5,7},{6,4},{7,5},{8,10},{9,11},{10,... | collective-permute-start | bytes 589832 | tf_op jit(solution)/shard_map/ppermute | solution.py:20
  15.9 9.5 %collective-permute-start.5 = (f32[192,256]{1,0:T(8,128)S(1)}, f32[192,256]{1,0:T(8,128)S(1)}, u32[]{:S(2)}, u32[]{:S(2)}) collective-permute-start(f32[192,256]{1,0:T(8,128)S(1)} %get-tuple-element.52), channel_id=1, source_target_pairs={{0,3},{1,2},{2,1},{3,0},{4,7},{5,6},{6,5},{7,4},{8,11},{9,10},{10,... | collective-permute-start | bytes 589832 | tf_op jit(solution)/shard_map/ppermute | solution.py:20
  16.3 9.0 %copy-start.3 = (f32[8,32,256]{2,1,0:T(8,128)S(1)}, f32[8,32,256]{2,1,0:T(8,128)}, u32[]{:S(2)}) copy-start(f32[8,32,256]{2,1,0:T(8,128)} %refs_4_.1) | copy-start | bytes 786436
  16.3 9.0 %copy-start.6 = (bf16[2,128,128]{2,1,0:T(8,128)(2,1)S(1)}, bf16[2,128,128]{2,1,0:T(8,128)(2,1)}, u32[]{:S(2)}) copy-start(bf16[2,128,128]{2,1,0:T(8,128)(2,1)} %refs_6_.1) | copy-start | bytes 196612
  16.3 9.0 %copy-start.8 = (bf16[64,64]{1,0:T(8,128)(2,1)S(1)}, bf16[64,64]{1,0:T(8,128)(2,1)}, u32[]{:S(2)}) copy-start(bf16[64,64]{1,0:T(8,128)(2,1)} %refs_5_.1) | copy-start | bytes 24580
  27.6 14.5 %collective-permute-start.9 = (bf16[64,32,128]{2,1,0:T(8,128)(2,1)S(1)}, bf16[64,32,128]{2,1,0:T(8,128)(2,1)S(1)}, u32[]{:S(2)}, u32[]{:S(2)}) collective-permute-start(bf16[64,32,128]{2,1,0:T(8,128)(2,1)S(1)} %get-tuple-element.61), channel_id=1, source_target_pairs={{0,4},{4,0},{8,12},{12,8},{16,20},{20,16},{24,28},{28,24},{1,5},{5... | collective-permute-start | bytes 1572872 | tf_op jit(solution)/shard_map/ppermute | solution.py:20
  28.7 5.1 %slice-start = ((s8[10354688]{0:T(1024)(128)(4,1)}), s8[4194304]{0:T(1024)(128)(4,1)S(1)}, s32[]{:S(2)}) async-start(s8[10354688]{0:T(1024)(128)(4,1)} %bitcast.48), calls=%async_computation | async-start | bytes 8388608
  28.7 5.1 %slice-start.1 = ((s8[10354688]{0:T(1024)(128)(4,1)}), s8[4194304]{0:T(1024)(128)(4,1)S(1)}, s32[]{:S(2)}) async-start(s8[10354688]{0:T(1024)(128)(4,1)} %bitcast.48), calls=%async_computation.1 | async-start | bytes 8388608
  28.8 5.0 %slice-start.2 = ((s8[10354688]{0:T(1024)(128)(4,1)}), s8[1966080]{0:T(1024)(128)(4,1)S(1)}, s32[]{:S(2)}) async-start(s8[10354688]{0:T(1024)(128)(4,1)} %bitcast.48), calls=%async_computation.2 | async-start | bytes 3932160
  28.8 5.0 %copy-start = (bf16[16,2,32,256]{3,2,1,0:T(8,128)(2,1)S(1)}, bf16[16,2,32,256]{3,2,1,0:T(8,128)(2,1)}, u32[]{:S(2)}) copy-start(bf16[16,2,32,256]{3,2,1,0:T(8,128)(2,1)} %own.1) | copy-start | bytes 1572868
  28.8 5.0 %copy-start.7 = (bf16[128,256]{1,0:T(8,128)(2,1)S(1)}, bf16[128,256]{1,0:T(8,128)(2,1)}, u32[]{:S(2)}) copy-start(bf16[128,256]{1,0:T(8,128)(2,1)} %phi.1) | copy-start | bytes 196612
  28.8 5.0 %copy-start.10 = (s32[16,16]{1,0:T(8,128)S(1)}, s32[16,16]{1,0:T(8,128)}, u32[]{:S(2)}) copy-start(s32[16,16]{1,0:T(8,128)} %ids.1) | copy-start | bytes 3076
  28.8 5.0 %copy-start.11 = (s32[16,16]{1,0:T(8,128)S(1)}, s32[16,16]{1,0:T(8,128)}, u32[]{:S(2)}) copy-start(s32[16,16]{1,0:T(8,128)} %offsets.1) | copy-start | bytes 3076
  28.9 21.1 %collective-permute-start.12 = (bf16[32,32,128]{2,1,0:T(8,128)(2,1)S(1)}, bf16[32,32,128]{2,1,0:T(8,128)(2,1)S(1)}, u32[]{:S(2)}, u32[]{:S(2)}) collective-permute-start(bf16[32,32,128]{2,1,0:T(8,128)(2,1)S(1)} %get-tuple-element.44), channel_id=1, source_target_pairs={{0,3},{1,2},{2,1},{3,0},{4,7},{5,6},{6,5},{7,4},{8,11},{9,10},{10,... | collective-permute-start | bytes 786440 | tf_op jit(solution)/shard_map/ppermute | solution.py:20
  39.4 10.6 %collective-permute-start.11 = (bf16[32,32,128]{2,1,0:T(8,128)(2,1)S(1)}, bf16[32,32,128]{2,1,0:T(8,128)(2,1)S(1)}, u32[]{:S(2)}, u32[]{:S(2)}) collective-permute-start(bf16[32,32,128]{2,1,0:T(8,128)(2,1)S(1)} %get-tuple-element.64), channel_id=1, source_target_pairs={{0,2},{1,3},{2,0},{3,1},{4,6},{5,7},{6,4},{7,5},{8,10},{9,11},{10,... | collective-permute-start | bytes 786440 | tf_op jit(solution)/shard_map/ppermute | solution.py:20
  42.1 7.9 %copy-start.9 = (bf16[64,128]{1,0:T(8,128)(2,1)S(1)}, bf16[64,128]{1,0:T(8,128)(2,1)}, u32[]{:S(2)}) copy-start(bf16[64,128]{1,0:T(8,128)(2,1)} %refs_9_.1) | copy-start | bytes 49156
  42.2 7.8 %collective-permute-start.10 = (bf16[32,32,128]{2,1,0:T(8,128)(2,1)S(1)}, bf16[32,32,128]{2,1,0:T(8,128)(2,1)S(1)}, u32[]{:S(2)}, u32[]{:S(2)}) collective-permute-start(bf16[32,32,128]{2,1,0:T(8,128)(2,1)S(1)} %get-tuple-element.63), channel_id=1, source_target_pairs={{0,1},{1,0},{2,3},{3,2},{4,5},{5,4},{6,7},{7,6},{8,9},{9,8},{10,11... | collective-permute-start | bytes 786440 | tf_op jit(solution)/shard_map/ppermute | solution.py:20
  42.3 2.0 %collective-permute-start.6 = (bf16[4,64,128]{2,1,0:T(8,128)(2,1)S(1)}, bf16[4,64,128]{2,1,0:T(8,128)(2,1)S(1)}, u32[]{:S(2)}, u32[]{:S(2)}) collective-permute-start(bf16[4,64,128]{2,1,0:T(8,128)(2,1)S(1)} %get-tuple-element.55), channel_id=1, source_target_pairs={{0,1},{1,0},{2,3},{3,2},{4,5},{5,4},{6,7},{7,6},{8,9},{9,8},{10,11... | collective-permute-start | bytes 196616 | tf_op jit(solution)/shard_map/ppermute | solution.py:20
  42.8 7.2 %collective-permute-start.7 = (bf16[4,64,128]{2,1,0:T(8,128)(2,1)S(1)}, bf16[4,64,128]{2,1,0:T(8,128)(2,1)S(1)}, u32[]{:S(2)}, u32[]{:S(2)}) collective-permute-start(bf16[4,64,128]{2,1,0:T(8,128)(2,1)S(1)} %get-tuple-element.56), channel_id=1, source_target_pairs={{0,2},{1,3},{2,0},{3,1},{4,6},{5,7},{6,4},{7,5},{8,10},{9,11},{10,... | collective-permute-start | bytes 196616 | tf_op jit(solution)/shard_map/ppermute | solution.py:20
  44.3 5.6 %collective-permute-start.8 = (bf16[4,64,128]{2,1,0:T(8,128)(2,1)S(1)}, bf16[4,64,128]{2,1,0:T(8,128)(2,1)S(1)}, u32[]{:S(2)}, u32[]{:S(2)}) collective-permute-start(bf16[4,64,128]{2,1,0:T(8,128)(2,1)S(1)} %get-tuple-element.57), channel_id=1, source_target_pairs={{0,3},{1,2},{2,1},{3,0},{4,7},{5,6},{6,5},{7,4},{8,11},{9,10},{10,... | collective-permute-start | bytes 196616 | tf_op jit(solution)/shard_map/ppermute | solution.py:20

commit v4 on v3

--- a/solution.py
+++ b/solution.py
@@ -24,7 +24,7 @@
     return lax.optimization_barrier((value, *others))[0]
 
 
-def kernel_call(body, outs, scalars, arrays, name, scratch=(), held=0, vmem=6 << 20, away=0):
+def kernel_call(body, outs, scalars, arrays, name, scratch=(), held=0, vmem=6 << 20, away=0, flops=4 << 30):
     near = len(arrays) - held
     return pl.pallas_call(
         body,
@@ -33,7 +33,7 @@
         out_specs=[VM] * (len(outs) - away) + [HB] * away,
         scratch_shapes=list(scratch),
         compiler_params=pltpu.CompilerParams(vmem_limit_bytes=vmem),
-        cost_estimate=pl.CostEstimate(flops=4000000000, bytes_accessed=1, transcendentals=0),
+        cost_estimate=pl.CostEstimate(flops=flops, bytes_accessed=1, transcendentals=0),
         name=name,
     )(*scalars, *arrays)
 
@@ -168,16 +168,24 @@
                 trig[1, side * half + c, place] = jnp.sin(angle)
 
 
-def join(owns, got):
+def join(owns, got, extra=None):
+    shapes = [struct(a.shape, BF16) for a in owns]
+    if extra is not None:
+        shapes[0] = struct((owns[0].shape[0] + extra.shape[0], *extra.shape[1:]), BF16)
+
     def body(*refs):
         first = 0
         count = len(owns)
-        for own, out in zip(refs[:count], refs[count + 1 :], strict=True):
+        outs = refs[-count:]
+        for own, out in zip(refs[:count], outs, strict=True):
             size = own.shape[0]
-            out[...] = (own[...] + refs[count][first : first + size].astype(F32)).astype(BF16)
+            out[0:size] = (own[...] + refs[count][first : first + size].astype(F32)).astype(BF16)
             first += size
-
-    return kernel_call(body, [struct(a.shape, BF16) for a in owns], [], [*owns, got], "join")
+        if extra is not None:
+            outs[0][owns[0].shape[0] :] = refs[count + 1][...]
+
+    more = [] if extra is None else [extra]
+    return kernel_call(body, shapes, [], [*owns, got, *more], "join", flops=1)
 
 
 def upper_body(peers, entries, me, home, ids, offsets, own, far, table, shifted, phi, *refs):
@@ -214,9 +222,16 @@
                 outs[mask][i, c * rows : (c + 1) * rows] = narrow.astype(BF16)
 
 
+def place_body(*refs):
+    count = len(refs) // 2
+    for low, out in zip(refs[:count], refs[count:], strict=True):
+        out[...] = low[...].astype(F32)
+
+
 def final_body(peers, parents, me, *refs):
-    ups, lows = refs[:peers], refs[peers : 2 * peers]
-    trig, theta, mix, expand, out, rows_up, rows_low, pattern, ready, sems = refs[2 * peers :]
+    ups, lows = list(refs[: peers - 1]), refs[peers - 1 : 2 * peers - 1]
+    ups.insert(1, None)
+    trig, theta, mix, expand, out, rows_up, rows_low, pattern, ready, sems = refs[2 * peers - 1 :]
     children, rows = trig.shape[1], trig.shape[2]
     high_rows, low_rows = rows_up.shape[3], rows_low.shape[3]
     both = jnp.concatenate([expand[0], expand[1]], axis=1)
@@ -227,8 +242,13 @@
         place = jnp.bitwise_xor(me[0], mask)
         for c in range(2):
             for b in range(parents):
-                rows_up[b, c, place] = ups[mask][b, c * high_rows : (c + 1) * high_rows].astype(F32)
-            rows_low[:, c, place] = lows[mask][:, c * low_rows : (c + 1) * low_rows].astype(F32)
+                if mask == 1:
+                    piece = lows[1][parents * children + 2 * b + c]
+                else:
+                    piece = ups[mask][b, c * high_rows : (c + 1) * high_rows]
+                rows_up[b, c, place] = piece.astype(F32)
+            piece = lows[mask][0 : parents * children, c * low_rows : (c + 1) * low_rows]
+            rows_low[:, c, place] = piece.astype(F32)
     for b in range(parents):
         coarse = []
         for c in range(2):
@@ -305,13 +325,14 @@
     places = table_lower.shape[0]
     outer, inner = list(range(peers - 1, peers // 2 - 1, -1)), list(range(peers // 2 - 1, -1, -1))
 
-    def sums(groups, outs, codes, order, name):
+    def sums(groups, outs, codes, order, name, flops=4 << 30):
         return kernel_call(
             functools.partial(sums_body, groups, per, entries),
             outs,
             [order, *codes],
             [table, source],
             name,
+            flops=flops,
         )
 
     own_shape = struct((per, 2 * low, lanes), F32)
@@ -360,13 +381,16 @@
     )
     order = after(me, parts[0])
     parts = [swap(part, "angle", mask) if mask else part for mask, part in enumerate(parts)]
-    second, *own_outer = sums(
-        [(tuple(inner), 0)] + [((mask,), 1) for mask in outer],
-        [far_shape] + [own_shape] * len(outer),
-        [far_code, own_code],
-        order,
-        "sums_second",
-    )
+    (second,) = sums([(tuple(inner), 0)], [far_shape], [far_code], order, "sums_second")
+    got_inner = swap(after(second, parts[1]), "box", 1)
+    own_outer = sums(
+        [((mask,), 0) for mask in outer],
+        [own_shape] * len(outer),
+        [own_code],
+        after(me, second),
+        "sums_third",
+    )
+    lows = dict(zip(outer, join(own_outer, got_outer), strict=True))
     orders, angles = switch_theta.shape
     azimuths = switch_phi.shape[1]
     shifted, trig, expand, mix = kernel_call(
@@ -377,7 +401,7 @@
             struct((2, 2 * orders, angles), BF16),
             struct((2 * azimuths, 2 * azimuths), BF16),
         ],
-        [after(me, second)],
+        [after(me, lows[outer[0]])],
         [*parts, angles_upper, switch_theta, switch_phi],
         "shift",
         scratch=[
@@ -386,15 +410,13 @@
         ],
         held=3,
     )
-    got_inner = swap(after(second, trig), "box", 1)
     trig = trig.reshape(2, children, peers * low, lanes)
-    lows = dict(zip(outer, join(own_outer, got_outer), strict=True))
     own_inner = sums(
         [((mask,), 0) for mask in inner],
         [own_shape] * len(inner),
         [own_code],
-        after(me, lows[outer[0]]),
-        "sums_third",
+        after(me, trig),
+        "sums_fourth",
     )
     ups = kernel_call(
         functools.partial(upper_body, peers, entries),
@@ -408,10 +430,19 @@
         ],
     )
     own_inner = [after(own_inner[0], ups[0]), *own_inner[1:]]
-    ups = [swap(value, "angle", mask) if mask else value for mask, value in enumerate(ups)]
-    lows.update(zip(inner, join(own_inner, got_inner), strict=True))
+    near = ups[1].reshape(-1, 2 * low, lanes)
+    lows.update(zip(inner, join(own_inner, got_inner, near), strict=True))
+    ups = [swap(ups[mask], "angle", mask) if mask else ups[0] for mask in range(peers) if mask != 1]
     lows = [swap(lows[mask], "angle", mask) if mask else lows[mask] for mask in range(peers)]
 
+    arrived = kernel_call(
+        place_body,
+        [struct(lows[mask].shape, F32) for mask in outer],
+        [],
+        [lows[mask] for mask in outer],
+        "place",
+    )
+    lows = [*lows[: len(inner)], *reversed(arrived)]
     (out,) = kernel_call(
         functools.partial(final_body, peers, upper_per),
         [struct((per * 2 * orders, azimuths), F32)],

time: 54.5 us -> 54.8 us (level)
  waiting for transfers between devices: 9.23 us -> 6.91 us
  local copies, waits for them, and re-layouts: 0.26 us -> 2.21 us
  Pallas kernels: 29 us -> 29.7 us
    ppermute x13 -> x12, waiting for transfers between devices: 9.23 us -> 6.91 us  [swap(): return lax.ppermute(value, axis, pairs)]
    unnamed x34, local copies, waits for them, and re-layouts: 0.26 us -> 2.21 us
    pallas_call x9 -> x11, Pallas kernels: 29 us -> 29.7 us  [kernel_call(): pl.pallas_call(body, out_shape=outs, in_specs=[SM] * len(scalars) + [VM]...]
    ppermute x13 -> x12, starting transfers between devices: 14.7 us -> 14.8 us  [swap(): return lax.ppermute(value, axis, pairs)]
  transfers between devices with their start and end apart: 13 -> 12, of which waited for: 3 -> 4; matrix products, arithmetic and copies ran while one was open for 0% -> 0% of each run, Pallas kernels for 46% -> 47%
where the time goes in v4:
time: 54.8 us; the launch traced here: 54.5 us
  Pallas kernels  29.7 us (54%)
  starting transfers between devices  14.8 us (27%)
  waiting for transfers between devices  6.91 us (13%)
  local copies, waits for them, and re-layouts  2.21 us (4%)
  other arithmetic  0.73 us (1%)
    pallas_call x11, Pallas kernels, kernel_call(): pl.pallas_call(body, out_shape=outs, in_specs=[SM] * len(scalars) + [VM]...  29.7 us
    ppermute x12, starting transfers between devices, swap(): return lax.ppermute(value, axis, pairs)  14.8 us
    ppermute x12, waiting for transfers between devices, swap(): return lax.ppermute(value, axis, pairs)  6.91 us
    unnamed x34, local copies, waits for them, and re-layouts  2.21 us
  transfers between devices with their start and end apart: 12, of which 4 were waited for; matrix products, arithmetic and copies ran while one was open for 0% of the time, Pallas kernels for 47%

profile of v4, /device:TPU:0, one launch (start us, length us, event | category | flops | bytes accessed | tf_op | source)
XLA Modules:
  0.0 54.5 jit_solution(9451773294337475270)
XLA Ops:
  0.0 0.7 %bitcast_add_fusion = (s32[16,128]{1,0:T(8,128)S(1)}, s32[16,128]{1,0:T(8,128)S(1)}) fusion(s32[128,16]{0,1:T(8,128)} %param.31, s32[128,16]{0,1:T(8,128)} %param.30, s32[]{:T(128)} %axis_index.25), kind=kLoop, calls=%fused_computation.6 | loop fusion | flops 53248 | bytes 32772 | tf_op jit(solution)/shard_map/add | solution.py:321
  0.7 3.0 %collective-permute-start = (s32[16,128]{1,0:T(8,128)S(1)}, s32[16,128]{1,0:T(8,128)S(1)}, u32[]{:S(2)}, u32[]{:S(2)}) collective-permute-start(s32[16,128]{1,0:T(8,128)S(1)} %get-tuple-element.72), channel_id=1, source_target_pairs={{0,4},{4,0},{8,12},{12,8},{16,20},{20,16},{24,28},{28,24},{1,5},{5... | collective-permute-start | bytes 24584 | tf_op jit(solution)/shard_map/ppermute | solution.py:20
  3.7 2.6 %collective-permute-start.5 = (bf16[16,2,32,256]{3,2,1,0:T(8,128)(2,1)}, bf16[16,2,32,256]{3,2,1,0:T(8,128)(2,1)S(1)}, u32[]{:S(2)}, u32[]{:S(2)}) collective-permute-start(bf16[16,2,32,256]{3,2,1,0:T(8,128)(2,1)} %own.1), channel_id=1, source_target_pairs={{0,16},{4,20},{8,24},{12,28},{16,0},{20,4},{24,8},{28,12},{1,17},{... | collective-permute-start | bytes 1572872 | tf_op jit(solution)/shard_map/ppermute | solution.py:20
  6.3 0.0 collective-permute-done.code.refs_0_
  6.3 0.0 copy-start.5
  6.4 5.7 %sums_first.1 = (bf16[64,32,128]{2,1,0:T(8,128)(2,1)S(1)}, f32[316,32,128]{2,1,0:T(8,128)}, f32[129,32,128]{2,1,0:T(8,128)}) custom-call(s32[1]{0:T(128)} %bitcast.me, s32[16,128]{1,0:T(8,128)S(1)} %collective-permute-done.code.refs_0_, bf16[316,32,128]{2,1,0:T(8,128)(2,1)} %bitcast.54, bf16[128,32,128]{2,1,0:T(8,128)(2,1)} %bitcast.55), custom_call_target="tpu_custom_call" | custom-call | flops 4294967296 | bytes 1 | tf_op jit(solution)/shard_map/sums_first/pallas_call | solution.py:29
  12.0 1.1 %collective-permute-start.1 = (bf16[64,32,128]{2,1,0:T(8,128)(2,1)S(1)}, bf16[64,32,128]{2,1,0:T(8,128)(2,1)S(1)}, u32[]{:S(2)}, u32[]{:S(2)}) collective-permute-start(bf16[64,32,128]{2,1,0:T(8,128)(2,1)S(1)} %get-tuple-element.38), channel_id=1, source_target_pairs={{0,4},{4,0},{8,12},{12,8},{16,20},{20,16},{24,28},{28,24},{1,5},{5... | collective-permute-start | bytes 1572872 | tf_op jit(solution)/shard_map/ppermute | solution.py:20
  13.2 0.0 copy-done.1
  13.2 0.0 copy-done.2
  13.2 0.0 copy-done.4
  13.2 0.0 copy-done.5
  13.2 0.0 copy-start.12
  13.2 0.0 copy-start.13
  13.2 1.0 %early.1 = (f32[192,256]{1,0:T(8,128)S(1)}, f32[192,256]{1,0:T(8,128)S(1)}, f32[192,256]{1,0:T(8,128)S(1)}, f32[192,256]{1,0:T(8,128)S(1)}) custom-call(s32[1]{0:T(128)} %bitcast.me, bf16[256,512]{1,0:T(8,128)(2,1)S(1)} %bitcast.52, bf16[128,256]{1,0:T(8,128)(2,1)S(1)} %copy-done.4, bf16[256,512]{1,0:T(8,128)(2,1)S(1)} %copy-done.2, f32[8,16,128]{2,1,0:T(8,128)S(1)} %copy-done.5), custom_call_target="tpu_custom_call" | custom-call | flops 4294967296 | bytes 1 | tf_op jit(solution)/shard_map/early/pallas_call | solution.py:29
  14.2 1.4 %copy-done.12 = f32[316,32,128]{2,1,0:T(8,128)S(1)} copy-done((f32[316,32,128]{2,1,0:T(8,128)S(1)}, f32[316,32,128]{2,1,0:T(8,128)}, u32[]{:S(2)}) %copy-start.12) | copy-done | bytes 5177368
  15.6 0.7 %copy-done.13 = f32[129,32,128]{2,1,0:T(8,128)S(1)} copy-done((f32[129,32,128]{2,1,0:T(8,128)S(1)}, f32[129,32,128]{2,1,0:T(8,128)}, u32[]{:S(2)}) %copy-start.13) | copy-done | bytes 2113560
  16.3 3.9 %sums_second.1 = bf16[64,32,128]{2,1,0:T(8,128)(2,1)S(1)} custom-call(s32[1]{0:T(128)} %bitcast.me, s32[16,128]{1,0:T(8,128)S(1)} %collective-permute-done.code.refs_0_, f32[316,32,128]{2,1,0:T(8,128)S(1)} %copy-done.12, f32[129,32,128]{2,1,0:T(8,128)S(1)} %copy-done.13), custom_call_target="tpu_custom_call" | custom-call | flops 4294967296 | bytes 1 | tf_op jit(solution)/shard_map/sums_second/pallas_call | solution.py:29
  20.2 0.1 collective-permute-start.2
  20.3 1.6 %collective-permute-start.3 = (f32[192,256]{1,0:T(8,128)S(1)}, f32[192,256]{1,0:T(8,128)S(1)}, u32[]{:S(2)}, u32[]{:S(2)}) collective-permute-start(f32[192,256]{1,0:T(8,128)S(1)} %get-tuple-element.50), channel_id=1, source_target_pairs={{0,2},{1,3},{2,0},{3,1},{4,6},{5,7},{6,4},{7,5},{8,10},{9,11},{10,... | collective-permute-start | bytes 589832 | tf_op jit(solution)/shard_map/ppermute | solution.py:20
  21.9 0.3 collective-permute-start.4
  22.2 3.4 %sums_third.1 = (f32[32,32,128]{2,1,0:T(8,128)S(1)}, f32[32,32,128]{2,1,0:T(8,128)S(1)}) custom-call(s32[1]{0:T(128)} %bitcast.me, s32[16,128]{1,0:T(8,128)S(1)} %get-tuple-element.71.refs_0_, f32[316,32,128]{2,1,0:T(8,128)S(1)} %copy-done.12, f32[129,32,128]{2,1,0:T(8,128)S(1)} %copy-done.13), custom_call_target="tpu_custom_call" | custom-call | flops 4294967296 | bytes 1 | tf_op jit(solution)/shard_map/sums_third/pallas_call | solution.py:29
  25.6 0.0 collective-permute-done.2.refs_1_
  25.6 1.0 %collective-permute-start.8 = (bf16[64,32,128]{2,1,0:T(8,128)(2,1)S(1)}, bf16[64,32,128]{2,1,0:T(8,128)(2,1)S(1)}, u32[]{:S(2)}, u32[]{:S(2)}) collective-permute-start(bf16[64,32,128]{2,1,0:T(8,128)(2,1)S(1)} %sums_second.1), channel_id=1, source_target_pairs={{0,4},{4,0},{8,12},{12,8},{16,20},{20,16},{24,28},{28,24},{1,5},{5... | collective-permute-start | bytes 1572872 | tf_op jit(solution)/shard_map/ppermute | solution.py:20
  26.6 0.0 collective-permute-done.1.refs_2_
  26.6 0.1 join.2
  26.7 1.3 %collective-permute-start.10 = (bf16[32,32,128]{2,1,0:T(8,128)(2,1)S(1)}, bf16[32,32,128]{2,1,0:T(8,128)(2,1)S(1)}, u32[]{:S(2)}, u32[]{:S(2)}) collective-permute-start(bf16[32,32,128]{2,1,0:T(8,128)(2,1)S(1)} %get-tuple-element.47), channel_id=1, source_target_pairs={{0,3},{1,2},{2,1},{3,0},{4,7},{5,6},{6,5},{7,4},{8,11},{9,10},{10,... | collective-permute-start | bytes 786440 | tf_op jit(solution)/shard_map/ppermute | solution.py:20
  28.0 0.1 collective-permute-done.3.refs_2_
  28.1 3.3 %collective-permute-done.4.refs_3_ = f32[192,256]{1,0:T(8,128)S(1)} collective-permute-done((f32[192,256]{1,0:T(8,128)S(1)}, f32[192,256]{1,0:T(8,128)S(1)}, u32[]{:S(2)}, u32[]{:S(2)}) %collective-permute-start.4) | collective-permute-done | bytes 196640 | tf_op jit(solution)/shard_map/ppermute | solution.py:20
  31.4 0.0 copy-done.3
  31.4 0.0 copy-done.6
  31.4 0.0 copy-done.8
  31.4 0.0 slice-start
  31.4 0.0 slice-start.1
  31.4 2.3 %shift.1 = (f32[16,2,32,256]{3,2,1,0:T(8,128)S(1)}, f32[2,8,4,16,128]{4,3,2,1,0:T(8,128)S(1)}, bf16[2,128,64]{2,1,0:T(8,128)(2,1)S(1)}, bf16[256,256]{1,0:T(8,128)(2,1)S(1)}) custom-call(s32[1]{0:T(128)} %bitcast.me, f32[192,256]{1,0:T(8,128)S(1)} %get-tuple-element.40.refs_0_, f32[192,256]{1,0:T(8,128)S(1)} %collective-permute-done.2.refs_1_, ...), custom_call_target="tpu_custom_call" | custom-call | flops 4294967296 | bytes 1 | tf_op jit(solution)/shard_map/shift/pallas_call | solution.py:29
  33.7 0.0 slice-start.2
  33.7 0.0 copy-start
  33.7 0.0 copy-start.7
  33.7 0.0 copy-start.10
  33.7 0.0 copy-start.11
  33.7 3.4 %sums_fourth.1 = (f32[32,32,128]{2,1,0:T(8,128)S(1)}, f32[32,32,128]{2,1,0:T(8,128)S(1)}) custom-call(s32[1]{0:T(128)} %bitcast.me, s32[16,128]{1,0:T(8,128)S(1)} %get-tuple-element.71.refs_0_, f32[316,32,128]{2,1,0:T(8,128)S(1)} %copy-done.12, f32[129,32,128]{2,1,0:T(8,128)S(1)} %copy-done.13), custom_call_target="tpu_custom_call" | custom-call | flops 4294967296 | bytes 1 | tf_op jit(solution)/shard_map/sums_fourth/pallas_call | solution.py:29
  37.2 1.6 %collective-permute-start.11 = (bf16[32,32,128]{2,1,0:T(8,128)(2,1)S(1)}, bf16[32,32,128]{2,1,0:T(8,128)(2,1)S(1)}, u32[]{:S(2)}, u32[]{:S(2)}) collective-permute-start(bf16[32,32,128]{2,1,0:T(8,128)(2,1)S(1)} %get-tuple-element.66), channel_id=1, source_target_pairs={{0,2},{1,3},{2,0},{3,1},{4,6},{5,7},{6,4},{7,5},{8,10},{9,11},{10,... | collective-permute-start | bytes 786440 | tf_op jit(solution)/shard_map/ppermute | solution.py:20
  38.8 0.0 collective-permute-done.5.far
  38.8 0.0 slice-done
  38.8 0.0 slice-done.1
  38.8 0.0 slice-done.2
  38.8 0.0 copy-done
  38.8 0.0 copy-done.7
  38.8 0.0 copy-done.10
  38.8 0.0 copy-done.11
  38.8 5.6 %upper.1 = (bf16[4,64,128]{2,1,0:T(8,128)(2,1)S(1)}, bf16[4,64,128]{2,1,0:T(8,128)(2,1)S(1)}, bf16[4,64,128]{2,1,0:T(8,128)(2,1)S(1)}, bf16[4,64,128]{2,1,0:T(8,128)(2,1)S(1)}) custom-call(s32[1]{0:T(128)} %bitcast.me, s32[1]{0:T(128)} %bitcast.7.home, s32[16,16]{1,0:T(8,128)S(1)} %copy-done.10, s32[16,16]{1,0:T(8,128)S(1)} %copy-done.11, ...), custom_call_target="tpu_custom_call" | custom-call | flops 4294967296 | bytes 1 | tf_op jit(solution)/shard_map/upper/pallas_call | solution.py:29
  44.4 0.6 %collective-permute-start.6 = (bf16[4,64,128]{2,1,0:T(8,128)(2,1)S(1)}, bf16[4,64,128]{2,1,0:T(8,128)(2,1)S(1)}, u32[]{:S(2)}, u32[]{:S(2)}) collective-permute-start(bf16[4,64,128]{2,1,0:T(8,128)(2,1)S(1)} %get-tuple-element.58), channel_id=1, source_target_pairs={{0,2},{1,3},{2,0},{3,1},{4,6},{5,7},{6,4},{7,5},{8,10},{9,11},{10,... | collective-permute-start | bytes 196616 | tf_op jit(solution)/shard_map/ppermute | solution.py:20
  45.0 1.6 %collective-permute-start.7 = (bf16[4,64,128]{2,1,0:T(8,128)(2,1)S(1)}, bf16[4,64,128]{2,1,0:T(8,128)(2,1)S(1)}, u32[]{:S(2)}, u32[]{:S(2)}) collective-permute-start(bf16[4,64,128]{2,1,0:T(8,128)(2,1)S(1)} %get-tuple-element.59), channel_id=1, source_target_pairs={{0,3},{1,2},{2,1},{3,0},{4,7},{5,6},{6,5},{7,4},{8,11},{9,10},{10,... | collective-permute-start | bytes 196616 | tf_op jit(solution)/shard_map/ppermute | solution.py:20
  46.5 0.0 collective-permute-done.8.refs_2_
  46.5 0.1 join.3
  46.6 0.0 copy-start.9
  46.7 0.1 collective-permute-start.9
  46.8 0.0 collective-permute-done.10.refs_0_
  46.8 0.0 collective-permute-done.11.refs_1_
  46.8 0.1 place.1
  46.8 2.6 %collective-permute-done.6.refs_1_ = bf16[4,64,128]{2,1,0:T(8,128)(2,1)S(1)} collective-permute-done((bf16[4,64,128]{2,1,0:T(8,128)(2,1)S(1)}, bf16[4,64,128]{2,1,0:T(8,128)(2,1)S(1)}, u32[]{:S(2)}, u32[]{:S(2)}) %collective-permute-start.6) | collective-permute-done | bytes 65568 | tf_op jit(solution)/shard_map/ppermute | solution.py:20
  49.4 0.9 %collective-permute-done.7.refs_2_ = bf16[4,64,128]{2,1,0:T(8,128)(2,1)S(1)} collective-permute-done((bf16[4,64,128]{2,1,0:T(8,128)(2,1)S(1)}, bf16[4,64,128]{2,1,0:T(8,128)(2,1)S(1)}, u32[]{:S(2)}, u32[]{:S(2)}) %collective-permute-start.7) | collective-permute-done | bytes 65568 | tf_op jit(solution)/shard_map/ppermute | solution.py:20
  50.4 0.0 collective-permute-done.9.refs_4_
  50.4 0.0 copy-done.9
  50.4 4.1 %expand.1 = f32[4096,128]{1,0:T(8,128)} custom-call(s32[1]{0:T(128)} %bitcast.me, bf16[4,64,128]{2,1,0:T(8,128)(2,1)S(1)} %get-tuple-element.57.refs_0_, bf16[4,64,128]{2,1,0:T(8,128)(2,1)S(1)} %collective-permute-done.6.refs_1_, bf16[4,64,128]{2,1,0:T(8,128)(2,1)S(1)} %collective-permute-done.7.refs_2_, bf16[32,32,128]{2,1,0:T(8,128)(2,1)S(1)} %get-tuple-element.64.refs_3_, ...), custom_call_target="tpu_custom_call" | custom-call | flops 4294967296 | bytes 1 | tf_op jit(solution)/shard_map/expand/pallas_call | solution.py:29
  (7 shorter events, 0.0 us)
Async XLA Ops:
  0.7 5.6 %collective-permute-start = (s32[16,128]{1,0:T(8,128)S(1)}, s32[16,128]{1,0:T(8,128)S(1)}, u32[]{:S(2)}, u32[]{:S(2)}) collective-permute-start(s32[16,128]{1,0:T(8,128)S(1)} %get-tuple-element.72), channel_id=1, source_target_pairs={{0,4},{4,0},{8,12},{12,8},{16,20},{20,16},{24,28},{28,24},{1,5},{5... | collective-permute-start | bytes 24584 | tf_op jit(solution)/shard_map/ppermute | solution.py:20
  3.7 35.0 %collective-permute-start.5 = (bf16[16,2,32,256]{3,2,1,0:T(8,128)(2,1)}, bf16[16,2,32,256]{3,2,1,0:T(8,128)(2,1)S(1)}, u32[]{:S(2)}, u32[]{:S(2)}) collective-permute-start(bf16[16,2,32,256]{3,2,1,0:T(8,128)(2,1)} %own.1), channel_id=1, source_target_pairs={{0,16},{4,20},{8,24},{12,28},{16,0},{20,4},{24,8},{28,12},{1,17},{... | collective-permute-start | bytes 1572872 | tf_op jit(solution)/shard_map/ppermute | solution.py:20
  6.3 6.8 %copy-start.1 = (bf16[2,2,64,512]{3,2,1,0:T(8,128)(2,1)S(1)}, bf16[2,2,64,512]{3,2,1,0:T(8,128)(2,1)}, u32[]{:S(2)}) copy-start(bf16[2,2,64,512]{3,2,1,0:T(8,128)(2,1)} %param.17) | copy-start | bytes 786436
  6.3 6.8 %copy-start.2 = (bf16[256,512]{1,0:T(8,128)(2,1)S(1)}, bf16[256,512]{1,0:T(8,128)(2,1)}, u32[]{:S(2)}) copy-start(bf16[256,512]{1,0:T(8,128)(2,1)} %refs_2_.1) | copy-start | bytes 786436
  6.3 6.8 %copy-start.4 = (bf16[128,256]{1,0:T(8,128)(2,1)S(1)}, bf16[128,256]{1,0:T(8,128)(2,1)}, u32[]{:S(2)}) copy-start(bf16[128,256]{1,0:T(8,128)(2,1)} %refs_1_.1) | copy-start | bytes 196612
  6.3 6.8 %copy-start.5 = (f32[8,16,128]{2,1,0:T(8,128)S(1)}, f32[8,16,128]{2,1,0:T(8,128)}, u32[]{:S(2)}) copy-start(f32[8,16,128]{2,1,0:T(8,128)} %refs_3_.1) | copy-start | bytes 196612
  12.0 14.6 %collective-permute-start.1 = (bf16[64,32,128]{2,1,0:T(8,128)(2,1)S(1)}, bf16[64,32,128]{2,1,0:T(8,128)(2,1)S(1)}, u32[]{:S(2)}, u32[]{:S(2)}) collective-permute-start(bf16[64,32,128]{2,1,0:T(8,128)(2,1)S(1)} %get-tuple-element.38), channel_id=1, source_target_pairs={{0,4},{4,0},{8,12},{12,8},{16,20},{20,16},{24,28},{28,24},{1,5},{5... | collective-permute-start | bytes 1572872 | tf_op jit(solution)/shard_map/ppermute | solution.py:20
  13.2 2.5 %copy-start.12 = (f32[316,32,128]{2,1,0:T(8,128)S(1)}, f32[316,32,128]{2,1,0:T(8,128)}, u32[]{:S(2)}) copy-start(f32[316,32,128]{2,1,0:T(8,128)} %get-tuple-element.42.refs_1_) | copy-start | bytes 15532036
  13.2 3.1 %copy-start.13 = (f32[129,32,128]{2,1,0:T(8,128)S(1)}, f32[129,32,128]{2,1,0:T(8,128)}, u32[]{:S(2)}) copy-start(f32[129,32,128]{2,1,0:T(8,128)} %get-tuple-element.43.refs_2_) | copy-start | bytes 6340612
  20.2 5.4 %collective-permute-start.2 = (f32[192,256]{1,0:T(8,128)S(1)}, f32[192,256]{1,0:T(8,128)S(1)}, u32[]{:S(2)}, u32[]{:S(2)}) collective-permute-start(f32[192,256]{1,0:T(8,128)S(1)} %get-tuple-element.49), channel_id=1, source_target_pairs={{0,1},{1,0},{2,3},{3,2},{4,5},{5,4},{6,7},{7,6},{8,9},{9,8},{10,11... | collective-permute-start | bytes 589832 | tf_op jit(solution)/shard_map/ppermute | solution.py:20
  20.3 7.8 %collective-permute-start.3 = (f32[192,256]{1,0:T(8,128)S(1)}, f32[192,256]{1,0:T(8,128)S(1)}, u32[]{:S(2)}, u32[]{:S(2)}) collective-permute-start(f32[192,256]{1,0:T(8,128)S(1)} %get-tuple-element.50), channel_id=1, source_target_pairs={{0,2},{1,3},{2,0},{3,1},{4,6},{5,7},{6,4},{7,5},{8,10},{9,11},{10,... | collective-permute-start | bytes 589832 | tf_op jit(solution)/shard_map/ppermute | solution.py:20
  21.9 9.5 %collective-permute-start.4 = (f32[192,256]{1,0:T(8,128)S(1)}, f32[192,256]{1,0:T(8,128)S(1)}, u32[]{:S(2)}, u32[]{:S(2)}) collective-permute-start(f32[192,256]{1,0:T(8,128)S(1)} %get-tuple-element.51), channel_id=1, source_target_pairs={{0,3},{1,2},{2,1},{3,0},{4,7},{5,6},{6,5},{7,4},{8,11},{9,10},{10,... | collective-permute-start | bytes 589832 | tf_op jit(solution)/shard_map/ppermute | solution.py:20
  22.1 9.2 %copy-start.3 = (f32[8,32,256]{2,1,0:T(8,128)S(1)}, f32[8,32,256]{2,1,0:T(8,128)}, u32[]{:S(2)}) copy-start(f32[8,32,256]{2,1,0:T(8,128)} %refs_4_.1) | copy-start | bytes 786436
  22.1 9.2 %copy-start.6 = (bf16[2,128,128]{2,1,0:T(8,128)(2,1)S(1)}, bf16[2,128,128]{2,1,0:T(8,128)(2,1)}, u32[]{:S(2)}) copy-start(bf16[2,128,128]{2,1,0:T(8,128)(2,1)} %refs_6_.1) | copy-start | bytes 196612
  22.2 9.2 %copy-start.8 = (bf16[64,64]{1,0:T(8,128)(2,1)S(1)}, bf16[64,64]{1,0:T(8,128)(2,1)}, u32[]{:S(2)}) copy-start(bf16[64,64]{1,0:T(8,128)(2,1)} %refs_5_.1) | copy-start | bytes 24580
  25.6 21.0 %collective-permute-start.8 = (bf16[64,32,128]{2,1,0:T(8,128)(2,1)S(1)}, bf16[64,32,128]{2,1,0:T(8,128)(2,1)S(1)}, u32[]{:S(2)}, u32[]{:S(2)}) collective-permute-start(bf16[64,32,128]{2,1,0:T(8,128)(2,1)S(1)} %sums_second.1), channel_id=1, source_target_pairs={{0,4},{4,0},{8,12},{12,8},{16,20},{20,16},{24,28},{28,24},{1,5},{5... | collective-permute-start | bytes 1572872 | tf_op jit(solution)/shard_map/ppermute | solution.py:20
  26.7 20.0 %collective-permute-start.10 = (bf16[32,32,128]{2,1,0:T(8,128)(2,1)S(1)}, bf16[32,32,128]{2,1,0:T(8,128)(2,1)S(1)}, u32[]{:S(2)}, u32[]{:S(2)}) collective-permute-start(bf16[32,32,128]{2,1,0:T(8,128)(2,1)S(1)} %get-tuple-element.47), channel_id=1, source_target_pairs={{0,3},{1,2},{2,1},{3,0},{4,7},{5,6},{6,5},{7,4},{8,11},{9,10},{10,... | collective-permute-start | bytes 786440 | tf_op jit(solution)/shard_map/ppermute | solution.py:20
  31.4 7.4 %slice-start = ((s8[10354688]{0:T(1024)(128)(4,1)}), s8[4194304]{0:T(1024)(128)(4,1)S(1)}, s32[]{:S(2)}) async-start(s8[10354688]{0:T(1024)(128)(4,1)} %bitcast.50), calls=%async_computation | async-start | bytes 8388608
  31.4 7.4 %slice-start.1 = ((s8[10354688]{0:T(1024)(128)(4,1)}), s8[4194304]{0:T(1024)(128)(4,1)S(1)}, s32[]{:S(2)}) async-start(s8[10354688]{0:T(1024)(128)(4,1)} %bitcast.50), calls=%async_computation.1 | async-start | bytes 8388608
  33.7 5.1 %slice-start.2 = ((s8[10354688]{0:T(1024)(128)(4,1)}), s8[1966080]{0:T(1024)(128)(4,1)S(1)}, s32[]{:S(2)}) async-start(s8[10354688]{0:T(1024)(128)(4,1)} %bitcast.50), calls=%async_computation.2 | async-start | bytes 3932160
  33.7 5.1 %copy-start = (bf16[16,2,32,256]{3,2,1,0:T(8,128)(2,1)S(1)}, bf16[16,2,32,256]{3,2,1,0:T(8,128)(2,1)}, u32[]{:S(2)}) copy-start(bf16[16,2,32,256]{3,2,1,0:T(8,128)(2,1)} %own.1) | copy-start | bytes 1572868
  33.7 5.1 %copy-start.7 = (bf16[128,256]{1,0:T(8,128)(2,1)S(1)}, bf16[128,256]{1,0:T(8,128)(2,1)}, u32[]{:S(2)}) copy-start(bf16[128,256]{1,0:T(8,128)(2,1)} %phi.1) | copy-start | bytes 196612
  33.7 5.1 %copy-start.10 = (s32[16,16]{1,0:T(8,128)S(1)}, s32[16,16]{1,0:T(8,128)}, u32[]{:S(2)}) copy-start(s32[16,16]{1,0:T(8,128)} %ids.1) | copy-start | bytes 3076
  33.7 5.1 %copy-start.11 = (s32[16,16]{1,0:T(8,128)S(1)}, s32[16,16]{1,0:T(8,128)}, u32[]{:S(2)}) copy-start(s32[16,16]{1,0:T(8,128)} %offsets.1) | copy-start | bytes 3076
  37.2 9.6 %collective-permute-start.11 = (bf16[32,32,128]{2,1,0:T(8,128)(2,1)S(1)}, bf16[32,32,128]{2,1,0:T(8,128)(2,1)S(1)}, u32[]{:S(2)}, u32[]{:S(2)}) collective-permute-start(bf16[32,32,128]{2,1,0:T(8,128)(2,1)S(1)} %get-tuple-element.66), channel_id=1, source_target_pairs={{0,2},{1,3},{2,0},{3,1},{4,6},{5,7},{6,4},{7,5},{8,10},{9,11},{10,... | collective-permute-start | bytes 786440 | tf_op jit(solution)/shard_map/ppermute | solution.py:20
  44.4 5.0 %collective-permute-start.6 = (bf16[4,64,128]{2,1,0:T(8,128)(2,1)S(1)}, bf16[4,64,128]{2,1,0:T(8,128)(2,1)S(1)}, u32[]{:S(2)}, u32[]{:S(2)}) collective-permute-start(bf16[4,64,128]{2,1,0:T(8,128)(2,1)S(1)} %get-tuple-element.58), channel_id=1, source_target_pairs={{0,2},{1,3},{2,0},{3,1},{4,6},{5,7},{6,4},{7,5},{8,10},{9,11},{10,... | collective-permute-start | bytes 196616 | tf_op jit(solution)/shard_map/ppermute | solution.py:20
  45.0 5.4 %collective-permute-start.7 = (bf16[4,64,128]{2,1,0:T(8,128)(2,1)S(1)}, bf16[4,64,128]{2,1,0:T(8,128)(2,1)S(1)}, u32[]{:S(2)}, u32[]{:S(2)}) collective-permute-start(bf16[4,64,128]{2,1,0:T(8,128)(2,1)S(1)} %get-tuple-element.59), channel_id=1, source_target_pairs={{0,3},{1,2},{2,1},{3,0},{4,7},{5,6},{6,5},{7,4},{8,11},{9,10},{10,... | collective-permute-start | bytes 196616 | tf_op jit(solution)/shard_map/ppermute | solution.py:20
  46.6 3.7 %copy-start.9 = (bf16[64,128]{1,0:T(8,128)(2,1)S(1)}, bf16[64,128]{1,0:T(8,128)(2,1)}, u32[]{:S(2)}) copy-start(bf16[64,128]{1,0:T(8,128)(2,1)} %refs_8_.1) | copy-start | bytes 49156
  46.7 3.7 %collective-permute-start.9 = (bf16[40,32,128]{2,1,0:T(8,128)(2,1)S(1)}, bf16[40,32,128]{2,1,0:T(8,128)(2,1)S(1)}, u32[]{:S(2)}, u32[]{:S(2)}) collective-permute-start(bf16[40,32,128]{2,1,0:T(8,128)(2,1)S(1)} %get-tuple-element.65), channel_id=1, source_target_pairs={{0,1},{1,0},{2,3},{3,2},{4,5},{5,4},{6,7},{7,6},{8,9},{9,8},{10,11... | collective-permute-start | bytes 983048 | tf_op jit(solution)/shard_map/ppermute | solution.py:20

commit v5 on v4

--- a/solution.py
+++ b/solution.py
@@ -20,11 +20,14 @@
     return lax.ppermute(value, axis, pairs)
 
 
+COSTS = {"join": 0, "sums_third": 0, "shift": 0, "sums_fourth": 0, "upper_near": 0}
+
+
 def after(value, *others):
     return lax.optimization_barrier((value, *others))[0]
 
 
-def kernel_call(body, outs, scalars, arrays, name, scratch=(), held=0, vmem=6 << 20, away=0, flops=4 << 30):
+def kernel_call(body, outs, scalars, arrays, name, scratch=(), held=0, vmem=6 << 20, away=0):
     near = len(arrays) - held
     return pl.pallas_call(
         body,
@@ -33,7 +36,7 @@
         out_specs=[VM] * (len(outs) - away) + [HB] * away,
         scratch_shapes=list(scratch),
         compiler_params=pltpu.CompilerParams(vmem_limit_bytes=vmem),
-        cost_estimate=pl.CostEstimate(flops=flops, bytes_accessed=1, transcendentals=0),
+        cost_estimate=pl.CostEstimate(flops=COSTS.get(name, 4) << 30, bytes_accessed=1, transcendentals=0),
         name=name,
     )(*scalars, *arrays)
 
@@ -185,41 +188,38 @@
             outs[0][owns[0].shape[0] :] = refs[count + 1][...]
 
     more = [] if extra is None else [extra]
-    return kernel_call(body, shapes, [], [*owns, got, *more], "join", flops=1)
-
-
-def upper_body(peers, entries, me, home, ids, offsets, own, far, table, shifted, phi, *refs):
-    outs, (pool, whole) = refs[:peers], refs[peers:]
+    return kernel_call(body, shapes, [], [*owns, got, *more], "join")
+
+
+def upper_body(masks, peers, entries, me, home, ids, offsets, own, far, table, shifted, phi, *refs):
+    outs, pool = refs[: len(masks)], refs[-1]
     boxes, _, rows, _ = own.shape
     pool[0:boxes] = own[...].astype(F32)
     pool[boxes:] = far[...].astype(F32)
-    step = min(16, rows)
+    spans = [slice(r, r + 8) for r in range(0, rows, 8)]
     per = boxes // peers
-
-    def one(box, carry):
-        for r in range(0, rows, step):
-            span = slice(r, r + step)
-            real, imag = shifted[box, 0, span], shifted[box, 1, span]
+    for mask, out in zip(masks, outs, strict=True):
+        first = jnp.bitwise_xor(me[0], mask) * per
+
+        def one(i, carry, first=first, out=out):
+            box = first + i
+            real = [shifted[box, 0, span] for span in spans]
+            imag = [shifted[box, 1, span] for span in spans]
             for entry in range(entries):
                 offset, ident = offsets[box, entry], ids[box, entry]
                 place = lax.rem(ident, boxes)
                 place = jnp.where(ident - place == home[0] * boxes, place, place + boxes)
-                fr, fi = table[offset, 0, span].astype(F32), table[offset, 1, span].astype(F32)
-                sr, si = pool[place, 0, span], pool[place, 1, span]
-                real = real + (fr * sr - fi * si)
-                imag = imag + (fr * si + fi * sr)
-            whole[box, 0, span] = real
-            whole[box, 1, span] = imag
-        return carry
-
-    lax.fori_loop(0, boxes, one, 0)
-    for mask in range(peers):
-        first = jnp.bitwise_xor(me[0], mask) * per
-        for i in range(per):
-            for c in range(2):
-                incoming = whole[first + i, c].astype(BF16)
-                narrow = lax.dot_general(incoming, phi[...], NT, preferred_element_type=F32)
-                outs[mask][i, c * rows : (c + 1) * rows] = narrow.astype(BF16)
+                for k, span in enumerate(spans):
+                    fr, fi = table[offset, 0, span].astype(F32), table[offset, 1, span].astype(F32)
+                    sr, si = pool[place, 0, span], pool[place, 1, span]
+                    real[k] = real[k] + (fr * sr - fi * si)
+                    imag[k] = imag[k] + (fr * si + fi * sr)
+            incoming = jnp.concatenate([*real, *imag], axis=0).astype(BF16)
+            narrow = lax.dot_general(incoming, phi[...], NT, preferred_element_type=F32)
+            out[i] = narrow.astype(BF16)
+            return carry
+
+        lax.fori_loop(0, per, one, 0)
 
 
 def place_body(*refs):
@@ -325,14 +325,13 @@
     places = table_lower.shape[0]
     outer, inner = list(range(peers - 1, peers // 2 - 1, -1)), list(range(peers // 2 - 1, -1, -1))
 
-    def sums(groups, outs, codes, order, name, flops=4 << 30):
+    def sums(groups, outs, codes, order, name):
         return kernel_call(
             functools.partial(sums_body, groups, per, entries),
             outs,
             [order, *codes],
             [table, source],
             name,
-            flops=flops,
         )
 
     own_shape = struct((per, 2 * low, lanes), F32)
@@ -411,25 +410,25 @@
         held=3,
     )
     trig = trig.reshape(2, children, peers * low, lanes)
+    def upper(masks, order, name):
+        return kernel_call(
+            functools.partial(upper_body, masks, peers, entries),
+            [struct((upper_per, 2 * rows, lanes), BF16)] * len(masks),
+            [order, home.astype(jnp.int32).reshape(1), list_upper, offset_upper],
+            [outgoing_upper, far_upper, table_upper, shifted, phi_lower],
+            name,
+            scratch=[pltpu.VMEM((2 * upper_boxes, 2, rows, wide), F32)],
+        )
+
+    ups = dict(zip(outer, upper(outer, me, "upper_far"), strict=True))
     own_inner = sums(
         [((mask,), 0) for mask in inner],
         [own_shape] * len(inner),
         [own_code],
-        after(me, trig),
+        after(me, ups[outer[0]]),
         "sums_fourth",
     )
-    ups = kernel_call(
-        functools.partial(upper_body, peers, entries),
-        [struct((upper_per, 2 * rows, lanes), BF16)] * peers,
-        [after(me, own_inner[0]), home.astype(jnp.int32).reshape(1), list_upper, offset_upper],
-        [outgoing_upper, far_upper, table_upper, shifted, phi_lower],
-        "upper",
-        scratch=[
-            pltpu.VMEM((2 * upper_boxes, 2, rows, wide), F32),
-            pltpu.VMEM((upper_boxes, 2, rows, wide), F32),
-        ],
-    )
-    own_inner = [after(own_inner[0], ups[0]), *own_inner[1:]]
+    ups.update(zip(inner, upper(inner, after(me, own_inner[0]), "upper_near"), strict=True))
     near = ups[1].reshape(-1, 2 * low, lanes)
     lows.update(zip(inner, join(own_inner, got_inner, near), strict=True))
     ups = [swap(ups[mask], "angle", mask) if mask else ups[0] for mask in range(peers) if mask != 1]

time: 54.8 us -> 50.5 us (0.922)
  waiting for transfers between devices: 6.91 us -> 3.36 us
  Pallas kernels: 29.7 us -> 32.3 us
  local copies, waits for them, and re-layouts: 2.21 us -> 0.26 us
  starting transfers between devices: 14.8 us -> 13.4 us
    ppermute x12, waiting for transfers between devices: 6.91 us -> 3.36 us  [swap(): return lax.ppermute(value, axis, pairs)]
    pallas_call x11 -> x12, Pallas kernels: 29.7 us -> 32.3 us  [kernel_call(): pl.pallas_call(body, out_shape=outs, in_specs=[SM] * len(scalars) + [VM]...]
    unnamed x34, local copies, waits for them, and re-layouts: 2.21 us -> 0.26 us
    ppermute x12, starting transfers between devices: 14.8 us -> 13.4 us  [swap(): return lax.ppermute(value, axis, pairs)]
  transfers between devices with their start and end apart: 12 -> 12, of which waited for: 4 -> 2; matrix products, arithmetic and copies ran while one was open for 0% -> 0% of each run, Pallas kernels for 47% -> 56%
where the time goes in v5:
time: 50.5 us; the launch traced here: 50.3 us
  Pallas kernels  32.3 us (64%)
  starting transfers between devices  13.4 us (27%)
  waiting for transfers between devices  3.36 us (7%)
  other arithmetic  0.73 us (1%)
    pallas_call x12, Pallas kernels, kernel_call(): pl.pallas_call(body, out_shape=outs, in_specs=[SM] * len(scalars) + [VM]...  32.3 us
    ppermute x12, starting transfers between devices, swap(): return lax.ppermute(value, axis, pairs)  13.4 us
    ppermute x12, waiting for transfers between devices, swap(): return lax.ppermute(value, axis, pairs)  3.36 us
  transfers between devices with their start and end apart: 12, of which 2 were waited for; matrix products, arithmetic and copies ran while one was open for 0% of the time, Pallas kernels for 56%

profile of v5, /device:TPU:0, one launch (start us, length us, event | category | flops | bytes accessed | tf_op | source)
XLA Modules:
  0.0 50.3 jit_solution(17920568315989135981)
XLA Ops:
  0.0 0.7 %bitcast_add_fusion = (s32[16,128]{1,0:T(8,128)S(1)}, s32[16,128]{1,0:T(8,128)S(1)}) fusion(s32[128,16]{0,1:T(8,128)} %param.31, s32[128,16]{0,1:T(8,128)} %param.30, s32[]{:T(128)} %axis_index.25), kind=kLoop, calls=%fused_computation.6 | loop fusion | flops 53248 | bytes 32772 | tf_op jit(solution)/shard_map/add | solution.py:321
  0.7 3.0 %collective-permute-start.1 = (s32[16,128]{1,0:T(8,128)S(1)}, s32[16,128]{1,0:T(8,128)S(1)}, u32[]{:S(2)}, u32[]{:S(2)}) collective-permute-start(s32[16,128]{1,0:T(8,128)S(1)} %get-tuple-element.70), channel_id=1, source_target_pairs={{0,4},{4,0},{8,12},{12,8},{16,20},{20,16},{24,28},{28,24},{1,5},{5... | collective-permute-start | bytes 24584 | tf_op jit(solution)/shard_map/ppermute | solution.py:20
  3.7 2.6 %collective-permute-start = (bf16[16,2,32,256]{3,2,1,0:T(8,128)(2,1)}, bf16[16,2,32,256]{3,2,1,0:T(8,128)(2,1)S(1)}, u32[]{:S(2)}, u32[]{:S(2)}) collective-permute-start(bf16[16,2,32,256]{3,2,1,0:T(8,128)(2,1)} %own.3), channel_id=1, source_target_pairs={{0,16},{4,20},{8,24},{12,28},{16,0},{20,4},{24,8},{28,12},{1,17},{... | collective-permute-start | bytes 1572872 | tf_op jit(solution)/shard_map/ppermute | solution.py:20
  6.3 0.0 collective-permute-done.1.code.refs_0_
  6.3 0.0 copy-start.9
  6.3 0.0 copy-start.11
  6.3 0.0 copy-start.12
  6.4 5.7 %sums_first.1 = (bf16[64,32,128]{2,1,0:T(8,128)(2,1)S(1)}, f32[316,32,128]{2,1,0:T(8,128)}, f32[129,32,128]{2,1,0:T(8,128)}) custom-call(s32[1]{0:T(128)} %bitcast.me, s32[16,128]{1,0:T(8,128)S(1)} %collective-permute-done.1.code.refs_0_, bf16[316,32,128]{2,1,0:T(8,128)(2,1)} %bitcast.54, bf16[128,32,128]{2,1,0:T(8,128)(2,1)} %bitcast.55), custom_call_target="tpu_custom_call" | custom-call | flops 4294967296 | bytes 1 | tf_op jit(solution)/shard_map/sums_first/pallas_call | solution.py:32
  12.0 1.1 %collective-permute-start.2 = (bf16[64,32,128]{2,1,0:T(8,128)(2,1)S(1)}, bf16[64,32,128]{2,1,0:T(8,128)(2,1)S(1)}, u32[]{:S(2)}, u32[]{:S(2)}) collective-permute-start(bf16[64,32,128]{2,1,0:T(8,128)(2,1)S(1)} %get-tuple-element.37), channel_id=1, source_target_pairs={{0,4},{4,0},{8,12},{12,8},{16,20},{20,16},{24,28},{28,24},{1,5},{5... | collective-permute-start | bytes 1572872 | tf_op jit(solution)/shard_map/ppermute | solution.py:20
  13.2 0.0 copy-done.9
  13.2 0.0 copy-done.10
  13.2 0.0 copy-done.11
  13.2 0.0 copy-done.12
  13.2 0.0 copy-start
  13.2 0.0 copy-start.1
  13.2 1.0 %early.1 = (f32[192,256]{1,0:T(8,128)S(1)}, f32[192,256]{1,0:T(8,128)S(1)}, f32[192,256]{1,0:T(8,128)S(1)}, f32[192,256]{1,0:T(8,128)S(1)}) custom-call(s32[1]{0:T(128)} %bitcast.me, bf16[256,512]{1,0:T(8,128)(2,1)S(1)} %bitcast.53, bf16[128,256]{1,0:T(8,128)(2,1)S(1)} %copy-done.11, bf16[256,512]{1,0:T(8,128)(2,1)S(1)} %copy-done.10, ...), custom_call_target="tpu_custom_call" | custom-call | flops 4294967296 | bytes 1 | tf_op jit(solution)/shard_map/early/pallas_call | solution.py:32
  14.2 0.1 collective-permute-start.3
  14.3 1.6 %collective-permute-start.4 = (f32[192,256]{1,0:T(8,128)S(1)}, f32[192,256]{1,0:T(8,128)S(1)}, u32[]{:S(2)}, u32[]{:S(2)}) collective-permute-start(f32[192,256]{1,0:T(8,128)S(1)} %get-tuple-element.49), channel_id=1, source_target_pairs={{0,2},{1,3},{2,0},{3,1},{4,6},{5,7},{6,4},{7,5},{8,10},{9,11},{10,... | collective-permute-start | bytes 589832 | tf_op jit(solution)/shard_map/ppermute | solution.py:20
  15.9 0.3 collective-permute-start.5
  16.1 0.0 copy-done
  16.1 0.2 copy-done.1
  16.3 3.9 %sums_second.1 = bf16[64,32,128]{2,1,0:T(8,128)(2,1)S(1)} custom-call(s32[1]{0:T(128)} %bitcast.me, s32[16,128]{1,0:T(8,128)S(1)} %collective-permute-done.1.code.refs_0_, f32[316,32,128]{2,1,0:T(8,128)S(1)} %copy-done, f32[129,32,128]{2,1,0:T(8,128)S(1)} %copy-done.1), custom_call_target="tpu_custom_call" | custom-call | flops 4294967296 | bytes 1 | tf_op jit(solution)/shard_map/sums_second/pallas_call | solution.py:32
  20.2 0.0 collective-permute-done.3.refs_1_
  20.2 1.0 %collective-permute-start.8 = (bf16[64,32,128]{2,1,0:T(8,128)(2,1)S(1)}, bf16[64,32,128]{2,1,0:T(8,128)(2,1)S(1)}, u32[]{:S(2)}, u32[]{:S(2)}) collective-permute-start(bf16[64,32,128]{2,1,0:T(8,128)(2,1)S(1)} %sums_second.1), channel_id=1, source_target_pairs={{0,4},{4,0},{8,12},{12,8},{16,20},{20,16},{24,28},{28,24},{1,5},{5... | collective-permute-start | bytes 1572872 | tf_op jit(solution)/shard_map/ppermute | solution.py:20
  21.3 3.8 %sums_third.1 = (f32[32,32,128]{2,1,0:T(8,128)S(1)}, f32[32,32,128]{2,1,0:T(8,128)S(1)}) custom-call(s32[1]{0:T(128)} %bitcast.me, s32[16,128]{1,0:T(8,128)S(1)} %get-tuple-element.69.refs_0_, f32[316,32,128]{2,1,0:T(8,128)S(1)} %copy-done, f32[129,32,128]{2,1,0:T(8,128)S(1)} %copy-done.1), custom_call_target="tpu_custom_call" | custom-call | bytes 1 | tf_op jit(solution)/shard_map/sums_third/pallas_call | solution.py:32
  25.1 0.0 copy-start.2
  25.1 0.0 copy-start.4
  25.1 0.0 copy-start.7
  25.1 0.0 copy-start.8
  25.1 1.8 %collective-permute-done.2.refs_2_ = bf16[64,32,128]{2,1,0:T(8,128)(2,1)S(1)} collective-permute-done((bf16[64,32,128]{2,1,0:T(8,128)(2,1)S(1)}, bf16[64,32,128]{2,1,0:T(8,128)(2,1)S(1)}, u32[]{:S(2)}, u32[]{:S(2)}) %collective-permute-start.2) | collective-permute-done | bytes 524320 | tf_op jit(solution)/shard_map/ppermute | solution.py:20
  27.0 0.1 join.2
  27.1 0.1 collective-permute-start.10
  27.2 0.0 collective-permute-done.4.refs_2_
  27.2 1.6 %collective-permute-start.11 = (bf16[32,32,128]{2,1,0:T(8,128)(2,1)S(1)}, bf16[32,32,128]{2,1,0:T(8,128)(2,1)S(1)}, u32[]{:S(2)}, u32[]{:S(2)}) collective-permute-start(bf16[32,32,128]{2,1,0:T(8,128)(2,1)S(1)} %get-tuple-element.63), channel_id=1, source_target_pairs={{0,2},{1,3},{2,0},{3,1},{4,6},{5,7},{6,4},{7,5},{8,10},{9,11},{10,... | collective-permute-start | bytes 786440 | tf_op jit(solution)/shard_map/ppermute | solution.py:20
  28.7 0.0 collective-permute-done.5.refs_3_
  28.8 0.0 copy-done.3
  28.8 0.0 copy-done.5
  28.8 0.0 copy-done.6
  28.8 2.3 %shift.1 = (f32[16,2,32,256]{3,2,1,0:T(8,128)S(1)}, f32[2,8,4,16,128]{4,3,2,1,0:T(8,128)S(1)}, bf16[2,128,64]{2,1,0:T(8,128)(2,1)S(1)}, bf16[256,256]{1,0:T(8,128)(2,1)S(1)}) custom-call(s32[1]{0:T(128)} %bitcast.me, f32[192,256]{1,0:T(8,128)S(1)} %get-tuple-element.39.refs_0_, f32[192,256]{1,0:T(8,128)S(1)} %collective-permute-done.3.refs_1_, ...), custom_call_target="tpu_custom_call" | custom-call | bytes 1 | tf_op jit(solution)/shard_map/shift/pallas_call | solution.py:32
  31.1 0.0 collective-permute-done.far
  31.1 0.0 slice-done
  31.1 0.0 slice-done.1
  31.1 0.0 slice-done.2
  31.1 0.0 copy-done.2
  31.1 0.0 copy-done.4
  31.1 0.0 copy-done.7
  31.1 0.0 copy-done.8
  31.1 3.7 %upper_far.1 = (bf16[4,64,128]{2,1,0:T(8,128)(2,1)S(1)}, bf16[4,64,128]{2,1,0:T(8,128)(2,1)S(1)}) custom-call(s32[1]{0:T(128)} %bitcast.me, s32[1]{0:T(128)} %bitcast.1.home, s32[16,16]{1,0:T(8,128)S(1)} %copy-done.7, s32[16,16]{1,0:T(8,128)S(1)} %copy-done.8, bf16[16,2,32,256]{3,2,1,0:T(8,128)(2,1)S(1)} %copy-done.2, ...), custom_call_target="tpu_custom_call" | custom-call | flops 4294967296 | bytes 1 | tf_op jit(solution)/shard_map/upper_far/pallas_call | solution.py:32
  34.8 1.4 %collective-permute-start.7 = (bf16[4,64,128]{2,1,0:T(8,128)(2,1)S(1)}, bf16[4,64,128]{2,1,0:T(8,128)(2,1)S(1)}, u32[]{:S(2)}, u32[]{:S(2)}) collective-permute-start(bf16[4,64,128]{2,1,0:T(8,128)(2,1)S(1)} %get-tuple-element.52), channel_id=1, source_target_pairs={{0,3},{1,2},{2,1},{3,0},{4,7},{5,6},{6,5},{7,4},{8,11},{9,10},{10,... | collective-permute-start | bytes 196616 | tf_op jit(solution)/shard_map/ppermute | solution.py:20
  36.2 3.8 %sums_fourth.1 = (f32[32,32,128]{2,1,0:T(8,128)S(1)}, f32[32,32,128]{2,1,0:T(8,128)S(1)}) custom-call(s32[1]{0:T(128)} %bitcast.me, s32[16,128]{1,0:T(8,128)S(1)} %get-tuple-element.69.refs_0_, f32[316,32,128]{2,1,0:T(8,128)S(1)} %copy-done, f32[129,32,128]{2,1,0:T(8,128)S(1)} %copy-done.1), custom_call_target="tpu_custom_call" | custom-call | bytes 1 | tf_op jit(solution)/shard_map/sums_fourth/pallas_call | solution.py:32
  40.0 0.6 %collective-permute-start.6 = (bf16[4,64,128]{2,1,0:T(8,128)(2,1)S(1)}, bf16[4,64,128]{2,1,0:T(8,128)(2,1)S(1)}, u32[]{:S(2)}, u32[]{:S(2)}) collective-permute-start(bf16[4,64,128]{2,1,0:T(8,128)(2,1)S(1)} %get-tuple-element.57), channel_id=1, source_target_pairs={{0,2},{1,3},{2,0},{3,1},{4,6},{5,7},{6,4},{7,5},{8,10},{9,11},{10,... | collective-permute-start | bytes 196616 | tf_op jit(solution)/shard_map/ppermute | solution.py:20
  40.6 3.7 %upper_near.1 = (bf16[4,64,128]{2,1,0:T(8,128)(2,1)S(1)}, bf16[4,64,128]{2,1,0:T(8,128)(2,1)S(1)}) custom-call(s32[1]{0:T(128)} %bitcast.me, s32[1]{0:T(128)} %bitcast.1.home, s32[16,16]{1,0:T(8,128)S(1)} %copy-done.7, s32[16,16]{1,0:T(8,128)S(1)} %copy-done.8, bf16[16,2,32,256]{3,2,1,0:T(8,128)(2,1)S(1)} %copy-done.2, ...), custom_call_target="tpu_custom_call" | custom-call | bytes 1 | tf_op jit(solution)/shard_map/upper_near/pallas_call | solution.py:32
  44.3 0.0 collective-permute-done.8.refs_2_
  44.3 0.1 join.3
  44.4 0.0 copy-start.13
  44.4 0.1 collective-permute-start.9
  44.5 0.0 collective-permute-done.10.refs_0_
  44.5 0.0 collective-permute-done.11.refs_1_
  44.5 0.1 place.1
  44.6 0.0 collective-permute-done.6.refs_1_
  44.6 0.0 collective-permute-done.7.refs_2_
  44.6 1.5 %collective-permute-done.9.refs_4_ = bf16[40,32,128]{2,1,0:T(8,128)(2,1)S(1)} collective-permute-done((bf16[40,32,128]{2,1,0:T(8,128)(2,1)S(1)}, bf16[40,32,128]{2,1,0:T(8,128)(2,1)S(1)}, u32[]{:S(2)}, u32[]{:S(2)}) %collective-permute-start.9) | collective-permute-done | bytes 327712 | tf_op jit(solution)/shard_map/ppermute | solution.py:20
  46.1 0.0 copy-done.13
  46.1 4.2 %expand.1 = f32[4096,128]{1,0:T(8,128)} custom-call(s32[1]{0:T(128)} %bitcast.me, bf16[4,64,128]{2,1,0:T(8,128)(2,1)S(1)} %get-tuple-element.56.refs_0_, bf16[4,64,128]{2,1,0:T(8,128)(2,1)S(1)} %collective-permute-done.6.refs_1_, bf16[4,64,128]{2,1,0:T(8,128)(2,1)S(1)} %collective-permute-done.7.refs_2_, bf16[32,32,128]{2,1,0:T(8,128)(2,1)S(1)} %get-tuple-element.61.refs_3_, ...), custom_call_target="tpu_custom_call" | custom-call | flops 4294967296 | bytes 1 | tf_op jit(solution)/shard_map/expand/pallas_call | solution.py:32
  (8 shorter events, 0.0 us)
Async XLA Ops:
  0.7 5.6 %collective-permute-start.1 = (s32[16,128]{1,0:T(8,128)S(1)}, s32[16,128]{1,0:T(8,128)S(1)}, u32[]{:S(2)}, u32[]{:S(2)}) collective-permute-start(s32[16,128]{1,0:T(8,128)S(1)} %get-tuple-element.70), channel_id=1, source_target_pairs={{0,4},{4,0},{8,12},{12,8},{16,20},{20,16},{24,28},{28,24},{1,5},{5... | collective-permute-start | bytes 24584 | tf_op jit(solution)/shard_map/ppermute | solution.py:20
  3.7 27.3 %collective-permute-start = (bf16[16,2,32,256]{3,2,1,0:T(8,128)(2,1)}, bf16[16,2,32,256]{3,2,1,0:T(8,128)(2,1)S(1)}, u32[]{:S(2)}, u32[]{:S(2)}) collective-permute-start(bf16[16,2,32,256]{3,2,1,0:T(8,128)(2,1)} %own.3), channel_id=1, source_target_pairs={{0,16},{4,20},{8,24},{12,28},{16,0},{20,4},{24,8},{28,12},{1,17},{... | collective-permute-start | bytes 1572872 | tf_op jit(solution)/shard_map/ppermute | solution.py:20
  6.3 6.8 %copy-start.9 = (bf16[2,2,64,512]{3,2,1,0:T(8,128)(2,1)S(1)}, bf16[2,2,64,512]{3,2,1,0:T(8,128)(2,1)}, u32[]{:S(2)}) copy-start(bf16[2,2,64,512]{3,2,1,0:T(8,128)(2,1)} %param.17) | copy-start | bytes 786436
  6.3 6.8 %copy-start.10 = (bf16[256,512]{1,0:T(8,128)(2,1)S(1)}, bf16[256,512]{1,0:T(8,128)(2,1)}, u32[]{:S(2)}) copy-start(bf16[256,512]{1,0:T(8,128)(2,1)} %refs_2_.1) | copy-start | bytes 786436
  6.3 6.8 %copy-start.11 = (bf16[128,256]{1,0:T(8,128)(2,1)S(1)}, bf16[128,256]{1,0:T(8,128)(2,1)}, u32[]{:S(2)}) copy-start(bf16[128,256]{1,0:T(8,128)(2,1)} %refs_1_.1) | copy-start | bytes 196612
  6.3 6.8 %copy-start.12 = (f32[8,16,128]{2,1,0:T(8,128)S(1)}, f32[8,16,128]{2,1,0:T(8,128)}, u32[]{:S(2)}) copy-start(f32[8,16,128]{2,1,0:T(8,128)} %refs_3_.1) | copy-start | bytes 196612
  12.0 14.9 %collective-permute-start.2 = (bf16[64,32,128]{2,1,0:T(8,128)(2,1)S(1)}, bf16[64,32,128]{2,1,0:T(8,128)(2,1)S(1)}, u32[]{:S(2)}, u32[]{:S(2)}) collective-permute-start(bf16[64,32,128]{2,1,0:T(8,128)(2,1)S(1)} %get-tuple-element.37), channel_id=1, source_target_pairs={{0,4},{4,0},{8,12},{12,8},{16,20},{20,16},{24,28},{28,24},{1,5},{5... | collective-permute-start | bytes 1572872 | tf_op jit(solution)/shard_map/ppermute | solution.py:20
  13.2 3.0 %copy-start = (f32[316,32,128]{2,1,0:T(8,128)S(1)}, f32[316,32,128]{2,1,0:T(8,128)}, u32[]{:S(2)}) copy-start(f32[316,32,128]{2,1,0:T(8,128)} %get-tuple-element.41.refs_1_) | copy-start | bytes 15532036
  13.2 3.1 %copy-start.1 = (f32[129,32,128]{2,1,0:T(8,128)S(1)}, f32[129,32,128]{2,1,0:T(8,128)}, u32[]{:S(2)}) copy-start(f32[129,32,128]{2,1,0:T(8,128)} %get-tuple-element.42.refs_2_) | copy-start | bytes 6340612
  14.2 6.0 %collective-permute-start.3 = (f32[192,256]{1,0:T(8,128)S(1)}, f32[192,256]{1,0:T(8,128)S(1)}, u32[]{:S(2)}, u32[]{:S(2)}) collective-permute-start(f32[192,256]{1,0:T(8,128)S(1)} %get-tuple-element.48), channel_id=1, source_target_pairs={{0,1},{1,0},{2,3},{3,2},{4,5},{5,4},{6,7},{7,6},{8,9},{9,8},{10,11... | collective-permute-start | bytes 589832 | tf_op jit(solution)/shard_map/ppermute | solution.py:20
  14.3 12.9 %collective-permute-start.4 = (f32[192,256]{1,0:T(8,128)S(1)}, f32[192,256]{1,0:T(8,128)S(1)}, u32[]{:S(2)}, u32[]{:S(2)}) collective-permute-start(f32[192,256]{1,0:T(8,128)S(1)} %get-tuple-element.49), channel_id=1, source_target_pairs={{0,2},{1,3},{2,0},{3,1},{4,6},{5,7},{6,4},{7,5},{8,10},{9,11},{10,... | collective-permute-start | bytes 589832 | tf_op jit(solution)/shard_map/ppermute | solution.py:20
  15.9 12.9 %collective-permute-start.5 = (f32[192,256]{1,0:T(8,128)S(1)}, f32[192,256]{1,0:T(8,128)S(1)}, u32[]{:S(2)}, u32[]{:S(2)}) collective-permute-start(f32[192,256]{1,0:T(8,128)S(1)} %get-tuple-element.50), channel_id=1, source_target_pairs={{0,3},{1,2},{2,1},{3,0},{4,7},{5,6},{6,5},{7,4},{8,11},{9,10},{10,... | collective-permute-start | bytes 589832 | tf_op jit(solution)/shard_map/ppermute | solution.py:20
  16.3 14.7 %slice-start = ((s8[10354688]{0:T(1024)(128)(4,1)}), s8[4194304]{0:T(1024)(128)(4,1)S(1)}, s32[]{:S(2)}) async-start(s8[10354688]{0:T(1024)(128)(4,1)} %bitcast.49), calls=%async_computation | async-start | bytes 8388608
  16.3 14.8 %slice-start.1 = ((s8[10354688]{0:T(1024)(128)(4,1)}), s8[4194304]{0:T(1024)(128)(4,1)S(1)}, s32[]{:S(2)}) async-start(s8[10354688]{0:T(1024)(128)(4,1)} %bitcast.49), calls=%async_computation.1 | async-start | bytes 8388608
  20.2 24.1 %collective-permute-start.8 = (bf16[64,32,128]{2,1,0:T(8,128)(2,1)S(1)}, bf16[64,32,128]{2,1,0:T(8,128)(2,1)S(1)}, u32[]{:S(2)}, u32[]{:S(2)}) collective-permute-start(bf16[64,32,128]{2,1,0:T(8,128)(2,1)S(1)} %sums_second.1), channel_id=1, source_target_pairs={{0,4},{4,0},{8,12},{12,8},{16,20},{20,16},{24,28},{28,24},{1,5},{5... | collective-permute-start | bytes 1572872 | tf_op jit(solution)/shard_map/ppermute | solution.py:20
  21.3 7.5 %copy-start.3 = (f32[8,32,256]{2,1,0:T(8,128)S(1)}, f32[8,32,256]{2,1,0:T(8,128)}, u32[]{:S(2)}) copy-start(f32[8,32,256]{2,1,0:T(8,128)} %refs_4_.1) | copy-start | bytes 786436
  21.3 7.5 %copy-start.5 = (bf16[2,128,128]{2,1,0:T(8,128)(2,1)S(1)}, bf16[2,128,128]{2,1,0:T(8,128)(2,1)}, u32[]{:S(2)}) copy-start(bf16[2,128,128]{2,1,0:T(8,128)(2,1)} %refs_6_.1) | copy-start | bytes 196612
  21.3 7.5 %copy-start.6 = (bf16[64,64]{1,0:T(8,128)(2,1)S(1)}, bf16[64,64]{1,0:T(8,128)(2,1)}, u32[]{:S(2)}) copy-start(bf16[64,64]{1,0:T(8,128)(2,1)} %refs_5_.1) | copy-start | bytes 24580
  21.3 9.8 %slice-start.2 = ((s8[10354688]{0:T(1024)(128)(4,1)}), s8[1966080]{0:T(1024)(128)(4,1)S(1)}, s32[]{:S(2)}) async-start(s8[10354688]{0:T(1024)(128)(4,1)} %bitcast.49), calls=%async_computation.2 | async-start | bytes 3932160
  25.1 6.0 %copy-start.2 = (bf16[16,2,32,256]{3,2,1,0:T(8,128)(2,1)S(1)}, bf16[16,2,32,256]{3,2,1,0:T(8,128)(2,1)}, u32[]{:S(2)}) copy-start(bf16[16,2,32,256]{3,2,1,0:T(8,128)(2,1)} %own.3) | copy-start | bytes 1572868
  25.1 6.0 %copy-start.4 = (bf16[128,256]{1,0:T(8,128)(2,1)S(1)}, bf16[128,256]{1,0:T(8,128)(2,1)}, u32[]{:S(2)}) copy-start(bf16[128,256]{1,0:T(8,128)(2,1)} %phi.3) | copy-start | bytes 196612
  25.1 6.0 %copy-start.7 = (s32[16,16]{1,0:T(8,128)S(1)}, s32[16,16]{1,0:T(8,128)}, u32[]{:S(2)}) copy-start(s32[16,16]{1,0:T(8,128)} %ids.3) | copy-start | bytes 3076
  25.1 6.0 %copy-start.8 = (s32[16,16]{1,0:T(8,128)S(1)}, s32[16,16]{1,0:T(8,128)}, u32[]{:S(2)}) copy-start(s32[16,16]{1,0:T(8,128)} %offsets.3) | copy-start | bytes 3076
  27.1 17.4 %collective-permute-start.10 = (bf16[32,32,128]{2,1,0:T(8,128)(2,1)S(1)}, bf16[32,32,128]{2,1,0:T(8,128)(2,1)S(1)}, u32[]{:S(2)}, u32[]{:S(2)}) collective-permute-start(bf16[32,32,128]{2,1,0:T(8,128)(2,1)S(1)} %get-tuple-element.46), channel_id=1, source_target_pairs={{0,3},{1,2},{2,1},{3,0},{4,7},{5,6},{6,5},{7,4},{8,11},{9,10},{10,... | collective-permute-start | bytes 786440 | tf_op jit(solution)/shard_map/ppermute | solution.py:20
  27.2 17.3 %collective-permute-start.11 = (bf16[32,32,128]{2,1,0:T(8,128)(2,1)S(1)}, bf16[32,32,128]{2,1,0:T(8,128)(2,1)S(1)}, u32[]{:S(2)}, u32[]{:S(2)}) collective-permute-start(bf16[32,32,128]{2,1,0:T(8,128)(2,1)S(1)} %get-tuple-element.63), channel_id=1, source_target_pairs={{0,2},{1,3},{2,0},{3,1},{4,6},{5,7},{6,4},{7,5},{8,10},{9,11},{10,... | collective-permute-start | bytes 786440 | tf_op jit(solution)/shard_map/ppermute | solution.py:20
  34.8 9.8 %collective-permute-start.7 = (bf16[4,64,128]{2,1,0:T(8,128)(2,1)S(1)}, bf16[4,64,128]{2,1,0:T(8,128)(2,1)S(1)}, u32[]{:S(2)}, u32[]{:S(2)}) collective-permute-start(bf16[4,64,128]{2,1,0:T(8,128)(2,1)S(1)} %get-tuple-element.52), channel_id=1, source_target_pairs={{0,3},{1,2},{2,1},{3,0},{4,7},{5,6},{6,5},{7,4},{8,11},{9,10},{10,... | collective-permute-start | bytes 196616 | tf_op jit(solution)/shard_map/ppermute | solution.py:20
  40.0 4.6 %collective-permute-start.6 = (bf16[4,64,128]{2,1,0:T(8,128)(2,1)S(1)}, bf16[4,64,128]{2,1,0:T(8,128)(2,1)S(1)}, u32[]{:S(2)}, u32[]{:S(2)}) collective-permute-start(bf16[4,64,128]{2,1,0:T(8,128)(2,1)S(1)} %get-tuple-element.57), channel_id=1, source_target_pairs={{0,2},{1,3},{2,0},{3,1},{4,6},{5,7},{6,4},{7,5},{8,10},{9,11},{10,... | collective-permute-start | bytes 196616 | tf_op jit(solution)/shard_map/ppermute | solution.py:20
  44.4 1.7 %copy-start.13 = (bf16[64,128]{1,0:T(8,128)(2,1)S(1)}, bf16[64,128]{1,0:T(8,128)(2,1)}, u32[]{:S(2)}) copy-start(bf16[64,128]{1,0:T(8,128)(2,1)} %refs_8_.1) | copy-start | bytes 49156
  44.4 1.7 %collective-permute-start.9 = (bf16[40,32,128]{2,1,0:T(8,128)(2,1)S(1)}, bf16[40,32,128]{2,1,0:T(8,128)(2,1)S(1)}, u32[]{:S(2)}, u32[]{:S(2)}) collective-permute-start(bf16[40,32,128]{2,1,0:T(8,128)(2,1)S(1)} %get-tuple-element.62), channel_id=1, source_target_pairs={{0,1},{1,0},{2,3},{3,2},{4,5},{5,4},{6,7},{7,6},{8,9},{9,8},{10,11... | collective-permute-start | bytes 983048 | tf_op jit(solution)/shard_map/ppermute | solution.py:20

commit v6 on v5

--- a/solution.py
+++ b/solution.py
@@ -20,7 +20,7 @@
     return lax.ppermute(value, axis, pairs)
 
 
-COSTS = {"join": 0, "sums_third": 0, "shift": 0, "sums_fourth": 0, "upper_near": 0}
+COSTS = {"join": 0, "sums_third": 0, "shift": 0, "close_peers": 0, "close_self": 0}
 
 
 def after(value, *others):
@@ -133,17 +133,10 @@
 
 
 def shift_body(peers, rows, low, me, *refs):
-    parts, near = refs[:peers], refs[peers : peers + 3]
-    shifted, trig, expand, mix, angles, theta, phi, sems = refs[peers + 3 :]
-    for copy in fetch(list(zip(near, (angles, theta, phi), strict=True)), sems):
+    parts, near = refs[:peers], refs[peers : peers + 2]
+    shifted, trig, mix, angles, phi, sems = refs[peers + 2 :]
+    for copy in fetch(list(zip(near, (angles, phi), strict=True)), sems):
         copy.wait()
-    orders = theta.shape[0]
-    line = lax.broadcasted_iota(jnp.int32, (2 * orders, orders), 0)
-    column = lax.broadcasted_iota(jnp.int32, (2 * orders, orders), 1)
-    for c in range(2):
-        pick = (line == 2 * column + c).astype(F32).astype(BF16)
-        spread = jnp.dot(pick, theta[...], preferred_element_type=F32)
-        expand[c] = spread.astype(BF16)
     size = phi.shape[1]
     mix[0:size, 0:size] = phi[0]
     mix[0:size, size:] = -phi[1]
@@ -171,24 +164,34 @@
                 trig[1, side * half + c, place] = jnp.sin(angle)
 
 
-def join(owns, got, extra=None):
-    shapes = [struct(a.shape, BF16) for a in owns]
-    if extra is not None:
-        shapes[0] = struct((owns[0].shape[0] + extra.shape[0], *extra.shape[1:]), BF16)
-
+def join(owns, got):
     def body(*refs):
         first = 0
         count = len(owns)
-        outs = refs[-count:]
-        for own, out in zip(refs[:count], outs, strict=True):
+        for own, out in zip(refs[:count], refs[count + 1 :], strict=True):
             size = own.shape[0]
-            out[0:size] = (own[...] + refs[count][first : first + size].astype(F32)).astype(BF16)
+            out[...] = (own[...] + refs[count][first : first + size].astype(F32)).astype(BF16)
             first += size
-        if extra is not None:
-            outs[0][owns[0].shape[0] :] = refs[count + 1][...]
-
-    more = [] if extra is None else [extra]
-    return kernel_call(body, shapes, [], [*owns, got, *more], "join")
+
+    return kernel_call(body, [struct(a.shape, BF16) for a in owns], [], [*owns, got], "join")
+
+
+def close_body(masks, firsts, per, entries, me, code, table, source, got, *refs):
+    count = len(masks)
+    rows = table.shape[1] // 2
+    for mask, begin, piece, out in zip(masks, firsts, refs[:count], refs[count:], strict=True):
+        first = jnp.bitwise_xor(me[0], mask) * per
+
+        def one(i, carry, first=first, begin=begin, out=out):
+            real, imag = box_sum(first + i, entries, code, table, source)
+            real = real + got[begin + i, 0:rows].astype(F32)
+            imag = imag + got[begin + i, rows:].astype(F32)
+            out[i, 0:rows] = real.astype(BF16)
+            out[i, rows:] = imag.astype(BF16)
+            return carry
+
+        lax.fori_loop(0, per, one, 0, unroll=2)
+        out[per:] = piece[...]
 
 
 def upper_body(masks, peers, entries, me, home, ids, offsets, own, far, table, shifted, phi, *refs):
@@ -229,26 +232,25 @@
 
 
 def final_body(peers, parents, me, *refs):
-    ups, lows = list(refs[: peers - 1]), refs[peers - 1 : 2 * peers - 1]
-    ups.insert(1, None)
-    trig, theta, mix, expand, out, rows_up, rows_low, pattern, ready, sems = refs[2 * peers - 1 :]
+    near = peers // 2
+    ups, lows = refs[:near], refs[near : near + peers]
+    trig, theta, mix, expand, out, rows_up, rows_low, turned, ready, sems = refs[near + peers :]
     children, rows = trig.shape[1], trig.shape[2]
     high_rows, low_rows = rows_up.shape[3], rows_low.shape[3]
-    both = jnp.concatenate([expand[0], expand[1]], axis=1)
-    size = both.shape[0]
-    block_rows = children * size
-    copies = []
+    orders = expand.shape[0]
+    boxes = parents * children
     for mask in range(peers):
         place = jnp.bitwise_xor(me[0], mask)
         for c in range(2):
             for b in range(parents):
-                if mask == 1:
-                    piece = lows[1][parents * children + 2 * b + c]
+                if mask < near:
+                    piece = lows[mask][boxes + 2 * b + c]
                 else:
-                    piece = ups[mask][b, c * high_rows : (c + 1) * high_rows]
+                    piece = ups[mask - near][b, c * high_rows : (c + 1) * high_rows]
                 rows_up[b, c, place] = piece.astype(F32)
-            piece = lows[mask][0 : parents * children, c * low_rows : (c + 1) * low_rows]
+            piece = lows[mask][0:boxes, c * low_rows : (c + 1) * low_rows]
             rows_low[:, c, place] = piece.astype(F32)
+    copies = []
     for b in range(parents):
         coarse = []
         for c in range(2):
@@ -259,24 +261,19 @@
             box = b * children + k
             real = coarse[0] * cosine - coarse[1] * sine + rows_low[box, 0].reshape(rows, 128)
             imag = coarse[0] * sine + coarse[1] * cosine + rows_low[box, 1].reshape(rows, 128)
-            pattern[k * rows : (k + 1) * rows, 0:128] = real.astype(BF16)
-            pattern[k * rows : (k + 1) * rows, 128:256] = imag.astype(BF16)
-        for k in range(0, children, 2):
-            block = pattern[k * rows : (k + 2) * rows]
-            turned = lax.dot_general(block, mix[...], NT, preferred_element_type=F32)
-            one, two = turned[:rows], turned[rows:]
-            stacked = jnp.concatenate(
-                [
-                    jnp.concatenate([one[:, :128], two[:, :128]], axis=1),
-                    jnp.concatenate([one[:, 128:], two[:, 128:]], axis=1),
-                ],
-                axis=0,
-            )
-            result = split_dot(both, stacked, (((1,), (0,)), ((), ())))
-            start = b * block_rows + k * size
-            ready[start : start + size] = result[:, :128]
-            ready[start + size : start + 2 * size] = result[:, 128:]
-        span = pl.ds(b * block_rows, block_rows)
+            pattern = jnp.concatenate([real.astype(BF16), imag.astype(BF16)], axis=1)
+            half = jnp.dot(expand[...], pattern, preferred_element_type=F32)
+            high = half.astype(BF16)
+            turned[k * orders : (k + 1) * orders] = high
+            low = (half - high.astype(F32)).astype(BF16)
+            turned[(children + k) * orders : (children + k + 1) * orders] = low
+        both = lax.dot_general(turned[...], mix[...], NT, preferred_element_type=F32)
+        size = children * orders
+        result = both[:size] + both[size:]
+        start = b * 2 * size
+        ready[pl.ds(start, size, stride=2)] = result[:, :128]
+        ready[pl.ds(start + 1, size, stride=2)] = result[:, 128:]
+        span = pl.ds(start, 2 * size)
         copies += fetch([(ready.at[span], out.at[span])], sems.at[pl.ds(b, 1)])
     for copy in copies:
         copy.wait()
@@ -390,48 +387,47 @@
         "sums_third",
     )
     lows = dict(zip(outer, join(own_outer, got_outer), strict=True))
-    orders, angles = switch_theta.shape
+    orders = switch_theta.shape[0]
     azimuths = switch_phi.shape[1]
-    shifted, trig, expand, mix = kernel_call(
+    shifted, trig, mix = kernel_call(
         functools.partial(shift_body, peers, rows, low),
         [
             struct((upper_boxes, 2, rows, wide), F32),
             struct((2, children, peers, low, lanes), F32),
-            struct((2, 2 * orders, angles), BF16),
             struct((2 * azimuths, 2 * azimuths), BF16),
         ],
         [after(me, lows[outer[0]])],
-        [*parts, angles_upper, switch_theta, switch_phi],
+        [*parts, angles_upper, switch_phi],
         "shift",
         scratch=[
-            *(pltpu.VMEM(a.shape, a.dtype) for a in (angles_upper, switch_theta, switch_phi)),
-            pltpu.SemaphoreType.DMA((3,)),
-        ],
-        held=3,
+            *(pltpu.VMEM(a.shape, a.dtype) for a in (angles_upper, switch_phi)),
+            pltpu.SemaphoreType.DMA((2,)),
+        ],
+        held=2,
     )
     trig = trig.reshape(2, children, peers * low, lanes)
-    def upper(masks, order, name):
-        return kernel_call(
-            functools.partial(upper_body, masks, peers, entries),
-            [struct((upper_per, 2 * rows, lanes), BF16)] * len(masks),
-            [order, home.astype(jnp.int32).reshape(1), list_upper, offset_upper],
-            [outgoing_upper, far_upper, table_upper, shifted, phi_lower],
+    ups = kernel_call(
+        functools.partial(upper_body, outer + inner, peers, entries),
+        [struct((upper_per, 2 * rows, lanes), BF16)] * peers,
+        [me, home.astype(jnp.int32).reshape(1), list_upper, offset_upper],
+        [outgoing_upper, far_upper, table_upper, shifted, phi_lower],
+        "upper",
+        scratch=[pltpu.VMEM((2 * upper_boxes, 2, rows, wide), F32)],
+    )
+    ups = dict(zip(outer + inner, ups, strict=True))
+    order = after(me, ups[0])
+    behind = {mask: ups.pop(mask).reshape(-1, 2 * low, lanes) for mask in inner}
+    for masks, name in ((inner[:-1], "close_peers"), (inner[-1:], "close_self")):
+        close = kernel_call(
+            functools.partial(close_body, masks, [per * inner.index(m) for m in masks], per, entries),
+            [struct((per + behind[0].shape[0], 2 * low, lanes), BF16)] * len(masks),
+            [order, own_code],
+            [table, source, got_inner, *(behind[mask] for mask in masks)],
             name,
-            scratch=[pltpu.VMEM((2 * upper_boxes, 2, rows, wide), F32)],
         )
-
-    ups = dict(zip(outer, upper(outer, me, "upper_far"), strict=True))
-    own_inner = sums(
-        [((mask,), 0) for mask in inner],
-        [own_shape] * len(inner),
-        [own_code],
-        after(me, ups[outer[0]]),
-        "sums_fourth",
-    )
-    ups.update(zip(inner, upper(inner, after(me, own_inner[0]), "upper_near"), strict=True))
-    near = ups[1].reshape(-1, 2 * low, lanes)
-    lows.update(zip(inner, join(own_inner, got_inner, near), strict=True))
-    ups = [swap(ups[mask], "angle", mask) if mask else ups[0] for mask in range(peers) if mask != 1]
+        lows.update(zip(masks, close, strict=True))
+        order = after(me, close[0])
+    ups = [swap(ups[mask], "angle", mask) for mask in reversed(outer)]
     lows = [swap(lows[mask], "angle", mask) if mask else lows[mask] for mask in range(peers)]
 
     arrived = kernel_call(
@@ -446,13 +442,13 @@
         functools.partial(final_body, peers, upper_per),
         [struct((per * 2 * orders, azimuths), F32)],
         [me],
-        [*ups, *lows, trig, theta_lower, mix, expand],
+        [*ups, *lows, trig, theta_lower, mix, switch_theta],
         "expand",
         scratch=[
             pltpu.VMEM((upper_per, 2, peers, rows, lanes), F32),
             pltpu.VMEM((per, 2, peers, low, lanes), F32),
-            pltpu.VMEM((children * peers * low, 2 * lanes), BF16),
-            pltpu.VMEM((per * 2 * orders, azimuths), F32),
+            pltpu.VMEM((2 * children * orders, 2 * lanes), BF16),
+            pltpu.VMEM((per * 2 * orders + 8, azimuths), F32),
             pltpu.SemaphoreType.DMA((upper_per,)),
         ],
         away=1,

time: 50.5 us -> 47.5 us (0.941)
  Pallas kernels: 32.3 us -> 29.1 us
  waiting for transfers between devices: 3.36 us -> 2.75 us
    pallas_call x12 -> x11, Pallas kernels: 32.3 us -> 29.1 us  [kernel_call(): pl.pallas_call(body, out_shape=outs, in_specs=[SM] * len(scalars) + [VM]...]
    ppermute x12, waiting for transfers between devices: 3.36 us -> 2.75 us  [swap(): return lax.ppermute(value, axis, pairs)]
where the time goes in v6:
time: 47.5 us; the launch traced here: 47.2 us
  Pallas kernels  29.1 us (61%)
  starting transfers between devices  13.6 us (29%)
  waiting for transfers between devices  2.75 us (6%)
  local copies, waits for them, and re-layouts  0.74 us (2%)
  other arithmetic  0.73 us (2%)
    pallas_call x11, Pallas kernels, kernel_call(): pl.pallas_call(body, out_shape=outs, in_specs=[SM] * len(scalars) + [VM]...  29.1 us
    ppermute x12, starting transfers between devices, swap(): return lax.ppermute(value, axis, pairs)  13.6 us
    ppermute x12, waiting for transfers between devices, swap(): return lax.ppermute(value, axis, pairs)  2.75 us
  transfers between devices with their start and end apart: 12, of which 2 were waited for; matrix products, arithmetic and copies ran while one was open for 0% of the time, Pallas kernels for 56%

profile of v6, /device:TPU:0, one launch (start us, length us, event | category | flops | bytes accessed | tf_op | source)
XLA Modules:
  0.0 47.2 jit_solution(16866552688669517604)
XLA Ops:
  0.0 0.7 %bitcast_add_fusion = (s32[16,128]{1,0:T(8,128)S(1)}, s32[16,128]{1,0:T(8,128)S(1)}) fusion(s32[128,16]{0,1:T(8,128)} %param.31, s32[128,16]{0,1:T(8,128)} %param.30, s32[]{:T(128)} %axis_index.25), kind=kLoop, calls=%fused_computation.6 | loop fusion | flops 53248 | bytes 32772 | tf_op jit(solution)/shard_map/add | solution.py:318
  0.7 3.0 %collective-permute-start.1 = (s32[16,128]{1,0:T(8,128)S(1)}, s32[16,128]{1,0:T(8,128)S(1)}, u32[]{:S(2)}, u32[]{:S(2)}) collective-permute-start(s32[16,128]{1,0:T(8,128)S(1)} %get-tuple-element.60), channel_id=1, source_target_pairs={{0,4},{4,0},{8,12},{12,8},{16,20},{20,16},{24,28},{28,24},{1,5},{5... | collective-permute-start | bytes 24584 | tf_op jit(solution)/shard_map/ppermute | solution.py:20
  3.7 2.6 %collective-permute-start = (bf16[16,2,32,256]{3,2,1,0:T(8,128)(2,1)}, bf16[16,2,32,256]{3,2,1,0:T(8,128)(2,1)S(1)}, u32[]{:S(2)}, u32[]{:S(2)}) collective-permute-start(bf16[16,2,32,256]{3,2,1,0:T(8,128)(2,1)} %own.1), channel_id=1, source_target_pairs={{0,16},{4,20},{8,24},{12,28},{16,0},{20,4},{24,8},{28,12},{1,17},{... | collective-permute-start | bytes 1572872 | tf_op jit(solution)/shard_map/ppermute | solution.py:20
  6.3 0.0 collective-permute-done.1.code.refs_0_
  6.3 0.0 copy-start.6
  6.3 0.0 copy-start.7
  6.3 0.0 copy-start.8
  6.4 5.7 %sums_first.1 = (bf16[64,32,128]{2,1,0:T(8,128)(2,1)S(1)}, f32[316,32,128]{2,1,0:T(8,128)}, f32[129,32,128]{2,1,0:T(8,128)}) custom-call(s32[1]{0:T(128)} %bitcast.me, s32[16,128]{1,0:T(8,128)S(1)} %collective-permute-done.1.code.refs_0_, bf16[316,32,128]{2,1,0:T(8,128)(2,1)} %bitcast.56, bf16[128,32,128]{2,1,0:T(8,128)(2,1)} %bitcast.57), custom_call_target="tpu_custom_call" | custom-call | flops 4294967296 | bytes 1 | tf_op jit(solution)/shard_map/sums_first/pallas_call | solution.py:32
  12.1 1.1 %collective-permute-start.2 = (bf16[64,32,128]{2,1,0:T(8,128)(2,1)S(1)}, bf16[64,32,128]{2,1,0:T(8,128)(2,1)S(1)}, u32[]{:S(2)}, u32[]{:S(2)}) collective-permute-start(bf16[64,32,128]{2,1,0:T(8,128)(2,1)S(1)} %get-tuple-element.32), channel_id=1, source_target_pairs={{0,4},{4,0},{8,12},{12,8},{16,20},{20,16},{24,28},{28,24},{1,5},{5... | collective-permute-start | bytes 1572872 | tf_op jit(solution)/shard_map/ppermute | solution.py:20
  13.2 0.0 copy-done.5
  13.2 0.0 copy-done.6
  13.2 0.0 copy-done.7
  13.2 0.0 copy-done.8
  13.2 0.0 copy-start
  13.2 0.0 copy-start.1
  13.2 1.0 %early.1 = (f32[192,256]{1,0:T(8,128)S(1)}, f32[192,256]{1,0:T(8,128)S(1)}, f32[192,256]{1,0:T(8,128)S(1)}, f32[192,256]{1,0:T(8,128)S(1)}) custom-call(s32[1]{0:T(128)} %bitcast.me, bf16[256,512]{1,0:T(8,128)(2,1)S(1)} %bitcast.55, bf16[128,256]{1,0:T(8,128)(2,1)S(1)} %copy-done.7, bf16[256,512]{1,0:T(8,128)(2,1)S(1)} %copy-done.6, f32[8,16,128]{2,1,0:T(8,128)S(1)} %copy-done.8), custom_call_target="tpu_custom_call" | custom-call | flops 4294967296 | bytes 1 | tf_op jit(solution)/shard_map/early/pallas_call | solution.py:32
  14.2 0.1 collective-permute-start.3
  14.3 1.6 %collective-permute-start.4 = (f32[192,256]{1,0:T(8,128)S(1)}, f32[192,256]{1,0:T(8,128)S(1)}, u32[]{:S(2)}, u32[]{:S(2)}) collective-permute-start(f32[192,256]{1,0:T(8,128)S(1)} %get-tuple-element.44), channel_id=1, source_target_pairs={{0,2},{1,3},{2,0},{3,1},{4,6},{5,7},{6,4},{7,5},{8,10},{9,11},{10,... | collective-permute-start | bytes 589832 | tf_op jit(solution)/shard_map/ppermute | solution.py:20
  15.9 0.3 collective-permute-start.5
  16.1 0.0 copy-done
  16.2 0.2 copy-done.1
  16.3 3.5 %sums_second.1 = bf16[64,32,128]{2,1,0:T(8,128)(2,1)S(1)} custom-call(s32[1]{0:T(128)} %bitcast.me, s32[16,128]{1,0:T(8,128)S(1)} %collective-permute-done.1.code.refs_0_, f32[316,32,128]{2,1,0:T(8,128)S(1)} %copy-done, f32[129,32,128]{2,1,0:T(8,128)S(1)} %copy-done.1), custom_call_target="tpu_custom_call" | custom-call | flops 4294967296 | bytes 1 | tf_op jit(solution)/shard_map/sums_second/pallas_call | solution.py:32
  19.8 0.0 collective-permute-done.3.refs_1_
  19.8 1.0 %collective-permute-start.8 = (bf16[64,32,128]{2,1,0:T(8,128)(2,1)S(1)}, bf16[64,32,128]{2,1,0:T(8,128)(2,1)S(1)}, u32[]{:S(2)}, u32[]{:S(2)}) collective-permute-start(bf16[64,32,128]{2,1,0:T(8,128)(2,1)S(1)} %sums_second.1), channel_id=1, source_target_pairs={{0,4},{4,0},{8,12},{12,8},{16,20},{20,16},{24,28},{28,24},{1,5},{5... | collective-permute-start | bytes 1572872 | tf_op jit(solution)/shard_map/ppermute | solution.py:20
  20.9 3.4 %sums_third.1 = (f32[32,32,128]{2,1,0:T(8,128)S(1)}, f32[32,32,128]{2,1,0:T(8,128)S(1)}) custom-call(s32[1]{0:T(128)} %bitcast.me, s32[16,128]{1,0:T(8,128)S(1)} %get-tuple-element.59.refs_0_.code, f32[316,32,128]{2,1,0:T(8,128)S(1)} %copy-done, f32[129,32,128]{2,1,0:T(8,128)S(1)} %copy-done.1), custom_call_target="tpu_custom_call" | custom-call | bytes 1 | tf_op jit(solution)/shard_map/sums_third/pallas_call | solution.py:32
  24.3 0.0 copy-start.4
  24.3 0.0 copy-start.9
  24.4 0.0 copy-start.12
  24.4 0.0 copy-start.13
  24.4 2.6 %collective-permute-done.2.refs_2_ = bf16[64,32,128]{2,1,0:T(8,128)(2,1)S(1)} collective-permute-done((bf16[64,32,128]{2,1,0:T(8,128)(2,1)S(1)}, bf16[64,32,128]{2,1,0:T(8,128)(2,1)S(1)}, u32[]{:S(2)}, u32[]{:S(2)}) %collective-permute-start.2) | collective-permute-done | bytes 524320 | tf_op jit(solution)/shard_map/ppermute | solution.py:20
  27.0 0.1 join.1
  27.1 0.1 collective-permute-start.10
  27.2 0.0 collective-permute-done.4.refs_2_
  27.2 1.6 %collective-permute-start.11 = (bf16[32,32,128]{2,1,0:T(8,128)(2,1)S(1)}, bf16[32,32,128]{2,1,0:T(8,128)(2,1)S(1)}, u32[]{:S(2)}, u32[]{:S(2)}) collective-permute-start(bf16[32,32,128]{2,1,0:T(8,128)(2,1)S(1)} %get-tuple-element.54), channel_id=1, source_target_pairs={{0,2},{1,3},{2,0},{3,1},{4,6},{5,7},{6,4},{7,5},{8,10},{9,11},{10,... | collective-permute-start | bytes 786440 | tf_op jit(solution)/shard_map/ppermute | solution.py:20
  28.8 0.0 collective-permute-done.5.refs_3_
  28.8 0.0 copy-done.2
  28.8 0.0 copy-done.3
  28.8 2.2 %shift.1 = (f32[16,2,32,256]{3,2,1,0:T(8,128)S(1)}, f32[2,8,4,16,128]{4,3,2,1,0:T(8,128)S(1)}, bf16[256,256]{1,0:T(8,128)(2,1)S(1)}) custom-call(s32[1]{0:T(128)} %bitcast.me, f32[192,256]{1,0:T(8,128)S(1)} %get-tuple-element.34.refs_0_, f32[192,256]{1,0:T(8,128)S(1)} %collective-permute-done.3.refs_1_, f32[192,256]{1,0:T(8,128)S(1)} %collective-permute-done.4.refs_2_, ...), custom_call_target="tpu_custom_call" | custom-call | bytes 1 | tf_op jit(solution)/shard_map/shift/pallas_call | solution.py:32
  31.0 0.0 collective-permute-done.far
  31.0 0.0 slice-done
  31.0 0.0 slice-done.1
  31.0 0.0 slice-done.2
  31.0 0.0 copy-done.4
  31.0 0.0 copy-done.9
  31.0 0.0 copy-done.12
  31.0 0.0 copy-done.13
  31.0 6.4 %upper.1 = (bf16[4,64,128]{2,1,0:T(8,128)(2,1)S(1)}, bf16[4,64,128]{2,1,0:T(8,128)(2,1)S(1)}, bf16[4,64,128]{2,1,0:T(8,128)(2,1)S(1)}, bf16[4,64,128]{2,1,0:T(8,128)(2,1)S(1)}) custom-call(s32[1]{0:T(128)} %bitcast.me, s32[1]{0:T(128)} %bitcast.1.home, s32[16,16]{1,0:T(8,128)S(1)} %copy-done.12, s32[16,16]{1,0:T(8,128)S(1)} %copy-done.13, ...), custom_call_target="tpu_custom_call" | custom-call | flops 4294967296 | bytes 1 | tf_op jit(solution)/shard_map/upper/pallas_call | solution.py:32
  37.4 0.5 %collective-permute-start.6 = (bf16[4,64,128]{2,1,0:T(8,128)(2,1)S(1)}, bf16[4,64,128]{2,1,0:T(8,128)(2,1)S(1)}, u32[]{:S(2)}, u32[]{:S(2)}) collective-permute-start(bf16[4,64,128]{2,1,0:T(8,128)(2,1)S(1)} %get-tuple-element.47), channel_id=1, source_target_pairs={{0,2},{1,3},{2,0},{3,1},{4,6},{5,7},{6,4},{7,5},{8,10},{9,11},{10,... | collective-permute-start | bytes 196616 | tf_op jit(solution)/shard_map/ppermute | solution.py:20
  38.0 1.1 %collective-permute-start.7 = (bf16[4,64,128]{2,1,0:T(8,128)(2,1)S(1)}, bf16[4,64,128]{2,1,0:T(8,128)(2,1)S(1)}, u32[]{:S(2)}, u32[]{:S(2)}) collective-permute-start(bf16[4,64,128]{2,1,0:T(8,128)(2,1)S(1)} %get-tuple-element.48), channel_id=1, source_target_pairs={{0,3},{1,2},{2,1},{3,0},{4,7},{5,6},{6,5},{7,4},{8,11},{9,10},{10,... | collective-permute-start | bytes 196616 | tf_op jit(solution)/shard_map/ppermute | solution.py:20
  39.1 0.0 collective-permute-done.8.got
  39.1 2.1 %close_peers.1 = bf16[40,32,128]{2,1,0:T(8,128)(2,1)S(1)} custom-call(s32[1]{0:T(128)} %bitcast.me, s32[16,128]{1,0:T(8,128)S(1)} %get-tuple-element.59.refs_0_.code, f32[316,32,128]{2,1,0:T(8,128)S(1)} %copy-done, f32[129,32,128]{2,1,0:T(8,128)S(1)} %copy-done.1, bf16[64,32,128]{2,1,0:T(8,128)(2,1)S(1)} %collective-permute-done.8.got, ...), custom_call_target="tpu_custom_call" | custom-call | bytes 1 | tf_op jit(solution)/shard_map/close_peers/pallas_call | solution.py:32
  41.2 0.6 %collective-permute-start.9 = (bf16[40,32,128]{2,1,0:T(8,128)(2,1)S(1)}, bf16[40,32,128]{2,1,0:T(8,128)(2,1)S(1)}, u32[]{:S(2)}, u32[]{:S(2)}) collective-permute-start(bf16[40,32,128]{2,1,0:T(8,128)(2,1)S(1)} %close_peers.1), channel_id=1, source_target_pairs={{0,1},{1,0},{2,3},{3,2},{4,5},{5,4},{6,7},{7,6},{8,9},{9,8},{10,11... | collective-permute-start | bytes 983048 | tf_op jit(solution)/shard_map/ppermute | solution.py:20
  41.8 2.1 %close_self.1.refs_2_ = bf16[40,32,128]{2,1,0:T(8,128)(2,1)S(1)} custom-call(s32[1]{0:T(128)} %bitcast.me, s32[16,128]{1,0:T(8,128)S(1)} %get-tuple-element.59.refs_0_.code, f32[316,32,128]{2,1,0:T(8,128)S(1)} %copy-done, f32[129,32,128]{2,1,0:T(8,128)S(1)} %copy-done.1, bf16[64,32,128]{2,1,0:T(8,128)(2,1)S(1)} %collective-permute-done.8.got, ...), custom_call_target="tpu_custom_call" | custom-call | bytes 1 | tf_op jit(solution)/shard_map/close_self/pallas_call | solution.py:32
  43.9 0.0 copy-start.10
  43.9 0.0 copy-start.11
  43.9 0.0 collective-permute-done.10.refs_0_
  43.9 0.0 collective-permute-done.11.refs_1_
  43.9 0.1 place.1
  44.0 0.0 collective-permute-done.6.refs_0_
  44.0 0.1 collective-permute-done.7.refs_1_
  44.1 0.0 collective-permute-done.9.refs_3_
  44.1 0.5 copy-done.10
  44.6 0.0 copy-done.11
  44.6 2.6 %expand.1 = f32[4096,128]{1,0:T(8,128)} custom-call(s32[1]{0:T(128)} %bitcast.me, bf16[4,64,128]{2,1,0:T(8,128)(2,1)S(1)} %collective-permute-done.6.refs_0_, bf16[4,64,128]{2,1,0:T(8,128)(2,1)S(1)} %collective-permute-done.7.refs_1_, bf16[40,32,128]{2,1,0:T(8,128)(2,1)S(1)} %close_self.1.refs_2_, bf16[40,32,128]{2,1,0:T(8,128)(2,1)S(1)} %collective-permute-done.9.refs_3_, ...), custom_call_target="tpu_custom_call" | custom-call | flops 4294967296 | bytes 1 | tf_op jit(solution)/shard_map/expand/pallas_call | solution.py:32
  (7 shorter events, 0.0 us)
Async XLA Ops:
  0.7 5.6 %collective-permute-start.1 = (s32[16,128]{1,0:T(8,128)S(1)}, s32[16,128]{1,0:T(8,128)S(1)}, u32[]{:S(2)}, u32[]{:S(2)}) collective-permute-start(s32[16,128]{1,0:T(8,128)S(1)} %get-tuple-element.60), channel_id=1, source_target_pairs={{0,4},{4,0},{8,12},{12,8},{16,20},{20,16},{24,28},{28,24},{1,5},{5... | collective-permute-start | bytes 24584 | tf_op jit(solution)/shard_map/ppermute | solution.py:20
  3.7 27.2 %collective-permute-start = (bf16[16,2,32,256]{3,2,1,0:T(8,128)(2,1)}, bf16[16,2,32,256]{3,2,1,0:T(8,128)(2,1)S(1)}, u32[]{:S(2)}, u32[]{:S(2)}) collective-permute-start(bf16[16,2,32,256]{3,2,1,0:T(8,128)(2,1)} %own.1), channel_id=1, source_target_pairs={{0,16},{4,20},{8,24},{12,28},{16,0},{20,4},{24,8},{28,12},{1,17},{... | collective-permute-start | bytes 1572872 | tf_op jit(solution)/shard_map/ppermute | solution.py:20
  6.3 6.8 %copy-start.5 = (bf16[2,2,64,512]{3,2,1,0:T(8,128)(2,1)S(1)}, bf16[2,2,64,512]{3,2,1,0:T(8,128)(2,1)}, u32[]{:S(2)}) copy-start(bf16[2,2,64,512]{3,2,1,0:T(8,128)(2,1)} %param.17) | copy-start | bytes 786436
  6.3 6.8 %copy-start.6 = (bf16[256,512]{1,0:T(8,128)(2,1)S(1)}, bf16[256,512]{1,0:T(8,128)(2,1)}, u32[]{:S(2)}) copy-start(bf16[256,512]{1,0:T(8,128)(2,1)} %refs_2_.1) | copy-start | bytes 786436
  6.3 6.8 %copy-start.7 = (bf16[128,256]{1,0:T(8,128)(2,1)S(1)}, bf16[128,256]{1,0:T(8,128)(2,1)}, u32[]{:S(2)}) copy-start(bf16[128,256]{1,0:T(8,128)(2,1)} %refs_1_.1) | copy-start | bytes 196612
  6.3 6.8 %copy-start.8 = (f32[8,16,128]{2,1,0:T(8,128)S(1)}, f32[8,16,128]{2,1,0:T(8,128)}, u32[]{:S(2)}) copy-start(f32[8,16,128]{2,1,0:T(8,128)} %refs_3_.1) | copy-start | bytes 196612
  12.1 14.9 %collective-permute-start.2 = (bf16[64,32,128]{2,1,0:T(8,128)(2,1)S(1)}, bf16[64,32,128]{2,1,0:T(8,128)(2,1)S(1)}, u32[]{:S(2)}, u32[]{:S(2)}) collective-permute-start(bf16[64,32,128]{2,1,0:T(8,128)(2,1)S(1)} %get-tuple-element.32), channel_id=1, source_target_pairs={{0,4},{4,0},{8,12},{12,8},{16,20},{20,16},{24,28},{28,24},{1,5},{5... | collective-permute-start | bytes 1572872 | tf_op jit(solution)/shard_map/ppermute | solution.py:20
  13.2 3.0 %copy-start = (f32[316,32,128]{2,1,0:T(8,128)S(1)}, f32[316,32,128]{2,1,0:T(8,128)}, u32[]{:S(2)}) copy-start(f32[316,32,128]{2,1,0:T(8,128)} %get-tuple-element.36.refs_1_.table) | copy-start | bytes 15532036
  13.2 3.1 %copy-start.1 = (f32[129,32,128]{2,1,0:T(8,128)S(1)}, f32[129,32,128]{2,1,0:T(8,128)}, u32[]{:S(2)}) copy-start(f32[129,32,128]{2,1,0:T(8,128)} %get-tuple-element.37.refs_2_.source) | copy-start | bytes 6340612
  14.2 5.6 %collective-permute-start.3 = (f32[192,256]{1,0:T(8,128)S(1)}, f32[192,256]{1,0:T(8,128)S(1)}, u32[]{:S(2)}, u32[]{:S(2)}) collective-permute-start(f32[192,256]{1,0:T(8,128)S(1)} %get-tuple-element.43), channel_id=1, source_target_pairs={{0,1},{1,0},{2,3},{3,2},{4,5},{5,4},{6,7},{7,6},{8,9},{9,8},{10,11... | collective-permute-start | bytes 589832 | tf_op jit(solution)/shard_map/ppermute | solution.py:20
  14.3 12.9 %collective-permute-start.4 = (f32[192,256]{1,0:T(8,128)S(1)}, f32[192,256]{1,0:T(8,128)S(1)}, u32[]{:S(2)}, u32[]{:S(2)}) collective-permute-start(f32[192,256]{1,0:T(8,128)S(1)} %get-tuple-element.44), channel_id=1, source_target_pairs={{0,2},{1,3},{2,0},{3,1},{4,6},{5,7},{6,4},{7,5},{8,10},{9,11},{10,... | collective-permute-start | bytes 589832 | tf_op jit(solution)/shard_map/ppermute | solution.py:20
  15.9 12.9 %collective-permute-start.5 = (f32[192,256]{1,0:T(8,128)S(1)}, f32[192,256]{1,0:T(8,128)S(1)}, u32[]{:S(2)}, u32[]{:S(2)}) collective-permute-start(f32[192,256]{1,0:T(8,128)S(1)} %get-tuple-element.45), channel_id=1, source_target_pairs={{0,3},{1,2},{2,1},{3,0},{4,7},{5,6},{6,5},{7,4},{8,11},{9,10},{10,... | collective-permute-start | bytes 589832 | tf_op jit(solution)/shard_map/ppermute | solution.py:20
  16.3 14.6 %slice-start = ((s8[10354688]{0:T(1024)(128)(4,1)}), s8[4194304]{0:T(1024)(128)(4,1)S(1)}, s32[]{:S(2)}) async-start(s8[10354688]{0:T(1024)(128)(4,1)} %bitcast.52), calls=%async_computation | async-start | bytes 8388608
  16.3 14.6 %slice-start.1 = ((s8[10354688]{0:T(1024)(128)(4,1)}), s8[4194304]{0:T(1024)(128)(4,1)S(1)}, s32[]{:S(2)}) async-start(s8[10354688]{0:T(1024)(128)(4,1)} %bitcast.52), calls=%async_computation.1 | async-start | bytes 8388608
  19.8 19.2 %collective-permute-start.8 = (bf16[64,32,128]{2,1,0:T(8,128)(2,1)S(1)}, bf16[64,32,128]{2,1,0:T(8,128)(2,1)S(1)}, u32[]{:S(2)}, u32[]{:S(2)}) collective-permute-start(bf16[64,32,128]{2,1,0:T(8,128)(2,1)S(1)} %sums_second.1), channel_id=1, source_target_pairs={{0,4},{4,0},{8,12},{12,8},{16,20},{20,16},{24,28},{28,24},{1,5},{5... | collective-permute-start | bytes 1572872 | tf_op jit(solution)/shard_map/ppermute | solution.py:20
  20.9 7.9 %copy-start.2 = (f32[8,32,256]{2,1,0:T(8,128)S(1)}, f32[8,32,256]{2,1,0:T(8,128)}, u32[]{:S(2)}) copy-start(f32[8,32,256]{2,1,0:T(8,128)} %refs_4_.1) | copy-start | bytes 786436
  20.9 7.9 %copy-start.3 = (bf16[2,128,128]{2,1,0:T(8,128)(2,1)S(1)}, bf16[2,128,128]{2,1,0:T(8,128)(2,1)}, u32[]{:S(2)}) copy-start(bf16[2,128,128]{2,1,0:T(8,128)(2,1)} %refs_5_.1) | copy-start | bytes 196612
  20.9 10.1 %slice-start.2 = ((s8[10354688]{0:T(1024)(128)(4,1)}), s8[1966080]{0:T(1024)(128)(4,1)S(1)}, s32[]{:S(2)}) async-start(s8[10354688]{0:T(1024)(128)(4,1)} %bitcast.52), calls=%async_computation.2 | async-start | bytes 3932160
  24.3 6.7 %copy-start.4 = (bf16[16,2,32,256]{3,2,1,0:T(8,128)(2,1)S(1)}, bf16[16,2,32,256]{3,2,1,0:T(8,128)(2,1)}, u32[]{:S(2)}) copy-start(bf16[16,2,32,256]{3,2,1,0:T(8,128)(2,1)} %own.1) | copy-start | bytes 1572868
  24.3 6.7 %copy-start.9 = (bf16[128,256]{1,0:T(8,128)(2,1)S(1)}, bf16[128,256]{1,0:T(8,128)(2,1)}, u32[]{:S(2)}) copy-start(bf16[128,256]{1,0:T(8,128)(2,1)} %phi.1) | copy-start | bytes 196612
  24.4 6.7 %copy-start.12 = (s32[16,16]{1,0:T(8,128)S(1)}, s32[16,16]{1,0:T(8,128)}, u32[]{:S(2)}) copy-start(s32[16,16]{1,0:T(8,128)} %ids.1) | copy-start | bytes 3076
  24.4 6.7 %copy-start.13 = (s32[16,16]{1,0:T(8,128)S(1)}, s32[16,16]{1,0:T(8,128)}, u32[]{:S(2)}) copy-start(s32[16,16]{1,0:T(8,128)} %offsets.1) | copy-start | bytes 3076
  27.1 16.8 %collective-permute-start.10 = (bf16[32,32,128]{2,1,0:T(8,128)(2,1)S(1)}, bf16[32,32,128]{2,1,0:T(8,128)(2,1)S(1)}, u32[]{:S(2)}, u32[]{:S(2)}) collective-permute-start(bf16[32,32,128]{2,1,0:T(8,128)(2,1)S(1)} %get-tuple-element.41), channel_id=1, source_target_pairs={{0,3},{1,2},{2,1},{3,0},{4,7},{5,6},{6,5},{7,4},{8,11},{9,10},{10,... | collective-permute-start | bytes 786440 | tf_op jit(solution)/shard_map/ppermute | solution.py:20
  27.2 16.7 %collective-permute-start.11 = (bf16[32,32,128]{2,1,0:T(8,128)(2,1)S(1)}, bf16[32,32,128]{2,1,0:T(8,128)(2,1)S(1)}, u32[]{:S(2)}, u32[]{:S(2)}) collective-permute-start(bf16[32,32,128]{2,1,0:T(8,128)(2,1)S(1)} %get-tuple-element.54), channel_id=1, source_target_pairs={{0,2},{1,3},{2,0},{3,1},{4,6},{5,7},{6,4},{7,5},{8,10},{9,11},{10,... | collective-permute-start | bytes 786440 | tf_op jit(solution)/shard_map/ppermute | solution.py:20
  37.4 6.6 %collective-permute-start.6 = (bf16[4,64,128]{2,1,0:T(8,128)(2,1)S(1)}, bf16[4,64,128]{2,1,0:T(8,128)(2,1)S(1)}, u32[]{:S(2)}, u32[]{:S(2)}) collective-permute-start(bf16[4,64,128]{2,1,0:T(8,128)(2,1)S(1)} %get-tuple-element.47), channel_id=1, source_target_pairs={{0,2},{1,3},{2,0},{3,1},{4,6},{5,7},{6,4},{7,5},{8,10},{9,11},{10,... | collective-permute-start | bytes 196616 | tf_op jit(solution)/shard_map/ppermute | solution.py:20
  38.0 6.2 %collective-permute-start.7 = (bf16[4,64,128]{2,1,0:T(8,128)(2,1)S(1)}, bf16[4,64,128]{2,1,0:T(8,128)(2,1)S(1)}, u32[]{:S(2)}, u32[]{:S(2)}) collective-permute-start(bf16[4,64,128]{2,1,0:T(8,128)(2,1)S(1)} %get-tuple-element.48), channel_id=1, source_target_pairs={{0,3},{1,2},{2,1},{3,0},{4,7},{5,6},{6,5},{7,4},{8,11},{9,10},{10,... | collective-permute-start | bytes 196616 | tf_op jit(solution)/shard_map/ppermute | solution.py:20
  41.2 3.0 %collective-permute-start.9 = (bf16[40,32,128]{2,1,0:T(8,128)(2,1)S(1)}, bf16[40,32,128]{2,1,0:T(8,128)(2,1)S(1)}, u32[]{:S(2)}, u32[]{:S(2)}) collective-permute-start(bf16[40,32,128]{2,1,0:T(8,128)(2,1)S(1)} %close_peers.1), channel_id=1, source_target_pairs={{0,1},{1,0},{2,3},{3,2},{4,5},{5,4},{6,7},{7,6},{8,9},{9,8},{10,11... | collective-permute-start | bytes 983048 | tf_op jit(solution)/shard_map/ppermute | solution.py:20
  43.9 0.7 %copy-start.10 = (bf16[64,128]{1,0:T(8,128)(2,1)S(1)}, bf16[64,128]{1,0:T(8,128)(2,1)}, u32[]{:S(2)}) copy-start(bf16[64,128]{1,0:T(8,128)(2,1)} %refs_7_.1) | copy-start | bytes 49156
  43.9 0.7 %copy-start.11 = (bf16[64,64]{1,0:T(8,128)(2,1)S(1)}, bf16[64,64]{1,0:T(8,128)(2,1)}, u32[]{:S(2)}) copy-start(bf16[64,64]{1,0:T(8,128)(2,1)} %refs_9_.1) | copy-start | bytes 24580

commit v7 on v6

--- a/solution.py
+++ b/solution.py
@@ -87,8 +87,9 @@
             lax.fori_loop(0, per, one, 0, unroll=2)
 
 
-def first_body(groups, per, entries, me, code, table, source, out, *refs):
-    table_out, source_out, table_in, source_in, wide_table, wide_source, sems, back = refs
+def first_body(groups, per, entries, me, code, table, source, *refs):
+    outs = refs[: len(groups)]
+    table_out, source_out, table_in, source_in, wide_table, wide_source, sems, back = refs[len(groups) :]
     count, total = source.shape[0], table.shape[0]
     step = -(-total // 4)
     spans = [(k, min(k + step, total)) for k in range(0, total, step)]
@@ -102,7 +103,7 @@
         copy.wait()
         wide_table[lo:hi] = table_in[lo:hi].astype(F32)
     copies = fetch([(wide_table, table_out), (wide_source, source_out)], back)
-    sums_body(groups, per, entries, me, code, wide_table, wide_source, out)
+    sums_body(groups, per, entries, me, code, wide_table, wide_source, *outs)
     for copy in copies:
         copy.wait()
 
@@ -133,10 +134,12 @@
 
 
 def shift_body(peers, rows, low, me, *refs):
-    parts, near = refs[:peers], refs[peers : peers + 2]
-    shifted, trig, mix, angles, phi, sems = refs[peers + 2 :]
-    for copy in fetch(list(zip(near, (angles, phi), strict=True)), sems):
+    parts, near = refs[:peers], refs[peers : peers + 4]
+    shifted, trig, mix, low_out, switch_out, angles, phi, theta, switch, sems = refs[peers + 4 :]
+    for copy in fetch(list(zip(near, (angles, phi, theta, switch), strict=True)), sems):
         copy.wait()
+    low_out[...] = theta[...]
+    switch_out[...] = switch[...]
     size = phi.shape[1]
     mix[0:size, 0:size] = phi[0]
     mix[0:size, size:] = -phi[1]
@@ -210,7 +213,10 @@
             imag = [shifted[box, 1, span] for span in spans]
             for entry in range(entries):
                 offset, ident = offsets[box, entry], ids[box, entry]
-                place = lax.rem(ident, boxes)
+                if boxes & (boxes - 1):
+                    place = lax.rem(ident, boxes)
+                else:
+                    place = ident & (boxes - 1)
                 place = jnp.where(ident - place == home[0] * boxes, place, place + boxes)
                 for k, span in enumerate(spans):
                     fr, fi = table[offset, 0, span].astype(F32), table[offset, 1, span].astype(F32)
@@ -333,10 +339,10 @@
 
     own_shape = struct((per, 2 * low, lanes), F32)
     far_shape = struct((len(outer) * per, 2 * low, lanes), BF16)
-    first, table, source = kernel_call(
-        functools.partial(first_body, [(tuple(outer), 0)], per, entries),
+    *first, table, source = kernel_call(
+        functools.partial(first_body, [((mask,), 0) for mask in outer], per, entries),
         [
-            far_shape,
+            *[struct((per, 2 * low, lanes), BF16)] * len(outer),
             struct((places, 2 * low, lanes), F32),
             struct((boxes + 1, 2 * low, lanes), F32),
         ],
@@ -355,7 +361,7 @@
         away=2,
         vmem=53 << 20,
     )
-    got_outer = swap(first, "box", 1)
+    got_outer = [swap(value, "box", 1) for value in first]
 
     children = angles_lower.shape[0]
     part_rows = 4 * rows + children * low // 2
@@ -364,7 +370,7 @@
     parts = kernel_call(
         functools.partial(early_body, peers, rows),
         [struct((part_rows, wide), F32)] * peers,
-        [after(me, first)],
+        [after(me, first[0])],
         [top, theta_upper, phi_upper, angles_lower],
         "early",
         scratch=[
@@ -377,39 +383,45 @@
     )
     order = after(me, parts[0])
     parts = [swap(part, "angle", mask) if mask else part for mask, part in enumerate(parts)]
-    (second,) = sums([(tuple(inner), 0)], [far_shape], [far_code], order, "sums_second")
-    got_inner = swap(after(second, parts[1]), "box", 1)
     own_outer = sums(
         [((mask,), 0) for mask in outer],
         [own_shape] * len(outer),
         [own_code],
-        after(me, second),
+        order,
         "sums_third",
     )
-    lows = dict(zip(outer, join(own_outer, got_outer), strict=True))
+    lows = {}
+    for mask, own, got in list(zip(outer, own_outer, got_outer, strict=True))[: len(outer) // 2]:
+        (lows[mask],) = join([own], got)
+    (second,) = sums([(tuple(inner), 0)], [far_shape], [far_code], after(me, lows[outer[0]]), "sums_second")
+    got_inner = swap(second, "box", 1)
     orders = switch_theta.shape[0]
     azimuths = switch_phi.shape[1]
-    shifted, trig, mix = kernel_call(
+    shifted, trig, mix, theta_low, theta_switch = kernel_call(
         functools.partial(shift_body, peers, rows, low),
         [
             struct((upper_boxes, 2, rows, wide), F32),
             struct((2, children, peers, low, lanes), F32),
             struct((2 * azimuths, 2 * azimuths), BF16),
-        ],
-        [after(me, lows[outer[0]])],
-        [*parts, angles_upper, switch_phi],
+            struct(theta_lower.shape, BF16),
+            struct(switch_theta.shape, BF16),
+        ],
+        [after(me, second)],
+        [*parts, angles_upper, switch_phi, theta_lower, switch_theta],
         "shift",
         scratch=[
-            *(pltpu.VMEM(a.shape, a.dtype) for a in (angles_upper, switch_phi)),
-            pltpu.SemaphoreType.DMA((2,)),
-        ],
-        held=2,
-    )
+            *(pltpu.VMEM(a.shape, a.dtype) for a in (angles_upper, switch_phi, theta_lower, switch_theta)),
+            pltpu.SemaphoreType.DMA((4,)),
+        ],
+        held=4,
+    )
+    for mask, own, got in list(zip(outer, own_outer, got_outer, strict=True))[len(outer) // 2 :]:
+        (lows[mask],) = join([after(own, trig)], got)
     trig = trig.reshape(2, children, peers * low, lanes)
     ups = kernel_call(
         functools.partial(upper_body, outer + inner, peers, entries),
         [struct((upper_per, 2 * rows, lanes), BF16)] * peers,
-        [me, home.astype(jnp.int32).reshape(1), list_upper, offset_upper],
+        [after(me, lows[outer[-1]]), home.astype(jnp.int32).reshape(1), list_upper, offset_upper],
         [outgoing_upper, far_upper, table_upper, shifted, phi_lower],
         "upper",
         scratch=[pltpu.VMEM((2 * upper_boxes, 2, rows, wide), F32)],
@@ -442,7 +454,7 @@
         functools.partial(final_body, peers, upper_per),
         [struct((per * 2 * orders, azimuths), F32)],
         [me],
-        [*ups, *lows, trig, theta_lower, mix, switch_theta],
+        [*ups, *lows, trig, theta_low, mix, theta_switch],
         "expand",
         scratch=[
             pltpu.VMEM((upper_per, 2, peers, rows, lanes), F32),

time: 47.5 us -> 46.7 us (0.983)
  waiting for transfers between devices: 2.75 us -> 1.94 us
    ppermute x12 -> x13, waiting for transfers between devices: 2.75 us -> 1.94 us  [swap(): return lax.ppermute(value, axis, pairs)]
    ppermute x12 -> x13, starting transfers between devices: 13.6 us -> 13.8 us  [swap(): return lax.ppermute(value, axis, pairs)]
    pallas_call x11 -> x12, Pallas kernels: 29.1 us -> 29.3 us  [kernel_call(): pl.pallas_call(body, out_shape=outs, in_specs=[SM] * len(scalars) + [VM]...]
  transfers between devices with their start and end apart: 12 -> 13, of which waited for: 2 -> 2; matrix products, arithmetic and copies ran while one was open for 0% -> 0% of each run, Pallas kernels for 56% -> 58%
where the time goes in v7:
time: 46.7 us; the launch traced here: 46.5 us
  Pallas kernels  29.3 us (63%)
  starting transfers between devices  13.8 us (30%)
  waiting for transfers between devices  1.94 us (4%)
  other arithmetic  0.73 us (2%)
    pallas_call x12, Pallas kernels, kernel_call(): pl.pallas_call(body, out_shape=outs, in_specs=[SM] * len(scalars) + [VM]...  29.3 us
    ppermute x13, starting transfers between devices, swap(): return lax.ppermute(value, axis, pairs)  13.8 us
    ppermute x13, waiting for transfers between devices, swap(): return lax.ppermute(value, axis, pairs)  1.94 us
  transfers between devices with their start and end apart: 13, of which 2 were waited for; matrix products, arithmetic and copies ran while one was open for 0% of the time, Pallas kernels for 58%

profile of v7, /device:TPU:0, one launch (start us, length us, event | category | flops | bytes accessed | tf_op | source)
XLA Modules:
  0.0 46.5 jit_solution(1418328354297689521)
XLA Ops:
  0.0 0.7 %bitcast_add_fusion = (s32[16,128]{1,0:T(8,128)S(1)}, s32[16,128]{1,0:T(8,128)S(1)}) fusion(s32[128,16]{0,1:T(8,128)} %param.31, s32[128,16]{0,1:T(8,128)} %param.30, s32[]{:T(128)} %axis_index.25), kind=kLoop, calls=%fused_computation.6 | loop fusion | flops 53248 | bytes 32772 | tf_op jit(solution)/shard_map/add | solution.py:324
  0.7 3.0 %collective-permute-start = (s32[16,128]{1,0:T(8,128)S(1)}, s32[16,128]{1,0:T(8,128)S(1)}, u32[]{:S(2)}, u32[]{:S(2)}) collective-permute-start(s32[16,128]{1,0:T(8,128)S(1)} %get-tuple-element.64), channel_id=1, source_target_pairs={{0,4},{4,0},{8,12},{12,8},{16,20},{20,16},{24,28},{28,24},{1,5},{5... | collective-permute-start | bytes 24584 | tf_op jit(solution)/shard_map/ppermute | solution.py:20
  3.7 2.6 %collective-permute-start.6 = (bf16[16,2,32,256]{3,2,1,0:T(8,128)(2,1)}, bf16[16,2,32,256]{3,2,1,0:T(8,128)(2,1)S(1)}, u32[]{:S(2)}, u32[]{:S(2)}) collective-permute-start(bf16[16,2,32,256]{3,2,1,0:T(8,128)(2,1)} %own.1), channel_id=1, source_target_pairs={{0,16},{4,20},{8,24},{12,28},{16,0},{20,4},{24,8},{28,12},{1,17},{... | collective-permute-start | bytes 1572872 | tf_op jit(solution)/shard_map/ppermute | solution.py:20
  6.3 0.0 collective-permute-done.code.refs_0_
  6.3 0.0 copy-start.9
  6.4 5.7 %sums_first.1 = (bf16[32,32,128]{2,1,0:T(8,128)(2,1)S(1)}, bf16[32,32,128]{2,1,0:T(8,128)(2,1)S(1)}, f32[316,32,128]{2,1,0:T(8,128)}, f32[129,32,128]{2,1,0:T(8,128)}) custom-call(s32[1]{0:T(128)} %bitcast.me, s32[16,128]{1,0:T(8,128)S(1)} %collective-permute-done.code.refs_0_, bf16[316,32,128]{2,1,0:T(8,128)(2,1)} %bitcast.58, bf16[128,32,128]{2,1,0:T(8,128)(2,1)} %bitcast.59), custom_call_target="tpu_custom_call" | custom-call | flops 4294967296 | bytes 1 | tf_op jit(solution)/shard_map/sums_first/pallas_call | solution.py:32
  12.0 1.1 %collective-permute-start.1 = (bf16[32,32,128]{2,1,0:T(8,128)(2,1)S(1)}, bf16[32,32,128]{2,1,0:T(8,128)(2,1)S(1)}, u32[]{:S(2)}, u32[]{:S(2)}) collective-permute-start(bf16[32,32,128]{2,1,0:T(8,128)(2,1)S(1)} %get-tuple-element.34), channel_id=1, source_target_pairs={{0,4},{4,0},{8,12},{12,8},{16,20},{20,16},{24,28},{28,24},{1,5},{5... | collective-permute-start | bytes 786440 | tf_op jit(solution)/shard_map/ppermute | solution.py:20
  13.2 0.0 copy-done.6
  13.2 0.0 copy-done.7
  13.2 0.0 copy-done.8
  13.2 0.0 copy-done.9
  13.2 0.0 slice-start.1
  13.2 0.0 copy-start
  13.2 1.0 %early.1 = (f32[192,256]{1,0:T(8,128)S(1)}, f32[192,256]{1,0:T(8,128)S(1)}, f32[192,256]{1,0:T(8,128)S(1)}, f32[192,256]{1,0:T(8,128)S(1)}) custom-call(s32[1]{0:T(128)} %bitcast.me, bf16[256,512]{1,0:T(8,128)(2,1)S(1)} %bitcast.57, bf16[128,256]{1,0:T(8,128)(2,1)S(1)} %copy-done.8, bf16[256,512]{1,0:T(8,128)(2,1)S(1)} %copy-done.7, f32[8,16,128]{2,1,0:T(8,128)S(1)} %copy-done.9), custom_call_target="tpu_custom_call" | custom-call | flops 4294967296 | bytes 1 | tf_op jit(solution)/shard_map/early/pallas_call | solution.py:32
  14.2 0.1 collective-permute-start.2
  14.3 1.6 %collective-permute-start.3 = (f32[192,256]{1,0:T(8,128)S(1)}, f32[192,256]{1,0:T(8,128)S(1)}, u32[]{:S(2)}, u32[]{:S(2)}) collective-permute-start(f32[192,256]{1,0:T(8,128)S(1)} %get-tuple-element.45), channel_id=1, source_target_pairs={{0,2},{1,3},{2,0},{3,1},{4,6},{5,7},{6,4},{7,5},{8,10},{9,11},{10,... | collective-permute-start | bytes 589832 | tf_op jit(solution)/shard_map/ppermute | solution.py:20
  15.9 0.3 collective-permute-start.4
  16.1 0.0 slice-done
  16.2 0.0 slice-done.1
  16.2 0.2 copy-done
  16.3 3.4 %sums_third.1 = (f32[32,32,128]{2,1,0:T(8,128)S(1)}, f32[32,32,128]{2,1,0:T(8,128)S(1)}) custom-call(s32[1]{0:T(128)} %bitcast.me, s32[16,128]{1,0:T(8,128)S(1)} %get-tuple-element.63.refs_0_.code, f32[316,32,128]{2,1,0:T(8,128)S(1)} %bitcast.51, f32[129,32,128]{2,1,0:T(8,128)S(1)} %copy-done), custom_call_target="tpu_custom_call" | custom-call | bytes 1 | tf_op jit(solution)/shard_map/sums_third/pallas_call | solution.py:32
  19.8 0.0 collective-permute-done.1.refs_1_
  19.8 1.0 %collective-permute-start.5 = (bf16[32,32,128]{2,1,0:T(8,128)(2,1)S(1)}, bf16[32,32,128]{2,1,0:T(8,128)(2,1)S(1)}, u32[]{:S(2)}, u32[]{:S(2)}) collective-permute-start(bf16[32,32,128]{2,1,0:T(8,128)(2,1)S(1)} %get-tuple-element.49), channel_id=1, source_target_pairs={{0,4},{4,0},{8,12},{12,8},{16,20},{20,16},{24,28},{28,24},{1,5},{5... | collective-permute-start | bytes 786440 | tf_op jit(solution)/shard_map/ppermute | solution.py:20
  20.8 0.1 join.2
  20.9 0.0 copy-start.1
  20.9 0.0 copy-start.2
  20.9 0.0 copy-start.3
  20.9 0.0 copy-start.4
  20.9 0.0 slice-start.3
  20.9 0.0 slice-start.4
  21.0 0.0 copy-start.5
  21.0 0.0 copy-start.10
  21.0 0.0 copy-start.11
  21.0 0.0 copy-start.12
  21.0 3.5 %sums_second.1 = bf16[64,32,128]{2,1,0:T(8,128)(2,1)S(1)} custom-call(s32[1]{0:T(128)} %bitcast.me, s32[16,128]{1,0:T(8,128)S(1)} %collective-permute-done.code.refs_0_, f32[316,32,128]{2,1,0:T(8,128)S(1)} %bitcast.51, f32[129,32,128]{2,1,0:T(8,128)S(1)} %copy-done), custom_call_target="tpu_custom_call" | custom-call | flops 4294967296 | bytes 1 | tf_op jit(solution)/shard_map/sums_second/pallas_call | solution.py:32
  24.5 0.0 collective-permute-done.2.refs_1_
  24.5 1.1 %collective-permute-start.9 = (bf16[64,32,128]{2,1,0:T(8,128)(2,1)S(1)}, bf16[64,32,128]{2,1,0:T(8,128)(2,1)S(1)}, u32[]{:S(2)}, u32[]{:S(2)}) collective-permute-start(bf16[64,32,128]{2,1,0:T(8,128)(2,1)S(1)} %sums_second.1), channel_id=1, source_target_pairs={{0,4},{4,0},{8,12},{12,8},{16,20},{20,16},{24,28},{28,24},{1,5},{5... | collective-permute-start | bytes 1572872 | tf_op jit(solution)/shard_map/ppermute | solution.py:20
  25.6 0.0 collective-permute-done.3.refs_2_
  25.6 0.7 %collective-permute-start.11 = (bf16[32,32,128]{2,1,0:T(8,128)(2,1)S(1)}, bf16[32,32,128]{2,1,0:T(8,128)(2,1)S(1)}, u32[]{:S(2)}, u32[]{:S(2)}) collective-permute-start(bf16[32,32,128]{2,1,0:T(8,128)(2,1)S(1)} %join.2), channel_id=1, source_target_pairs={{0,3},{1,2},{2,1},{3,0},{4,7},{5,6},{6,5},{7,4},{8,11},{9,10},{10,... | collective-permute-start | bytes 786440 | tf_op jit(solution)/shard_map/ppermute | solution.py:20
  26.4 0.0 collective-permute-done.4.refs_3_
  26.4 0.0 copy-done.1
  26.4 0.0 copy-done.2
  26.4 0.0 copy-done.3
  26.4 0.0 copy-done.4
  26.4 2.2 %shift.1 = (f32[16,2,32,256]{3,2,1,0:T(8,128)S(1)}, f32[2,8,4,16,128]{4,3,2,1,0:T(8,128)S(1)}, bf16[256,256]{1,0:T(8,128)(2,1)S(1)}, bf16[64,128]{1,0:T(8,128)(2,1)S(1)}, bf16[64,64]{1,0:T(8,128)(2,1)S(1)}) custom-call(s32[1]{0:T(128)} %bitcast.me, f32[192,256]{1,0:T(8,128)S(1)} %get-tuple-element.36.refs_0_, f32[192,256]{1,0:T(8,128)S(1)} %collective-permute-done.2.refs_1_, ...), custom_call_target="tpu_custom_call" | custom-call | bytes 1 | tf_op jit(solution)/shard_map/shift/pallas_call | solution.py:32
  28.7 0.3 collective-permute-done.5.refs_1_
  29.0 1.6 %collective-permute-start.12 = (bf16[32,32,128]{2,1,0:T(8,128)(2,1)S(1)}, bf16[32,32,128]{2,1,0:T(8,128)(2,1)S(1)}, u32[]{:S(2)}, u32[]{:S(2)}) collective-permute-start(bf16[32,32,128]{2,1,0:T(8,128)(2,1)S(1)} %join.3), channel_id=1, source_target_pairs={{0,2},{1,3},{2,0},{3,1},{4,6},{5,7},{6,4},{7,5},{8,10},{9,11},{10,... | collective-permute-start | bytes 786440 | tf_op jit(solution)/shard_map/ppermute | solution.py:20
  30.6 0.0 collective-permute-done.6.far
  30.6 0.0 slice-done.2
  30.6 0.0 slice-done.3
  30.7 6.5 %upper.1 = (bf16[4,64,128]{2,1,0:T(8,128)(2,1)S(1)}, bf16[4,64,128]{2,1,0:T(8,128)(2,1)S(1)}, bf16[4,64,128]{2,1,0:T(8,128)(2,1)S(1)}, bf16[4,64,128]{2,1,0:T(8,128)(2,1)S(1)}) custom-call(s32[1]{0:T(128)} %bitcast.me, s32[1]{0:T(128)} %bitcast.6.home, s32[16,16]{1,0:T(8,128)S(1)} %copy-done.11, s32[16,16]{1,0:T(8,128)S(1)} %copy-done.12, ...), custom_call_target="tpu_custom_call" | custom-call | flops 4294967296 | bytes 1 | tf_op jit(solution)/shard_map/upper/pallas_call | solution.py:32
  37.2 0.5 %collective-permute-start.7 = (bf16[4,64,128]{2,1,0:T(8,128)(2,1)S(1)}, bf16[4,64,128]{2,1,0:T(8,128)(2,1)S(1)}, u32[]{:S(2)}, u32[]{:S(2)}) collective-permute-start(bf16[4,64,128]{2,1,0:T(8,128)(2,1)S(1)} %get-tuple-element.52), channel_id=1, source_target_pairs={{0,2},{1,3},{2,0},{3,1},{4,6},{5,7},{6,4},{7,5},{8,10},{9,11},{10,... | collective-permute-start | bytes 196616 | tf_op jit(solution)/shard_map/ppermute | solution.py:20
  37.7 0.1 collective-permute-start.8
  37.9 1.6 %collective-permute-done.9.got = bf16[64,32,128]{2,1,0:T(8,128)(2,1)S(1)} collective-permute-done((bf16[64,32,128]{2,1,0:T(8,128)(2,1)S(1)}, bf16[64,32,128]{2,1,0:T(8,128)(2,1)S(1)}, u32[]{:S(2)}, u32[]{:S(2)}) %collective-permute-start.9) | collective-permute-done | bytes 524320 | tf_op jit(solution)/shard_map/ppermute | solution.py:20
  39.5 2.1 %close_peers.1 = bf16[40,32,128]{2,1,0:T(8,128)(2,1)S(1)} custom-call(s32[1]{0:T(128)} %bitcast.me, s32[16,128]{1,0:T(8,128)S(1)} %get-tuple-element.63.refs_0_.code, f32[316,32,128]{2,1,0:T(8,128)S(1)} %bitcast.51, f32[129,32,128]{2,1,0:T(8,128)S(1)} %copy-done, bf16[64,32,128]{2,1,0:T(8,128)(2,1)S(1)} %collective-permute-done.9.got, ...), custom_call_target="tpu_custom_call" | custom-call | bytes 1 | tf_op jit(solution)/shard_map/close_peers/pallas_call | solution.py:32
  41.6 0.1 collective-permute-start.10
  41.6 0.0 collective-permute-done.11.refs_0_
  41.7 0.0 collective-permute-done.12.refs_1_
  41.7 0.1 place.1
  41.7 2.1 %close_self.1.refs_2_ = bf16[40,32,128]{2,1,0:T(8,128)(2,1)S(1)} custom-call(s32[1]{0:T(128)} %bitcast.me, s32[16,128]{1,0:T(8,128)S(1)} %get-tuple-element.63.refs_0_.code, f32[316,32,128]{2,1,0:T(8,128)S(1)} %bitcast.51, f32[129,32,128]{2,1,0:T(8,128)S(1)} %copy-done, bf16[64,32,128]{2,1,0:T(8,128)(2,1)S(1)} %collective-permute-done.9.got, ...), custom_call_target="tpu_custom_call" | custom-call | bytes 1 | tf_op jit(solution)/shard_map/close_self/pallas_call | solution.py:32
  43.9 0.0 collective-permute-done.7.refs_0_
  43.9 0.0 collective-permute-done.8.refs_1_
  43.9 0.0 collective-permute-done.10.refs_3_
  43.9 2.6 %expand.1 = f32[4096,128]{1,0:T(8,128)} custom-call(s32[1]{0:T(128)} %bitcast.me, bf16[4,64,128]{2,1,0:T(8,128)(2,1)S(1)} %collective-permute-done.7.refs_0_, bf16[4,64,128]{2,1,0:T(8,128)(2,1)S(1)} %collective-permute-done.8.refs_1_, bf16[40,32,128]{2,1,0:T(8,128)(2,1)S(1)} %close_self.1.refs_2_, bf16[40,32,128]{2,1,0:T(8,128)(2,1)S(1)} %collective-permute-done.10.refs_3_, ...), custom_call_target="tpu_custom_call" | custom-call | flops 4294967296 | bytes 1 | tf_op jit(solution)/shard_map/expand/pallas_call | solution.py:32
  (13 shorter events, 0.1 us)
Async XLA Ops:
  0.7 5.6 %collective-permute-start = (s32[16,128]{1,0:T(8,128)S(1)}, s32[16,128]{1,0:T(8,128)S(1)}, u32[]{:S(2)}, u32[]{:S(2)}) collective-permute-start(s32[16,128]{1,0:T(8,128)S(1)} %get-tuple-element.64), channel_id=1, source_target_pairs={{0,4},{4,0},{8,12},{12,8},{16,20},{20,16},{24,28},{28,24},{1,5},{5... | collective-permute-start | bytes 24584 | tf_op jit(solution)/shard_map/ppermute | solution.py:20
  3.7 26.9 %collective-permute-start.6 = (bf16[16,2,32,256]{3,2,1,0:T(8,128)(2,1)}, bf16[16,2,32,256]{3,2,1,0:T(8,128)(2,1)S(1)}, u32[]{:S(2)}, u32[]{:S(2)}) collective-permute-start(bf16[16,2,32,256]{3,2,1,0:T(8,128)(2,1)} %own.1), channel_id=1, source_target_pairs={{0,16},{4,20},{8,24},{12,28},{16,0},{20,4},{24,8},{28,12},{1,17},{... | collective-permute-start | bytes 1572872 | tf_op jit(solution)/shard_map/ppermute | solution.py:20
  6.3 6.8 %copy-start.6 = (bf16[2,2,64,512]{3,2,1,0:T(8,128)(2,1)S(1)}, bf16[2,2,64,512]{3,2,1,0:T(8,128)(2,1)}, u32[]{:S(2)}) copy-start(bf16[2,2,64,512]{3,2,1,0:T(8,128)(2,1)} %param.17) | copy-start | bytes 786436
  6.3 6.8 %copy-start.7 = (bf16[256,512]{1,0:T(8,128)(2,1)S(1)}, bf16[256,512]{1,0:T(8,128)(2,1)}, u32[]{:S(2)}) copy-start(bf16[256,512]{1,0:T(8,128)(2,1)} %refs_2_.1) | copy-start | bytes 786436
  6.3 6.8 %copy-start.8 = (bf16[128,256]{1,0:T(8,128)(2,1)S(1)}, bf16[128,256]{1,0:T(8,128)(2,1)}, u32[]{:S(2)}) copy-start(bf16[128,256]{1,0:T(8,128)(2,1)} %refs_1_.1) | copy-start | bytes 196612
  6.3 6.8 %copy-start.9 = (f32[8,16,128]{2,1,0:T(8,128)S(1)}, f32[8,16,128]{2,1,0:T(8,128)}, u32[]{:S(2)}) copy-start(f32[8,16,128]{2,1,0:T(8,128)} %refs_3_.1) | copy-start | bytes 196612
  12.0 7.7 %collective-permute-start.1 = (bf16[32,32,128]{2,1,0:T(8,128)(2,1)S(1)}, bf16[32,32,128]{2,1,0:T(8,128)(2,1)S(1)}, u32[]{:S(2)}, u32[]{:S(2)}) collective-permute-start(bf16[32,32,128]{2,1,0:T(8,128)(2,1)S(1)} %get-tuple-element.34), channel_id=1, source_target_pairs={{0,4},{4,0},{8,12},{12,8},{16,20},{20,16},{24,28},{28,24},{1,5},{5... | collective-permute-start | bytes 786440 | tf_op jit(solution)/shard_map/ppermute | solution.py:20
  13.2 3.0 %slice-start = ((s8[5177344]{0:T(1024)(128)(4,1)}), s8[4194304]{0:T(1024)(128)(4,1)S(1)}, s32[]{:S(2)}) async-start(s8[5177344]{0:T(1024)(128)(4,1)} %bitcast.50), calls=%async_computation | async-start | bytes 8388608
  13.2 3.0 %slice-start.1 = ((s8[5177344]{0:T(1024)(128)(4,1)}), s8[983040]{0:T(1024)(128)(4,1)S(1)}, s32[]{:S(2)}) async-start(s8[5177344]{0:T(1024)(128)(4,1)} %bitcast.50), calls=%async_computation.1 | async-start | bytes 1966080
  13.2 3.1 %copy-start = (f32[129,32,128]{2,1,0:T(8,128)S(1)}, f32[129,32,128]{2,1,0:T(8,128)}, u32[]{:S(2)}) copy-start(f32[129,32,128]{2,1,0:T(8,128)} %get-tuple-element.39.refs_2_.source) | copy-start | bytes 6340612
  14.2 10.3 %collective-permute-start.2 = (f32[192,256]{1,0:T(8,128)S(1)}, f32[192,256]{1,0:T(8,128)S(1)}, u32[]{:S(2)}, u32[]{:S(2)}) collective-permute-start(f32[192,256]{1,0:T(8,128)S(1)} %get-tuple-element.44), channel_id=1, source_target_pairs={{0,1},{1,0},{2,3},{3,2},{4,5},{5,4},{6,7},{7,6},{8,9},{9,8},{10,11... | collective-permute-start | bytes 589832 | tf_op jit(solution)/shard_map/ppermute | solution.py:20
  14.3 11.3 %collective-permute-start.3 = (f32[192,256]{1,0:T(8,128)S(1)}, f32[192,256]{1,0:T(8,128)S(1)}, u32[]{:S(2)}, u32[]{:S(2)}) collective-permute-start(f32[192,256]{1,0:T(8,128)S(1)} %get-tuple-element.45), channel_id=1, source_target_pairs={{0,2},{1,3},{2,0},{3,1},{4,6},{5,7},{6,4},{7,5},{8,10},{9,11},{10,... | collective-permute-start | bytes 589832 | tf_op jit(solution)/shard_map/ppermute | solution.py:20
  15.9 10.5 %collective-permute-start.4 = (f32[192,256]{1,0:T(8,128)S(1)}, f32[192,256]{1,0:T(8,128)S(1)}, u32[]{:S(2)}, u32[]{:S(2)}) collective-permute-start(f32[192,256]{1,0:T(8,128)S(1)} %get-tuple-element.46), channel_id=1, source_target_pairs={{0,3},{1,2},{2,1},{3,0},{4,7},{5,6},{6,5},{7,4},{8,11},{9,10},{10,... | collective-permute-start | bytes 589832 | tf_op jit(solution)/shard_map/ppermute | solution.py:20
  19.8 9.2 %collective-permute-start.5 = (bf16[32,32,128]{2,1,0:T(8,128)(2,1)S(1)}, bf16[32,32,128]{2,1,0:T(8,128)(2,1)S(1)}, u32[]{:S(2)}, u32[]{:S(2)}) collective-permute-start(bf16[32,32,128]{2,1,0:T(8,128)(2,1)S(1)} %get-tuple-element.49), channel_id=1, source_target_pairs={{0,4},{4,0},{8,12},{12,8},{16,20},{20,16},{24,28},{28,24},{1,5},{5... | collective-permute-start | bytes 786440 | tf_op jit(solution)/shard_map/ppermute | solution.py:20
  20.8 9.8 %slice-start.2 = ((s8[10354688]{0:T(1024)(128)(4,1)}), s8[4194304]{0:T(1024)(128)(4,1)S(1)}, s32[]{:S(2)}) async-start(s8[10354688]{0:T(1024)(128)(4,1)} %bitcast.54), calls=%async_computation.2 | async-start | bytes 8388608
  20.9 5.5 %copy-start.1 = (f32[8,32,256]{2,1,0:T(8,128)S(1)}, f32[8,32,256]{2,1,0:T(8,128)}, u32[]{:S(2)}) copy-start(f32[8,32,256]{2,1,0:T(8,128)} %refs_4_.1) | copy-start | bytes 786436
  20.9 5.5 %copy-start.2 = (bf16[2,128,128]{2,1,0:T(8,128)(2,1)S(1)}, bf16[2,128,128]{2,1,0:T(8,128)(2,1)}, u32[]{:S(2)}) copy-start(bf16[2,128,128]{2,1,0:T(8,128)(2,1)} %refs_5_.1) | copy-start | bytes 196612
  20.9 5.5 %copy-start.3 = (bf16[64,128]{1,0:T(8,128)(2,1)S(1)}, bf16[64,128]{1,0:T(8,128)(2,1)}, u32[]{:S(2)}) copy-start(bf16[64,128]{1,0:T(8,128)(2,1)} %refs_6_.1) | copy-start | bytes 49156
  20.9 5.5 %copy-start.4 = (bf16[64,64]{1,0:T(8,128)(2,1)S(1)}, bf16[64,64]{1,0:T(8,128)(2,1)}, u32[]{:S(2)}) copy-start(bf16[64,64]{1,0:T(8,128)(2,1)} %refs_7_.1) | copy-start | bytes 24580
  20.9 9.7 %slice-start.3 = ((s8[10354688]{0:T(1024)(128)(4,1)}), s8[4194304]{0:T(1024)(128)(4,1)S(1)}, s32[]{:S(2)}) async-start(s8[10354688]{0:T(1024)(128)(4,1)} %bitcast.54), calls=%async_computation.3 | async-start | bytes 8388608
  20.9 9.7 %slice-start.4 = ((s8[10354688]{0:T(1024)(128)(4,1)}), s8[1966080]{0:T(1024)(128)(4,1)S(1)}, s32[]{:S(2)}) async-start(s8[10354688]{0:T(1024)(128)(4,1)} %bitcast.54), calls=%async_computation.4 | async-start | bytes 3932160
  21.0 9.7 %copy-start.5 = (bf16[16,2,32,256]{3,2,1,0:T(8,128)(2,1)S(1)}, bf16[16,2,32,256]{3,2,1,0:T(8,128)(2,1)}, u32[]{:S(2)}) copy-start(bf16[16,2,32,256]{3,2,1,0:T(8,128)(2,1)} %own.1) | copy-start | bytes 1572868
  21.0 9.7 %copy-start.10 = (bf16[128,256]{1,0:T(8,128)(2,1)S(1)}, bf16[128,256]{1,0:T(8,128)(2,1)}, u32[]{:S(2)}) copy-start(bf16[128,256]{1,0:T(8,128)(2,1)} %phi.1) | copy-start | bytes 196612
  21.0 9.7 %copy-start.11 = (s32[16,16]{1,0:T(8,128)S(1)}, s32[16,16]{1,0:T(8,128)}, u32[]{:S(2)}) copy-start(s32[16,16]{1,0:T(8,128)} %ids.1) | copy-start | bytes 3076
  21.0 9.7 %copy-start.12 = (s32[16,16]{1,0:T(8,128)S(1)}, s32[16,16]{1,0:T(8,128)}, u32[]{:S(2)}) copy-start(s32[16,16]{1,0:T(8,128)} %offsets.1) | copy-start | bytes 3076
  24.5 14.9 %collective-permute-start.9 = (bf16[64,32,128]{2,1,0:T(8,128)(2,1)S(1)}, bf16[64,32,128]{2,1,0:T(8,128)(2,1)S(1)}, u32[]{:S(2)}, u32[]{:S(2)}) collective-permute-start(bf16[64,32,128]{2,1,0:T(8,128)(2,1)S(1)} %sums_second.1), channel_id=1, source_target_pairs={{0,4},{4,0},{8,12},{12,8},{16,20},{20,16},{24,28},{28,24},{1,5},{5... | collective-permute-start | bytes 1572872 | tf_op jit(solution)/shard_map/ppermute | solution.py:20
  25.6 16.0 %collective-permute-start.11 = (bf16[32,32,128]{2,1,0:T(8,128)(2,1)S(1)}, bf16[32,32,128]{2,1,0:T(8,128)(2,1)S(1)}, u32[]{:S(2)}, u32[]{:S(2)}) collective-permute-start(bf16[32,32,128]{2,1,0:T(8,128)(2,1)S(1)} %join.2), channel_id=1, source_target_pairs={{0,3},{1,2},{2,1},{3,0},{4,7},{5,6},{6,5},{7,4},{8,11},{9,10},{10,... | collective-permute-start | bytes 786440 | tf_op jit(solution)/shard_map/ppermute | solution.py:20
  29.0 12.6 %collective-permute-start.12 = (bf16[32,32,128]{2,1,0:T(8,128)(2,1)S(1)}, bf16[32,32,128]{2,1,0:T(8,128)(2,1)S(1)}, u32[]{:S(2)}, u32[]{:S(2)}) collective-permute-start(bf16[32,32,128]{2,1,0:T(8,128)(2,1)S(1)} %join.3), channel_id=1, source_target_pairs={{0,2},{1,3},{2,0},{3,1},{4,6},{5,7},{6,4},{7,5},{8,10},{9,11},{10,... | collective-permute-start | bytes 786440 | tf_op jit(solution)/shard_map/ppermute | solution.py:20
  37.2 6.6 %collective-permute-start.7 = (bf16[4,64,128]{2,1,0:T(8,128)(2,1)S(1)}, bf16[4,64,128]{2,1,0:T(8,128)(2,1)S(1)}, u32[]{:S(2)}, u32[]{:S(2)}) collective-permute-start(bf16[4,64,128]{2,1,0:T(8,128)(2,1)S(1)} %get-tuple-element.52), channel_id=1, source_target_pairs={{0,2},{1,3},{2,0},{3,1},{4,6},{5,7},{6,4},{7,5},{8,10},{9,11},{10,... | collective-permute-start | bytes 196616 | tf_op jit(solution)/shard_map/ppermute | solution.py:20
  37.7 6.1 %collective-permute-start.8 = (bf16[4,64,128]{2,1,0:T(8,128)(2,1)S(1)}, bf16[4,64,128]{2,1,0:T(8,128)(2,1)S(1)}, u32[]{:S(2)}, u32[]{:S(2)}) collective-permute-start(bf16[4,64,128]{2,1,0:T(8,128)(2,1)S(1)} %get-tuple-element.53), channel_id=1, source_target_pairs={{0,3},{1,2},{2,1},{3,0},{4,7},{5,6},{6,5},{7,4},{8,11},{9,10},{10,... | collective-permute-start | bytes 196616 | tf_op jit(solution)/shard_map/ppermute | solution.py:20
  41.6 2.3 %collective-permute-start.10 = (bf16[40,32,128]{2,1,0:T(8,128)(2,1)S(1)}, bf16[40,32,128]{2,1,0:T(8,128)(2,1)S(1)}, u32[]{:S(2)}, u32[]{:S(2)}) collective-permute-start(bf16[40,32,128]{2,1,0:T(8,128)(2,1)S(1)} %close_peers.1), channel_id=1, source_target_pairs={{0,1},{1,0},{2,3},{3,2},{4,5},{5,4},{6,7},{7,6},{8,9},{9,8},{10,11... | collective-permute-start | bytes 983048 | tf_op jit(solution)/shard_map/ppermute | solution.py:20

commit v8 on v7

--- a/solution.py
+++ b/solution.py
@@ -198,16 +198,16 @@
 
 
 def upper_body(masks, peers, entries, me, home, ids, offsets, own, far, table, shifted, phi, *refs):
-    outs, pool = refs[: len(masks)], refs[-1]
-    boxes, _, rows, _ = own.shape
+    outs, (pool, rounded) = refs[: len(masks)], refs[len(masks) :]
+    boxes, _, rows, wide = own.shape
     pool[0:boxes] = own[...].astype(F32)
     pool[boxes:] = far[...].astype(F32)
     spans = [slice(r, r + 8) for r in range(0, rows, 8)]
     per = boxes // peers
-    for mask, out in zip(masks, outs, strict=True):
+    for turn, mask in enumerate(masks):
         first = jnp.bitwise_xor(me[0], mask) * per
 
-        def one(i, carry, first=first, out=out):
+        def one(i, carry, first=first, turn=turn):
             box = first + i
             real = [shifted[box, 0, span] for span in spans]
             imag = [shifted[box, 1, span] for span in spans]
@@ -223,12 +223,14 @@
                     sr, si = pool[place, 0, span], pool[place, 1, span]
                     real[k] = real[k] + (fr * sr - fi * si)
                     imag[k] = imag[k] + (fr * si + fi * sr)
-            incoming = jnp.concatenate([*real, *imag], axis=0).astype(BF16)
-            narrow = lax.dot_general(incoming, phi[...], NT, preferred_element_type=F32)
-            out[i] = narrow.astype(BF16)
+            rounded[turn * per + i] = jnp.concatenate([*real, *imag], axis=0).astype(BF16)
             return carry
 
         lax.fori_loop(0, per, one, 0)
+    for turn, out in enumerate(outs):
+        incoming = rounded[turn * per : (turn + 1) * per].reshape(per * 2 * rows, wide)
+        narrow = lax.dot_general(incoming, phi[...], NT, preferred_element_type=F32)
+        out[...] = narrow.astype(BF16).reshape(out.shape)
 
 
 def place_body(*refs):
@@ -382,7 +384,7 @@
         held=4,
     )
     order = after(me, parts[0])
-    parts = [swap(part, "angle", mask) if mask else part for mask, part in enumerate(parts)]
+    parts = [swap(part, "angle", mask) if mask in outer else part for mask, part in enumerate(parts)]
     own_outer = sums(
         [((mask,), 0) for mask in outer],
         [own_shape] * len(outer),
@@ -395,6 +397,8 @@
         (lows[mask],) = join([own], got)
     (second,) = sums([(tuple(inner), 0)], [far_shape], [far_code], after(me, lows[outer[0]]), "sums_second")
     got_inner = swap(second, "box", 1)
+    late = after(parts[1], second)
+    parts = [parts[0]] + [swap(late if mask == 1 else parts[mask], "angle", mask) for mask in inner[-2::-1]] + [*parts[len(inner) :]]
     orders = switch_theta.shape[0]
     azimuths = switch_phi.shape[1]
     shifted, trig, mix, theta_low, theta_switch = kernel_call(
@@ -424,7 +428,10 @@
         [after(me, lows[outer[-1]]), home.astype(jnp.int32).reshape(1), list_upper, offset_upper],
         [outgoing_upper, far_upper, table_upper, shifted, phi_lower],
         "upper",
-        scratch=[pltpu.VMEM((2 * upper_boxes, 2, rows, wide), F32)],
+        scratch=[
+            pltpu.VMEM((2 * upper_boxes, 2, rows, wide), F32),
+            pltpu.VMEM((upper_boxes, 2 * rows, wide), BF16),
+        ],
     )
     ups = dict(zip(outer + inner, ups, strict=True))
     order = after(me, ups[0])

time: 46.7 us -> 45.6 us (0.976)
  Pallas kernels: 29.3 us -> 27.9 us
    pallas_call x12, Pallas kernels: 29.3 us -> 27.9 us  [kernel_call(): pl.pallas_call(body, out_shape=outs, in_specs=[SM] * len(scalars) + [VM]...]
  transfers between devices with their start and end apart: 13 -> 13, of which waited for: 2 -> 2; matrix products, arithmetic and copies ran while one was open for 0% -> 0% of each run, Pallas kernels for 58% -> 56%
where the time goes in v8:
time: 45.6 us; the launch traced here: 45.3 us
  Pallas kernels  27.9 us (61%)
  starting transfers between devices  14 us (31%)
  waiting for transfers between devices  2.24 us (5%)
  other arithmetic  0.73 us (2%)
    pallas_call x12, Pallas kernels, kernel_call(): pl.pallas_call(body, out_shape=outs, in_specs=[SM] * len(scalars) + [VM]...  27.9 us
    ppermute x13, starting transfers between devices, swap(): return lax.ppermute(value, axis, pairs)  14 us
    ppermute x13, waiting for transfers between devices, swap(): return lax.ppermute(value, axis, pairs)  2.24 us
  transfers between devices with their start and end apart: 13, of which 2 were waited for; matrix products, arithmetic and copies ran while one was open for 0% of the time, Pallas kernels for 56%

profile of v8, /device:TPU:0, one launch (start us, length us, event | category | flops | bytes accessed | tf_op | source)
XLA Modules:
  0.0 45.3 jit_solution(6604596522426911831)
XLA Ops:
  0.0 0.7 %bitcast_add_fusion = (s32[16,128]{1,0:T(8,128)S(1)}, s32[16,128]{1,0:T(8,128)S(1)}) fusion(s32[128,16]{0,1:T(8,128)} %param.31, s32[128,16]{0,1:T(8,128)} %param.30, s32[]{:T(128)} %axis_index.25), kind=kLoop, calls=%fused_computation.6 | loop fusion | flops 53248 | bytes 32772 | tf_op jit(solution)/shard_map/add | solution.py:326
  0.7 3.0 %collective-permute-start = (s32[16,128]{1,0:T(8,128)S(1)}, s32[16,128]{1,0:T(8,128)S(1)}, u32[]{:S(2)}, u32[]{:S(2)}) collective-permute-start(s32[16,128]{1,0:T(8,128)S(1)} %get-tuple-element.66), channel_id=1, source_target_pairs={{0,4},{4,0},{8,12},{12,8},{16,20},{20,16},{24,28},{28,24},{1,5},{5... | collective-permute-start | bytes 24584 | tf_op jit(solution)/shard_map/ppermute | solution.py:20
  3.7 2.6 %collective-permute-start.6 = (bf16[16,2,32,256]{3,2,1,0:T(8,128)(2,1)}, bf16[16,2,32,256]{3,2,1,0:T(8,128)(2,1)S(1)}, u32[]{:S(2)}, u32[]{:S(2)}) collective-permute-start(bf16[16,2,32,256]{3,2,1,0:T(8,128)(2,1)} %own.1), channel_id=1, source_target_pairs={{0,16},{4,20},{8,24},{12,28},{16,0},{20,4},{24,8},{28,12},{1,17},{... | collective-permute-start | bytes 1572872 | tf_op jit(solution)/shard_map/ppermute | solution.py:20
  6.3 0.0 collective-permute-done.code.refs_0_
  6.3 0.0 copy-start.9
  6.4 5.7 %sums_first.1 = (bf16[32,32,128]{2,1,0:T(8,128)(2,1)S(1)}, bf16[32,32,128]{2,1,0:T(8,128)(2,1)S(1)}, f32[316,32,128]{2,1,0:T(8,128)}, f32[129,32,128]{2,1,0:T(8,128)}) custom-call(s32[1]{0:T(128)} %bitcast.me, s32[16,128]{1,0:T(8,128)S(1)} %collective-permute-done.code.refs_0_, bf16[316,32,128]{2,1,0:T(8,128)(2,1)} %bitcast.58, bf16[128,32,128]{2,1,0:T(8,128)(2,1)} %bitcast.59), custom_call_target="tpu_custom_call" | custom-call | flops 4294967296 | bytes 1 | tf_op jit(solution)/shard_map/sums_first/pallas_call | solution.py:32
  12.0 1.1 %collective-permute-start.1 = (bf16[32,32,128]{2,1,0:T(8,128)(2,1)S(1)}, bf16[32,32,128]{2,1,0:T(8,128)(2,1)S(1)}, u32[]{:S(2)}, u32[]{:S(2)}) collective-permute-start(bf16[32,32,128]{2,1,0:T(8,128)(2,1)S(1)} %get-tuple-element.35), channel_id=1, source_target_pairs={{0,4},{4,0},{8,12},{12,8},{16,20},{20,16},{24,28},{28,24},{1,5},{5... | collective-permute-start | bytes 786440 | tf_op jit(solution)/shard_map/ppermute | solution.py:20
  13.2 0.0 copy-done.6
  13.2 0.0 copy-done.7
  13.2 0.0 copy-done.8
  13.2 0.0 copy-done.9
  13.2 0.0 slice-start.1
  13.2 0.0 copy-start
  13.2 1.0 %early.1 = (f32[192,256]{1,0:T(8,128)S(1)}, f32[192,256]{1,0:T(8,128)S(1)}, f32[192,256]{1,0:T(8,128)S(1)}, f32[192,256]{1,0:T(8,128)S(1)}) custom-call(s32[1]{0:T(128)} %bitcast.me, bf16[256,512]{1,0:T(8,128)(2,1)S(1)} %bitcast.57, bf16[128,256]{1,0:T(8,128)(2,1)S(1)} %copy-done.8, bf16[256,512]{1,0:T(8,128)(2,1)S(1)} %copy-done.7, f32[8,16,128]{2,1,0:T(8,128)S(1)} %copy-done.9), custom_call_target="tpu_custom_call" | custom-call | flops 4294967296 | bytes 1 | tf_op jit(solution)/shard_map/early/pallas_call | solution.py:32
  14.2 1.6 %collective-permute-start.3 = (f32[192,256]{1,0:T(8,128)S(1)}, f32[192,256]{1,0:T(8,128)S(1)}, u32[]{:S(2)}, u32[]{:S(2)}) collective-permute-start(f32[192,256]{1,0:T(8,128)S(1)} %get-tuple-element.47), channel_id=1, source_target_pairs={{0,2},{1,3},{2,0},{3,1},{4,6},{5,7},{6,4},{7,5},{8,10},{9,11},{10,... | collective-permute-start | bytes 589832 | tf_op jit(solution)/shard_map/ppermute | solution.py:20
  15.8 0.0 collective-permute-start.4
  15.8 1.0 %collective-permute-start.5 = (bf16[32,32,128]{2,1,0:T(8,128)(2,1)S(1)}, bf16[32,32,128]{2,1,0:T(8,128)(2,1)S(1)}, u32[]{:S(2)}, u32[]{:S(2)}) collective-permute-start(bf16[32,32,128]{2,1,0:T(8,128)(2,1)S(1)} %get-tuple-element.51), channel_id=1, source_target_pairs={{0,4},{4,0},{8,12},{12,8},{16,20},{20,16},{24,28},{28,24},{1,5},{5... | collective-permute-start | bytes 786440 | tf_op jit(solution)/shard_map/ppermute | solution.py:20
  16.8 0.0 slice-done
  16.8 0.0 slice-done.1
  16.8 0.0 copy-done
  16.8 3.4 %sums_third.1 = (f32[32,32,128]{2,1,0:T(8,128)S(1)}, f32[32,32,128]{2,1,0:T(8,128)S(1)}) custom-call(s32[1]{0:T(128)} %bitcast.me, s32[16,128]{1,0:T(8,128)S(1)} %get-tuple-element.65.refs_0_.code, f32[316,32,128]{2,1,0:T(8,128)S(1)} %bitcast.51, f32[129,32,128]{2,1,0:T(8,128)S(1)} %copy-done), custom_call_target="tpu_custom_call" | custom-call | bytes 1 | tf_op jit(solution)/shard_map/sums_third/pallas_call | solution.py:32
  20.2 0.0 collective-permute-done.1.refs_1_
  20.2 0.0 slice-start.2
  20.3 0.1 join.2
  20.3 0.0 copy-start.1
  20.3 0.0 copy-start.2
  20.3 0.0 copy-start.3
  20.4 0.0 copy-start.4
  20.4 0.0 slice-start.3
  20.4 0.0 slice-start.4
  20.4 0.0 copy-start.5
  20.4 0.0 copy-start.10
  20.4 0.0 copy-start.11
  20.4 0.0 copy-start.12
  20.4 3.5 %sums_second.1 = bf16[64,32,128]{2,1,0:T(8,128)(2,1)S(1)} custom-call(s32[1]{0:T(128)} %bitcast.me, s32[16,128]{1,0:T(8,128)S(1)} %collective-permute-done.code.refs_0_, f32[316,32,128]{2,1,0:T(8,128)S(1)} %bitcast.51, f32[129,32,128]{2,1,0:T(8,128)S(1)} %copy-done), custom_call_target="tpu_custom_call" | custom-call | flops 4294967296 | bytes 1 | tf_op jit(solution)/shard_map/sums_second/pallas_call | solution.py:32
  23.9 0.4 collective-permute-start.2
  24.3 0.0 collective-permute-done.3.refs_2_
  24.4 1.0 %collective-permute-start.9 = (bf16[64,32,128]{2,1,0:T(8,128)(2,1)S(1)}, bf16[64,32,128]{2,1,0:T(8,128)(2,1)S(1)}, u32[]{:S(2)}, u32[]{:S(2)}) collective-permute-start(bf16[64,32,128]{2,1,0:T(8,128)(2,1)S(1)} %sums_second.1), channel_id=1, source_target_pairs={{0,4},{4,0},{8,12},{12,8},{16,20},{20,16},{24,28},{28,24},{1,5},{5... | collective-permute-start | bytes 1572872 | tf_op jit(solution)/shard_map/ppermute | solution.py:20
  25.4 0.0 collective-permute-done.4.refs_3_
  25.4 0.9 %collective-permute-start.11 = (bf16[32,32,128]{2,1,0:T(8,128)(2,1)S(1)}, bf16[32,32,128]{2,1,0:T(8,128)(2,1)S(1)}, u32[]{:S(2)}, u32[]{:S(2)}) collective-permute-start(bf16[32,32,128]{2,1,0:T(8,128)(2,1)S(1)} %join.2), channel_id=1, source_target_pairs={{0,3},{1,2},{2,1},{3,0},{4,7},{5,6},{6,5},{7,4},{8,11},{9,10},{10,... | collective-permute-start | bytes 786440 | tf_op jit(solution)/shard_map/ppermute | solution.py:20
  26.3 0.0 collective-permute-done.2.refs_1_
  26.3 0.0 copy-done.1
  26.3 0.0 copy-done.2
  26.3 0.0 copy-done.3
  26.4 0.0 copy-done.4
  26.4 2.2 %shift.1 = (f32[16,2,32,256]{3,2,1,0:T(8,128)S(1)}, f32[2,8,4,16,128]{4,3,2,1,0:T(8,128)S(1)}, bf16[256,256]{1,0:T(8,128)(2,1)S(1)}, bf16[64,128]{1,0:T(8,128)(2,1)S(1)}, bf16[64,64]{1,0:T(8,128)(2,1)S(1)}) custom-call(s32[1]{0:T(128)} %bitcast.me, f32[192,256]{1,0:T(8,128)S(1)} %get-tuple-element.37.refs_0_, f32[192,256]{1,0:T(8,128)S(1)} %collective-permute-done.2.refs_1_, ...), custom_call_target="tpu_custom_call" | custom-call | bytes 1 | tf_op jit(solution)/shard_map/shift/pallas_call | solution.py:32
  28.6 0.0 collective-permute-done.5.refs_1_
  28.6 0.7 %collective-permute-start.12 = (bf16[32,32,128]{2,1,0:T(8,128)(2,1)S(1)}, bf16[32,32,128]{2,1,0:T(8,128)(2,1)S(1)}, u32[]{:S(2)}, u32[]{:S(2)}) collective-permute-start(bf16[32,32,128]{2,1,0:T(8,128)(2,1)S(1)} %join.3), channel_id=1, source_target_pairs={{0,2},{1,3},{2,0},{3,1},{4,6},{5,7},{6,4},{7,5},{8,10},{9,11},{10,... | collective-permute-start | bytes 786440 | tf_op jit(solution)/shard_map/ppermute | solution.py:20
  29.3 0.1 collective-permute-done.6.far
  29.5 0.0 slice-done.2
  29.5 5.1 %upper.1 = (bf16[4,64,128]{2,1,0:T(8,128)(2,1)S(1)}, bf16[4,64,128]{2,1,0:T(8,128)(2,1)S(1)}, bf16[4,64,128]{2,1,0:T(8,128)(2,1)S(1)}, bf16[4,64,128]{2,1,0:T(8,128)(2,1)S(1)}) custom-call(s32[1]{0:T(128)} %bitcast.me, s32[1]{0:T(128)} %bitcast.6.home, s32[16,16]{1,0:T(8,128)S(1)} %copy-done.11, s32[16,16]{1,0:T(8,128)S(1)} %copy-done.12, ...), custom_call_target="tpu_custom_call" | custom-call | flops 4294967296 | bytes 1 | tf_op jit(solution)/shard_map/upper/pallas_call | solution.py:32
  34.7 1.6 %collective-permute-start.7 = (bf16[4,64,128]{2,1,0:T(8,128)(2,1)S(1)}, bf16[4,64,128]{2,1,0:T(8,128)(2,1)S(1)}, u32[]{:S(2)}, u32[]{:S(2)}) collective-permute-start(bf16[4,64,128]{2,1,0:T(8,128)(2,1)S(1)} %get-tuple-element.54), channel_id=1, source_target_pairs={{0,2},{1,3},{2,0},{3,1},{4,6},{5,7},{6,4},{7,5},{8,10},{9,11},{10,... | collective-permute-start | bytes 196616 | tf_op jit(solution)/shard_map/ppermute | solution.py:20
  36.2 0.0 collective-permute-start.8
  36.3 2.1 %collective-permute-done.9.got = bf16[64,32,128]{2,1,0:T(8,128)(2,1)S(1)} collective-permute-done((bf16[64,32,128]{2,1,0:T(8,128)(2,1)S(1)}, bf16[64,32,128]{2,1,0:T(8,128)(2,1)S(1)}, u32[]{:S(2)}, u32[]{:S(2)}) %collective-permute-start.9) | collective-permute-done | bytes 524320 | tf_op jit(solution)/shard_map/ppermute | solution.py:20
  38.4 2.1 %close_peers.1 = bf16[40,32,128]{2,1,0:T(8,128)(2,1)S(1)} custom-call(s32[1]{0:T(128)} %bitcast.me, s32[16,128]{1,0:T(8,128)S(1)} %get-tuple-element.65.refs_0_.code, f32[316,32,128]{2,1,0:T(8,128)S(1)} %bitcast.51, f32[129,32,128]{2,1,0:T(8,128)S(1)} %copy-done, bf16[64,32,128]{2,1,0:T(8,128)(2,1)S(1)} %collective-permute-done.9.got, ...), custom_call_target="tpu_custom_call" | custom-call | bytes 1 | tf_op jit(solution)/shard_map/close_peers/pallas_call | solution.py:32
  40.5 0.1 collective-permute-start.10
  40.5 0.0 collective-permute-done.11.refs_0_
  40.5 0.0 collective-permute-done.12.refs_1_
  40.6 0.1 place.1
  40.6 2.1 %close_self.1.refs_2_ = bf16[40,32,128]{2,1,0:T(8,128)(2,1)S(1)} custom-call(s32[1]{0:T(128)} %bitcast.me, s32[16,128]{1,0:T(8,128)S(1)} %get-tuple-element.65.refs_0_.code, f32[316,32,128]{2,1,0:T(8,128)S(1)} %bitcast.51, f32[129,32,128]{2,1,0:T(8,128)S(1)} %copy-done, bf16[64,32,128]{2,1,0:T(8,128)(2,1)S(1)} %collective-permute-done.9.got, ...), custom_call_target="tpu_custom_call" | custom-call | bytes 1 | tf_op jit(solution)/shard_map/close_self/pallas_call | solution.py:32
  42.7 0.0 collective-permute-done.7.refs_0_
  42.7 0.0 collective-permute-done.8.refs_1_
  42.8 0.0 collective-permute-done.10.refs_3_
  42.8 2.6 %expand.1 = f32[4096,128]{1,0:T(8,128)} custom-call(s32[1]{0:T(128)} %bitcast.me, bf16[4,64,128]{2,1,0:T(8,128)(2,1)S(1)} %collective-permute-done.7.refs_0_, bf16[4,64,128]{2,1,0:T(8,128)(2,1)S(1)} %collective-permute-done.8.refs_1_, bf16[40,32,128]{2,1,0:T(8,128)(2,1)S(1)} %close_self.1.refs_2_, bf16[40,32,128]{2,1,0:T(8,128)(2,1)S(1)} %collective-permute-done.10.refs_3_, ...), custom_call_target="tpu_custom_call" | custom-call | flops 4294967296 | bytes 1 | tf_op jit(solution)/shard_map/expand/pallas_call | solution.py:32
  (13 shorter events, 0.1 us)
Async XLA Ops:
  0.7 5.6 %collective-permute-start = (s32[16,128]{1,0:T(8,128)S(1)}, s32[16,128]{1,0:T(8,128)S(1)}, u32[]{:S(2)}, u32[]{:S(2)}) collective-permute-start(s32[16,128]{1,0:T(8,128)S(1)} %get-tuple-element.66), channel_id=1, source_target_pairs={{0,4},{4,0},{8,12},{12,8},{16,20},{20,16},{24,28},{28,24},{1,5},{5... | collective-permute-start | bytes 24584 | tf_op jit(solution)/shard_map/ppermute | solution.py:20
  3.7 25.7 %collective-permute-start.6 = (bf16[16,2,32,256]{3,2,1,0:T(8,128)(2,1)}, bf16[16,2,32,256]{3,2,1,0:T(8,128)(2,1)S(1)}, u32[]{:S(2)}, u32[]{:S(2)}) collective-permute-start(bf16[16,2,32,256]{3,2,1,0:T(8,128)(2,1)} %own.1), channel_id=1, source_target_pairs={{0,16},{4,20},{8,24},{12,28},{16,0},{20,4},{24,8},{28,12},{1,17},{... | collective-permute-start | bytes 1572872 | tf_op jit(solution)/shard_map/ppermute | solution.py:20
  6.3 6.8 %copy-start.6 = (bf16[2,2,64,512]{3,2,1,0:T(8,128)(2,1)S(1)}, bf16[2,2,64,512]{3,2,1,0:T(8,128)(2,1)}, u32[]{:S(2)}) copy-start(bf16[2,2,64,512]{3,2,1,0:T(8,128)(2,1)} %param.17) | copy-start | bytes 786436
  6.3 6.8 %copy-start.7 = (bf16[256,512]{1,0:T(8,128)(2,1)S(1)}, bf16[256,512]{1,0:T(8,128)(2,1)}, u32[]{:S(2)}) copy-start(bf16[256,512]{1,0:T(8,128)(2,1)} %refs_2_.1) | copy-start | bytes 786436
  6.3 6.8 %copy-start.8 = (bf16[128,256]{1,0:T(8,128)(2,1)S(1)}, bf16[128,256]{1,0:T(8,128)(2,1)}, u32[]{:S(2)}) copy-start(bf16[128,256]{1,0:T(8,128)(2,1)} %refs_1_.1) | copy-start | bytes 196612
  6.3 6.8 %copy-start.9 = (f32[8,16,128]{2,1,0:T(8,128)S(1)}, f32[8,16,128]{2,1,0:T(8,128)}, u32[]{:S(2)}) copy-start(f32[8,16,128]{2,1,0:T(8,128)} %refs_3_.1) | copy-start | bytes 196612
  12.0 8.2 %collective-permute-start.1 = (bf16[32,32,128]{2,1,0:T(8,128)(2,1)S(1)}, bf16[32,32,128]{2,1,0:T(8,128)(2,1)S(1)}, u32[]{:S(2)}, u32[]{:S(2)}) collective-permute-start(bf16[32,32,128]{2,1,0:T(8,128)(2,1)S(1)} %get-tuple-element.35), channel_id=1, source_target_pairs={{0,4},{4,0},{8,12},{12,8},{16,20},{20,16},{24,28},{28,24},{1,5},{5... | collective-permute-start | bytes 786440 | tf_op jit(solution)/shard_map/ppermute | solution.py:20
  13.2 3.6 %slice-start = ((s8[5177344]{0:T(1024)(128)(4,1)}), s8[4194304]{0:T(1024)(128)(4,1)S(1)}, s32[]{:S(2)}) async-start(s8[5177344]{0:T(1024)(128)(4,1)} %bitcast.50), calls=%async_computation | async-start | bytes 8388608
  13.2 3.6 %slice-start.1 = ((s8[5177344]{0:T(1024)(128)(4,1)}), s8[983040]{0:T(1024)(128)(4,1)S(1)}, s32[]{:S(2)}) async-start(s8[5177344]{0:T(1024)(128)(4,1)} %bitcast.50), calls=%async_computation.1 | async-start | bytes 1966080
  13.2 3.6 %copy-start = (f32[129,32,128]{2,1,0:T(8,128)S(1)}, f32[129,32,128]{2,1,0:T(8,128)}, u32[]{:S(2)}) copy-start(f32[129,32,128]{2,1,0:T(8,128)} %get-tuple-element.40.refs_2_.source) | copy-start | bytes 6340612
  14.2 10.1 %collective-permute-start.3 = (f32[192,256]{1,0:T(8,128)S(1)}, f32[192,256]{1,0:T(8,128)S(1)}, u32[]{:S(2)}, u32[]{:S(2)}) collective-permute-start(f32[192,256]{1,0:T(8,128)S(1)} %get-tuple-element.47), channel_id=1, source_target_pairs={{0,2},{1,3},{2,0},{3,1},{4,6},{5,7},{6,4},{7,5},{8,10},{9,11},{10,... | collective-permute-start | bytes 589832 | tf_op jit(solution)/shard_map/ppermute | solution.py:20
  15.8 9.6 %collective-permute-start.4 = (f32[192,256]{1,0:T(8,128)S(1)}, f32[192,256]{1,0:T(8,128)S(1)}, u32[]{:S(2)}, u32[]{:S(2)}) collective-permute-start(f32[192,256]{1,0:T(8,128)S(1)} %get-tuple-element.48), channel_id=1, source_target_pairs={{0,3},{1,2},{2,1},{3,0},{4,7},{5,6},{6,5},{7,4},{8,11},{9,10},{10,... | collective-permute-start | bytes 589832 | tf_op jit(solution)/shard_map/ppermute | solution.py:20
  15.8 12.8 %collective-permute-start.5 = (bf16[32,32,128]{2,1,0:T(8,128)(2,1)S(1)}, bf16[32,32,128]{2,1,0:T(8,128)(2,1)S(1)}, u32[]{:S(2)}, u32[]{:S(2)}) collective-permute-start(bf16[32,32,128]{2,1,0:T(8,128)(2,1)S(1)} %get-tuple-element.51), channel_id=1, source_target_pairs={{0,4},{4,0},{8,12},{12,8},{16,20},{20,16},{24,28},{28,24},{1,5},{5... | collective-permute-start | bytes 786440 | tf_op jit(solution)/shard_map/ppermute | solution.py:20
  20.2 9.2 %slice-start.2 = ((s8[10354688]{0:T(1024)(128)(4,1)}), s8[4194304]{0:T(1024)(128)(4,1)S(1)}, s32[]{:S(2)}) async-start(s8[10354688]{0:T(1024)(128)(4,1)} %bitcast.54), calls=%async_computation.2 | async-start | bytes 8388608
  20.3 6.0 %copy-start.1 = (f32[8,32,256]{2,1,0:T(8,128)S(1)}, f32[8,32,256]{2,1,0:T(8,128)}, u32[]{:S(2)}) copy-start(f32[8,32,256]{2,1,0:T(8,128)} %refs_4_.1) | copy-start | bytes 786436
  20.3 6.0 %copy-start.2 = (bf16[2,128,128]{2,1,0:T(8,128)(2,1)S(1)}, bf16[2,128,128]{2,1,0:T(8,128)(2,1)}, u32[]{:S(2)}) copy-start(bf16[2,128,128]{2,1,0:T(8,128)(2,1)} %refs_5_.1) | copy-start | bytes 196612
  20.3 6.0 %copy-start.3 = (bf16[64,128]{1,0:T(8,128)(2,1)S(1)}, bf16[64,128]{1,0:T(8,128)(2,1)}, u32[]{:S(2)}) copy-start(bf16[64,128]{1,0:T(8,128)(2,1)} %refs_6_.1) | copy-start | bytes 49156
  20.4 6.0 %copy-start.4 = (bf16[64,64]{1,0:T(8,128)(2,1)S(1)}, bf16[64,64]{1,0:T(8,128)(2,1)}, u32[]{:S(2)}) copy-start(bf16[64,64]{1,0:T(8,128)(2,1)} %refs_7_.1) | copy-start | bytes 24580
  20.4 9.1 %slice-start.3 = ((s8[10354688]{0:T(1024)(128)(4,1)}), s8[4194304]{0:T(1024)(128)(4,1)S(1)}, s32[]{:S(2)}) async-start(s8[10354688]{0:T(1024)(128)(4,1)} %bitcast.54), calls=%async_computation.3 | async-start | bytes 8388608
  20.4 9.1 %slice-start.4 = ((s8[10354688]{0:T(1024)(128)(4,1)}), s8[1966080]{0:T(1024)(128)(4,1)S(1)}, s32[]{:S(2)}) async-start(s8[10354688]{0:T(1024)(128)(4,1)} %bitcast.54), calls=%async_computation.4 | async-start | bytes 3932160
  20.4 9.1 %copy-start.5 = (bf16[16,2,32,256]{3,2,1,0:T(8,128)(2,1)S(1)}, bf16[16,2,32,256]{3,2,1,0:T(8,128)(2,1)}, u32[]{:S(2)}) copy-start(bf16[16,2,32,256]{3,2,1,0:T(8,128)(2,1)} %own.1) | copy-start | bytes 1572868
  20.4 9.1 %copy-start.10 = (bf16[128,256]{1,0:T(8,128)(2,1)S(1)}, bf16[128,256]{1,0:T(8,128)(2,1)}, u32[]{:S(2)}) copy-start(bf16[128,256]{1,0:T(8,128)(2,1)} %phi.1) | copy-start | bytes 196612
  20.4 9.1 %copy-start.11 = (s32[16,16]{1,0:T(8,128)S(1)}, s32[16,16]{1,0:T(8,128)}, u32[]{:S(2)}) copy-start(s32[16,16]{1,0:T(8,128)} %ids.1) | copy-start | bytes 3076
  20.4 9.1 %copy-start.12 = (s32[16,16]{1,0:T(8,128)S(1)}, s32[16,16]{1,0:T(8,128)}, u32[]{:S(2)}) copy-start(s32[16,16]{1,0:T(8,128)} %offsets.1) | copy-start | bytes 3076
  23.9 2.4 %collective-permute-start.2 = (f32[192,256]{1,0:T(8,128)S(1)}, f32[192,256]{1,0:T(8,128)S(1)}, u32[]{:S(2)}, u32[]{:S(2)}) collective-permute-start(f32[192,256]{1,0:T(8,128)S(1)} %get-tuple-element.46), channel_id=1, source_target_pairs={{0,1},{1,0},{2,3},{3,2},{4,5},{5,4},{6,7},{7,6},{8,9},{9,8},{10,11... | collective-permute-start | bytes 589832 | tf_op jit(solution)/shard_map/ppermute | solution.py:20
  24.4 14.0 %collective-permute-start.9 = (bf16[64,32,128]{2,1,0:T(8,128)(2,1)S(1)}, bf16[64,32,128]{2,1,0:T(8,128)(2,1)S(1)}, u32[]{:S(2)}, u32[]{:S(2)}) collective-permute-start(bf16[64,32,128]{2,1,0:T(8,128)(2,1)S(1)} %sums_second.1), channel_id=1, source_target_pairs={{0,4},{4,0},{8,12},{12,8},{16,20},{20,16},{24,28},{28,24},{1,5},{5... | collective-permute-start | bytes 1572872 | tf_op jit(solution)/shard_map/ppermute | solution.py:20
  25.4 15.1 %collective-permute-start.11 = (bf16[32,32,128]{2,1,0:T(8,128)(2,1)S(1)}, bf16[32,32,128]{2,1,0:T(8,128)(2,1)S(1)}, u32[]{:S(2)}, u32[]{:S(2)}) collective-permute-start(bf16[32,32,128]{2,1,0:T(8,128)(2,1)S(1)} %join.2), channel_id=1, source_target_pairs={{0,3},{1,2},{2,1},{3,0},{4,7},{5,6},{6,5},{7,4},{8,11},{9,10},{10,... | collective-permute-start | bytes 786440 | tf_op jit(solution)/shard_map/ppermute | solution.py:20
  28.6 11.9 %collective-permute-start.12 = (bf16[32,32,128]{2,1,0:T(8,128)(2,1)S(1)}, bf16[32,32,128]{2,1,0:T(8,128)(2,1)S(1)}, u32[]{:S(2)}, u32[]{:S(2)}) collective-permute-start(bf16[32,32,128]{2,1,0:T(8,128)(2,1)S(1)} %join.3), channel_id=1, source_target_pairs={{0,2},{1,3},{2,0},{3,1},{4,6},{5,7},{6,4},{7,5},{8,10},{9,11},{10,... | collective-permute-start | bytes 786440 | tf_op jit(solution)/shard_map/ppermute | solution.py:20
  34.7 8.1 %collective-permute-start.7 = (bf16[4,64,128]{2,1,0:T(8,128)(2,1)S(1)}, bf16[4,64,128]{2,1,0:T(8,128)(2,1)S(1)}, u32[]{:S(2)}, u32[]{:S(2)}) collective-permute-start(bf16[4,64,128]{2,1,0:T(8,128)(2,1)S(1)} %get-tuple-element.54), channel_id=1, source_target_pairs={{0,2},{1,3},{2,0},{3,1},{4,6},{5,7},{6,4},{7,5},{8,10},{9,11},{10,... | collective-permute-start | bytes 196616 | tf_op jit(solution)/shard_map/ppermute | solution.py:20
  36.2 6.5 %collective-permute-start.8 = (bf16[4,64,128]{2,1,0:T(8,128)(2,1)S(1)}, bf16[4,64,128]{2,1,0:T(8,128)(2,1)S(1)}, u32[]{:S(2)}, u32[]{:S(2)}) collective-permute-start(bf16[4,64,128]{2,1,0:T(8,128)(2,1)S(1)} %get-tuple-element.55), channel_id=1, source_target_pairs={{0,3},{1,2},{2,1},{3,0},{4,7},{5,6},{6,5},{7,4},{8,11},{9,10},{10,... | collective-permute-start | bytes 196616 | tf_op jit(solution)/shard_map/ppermute | solution.py:20
  40.5 2.3 %collective-permute-start.10 = (bf16[40,32,128]{2,1,0:T(8,128)(2,1)S(1)}, bf16[40,32,128]{2,1,0:T(8,128)(2,1)S(1)}, u32[]{:S(2)}, u32[]{:S(2)}) collective-permute-start(bf16[40,32,128]{2,1,0:T(8,128)(2,1)S(1)} %close_peers.1), channel_id=1, source_target_pairs={{0,1},{1,0},{2,3},{3,2},{4,5},{5,4},{6,7},{7,6},{8,9},{9,8},{10,11... | collective-permute-start | bytes 983048 | tf_op jit(solution)/shard_map/ppermute | solution.py:20

commit v9 on v8

--- a/solution.py
+++ b/solution.py
@@ -20,7 +20,7 @@
     return lax.ppermute(value, axis, pairs)
 
 
-COSTS = {"join": 0, "sums_third": 0, "shift": 0, "close_peers": 0, "close_self": 0}
+COSTS = {"join": 0, "sums_third": 0, "sums_second": 0, "shift": 0, "upper": 1, "close_peers": 0, "close_self": 0}
 
 
 def after(value, *others):
@@ -179,16 +179,17 @@
     return kernel_call(body, [struct(a.shape, BF16) for a in owns], [], [*owns, got], "join")
 
 
-def close_body(masks, firsts, per, entries, me, code, table, source, got, *refs):
+def close_body(masks, per, entries, me, code, table, source, *refs):
     count = len(masks)
     rows = table.shape[1] // 2
-    for mask, begin, piece, out in zip(masks, firsts, refs[:count], refs[count:], strict=True):
+    for k, mask in enumerate(masks):
+        got, piece, out = refs[k], refs[count + k], refs[2 * count + k]
         first = jnp.bitwise_xor(me[0], mask) * per
 
-        def one(i, carry, first=first, begin=begin, out=out):
+        def one(i, carry, first=first, got=got, out=out):
             real, imag = box_sum(first + i, entries, code, table, source)
-            real = real + got[begin + i, 0:rows].astype(F32)
-            imag = imag + got[begin + i, rows:].astype(F32)
+            real = real + got[i, 0:rows].astype(F32)
+            imag = imag + got[i, rows:].astype(F32)
             out[i, 0:rows] = real.astype(BF16)
             out[i, rows:] = imag.astype(BF16)
             return carry
@@ -340,7 +341,6 @@
         )
 
     own_shape = struct((per, 2 * low, lanes), F32)
-    far_shape = struct((len(outer) * per, 2 * low, lanes), BF16)
     *first, table, source = kernel_call(
         functools.partial(first_body, [((mask,), 0) for mask in outer], per, entries),
         [
@@ -395,9 +395,15 @@
     lows = {}
     for mask, own, got in list(zip(outer, own_outer, got_outer, strict=True))[: len(outer) // 2]:
         (lows[mask],) = join([own], got)
-    (second,) = sums([(tuple(inner), 0)], [far_shape], [far_code], after(me, lows[outer[0]]), "sums_second")
-    got_inner = swap(second, "box", 1)
-    late = after(parts[1], second)
+    second = sums(
+        [((mask,), 0) for mask in inner],
+        [struct((per, 2 * low, lanes), BF16)] * len(inner),
+        [far_code],
+        after(me, lows[outer[0]]),
+        "sums_second",
+    )
+    got_inner = {mask: swap(value, "box", 1) for mask, value in zip(inner, second, strict=True)}
+    late = after(parts[1], second[0])
     parts = [parts[0]] + [swap(late if mask == 1 else parts[mask], "angle", mask) for mask in inner[-2::-1]] + [*parts[len(inner) :]]
     orders = switch_theta.shape[0]
     azimuths = switch_phi.shape[1]
@@ -410,7 +416,7 @@
             struct(theta_lower.shape, BF16),
             struct(switch_theta.shape, BF16),
         ],
-        [after(me, second)],
+        [after(me, second[0])],
         [*parts, angles_upper, switch_phi, theta_lower, switch_theta],
         "shift",
         scratch=[
@@ -438,10 +444,10 @@
     behind = {mask: ups.pop(mask).reshape(-1, 2 * low, lanes) for mask in inner}
     for masks, name in ((inner[:-1], "close_peers"), (inner[-1:], "close_self")):
         close = kernel_call(
-            functools.partial(close_body, masks, [per * inner.index(m) for m in masks], per, entries),
+            functools.partial(close_body, masks, per, entries),
             [struct((per + behind[0].shape[0], 2 * low, lanes), BF16)] * len(masks),
             [order, own_code],
-            [table, source, got_inner, *(behind[mask] for mask in masks)],
+            [table, source, *(got_inner[mask] for mask in masks), *(behind[mask] for mask in masks)],
             name,
         )
         lows.update(zip(masks, close, strict=True))

time: 45.6 us -> 46.1 us (1.011)
  starting transfers between devices: 14 us -> 15.7 us
  waiting for transfers between devices: 2.24 us -> 0.65 us
  local copies, waits for them, and re-layouts: 0.1 us -> 0.59 us
    ppermute x13 -> x14, starting transfers between devices: 14 us -> 15.7 us  [swap(): return lax.ppermute(value, axis, pairs)]
    ppermute x13 -> x14, waiting for transfers between devices: 2.24 us -> 0.65 us  [swap(): return lax.ppermute(value, axis, pairs)]
    unnamed x36, local copies, waits for them, and re-layouts: 0.1 us -> 0.59 us
  transfers between devices with their start and end apart: 13 -> 14, of which waited for: 2 -> 1; matrix products, arithmetic and copies ran while one was open for 0% -> 0% of each run, Pallas kernels for 56% -> 55%
where the time goes in v9:
time: 46.1 us; the launch traced here: 45.8 us
  Pallas kernels  27.9 us (61%)
  starting transfers between devices  15.7 us (34%)
  other arithmetic  0.73 us (2%)
  waiting for transfers between devices  0.65 us (1%)
  local copies, waits for them, and re-layouts  0.59 us (1%)
    pallas_call x12, Pallas kernels, kernel_call(): pl.pallas_call(body, out_shape=outs, in_specs=[SM] * len(scalars) + [VM]...  27.9 us
    ppermute x14, starting transfers between devices, swap(): return lax.ppermute(value, axis, pairs)  15.7 us
  transfers between devices with their start and end apart: 14, of which 1 were waited for; matrix products, arithmetic and copies ran while one was open for 0% of the time, Pallas kernels for 55%

profile of v9, /device:TPU:0, one launch (start us, length us, event | category | flops | bytes accessed | tf_op | source)
XLA Modules:
  0.0 45.8 jit_solution(14665201422820976816)
XLA Ops:
  0.0 0.7 %bitcast_add_fusion = (s32[16,128]{1,0:T(8,128)S(1)}, s32[16,128]{1,0:T(8,128)S(1)}) fusion(s32[128,16]{0,1:T(8,128)} %param.31, s32[128,16]{0,1:T(8,128)} %param.30, s32[]{:T(128)} %axis_index.25), kind=kLoop, calls=%fused_computation.6 | loop fusion | flops 53248 | bytes 32772 | tf_op jit(solution)/shard_map/add | solution.py:327
  0.7 3.0 %collective-permute-start = (s32[16,128]{1,0:T(8,128)S(1)}, s32[16,128]{1,0:T(8,128)S(1)}, u32[]{:S(2)}, u32[]{:S(2)}) collective-permute-start(s32[16,128]{1,0:T(8,128)S(1)} %get-tuple-element.70), channel_id=1, source_target_pairs={{0,4},{4,0},{8,12},{12,8},{16,20},{20,16},{24,28},{28,24},{1,5},{5... | collective-permute-start | bytes 24584 | tf_op jit(solution)/shard_map/ppermute | solution.py:20
  3.7 2.6 %collective-permute-start.6 = (bf16[16,2,32,256]{3,2,1,0:T(8,128)(2,1)}, bf16[16,2,32,256]{3,2,1,0:T(8,128)(2,1)S(1)}, u32[]{:S(2)}, u32[]{:S(2)}) collective-permute-start(bf16[16,2,32,256]{3,2,1,0:T(8,128)(2,1)} %own.1), channel_id=1, source_target_pairs={{0,16},{4,20},{8,24},{12,28},{16,0},{20,4},{24,8},{28,12},{1,17},{... | collective-permute-start | bytes 1572872 | tf_op jit(solution)/shard_map/ppermute | solution.py:20
  6.3 0.0 collective-permute-done.code.refs_0_
  6.3 0.0 copy-start.12
  6.4 5.7 %sums_first.1 = (bf16[32,32,128]{2,1,0:T(8,128)(2,1)S(1)}, bf16[32,32,128]{2,1,0:T(8,128)(2,1)S(1)}, f32[316,32,128]{2,1,0:T(8,128)}, f32[129,32,128]{2,1,0:T(8,128)}) custom-call(s32[1]{0:T(128)} %bitcast.me, s32[16,128]{1,0:T(8,128)S(1)} %collective-permute-done.code.refs_0_, bf16[316,32,128]{2,1,0:T(8,128)(2,1)} %bitcast.58, bf16[128,32,128]{2,1,0:T(8,128)(2,1)} %bitcast.59), custom_call_target="tpu_custom_call" | custom-call | flops 4294967296 | bytes 1 | tf_op jit(solution)/shard_map/sums_first/pallas_call | solution.py:32
  12.0 1.1 %collective-permute-start.1 = (bf16[32,32,128]{2,1,0:T(8,128)(2,1)S(1)}, bf16[32,32,128]{2,1,0:T(8,128)(2,1)S(1)}, u32[]{:S(2)}, u32[]{:S(2)}) collective-permute-start(bf16[32,32,128]{2,1,0:T(8,128)(2,1)S(1)} %get-tuple-element.37), channel_id=1, source_target_pairs={{0,4},{4,0},{8,12},{12,8},{16,20},{20,16},{24,28},{28,24},{1,5},{5... | collective-permute-start | bytes 786440 | tf_op jit(solution)/shard_map/ppermute | solution.py:20
  13.1 1.0 %collective-permute-start.5 = (bf16[32,32,128]{2,1,0:T(8,128)(2,1)S(1)}, bf16[32,32,128]{2,1,0:T(8,128)(2,1)S(1)}, u32[]{:S(2)}, u32[]{:S(2)}) collective-permute-start(bf16[32,32,128]{2,1,0:T(8,128)(2,1)S(1)} %get-tuple-element.54), channel_id=1, source_target_pairs={{0,4},{4,0},{8,12},{12,8},{16,20},{20,16},{24,28},{28,24},{1,5},{5... | collective-permute-start | bytes 786440 | tf_op jit(solution)/shard_map/ppermute | solution.py:20
  14.1 0.0 copy-done.9
  14.1 0.0 copy-done.10
  14.1 0.0 copy-done.12
  14.2 0.0 slice-start.1
  14.2 0.0 slice-start.2
  14.2 0.0 slice-start.3
  14.2 1.0 %early.1 = (f32[192,256]{1,0:T(8,128)S(1)}, f32[192,256]{1,0:T(8,128)S(1)}, f32[192,256]{1,0:T(8,128)S(1)}, f32[192,256]{1,0:T(8,128)S(1)}) custom-call(s32[1]{0:T(128)} %bitcast.me, bf16[256,512]{1,0:T(8,128)(2,1)S(1)} %bitcast.57, bf16[128,256]{1,0:T(8,128)(2,1)S(1)} %copy-done.11, bf16[256,512]{1,0:T(8,128)(2,1)S(1)} %copy-done.10, ...), custom_call_target="tpu_custom_call" | custom-call | flops 4294967296 | bytes 1 | tf_op jit(solution)/shard_map/early/pallas_call | solution.py:32
  15.2 1.6 %collective-permute-start.3 = (f32[192,256]{1,0:T(8,128)S(1)}, f32[192,256]{1,0:T(8,128)S(1)}, u32[]{:S(2)}, u32[]{:S(2)}) collective-permute-start(f32[192,256]{1,0:T(8,128)S(1)} %get-tuple-element.50), channel_id=1, source_target_pairs={{0,2},{1,3},{2,0},{3,1},{4,6},{5,7},{6,4},{7,5},{8,10},{9,11},{10,... | collective-permute-start | bytes 589832 | tf_op jit(solution)/shard_map/ppermute | solution.py:20
  16.8 0.0 collective-permute-start.4
  16.8 0.0 slice-done
  16.8 0.5 %copy-done = f32[129,32,128]{2,1,0:T(8,128)S(1)} copy-done((f32[129,32,128]{2,1,0:T(8,128)S(1)}, f32[129,32,128]{2,1,0:T(8,128)}, u32[]{:S(2)}) %copy-start) | copy-done | bytes 2113560
  17.3 3.4 %sums_third.1 = (f32[32,32,128]{2,1,0:T(8,128)S(1)}, f32[32,32,128]{2,1,0:T(8,128)S(1)}) custom-call(s32[1]{0:T(128)} %bitcast.me, s32[16,128]{1,0:T(8,128)S(1)} %get-tuple-element.69.refs_0_.code, f32[316,32,128]{2,1,0:T(8,128)S(1)} %bitcast.51, f32[129,32,128]{2,1,0:T(8,128)S(1)} %copy-done), custom_call_target="tpu_custom_call" | custom-call | bytes 1 | tf_op jit(solution)/shard_map/sums_third/pallas_call | solution.py:32
  20.7 0.6 %collective-permute-done.1.refs_1_ = bf16[32,32,128]{2,1,0:T(8,128)(2,1)S(1)} collective-permute-done((bf16[32,32,128]{2,1,0:T(8,128)(2,1)S(1)}, bf16[32,32,128]{2,1,0:T(8,128)(2,1)S(1)}, u32[]{:S(2)}, u32[]{:S(2)}) %collective-permute-start.1) | collective-permute-done | bytes 262176 | tf_op jit(solution)/shard_map/ppermute | solution.py:20
  21.3 0.1 join.2
  21.4 0.0 copy-start.2
  21.4 0.0 copy-start.4
  21.4 0.0 copy-start.5
  21.5 0.0 copy-start.6
  21.5 0.0 copy-start.1
  21.5 0.0 copy-start.3
  21.5 0.0 copy-start.7
  21.5 0.0 copy-start.8
  21.5 3.5 %sums_second.1 = (bf16[32,32,128]{2,1,0:T(8,128)(2,1)S(1)}, bf16[32,32,128]{2,1,0:T(8,128)(2,1)S(1)}) custom-call(s32[1]{0:T(128)} %bitcast.me, s32[16,128]{1,0:T(8,128)S(1)} %collective-permute-done.code.refs_0_, f32[316,32,128]{2,1,0:T(8,128)S(1)} %bitcast.51, f32[129,32,128]{2,1,0:T(8,128)S(1)} %copy-done), custom_call_target="tpu_custom_call" | custom-call | bytes 1 | tf_op jit(solution)/shard_map/sums_second/pallas_call | solution.py:32
  25.0 0.1 collective-permute-start.2
  25.1 0.0 collective-permute-done.3.refs_2_
  25.1 1.1 %collective-permute-start.9 = (bf16[32,32,128]{2,1,0:T(8,128)(2,1)S(1)}, bf16[32,32,128]{2,1,0:T(8,128)(2,1)S(1)}, u32[]{:S(2)}, u32[]{:S(2)}) collective-permute-start(bf16[32,32,128]{2,1,0:T(8,128)(2,1)S(1)} %get-tuple-element.46), channel_id=1, source_target_pairs={{0,4},{4,0},{8,12},{12,8},{16,20},{20,16},{24,28},{28,24},{1,5},{5... | collective-permute-start | bytes 786440 | tf_op jit(solution)/shard_map/ppermute | solution.py:20
  26.2 0.0 collective-permute-done.4.refs_3_
  26.2 1.3 %collective-permute-start.12 = (bf16[32,32,128]{2,1,0:T(8,128)(2,1)S(1)}, bf16[32,32,128]{2,1,0:T(8,128)(2,1)S(1)}, u32[]{:S(2)}, u32[]{:S(2)}) collective-permute-start(bf16[32,32,128]{2,1,0:T(8,128)(2,1)S(1)} %join.2), channel_id=1, source_target_pairs={{0,3},{1,2},{2,1},{3,0},{4,7},{5,6},{6,5},{7,4},{8,11},{9,10},{10,... | collective-permute-start | bytes 786440 | tf_op jit(solution)/shard_map/ppermute | solution.py:20
  27.5 0.0 collective-permute-done.2.refs_1_
  27.5 1.0 %collective-permute-start.10 = (bf16[32,32,128]{2,1,0:T(8,128)(2,1)S(1)}, bf16[32,32,128]{2,1,0:T(8,128)(2,1)S(1)}, u32[]{:S(2)}, u32[]{:S(2)}) collective-permute-start(bf16[32,32,128]{2,1,0:T(8,128)(2,1)S(1)} %get-tuple-element.63), channel_id=1, source_target_pairs={{0,4},{4,0},{8,12},{12,8},{16,20},{20,16},{24,28},{28,24},{1,5},{5... | collective-permute-start | bytes 786440 | tf_op jit(solution)/shard_map/ppermute | solution.py:20
  28.5 0.0 copy-done.4
  28.5 0.0 copy-done.6
  28.5 2.2 %shift.1 = (f32[16,2,32,256]{3,2,1,0:T(8,128)S(1)}, f32[2,8,4,16,128]{4,3,2,1,0:T(8,128)S(1)}, bf16[256,256]{1,0:T(8,128)(2,1)S(1)}, bf16[64,128]{1,0:T(8,128)(2,1)S(1)}, bf16[64,64]{1,0:T(8,128)(2,1)S(1)}) custom-call(s32[1]{0:T(128)} %bitcast.me, f32[192,256]{1,0:T(8,128)S(1)} %get-tuple-element.39.refs_0_, f32[192,256]{1,0:T(8,128)S(1)} %collective-permute-done.2.refs_1_, ...), custom_call_target="tpu_custom_call" | custom-call | bytes 1 | tf_op jit(solution)/shard_map/shift/pallas_call | solution.py:32
  30.7 0.0 collective-permute-done.5.refs_1_
  30.8 0.7 %collective-permute-start.13 = (bf16[32,32,128]{2,1,0:T(8,128)(2,1)S(1)}, bf16[32,32,128]{2,1,0:T(8,128)(2,1)S(1)}, u32[]{:S(2)}, u32[]{:S(2)}) collective-permute-start(bf16[32,32,128]{2,1,0:T(8,128)(2,1)S(1)} %join.3), channel_id=1, source_target_pairs={{0,2},{1,3},{2,0},{3,1},{4,6},{5,7},{6,4},{7,5},{8,10},{9,11},{10,... | collective-permute-start | bytes 786440 | tf_op jit(solution)/shard_map/ppermute | solution.py:20
  31.4 0.0 collective-permute-done.6.far
  31.5 0.0 slice-done.4
  31.5 0.0 copy-done.1
  31.5 0.0 copy-done.3
  31.5 0.0 copy-done.7
  31.5 0.0 copy-done.8
  31.5 5.1 %upper.1 = (bf16[4,64,128]{2,1,0:T(8,128)(2,1)S(1)}, bf16[4,64,128]{2,1,0:T(8,128)(2,1)S(1)}, bf16[4,64,128]{2,1,0:T(8,128)(2,1)S(1)}, bf16[4,64,128]{2,1,0:T(8,128)(2,1)S(1)}) custom-call(s32[1]{0:T(128)} %bitcast.me, s32[1]{0:T(128)} %bitcast.6.home, s32[16,16]{1,0:T(8,128)S(1)} %copy-done.7, s32[16,16]{1,0:T(8,128)S(1)} %copy-done.8, ...), custom_call_target="tpu_custom_call" | custom-call | flops 1073741824 | bytes 1 | tf_op jit(solution)/shard_map/upper/pallas_call | solution.py:32
  36.7 1.5 %collective-permute-start.7 = (bf16[4,64,128]{2,1,0:T(8,128)(2,1)S(1)}, bf16[4,64,128]{2,1,0:T(8,128)(2,1)S(1)}, u32[]{:S(2)}, u32[]{:S(2)}) collective-permute-start(bf16[4,64,128]{2,1,0:T(8,128)(2,1)S(1)} %get-tuple-element.57), channel_id=1, source_target_pairs={{0,2},{1,3},{2,0},{3,1},{4,6},{5,7},{6,4},{7,5},{8,10},{9,11},{10,... | collective-permute-start | bytes 196616 | tf_op jit(solution)/shard_map/ppermute | solution.py:20
  38.1 0.0 collective-permute-done.9.refs_0_
  38.2 0.0 collective-permute-start.8
  38.2 2.1 %close_peers.1 = bf16[40,32,128]{2,1,0:T(8,128)(2,1)S(1)} custom-call(s32[1]{0:T(128)} %bitcast.me, s32[16,128]{1,0:T(8,128)S(1)} %get-tuple-element.69.refs_0_.code, f32[316,32,128]{2,1,0:T(8,128)S(1)} %bitcast.51, f32[129,32,128]{2,1,0:T(8,128)S(1)} %copy-done, bf16[32,32,128]{2,1,0:T(8,128)(2,1)S(1)} %collective-permute-done.9.refs_0_, ...), custom_call_target="tpu_custom_call" | custom-call | bytes 1 | tf_op jit(solution)/shard_map/close_peers/pallas_call | solution.py:32
  40.3 0.0 collective-permute-done.10.refs_0_
  40.3 0.8 %collective-permute-start.11 = (bf16[40,32,128]{2,1,0:T(8,128)(2,1)S(1)}, bf16[40,32,128]{2,1,0:T(8,128)(2,1)S(1)}, u32[]{:S(2)}, u32[]{:S(2)}) collective-permute-start(bf16[40,32,128]{2,1,0:T(8,128)(2,1)S(1)} %close_peers.1), channel_id=1, source_target_pairs={{0,1},{1,0},{2,3},{3,2},{4,5},{5,4},{6,7},{7,6},{8,9},{9,8},{10,11... | collective-permute-start | bytes 983048 | tf_op jit(solution)/shard_map/ppermute | solution.py:20
  41.0 2.1 %close_self.1.refs_2_ = bf16[40,32,128]{2,1,0:T(8,128)(2,1)S(1)} custom-call(s32[1]{0:T(128)} %bitcast.me, s32[16,128]{1,0:T(8,128)S(1)} %get-tuple-element.69.refs_0_.code, f32[316,32,128]{2,1,0:T(8,128)S(1)} %bitcast.51, f32[129,32,128]{2,1,0:T(8,128)S(1)} %copy-done, bf16[32,32,128]{2,1,0:T(8,128)(2,1)S(1)} %collective-permute-done.10.refs_0_, ...), custom_call_target="tpu_custom_call" | custom-call | bytes 1 | tf_op jit(solution)/shard_map/close_self/pallas_call | solution.py:32
  43.1 0.0 collective-permute-done.12.refs_0_
  43.2 0.0 collective-permute-done.13.refs_1_
  43.2 0.1 place.1
  43.2 0.0 collective-permute-done.7.refs_0_
  43.3 0.0 collective-permute-done.8.refs_1_
  43.3 0.0 collective-permute-done.11.refs_3_
  43.3 2.6 %expand.1 = f32[4096,128]{1,0:T(8,128)} custom-call(s32[1]{0:T(128)} %bitcast.me, bf16[4,64,128]{2,1,0:T(8,128)(2,1)S(1)} %collective-permute-done.7.refs_0_, bf16[4,64,128]{2,1,0:T(8,128)(2,1)S(1)} %collective-permute-done.8.refs_1_, bf16[40,32,128]{2,1,0:T(8,128)(2,1)S(1)} %close_self.1.refs_2_, bf16[40,32,128]{2,1,0:T(8,128)(2,1)S(1)} %collective-permute-done.11.refs_3_, ...), custom_call_target="tpu_custom_call" | custom-call | flops 4294967296 | bytes 1 | tf_op jit(solution)/shard_map/expand/pallas_call | solution.py:32
  (15 shorter events, 0.1 us)
Async XLA Ops:
  0.7 5.6 %collective-permute-start = (s32[16,128]{1,0:T(8,128)S(1)}, s32[16,128]{1,0:T(8,128)S(1)}, u32[]{:S(2)}, u32[]{:S(2)}) collective-permute-start(s32[16,128]{1,0:T(8,128)S(1)} %get-tuple-element.70), channel_id=1, source_target_pairs={{0,4},{4,0},{8,12},{12,8},{16,20},{20,16},{24,28},{28,24},{1,5},{5... | collective-permute-start | bytes 24584 | tf_op jit(solution)/shard_map/ppermute | solution.py:20
  3.7 27.7 %collective-permute-start.6 = (bf16[16,2,32,256]{3,2,1,0:T(8,128)(2,1)}, bf16[16,2,32,256]{3,2,1,0:T(8,128)(2,1)S(1)}, u32[]{:S(2)}, u32[]{:S(2)}) collective-permute-start(bf16[16,2,32,256]{3,2,1,0:T(8,128)(2,1)} %own.1), channel_id=1, source_target_pairs={{0,16},{4,20},{8,24},{12,28},{16,0},{20,4},{24,8},{28,12},{1,17},{... | collective-permute-start | bytes 1572872 | tf_op jit(solution)/shard_map/ppermute | solution.py:20
  6.3 7.8 %copy-start.9 = (bf16[2,2,64,512]{3,2,1,0:T(8,128)(2,1)S(1)}, bf16[2,2,64,512]{3,2,1,0:T(8,128)(2,1)}, u32[]{:S(2)}) copy-start(bf16[2,2,64,512]{3,2,1,0:T(8,128)(2,1)} %param.17) | copy-start | bytes 786436
  6.3 7.8 %copy-start.10 = (bf16[256,512]{1,0:T(8,128)(2,1)S(1)}, bf16[256,512]{1,0:T(8,128)(2,1)}, u32[]{:S(2)}) copy-start(bf16[256,512]{1,0:T(8,128)(2,1)} %refs_2_.1) | copy-start | bytes 786436
  6.3 7.8 %copy-start.11 = (bf16[128,256]{1,0:T(8,128)(2,1)S(1)}, bf16[128,256]{1,0:T(8,128)(2,1)}, u32[]{:S(2)}) copy-start(bf16[128,256]{1,0:T(8,128)(2,1)} %refs_1_.1) | copy-start | bytes 196612
  6.3 7.8 %copy-start.12 = (f32[8,16,128]{2,1,0:T(8,128)S(1)}, f32[8,16,128]{2,1,0:T(8,128)}, u32[]{:S(2)}) copy-start(f32[8,16,128]{2,1,0:T(8,128)} %refs_3_.1) | copy-start | bytes 196612
  12.0 9.3 %collective-permute-start.1 = (bf16[32,32,128]{2,1,0:T(8,128)(2,1)S(1)}, bf16[32,32,128]{2,1,0:T(8,128)(2,1)S(1)}, u32[]{:S(2)}, u32[]{:S(2)}) collective-permute-start(bf16[32,32,128]{2,1,0:T(8,128)(2,1)S(1)} %get-tuple-element.37), channel_id=1, source_target_pairs={{0,4},{4,0},{8,12},{12,8},{16,20},{20,16},{24,28},{28,24},{1,5},{5... | collective-permute-start | bytes 786440 | tf_op jit(solution)/shard_map/ppermute | solution.py:20
  13.1 17.6 %collective-permute-start.5 = (bf16[32,32,128]{2,1,0:T(8,128)(2,1)S(1)}, bf16[32,32,128]{2,1,0:T(8,128)(2,1)S(1)}, u32[]{:S(2)}, u32[]{:S(2)}) collective-permute-start(bf16[32,32,128]{2,1,0:T(8,128)(2,1)S(1)} %get-tuple-element.54), channel_id=1, source_target_pairs={{0,4},{4,0},{8,12},{12,8},{16,20},{20,16},{24,28},{28,24},{1,5},{5... | collective-permute-start | bytes 786440 | tf_op jit(solution)/shard_map/ppermute | solution.py:20
  14.1 2.7 %slice-start = ((s8[5177344]{0:T(1024)(128)(4,1)}), s8[4194304]{0:T(1024)(128)(4,1)S(1)}, s32[]{:S(2)}) async-start(s8[5177344]{0:T(1024)(128)(4,1)} %bitcast.50), calls=%async_computation | async-start | bytes 8388608
  14.2 2.6 %slice-start.1 = ((s8[5177344]{0:T(1024)(128)(4,1)}), s8[983040]{0:T(1024)(128)(4,1)S(1)}, s32[]{:S(2)}) async-start(s8[5177344]{0:T(1024)(128)(4,1)} %bitcast.50), calls=%async_computation.1 | async-start | bytes 1966080
  14.2 3.1 %copy-start = (f32[129,32,128]{2,1,0:T(8,128)S(1)}, f32[129,32,128]{2,1,0:T(8,128)}, u32[]{:S(2)}) copy-start(f32[129,32,128]{2,1,0:T(8,128)} %get-tuple-element.42.refs_2_.source) | copy-start | bytes 6340612
  14.2 17.3 %slice-start.2 = ((s8[10354688]{0:T(1024)(128)(4,1)}), s8[4194304]{0:T(1024)(128)(4,1)S(1)}, s32[]{:S(2)}) async-start(s8[10354688]{0:T(1024)(128)(4,1)} %bitcast.52), calls=%async_computation.2 | async-start | bytes 8388608
  14.2 17.3 %slice-start.3 = ((s8[10354688]{0:T(1024)(128)(4,1)}), s8[4194304]{0:T(1024)(128)(4,1)S(1)}, s32[]{:S(2)}) async-start(s8[10354688]{0:T(1024)(128)(4,1)} %bitcast.52), calls=%async_computation.3 | async-start | bytes 8388608
  15.2 9.9 %collective-permute-start.3 = (f32[192,256]{1,0:T(8,128)S(1)}, f32[192,256]{1,0:T(8,128)S(1)}, u32[]{:S(2)}, u32[]{:S(2)}) collective-permute-start(f32[192,256]{1,0:T(8,128)S(1)} %get-tuple-element.50), channel_id=1, source_target_pairs={{0,2},{1,3},{2,0},{3,1},{4,6},{5,7},{6,4},{7,5},{8,10},{9,11},{10,... | collective-permute-start | bytes 589832 | tf_op jit(solution)/shard_map/ppermute | solution.py:20
  16.8 9.4 %collective-permute-start.4 = (f32[192,256]{1,0:T(8,128)S(1)}, f32[192,256]{1,0:T(8,128)S(1)}, u32[]{:S(2)}, u32[]{:S(2)}) collective-permute-start(f32[192,256]{1,0:T(8,128)S(1)} %get-tuple-element.51), channel_id=1, source_target_pairs={{0,3},{1,2},{2,1},{3,0},{4,7},{5,6},{6,5},{7,4},{8,11},{9,10},{10,... | collective-permute-start | bytes 589832 | tf_op jit(solution)/shard_map/ppermute | solution.py:20
  17.3 14.2 %slice-start.4 = ((s8[10354688]{0:T(1024)(128)(4,1)}), s8[1966080]{0:T(1024)(128)(4,1)S(1)}, s32[]{:S(2)}) async-start(s8[10354688]{0:T(1024)(128)(4,1)} %bitcast.52), calls=%async_computation.4 | async-start | bytes 3932160
  21.4 7.1 %copy-start.2 = (f32[8,32,256]{2,1,0:T(8,128)S(1)}, f32[8,32,256]{2,1,0:T(8,128)}, u32[]{:S(2)}) copy-start(f32[8,32,256]{2,1,0:T(8,128)} %refs_4_.1) | copy-start | bytes 786436
  21.4 7.1 %copy-start.4 = (bf16[2,128,128]{2,1,0:T(8,128)(2,1)S(1)}, bf16[2,128,128]{2,1,0:T(8,128)(2,1)}, u32[]{:S(2)}) copy-start(bf16[2,128,128]{2,1,0:T(8,128)(2,1)} %refs_5_.1) | copy-start | bytes 196612
  21.4 7.0 %copy-start.5 = (bf16[64,128]{1,0:T(8,128)(2,1)S(1)}, bf16[64,128]{1,0:T(8,128)(2,1)}, u32[]{:S(2)}) copy-start(bf16[64,128]{1,0:T(8,128)(2,1)} %refs_6_.1) | copy-start | bytes 49156
  21.5 7.0 %copy-start.6 = (bf16[64,64]{1,0:T(8,128)(2,1)S(1)}, bf16[64,64]{1,0:T(8,128)(2,1)}, u32[]{:S(2)}) copy-start(bf16[64,64]{1,0:T(8,128)(2,1)} %refs_7_.1) | copy-start | bytes 24580
  21.5 10.0 %copy-start.1 = (bf16[16,2,32,256]{3,2,1,0:T(8,128)(2,1)S(1)}, bf16[16,2,32,256]{3,2,1,0:T(8,128)(2,1)}, u32[]{:S(2)}) copy-start(bf16[16,2,32,256]{3,2,1,0:T(8,128)(2,1)} %own.1) | copy-start | bytes 1572868
  21.5 10.0 %copy-start.3 = (bf16[128,256]{1,0:T(8,128)(2,1)S(1)}, bf16[128,256]{1,0:T(8,128)(2,1)}, u32[]{:S(2)}) copy-start(bf16[128,256]{1,0:T(8,128)(2,1)} %phi.1) | copy-start | bytes 196612
  21.5 10.0 %copy-start.7 = (s32[16,16]{1,0:T(8,128)S(1)}, s32[16,16]{1,0:T(8,128)}, u32[]{:S(2)}) copy-start(s32[16,16]{1,0:T(8,128)} %ids.1) | copy-start | bytes 3076
  21.5 10.0 %copy-start.8 = (s32[16,16]{1,0:T(8,128)S(1)}, s32[16,16]{1,0:T(8,128)}, u32[]{:S(2)}) copy-start(s32[16,16]{1,0:T(8,128)} %offsets.1) | copy-start | bytes 3076
  25.0 2.5 %collective-permute-start.2 = (f32[192,256]{1,0:T(8,128)S(1)}, f32[192,256]{1,0:T(8,128)S(1)}, u32[]{:S(2)}, u32[]{:S(2)}) collective-permute-start(f32[192,256]{1,0:T(8,128)S(1)} %get-tuple-element.49), channel_id=1, source_target_pairs={{0,1},{1,0},{2,3},{3,2},{4,5},{5,4},{6,7},{7,6},{8,9},{9,8},{10,11... | collective-permute-start | bytes 589832 | tf_op jit(solution)/shard_map/ppermute | solution.py:20
  25.1 13.1 %collective-permute-start.9 = (bf16[32,32,128]{2,1,0:T(8,128)(2,1)S(1)}, bf16[32,32,128]{2,1,0:T(8,128)(2,1)S(1)}, u32[]{:S(2)}, u32[]{:S(2)}) collective-permute-start(bf16[32,32,128]{2,1,0:T(8,128)(2,1)S(1)} %get-tuple-element.46), channel_id=1, source_target_pairs={{0,4},{4,0},{8,12},{12,8},{16,20},{20,16},{24,28},{28,24},{1,5},{5... | collective-permute-start | bytes 786440 | tf_op jit(solution)/shard_map/ppermute | solution.py:20
  26.2 16.9 %collective-permute-start.12 = (bf16[32,32,128]{2,1,0:T(8,128)(2,1)S(1)}, bf16[32,32,128]{2,1,0:T(8,128)(2,1)S(1)}, u32[]{:S(2)}, u32[]{:S(2)}) collective-permute-start(bf16[32,32,128]{2,1,0:T(8,128)(2,1)S(1)} %join.2), channel_id=1, source_target_pairs={{0,3},{1,2},{2,1},{3,0},{4,7},{5,6},{6,5},{7,4},{8,11},{9,10},{10,... | collective-permute-start | bytes 786440 | tf_op jit(solution)/shard_map/ppermute | solution.py:20
  27.5 12.8 %collective-permute-start.10 = (bf16[32,32,128]{2,1,0:T(8,128)(2,1)S(1)}, bf16[32,32,128]{2,1,0:T(8,128)(2,1)S(1)}, u32[]{:S(2)}, u32[]{:S(2)}) collective-permute-start(bf16[32,32,128]{2,1,0:T(8,128)(2,1)S(1)} %get-tuple-element.63), channel_id=1, source_target_pairs={{0,4},{4,0},{8,12},{12,8},{16,20},{20,16},{24,28},{28,24},{1,5},{5... | collective-permute-start | bytes 786440 | tf_op jit(solution)/shard_map/ppermute | solution.py:20
  30.8 12.4 %collective-permute-start.13 = (bf16[32,32,128]{2,1,0:T(8,128)(2,1)S(1)}, bf16[32,32,128]{2,1,0:T(8,128)(2,1)S(1)}, u32[]{:S(2)}, u32[]{:S(2)}) collective-permute-start(bf16[32,32,128]{2,1,0:T(8,128)(2,1)S(1)} %join.3), channel_id=1, source_target_pairs={{0,2},{1,3},{2,0},{3,1},{4,6},{5,7},{6,4},{7,5},{8,10},{9,11},{10,... | collective-permute-start | bytes 786440 | tf_op jit(solution)/shard_map/ppermute | solution.py:20
  36.7 6.6 %collective-permute-start.7 = (bf16[4,64,128]{2,1,0:T(8,128)(2,1)S(1)}, bf16[4,64,128]{2,1,0:T(8,128)(2,1)S(1)}, u32[]{:S(2)}, u32[]{:S(2)}) collective-permute-start(bf16[4,64,128]{2,1,0:T(8,128)(2,1)S(1)} %get-tuple-element.57), channel_id=1, source_target_pairs={{0,2},{1,3},{2,0},{3,1},{4,6},{5,7},{6,4},{7,5},{8,10},{9,11},{10,... | collective-permute-start | bytes 196616 | tf_op jit(solution)/shard_map/ppermute | solution.py:20
  38.2 5.1 %collective-permute-start.8 = (bf16[4,64,128]{2,1,0:T(8,128)(2,1)S(1)}, bf16[4,64,128]{2,1,0:T(8,128)(2,1)S(1)}, u32[]{:S(2)}, u32[]{:S(2)}) collective-permute-start(bf16[4,64,128]{2,1,0:T(8,128)(2,1)S(1)} %get-tuple-element.58), channel_id=1, source_target_pairs={{0,3},{1,2},{2,1},{3,0},{4,7},{5,6},{6,5},{7,4},{8,11},{9,10},{10,... | collective-permute-start | bytes 196616 | tf_op jit(solution)/shard_map/ppermute | solution.py:20
  40.3 3.0 %collective-permute-start.11 = (bf16[40,32,128]{2,1,0:T(8,128)(2,1)S(1)}, bf16[40,32,128]{2,1,0:T(8,128)(2,1)S(1)}, u32[]{:S(2)}, u32[]{:S(2)}) collective-permute-start(bf16[40,32,128]{2,1,0:T(8,128)(2,1)S(1)} %close_peers.1), channel_id=1, source_target_pairs={{0,1},{1,0},{2,3},{3,2},{4,5},{5,4},{6,7},{7,6},{8,9},{9,8},{10,11... | collective-permute-start | bytes 983048 | tf_op jit(solution)/shard_map/ppermute | solution.py:20

commit v10 on v8

--- a/solution.py
+++ b/solution.py
@@ -20,7 +20,7 @@
     return lax.ppermute(value, axis, pairs)
 
 
-COSTS = {"join": 0, "sums_third": 0, "shift": 0, "close_peers": 0, "close_self": 0}
+COSTS = {"join": 0, "sums_third": 0, "shift": 0, "close_self": 0}
 
 
 def after(value, *others):
@@ -167,16 +167,21 @@
                 trig[1, side * half + c, place] = jnp.sin(angle)
 
 
-def join(owns, got):
+def join(owns, got, extras=()):
+    count, more = len(owns), len(extras)
+    behind = [extras[k].shape[0] if extras else 0 for k in range(count)]
+
     def body(*refs):
         first = 0
-        count = len(owns)
-        for own, out in zip(refs[:count], refs[count + 1 :], strict=True):
+        for k, (own, out) in enumerate(zip(refs[:count], refs[count + 1 + more :], strict=True)):
             size = own.shape[0]
-            out[...] = (own[...] + refs[count][first : first + size].astype(F32)).astype(BF16)
+            out[0:size] = (own[...] + refs[count][first : first + size].astype(F32)).astype(BF16)
+            if extras:
+                out[size:] = refs[count + 1 + k][...]
             first += size
 
-    return kernel_call(body, [struct(a.shape, BF16) for a in owns], [], [*owns, got], "join")
+    shapes = [struct((a.shape[0] + n, *a.shape[1:]), BF16) for a, n in zip(owns, behind, strict=True)]
+    return kernel_call(body, shapes, [], [*owns, got, *extras], "join")
 
 
 def close_body(masks, firsts, per, entries, me, code, table, source, got, *refs):
@@ -436,16 +441,22 @@
     ups = dict(zip(outer + inner, ups, strict=True))
     order = after(me, ups[0])
     behind = {mask: ups.pop(mask).reshape(-1, 2 * low, lanes) for mask in inner}
-    for masks, name in ((inner[:-1], "close_peers"), (inner[-1:], "close_self")):
-        close = kernel_call(
-            functools.partial(close_body, masks, [per * inner.index(m) for m in masks], per, entries),
-            [struct((per + behind[0].shape[0], 2 * low, lanes), BF16)] * len(masks),
-            [order, own_code],
-            [table, source, got_inner, *(behind[mask] for mask in masks)],
-            name,
-        )
-        lows.update(zip(masks, close, strict=True))
-        order = after(me, close[0])
+    own_inner = sums(
+        [((mask,), 0) for mask in inner[:-1]],
+        [own_shape] * (len(inner) - 1),
+        [own_code],
+        order,
+        "sums_fourth",
+    )
+    close = join(own_inner, got_inner, [behind[mask] for mask in inner[:-1]])
+    lows.update(zip(inner[:-1], close, strict=True))
+    (lows[0],) = kernel_call(
+        functools.partial(close_body, [0], [per * inner.index(0)], per, entries),
+        [struct((per + behind[0].shape[0], 2 * low, lanes), BF16)],
+        [after(me, close[0]), own_code],
+        [table, source, got_inner, behind[0]],
+        "close_self",
+    )
     ups = [swap(ups[mask], "angle", mask) for mask in reversed(outer)]
     lows = [swap(lows[mask], "angle", mask) if mask else lows[mask] for mask in range(peers)]
 

time: 45.6 us -> 45.2 us (level)
  waiting for transfers between devices: 2.24 us -> 1.26 us
  starting transfers between devices: 14 us -> 14.6 us
    ppermute x13, waiting for transfers between devices: 2.24 us -> 1.26 us  [swap(): return lax.ppermute(value, axis, pairs)]
    ppermute x13, starting transfers between devices: 14 us -> 14.6 us  [swap(): return lax.ppermute(value, axis, pairs)]
    pallas_call x12 -> x13, Pallas kernels: 27.9 us -> 27.9 us  [kernel_call(): pl.pallas_call(body, out_shape=outs, in_specs=[SM] * len(scalars) + [VM]...]
  transfers between devices with their start and end apart: 13 -> 13, of which waited for: 2 -> 3; matrix products, arithmetic and copies ran while one was open for 0% -> 0% of each run, Pallas kernels for 56% -> 56%
where the time goes in v10:
time: 45.2 us; the launch traced here: 44.9 us
  Pallas kernels  27.9 us (62%)
  starting transfers between devices  14.6 us (32%)
  waiting for transfers between devices  1.26 us (3%)
  other arithmetic  0.73 us (2%)
    pallas_call x13, Pallas kernels, kernel_call(): pl.pallas_call(body, out_shape=outs, in_specs=[SM] * len(scalars) + [VM]...  27.9 us
    ppermute x13, starting transfers between devices, swap(): return lax.ppermute(value, axis, pairs)  14.6 us
    ppermute x13, waiting for transfers between devices, swap(): return lax.ppermute(value, axis, pairs)  1.26 us
  transfers between devices with their start and end apart: 13, of which 3 were waited for; matrix products, arithmetic and copies ran while one was open for 0% of the time, Pallas kernels for 56%

profile of v10, /device:TPU:0, one launch (start us, length us, event | category | flops | bytes accessed | tf_op | source)
XLA Modules:
  0.0 44.9 jit_solution(11383266795141437354)
XLA Ops:
  0.0 0.7 %bitcast_add_fusion = (s32[16,128]{1,0:T(8,128)S(1)}, s32[16,128]{1,0:T(8,128)S(1)}) fusion(s32[128,16]{0,1:T(8,128)} %param.31, s32[128,16]{0,1:T(8,128)} %param.30, s32[]{:T(128)} %axis_index.25), kind=kLoop, calls=%fused_computation.6 | loop fusion | flops 53248 | bytes 32772 | tf_op jit(solution)/shard_map/add | solution.py:331
  0.7 3.0 %collective-permute-start = (s32[16,128]{1,0:T(8,128)S(1)}, s32[16,128]{1,0:T(8,128)S(1)}, u32[]{:S(2)}, u32[]{:S(2)}) collective-permute-start(s32[16,128]{1,0:T(8,128)S(1)} %get-tuple-element.66), channel_id=1, source_target_pairs={{0,4},{4,0},{8,12},{12,8},{16,20},{20,16},{24,28},{28,24},{1,5},{5... | collective-permute-start | bytes 24584 | tf_op jit(solution)/shard_map/ppermute | solution.py:20
  3.7 2.6 %collective-permute-start.6 = (bf16[16,2,32,256]{3,2,1,0:T(8,128)(2,1)}, bf16[16,2,32,256]{3,2,1,0:T(8,128)(2,1)S(1)}, u32[]{:S(2)}, u32[]{:S(2)}) collective-permute-start(bf16[16,2,32,256]{3,2,1,0:T(8,128)(2,1)} %own.1), channel_id=1, source_target_pairs={{0,16},{4,20},{8,24},{12,28},{16,0},{20,4},{24,8},{28,12},{1,17},{... | collective-permute-start | bytes 1572872 | tf_op jit(solution)/shard_map/ppermute | solution.py:20
  6.3 0.0 collective-permute-done.code.refs_0_
  6.3 0.0 copy-start.9
  6.4 5.7 %sums_first.1 = (bf16[32,32,128]{2,1,0:T(8,128)(2,1)S(1)}, bf16[32,32,128]{2,1,0:T(8,128)(2,1)S(1)}, f32[316,32,128]{2,1,0:T(8,128)}, f32[129,32,128]{2,1,0:T(8,128)}) custom-call(s32[1]{0:T(128)} %bitcast.me, s32[16,128]{1,0:T(8,128)S(1)} %collective-permute-done.code.refs_0_, bf16[316,32,128]{2,1,0:T(8,128)(2,1)} %bitcast.58, bf16[128,32,128]{2,1,0:T(8,128)(2,1)} %bitcast.59), custom_call_target="tpu_custom_call" | custom-call | flops 4294967296 | bytes 1 | tf_op jit(solution)/shard_map/sums_first/pallas_call | solution.py:32
  12.0 1.1 %collective-permute-start.1 = (bf16[32,32,128]{2,1,0:T(8,128)(2,1)S(1)}, bf16[32,32,128]{2,1,0:T(8,128)(2,1)S(1)}, u32[]{:S(2)}, u32[]{:S(2)}) collective-permute-start(bf16[32,32,128]{2,1,0:T(8,128)(2,1)S(1)} %get-tuple-element.35), channel_id=1, source_target_pairs={{0,4},{4,0},{8,12},{12,8},{16,20},{20,16},{24,28},{28,24},{1,5},{5... | collective-permute-start | bytes 786440 | tf_op jit(solution)/shard_map/ppermute | solution.py:20
  13.2 0.0 copy-done.6
  13.2 0.0 copy-done.7
  13.2 0.0 copy-done.8
  13.2 0.0 copy-done.9
  13.2 0.0 slice-start.1
  13.2 0.0 copy-start
  13.2 1.0 %early.1 = (f32[192,256]{1,0:T(8,128)S(1)}, f32[192,256]{1,0:T(8,128)S(1)}, f32[192,256]{1,0:T(8,128)S(1)}, f32[192,256]{1,0:T(8,128)S(1)}) custom-call(s32[1]{0:T(128)} %bitcast.me, bf16[256,512]{1,0:T(8,128)(2,1)S(1)} %bitcast.57, bf16[128,256]{1,0:T(8,128)(2,1)S(1)} %copy-done.8, bf16[256,512]{1,0:T(8,128)(2,1)S(1)} %copy-done.7, f32[8,16,128]{2,1,0:T(8,128)S(1)} %copy-done.9), custom_call_target="tpu_custom_call" | custom-call | flops 4294967296 | bytes 1 | tf_op jit(solution)/shard_map/early/pallas_call | solution.py:32
  14.2 1.6 %collective-permute-start.3 = (f32[192,256]{1,0:T(8,128)S(1)}, f32[192,256]{1,0:T(8,128)S(1)}, u32[]{:S(2)}, u32[]{:S(2)}) collective-permute-start(f32[192,256]{1,0:T(8,128)S(1)} %get-tuple-element.47), channel_id=1, source_target_pairs={{0,2},{1,3},{2,0},{3,1},{4,6},{5,7},{6,4},{7,5},{8,10},{9,11},{10,... | collective-permute-start | bytes 589832 | tf_op jit(solution)/shard_map/ppermute | solution.py:20
  15.8 0.0 collective-permute-start.4
  15.8 1.0 %collective-permute-start.5 = (bf16[32,32,128]{2,1,0:T(8,128)(2,1)S(1)}, bf16[32,32,128]{2,1,0:T(8,128)(2,1)S(1)}, u32[]{:S(2)}, u32[]{:S(2)}) collective-permute-start(bf16[32,32,128]{2,1,0:T(8,128)(2,1)S(1)} %get-tuple-element.51), channel_id=1, source_target_pairs={{0,4},{4,0},{8,12},{12,8},{16,20},{20,16},{24,28},{28,24},{1,5},{5... | collective-permute-start | bytes 786440 | tf_op jit(solution)/shard_map/ppermute | solution.py:20
  16.8 0.0 slice-done
  16.8 0.0 slice-done.1
  16.8 0.0 copy-done
  16.8 3.4 %sums_third.1 = (f32[32,32,128]{2,1,0:T(8,128)S(1)}, f32[32,32,128]{2,1,0:T(8,128)S(1)}) custom-call(s32[1]{0:T(128)} %bitcast.me, s32[16,128]{1,0:T(8,128)S(1)} %get-tuple-element.65.refs_0_.code, f32[316,32,128]{2,1,0:T(8,128)S(1)} %bitcast.51, f32[129,32,128]{2,1,0:T(8,128)S(1)} %copy-done), custom_call_target="tpu_custom_call" | custom-call | bytes 1 | tf_op jit(solution)/shard_map/sums_third/pallas_call | solution.py:32
  20.2 0.0 collective-permute-done.1.refs_1_
  20.2 0.0 slice-start.2
  20.3 0.1 join.3
  20.3 0.0 copy-start.1
  20.3 0.0 copy-start.2
  20.3 0.0 copy-start.3
  20.4 0.0 copy-start.4
  20.4 0.0 slice-start.3
  20.4 0.0 slice-start.4
  20.4 0.0 copy-start.5
  20.4 0.0 copy-start.10
  20.4 0.0 copy-start.11
  20.4 0.0 copy-start.12
  20.4 3.5 %sums_second.1 = bf16[64,32,128]{2,1,0:T(8,128)(2,1)S(1)} custom-call(s32[1]{0:T(128)} %bitcast.me, s32[16,128]{1,0:T(8,128)S(1)} %collective-permute-done.code.refs_0_, f32[316,32,128]{2,1,0:T(8,128)S(1)} %bitcast.51, f32[129,32,128]{2,1,0:T(8,128)S(1)} %copy-done), custom_call_target="tpu_custom_call" | custom-call | flops 4294967296 | bytes 1 | tf_op jit(solution)/shard_map/sums_second/pallas_call | solution.py:32
  23.9 0.4 collective-permute-start.2
  24.3 0.0 collective-permute-done.3.refs_2_
  24.4 1.0 %collective-permute-start.9 = (bf16[64,32,128]{2,1,0:T(8,128)(2,1)S(1)}, bf16[64,32,128]{2,1,0:T(8,128)(2,1)S(1)}, u32[]{:S(2)}, u32[]{:S(2)}) collective-permute-start(bf16[64,32,128]{2,1,0:T(8,128)(2,1)S(1)} %sums_second.1), channel_id=1, source_target_pairs={{0,4},{4,0},{8,12},{12,8},{16,20},{20,16},{24,28},{28,24},{1,5},{5... | collective-permute-start | bytes 1572872 | tf_op jit(solution)/shard_map/ppermute | solution.py:20
  25.4 0.0 collective-permute-done.4.refs_3_
  25.4 0.9 %collective-permute-start.11 = (bf16[32,32,128]{2,1,0:T(8,128)(2,1)S(1)}, bf16[32,32,128]{2,1,0:T(8,128)(2,1)S(1)}, u32[]{:S(2)}, u32[]{:S(2)}) collective-permute-start(bf16[32,32,128]{2,1,0:T(8,128)(2,1)S(1)} %join.3), channel_id=1, source_target_pairs={{0,3},{1,2},{2,1},{3,0},{4,7},{5,6},{6,5},{7,4},{8,11},{9,10},{10,... | collective-permute-start | bytes 786440 | tf_op jit(solution)/shard_map/ppermute | solution.py:20
  26.3 0.0 collective-permute-done.2.refs_1_
  26.3 0.0 copy-done.1
  26.3 0.0 copy-done.2
  26.3 0.0 copy-done.3
  26.4 2.2 %shift.1 = (f32[16,2,32,256]{3,2,1,0:T(8,128)S(1)}, f32[2,8,4,16,128]{4,3,2,1,0:T(8,128)S(1)}, bf16[256,256]{1,0:T(8,128)(2,1)S(1)}, bf16[64,128]{1,0:T(8,128)(2,1)S(1)}, bf16[64,64]{1,0:T(8,128)(2,1)S(1)}) custom-call(s32[1]{0:T(128)} %bitcast.me, f32[192,256]{1,0:T(8,128)S(1)} %get-tuple-element.37.refs_0_, f32[192,256]{1,0:T(8,128)S(1)} %collective-permute-done.2.refs_1_, ...), custom_call_target="tpu_custom_call" | custom-call | bytes 1 | tf_op jit(solution)/shard_map/shift/pallas_call | solution.py:32
  28.6 0.0 collective-permute-done.5.refs_1_
  28.6 0.7 %collective-permute-start.12 = (bf16[32,32,128]{2,1,0:T(8,128)(2,1)S(1)}, bf16[32,32,128]{2,1,0:T(8,128)(2,1)S(1)}, u32[]{:S(2)}, u32[]{:S(2)}) collective-permute-start(bf16[32,32,128]{2,1,0:T(8,128)(2,1)S(1)} %join.4), channel_id=1, source_target_pairs={{0,2},{1,3},{2,0},{3,1},{4,6},{5,7},{6,4},{7,5},{8,10},{9,11},{10,... | collective-permute-start | bytes 786440 | tf_op jit(solution)/shard_map/ppermute | solution.py:20
  29.3 0.1 collective-permute-done.6.far
  29.5 0.0 slice-done.2
  29.5 5.1 %upper.1 = (bf16[4,64,128]{2,1,0:T(8,128)(2,1)S(1)}, bf16[4,64,128]{2,1,0:T(8,128)(2,1)S(1)}, bf16[4,64,128]{2,1,0:T(8,128)(2,1)S(1)}, bf16[4,64,128]{2,1,0:T(8,128)(2,1)S(1)}) custom-call(s32[1]{0:T(128)} %bitcast.me, s32[1]{0:T(128)} %bitcast.6.home, s32[16,16]{1,0:T(8,128)S(1)} %copy-done.11, s32[16,16]{1,0:T(8,128)S(1)} %copy-done.12, ...), custom_call_target="tpu_custom_call" | custom-call | flops 4294967296 | bytes 1 | tf_op jit(solution)/shard_map/upper/pallas_call | solution.py:32
  34.7 1.6 %collective-permute-start.7 = (bf16[4,64,128]{2,1,0:T(8,128)(2,1)S(1)}, bf16[4,64,128]{2,1,0:T(8,128)(2,1)S(1)}, u32[]{:S(2)}, u32[]{:S(2)}) collective-permute-start(bf16[4,64,128]{2,1,0:T(8,128)(2,1)S(1)} %get-tuple-element.54), channel_id=1, source_target_pairs={{0,2},{1,3},{2,0},{3,1},{4,6},{5,7},{6,4},{7,5},{8,10},{9,11},{10,... | collective-permute-start | bytes 196616 | tf_op jit(solution)/shard_map/ppermute | solution.py:20
  36.2 0.0 collective-permute-start.8
  36.3 2.1 %sums_fourth.1.refs_0_ = f32[32,32,128]{2,1,0:T(8,128)S(1)} custom-call(s32[1]{0:T(128)} %bitcast.me, s32[16,128]{1,0:T(8,128)S(1)} %get-tuple-element.65.refs_0_.code, f32[316,32,128]{2,1,0:T(8,128)S(1)} %bitcast.51, f32[129,32,128]{2,1,0:T(8,128)S(1)} %copy-done), custom_call_target="tpu_custom_call" | custom-call | flops 4294967296 | bytes 1 | tf_op jit(solution)/shard_map/sums_fourth/pallas_call | solution.py:32
  38.3 0.0 collective-permute-done.9.refs_1_.got
  38.4 0.1 join.5
  38.4 0.6 %collective-permute-start.10 = (bf16[40,32,128]{2,1,0:T(8,128)(2,1)S(1)}, bf16[40,32,128]{2,1,0:T(8,128)(2,1)S(1)}, u32[]{:S(2)}, u32[]{:S(2)}) collective-permute-start(bf16[40,32,128]{2,1,0:T(8,128)(2,1)S(1)} %join.5), channel_id=1, source_target_pairs={{0,1},{1,0},{2,3},{3,2},{4,5},{5,4},{6,7},{7,6},{8,9},{9,8},{10,11... | collective-permute-start | bytes 983048 | tf_op jit(solution)/shard_map/ppermute | solution.py:20
  39.1 0.0 collective-permute-done.11.refs_0_
  39.1 0.6 %collective-permute-done.12.refs_1_ = bf16[32,32,128]{2,1,0:T(8,128)(2,1)S(1)} collective-permute-done((bf16[32,32,128]{2,1,0:T(8,128)(2,1)S(1)}, bf16[32,32,128]{2,1,0:T(8,128)(2,1)S(1)}, u32[]{:S(2)}, u32[]{:S(2)}) %collective-permute-start.12) | collective-permute-done | bytes 262176 | tf_op jit(solution)/shard_map/ppermute | solution.py:20
  39.7 0.1 place.1
  39.8 2.1 %close_self.1.refs_2_ = bf16[40,32,128]{2,1,0:T(8,128)(2,1)S(1)} custom-call(s32[1]{0:T(128)} %bitcast.me, s32[16,128]{1,0:T(8,128)S(1)} %get-tuple-element.65.refs_0_.code, f32[316,32,128]{2,1,0:T(8,128)S(1)} %bitcast.51, f32[129,32,128]{2,1,0:T(8,128)S(1)} %copy-done, bf16[64,32,128]{2,1,0:T(8,128)(2,1)S(1)} %collective-permute-done.9.refs_1_.got, ...), custom_call_target="tpu_custom_call" | custom-call | bytes 1 | tf_op jit(solution)/shard_map/close_self/pallas_call | solution.py:32
  41.9 0.0 collective-permute-done.7.refs_0_
  41.9 0.5 %collective-permute-done.8.refs_1_ = bf16[4,64,128]{2,1,0:T(8,128)(2,1)S(1)} collective-permute-done((bf16[4,64,128]{2,1,0:T(8,128)(2,1)S(1)}, bf16[4,64,128]{2,1,0:T(8,128)(2,1)S(1)}, u32[]{:S(2)}, u32[]{:S(2)}) %collective-permute-start.8) | collective-permute-done | bytes 65568 | tf_op jit(solution)/shard_map/ppermute | solution.py:20
  42.4 0.0 collective-permute-done.10.refs_3_
  42.4 2.6 %expand.1 = f32[4096,128]{1,0:T(8,128)} custom-call(s32[1]{0:T(128)} %bitcast.me, bf16[4,64,128]{2,1,0:T(8,128)(2,1)S(1)} %collective-permute-done.7.refs_0_, bf16[4,64,128]{2,1,0:T(8,128)(2,1)S(1)} %collective-permute-done.8.refs_1_, bf16[40,32,128]{2,1,0:T(8,128)(2,1)S(1)} %close_self.1.refs_2_, bf16[40,32,128]{2,1,0:T(8,128)(2,1)S(1)} %collective-permute-done.10.refs_3_, ...), custom_call_target="tpu_custom_call" | custom-call | flops 4294967296 | bytes 1 | tf_op jit(solution)/shard_map/expand/pallas_call | solution.py:32
  (14 shorter events, 0.1 us)
Async XLA Ops:
  0.7 5.6 %collective-permute-start = (s32[16,128]{1,0:T(8,128)S(1)}, s32[16,128]{1,0:T(8,128)S(1)}, u32[]{:S(2)}, u32[]{:S(2)}) collective-permute-start(s32[16,128]{1,0:T(8,128)S(1)} %get-tuple-element.66), channel_id=1, source_target_pairs={{0,4},{4,0},{8,12},{12,8},{16,20},{20,16},{24,28},{28,24},{1,5},{5... | collective-permute-start | bytes 24584 | tf_op jit(solution)/shard_map/ppermute | solution.py:20
  3.7 25.7 %collective-permute-start.6 = (bf16[16,2,32,256]{3,2,1,0:T(8,128)(2,1)}, bf16[16,2,32,256]{3,2,1,0:T(8,128)(2,1)S(1)}, u32[]{:S(2)}, u32[]{:S(2)}) collective-permute-start(bf16[16,2,32,256]{3,2,1,0:T(8,128)(2,1)} %own.1), channel_id=1, source_target_pairs={{0,16},{4,20},{8,24},{12,28},{16,0},{20,4},{24,8},{28,12},{1,17},{... | collective-permute-start | bytes 1572872 | tf_op jit(solution)/shard_map/ppermute | solution.py:20
  6.3 6.8 %copy-start.6 = (bf16[2,2,64,512]{3,2,1,0:T(8,128)(2,1)S(1)}, bf16[2,2,64,512]{3,2,1,0:T(8,128)(2,1)}, u32[]{:S(2)}) copy-start(bf16[2,2,64,512]{3,2,1,0:T(8,128)(2,1)} %param.17) | copy-start | bytes 786436
  6.3 6.8 %copy-start.7 = (bf16[256,512]{1,0:T(8,128)(2,1)S(1)}, bf16[256,512]{1,0:T(8,128)(2,1)}, u32[]{:S(2)}) copy-start(bf16[256,512]{1,0:T(8,128)(2,1)} %refs_2_.1) | copy-start | bytes 786436
  6.3 6.8 %copy-start.8 = (bf16[128,256]{1,0:T(8,128)(2,1)S(1)}, bf16[128,256]{1,0:T(8,128)(2,1)}, u32[]{:S(2)}) copy-start(bf16[128,256]{1,0:T(8,128)(2,1)} %refs_1_.1) | copy-start | bytes 196612
  6.3 6.8 %copy-start.9 = (f32[8,16,128]{2,1,0:T(8,128)S(1)}, f32[8,16,128]{2,1,0:T(8,128)}, u32[]{:S(2)}) copy-start(f32[8,16,128]{2,1,0:T(8,128)} %refs_3_.1) | copy-start | bytes 196612
  12.0 8.2 %collective-permute-start.1 = (bf16[32,32,128]{2,1,0:T(8,128)(2,1)S(1)}, bf16[32,32,128]{2,1,0:T(8,128)(2,1)S(1)}, u32[]{:S(2)}, u32[]{:S(2)}) collective-permute-start(bf16[32,32,128]{2,1,0:T(8,128)(2,1)S(1)} %get-tuple-element.35), channel_id=1, source_target_pairs={{0,4},{4,0},{8,12},{12,8},{16,20},{20,16},{24,28},{28,24},{1,5},{5... | collective-permute-start | bytes 786440 | tf_op jit(solution)/shard_map/ppermute | solution.py:20
  13.2 3.6 %slice-start = ((s8[5177344]{0:T(1024)(128)(4,1)}), s8[4194304]{0:T(1024)(128)(4,1)S(1)}, s32[]{:S(2)}) async-start(s8[5177344]{0:T(1024)(128)(4,1)} %bitcast.50), calls=%async_computation | async-start | bytes 8388608
  13.2 3.6 %slice-start.1 = ((s8[5177344]{0:T(1024)(128)(4,1)}), s8[983040]{0:T(1024)(128)(4,1)S(1)}, s32[]{:S(2)}) async-start(s8[5177344]{0:T(1024)(128)(4,1)} %bitcast.50), calls=%async_computation.1 | async-start | bytes 1966080
  13.2 3.6 %copy-start = (f32[129,32,128]{2,1,0:T(8,128)S(1)}, f32[129,32,128]{2,1,0:T(8,128)}, u32[]{:S(2)}) copy-start(f32[129,32,128]{2,1,0:T(8,128)} %get-tuple-element.40.refs_2_.source) | copy-start | bytes 6340612
  14.2 10.1 %collective-permute-start.3 = (f32[192,256]{1,0:T(8,128)S(1)}, f32[192,256]{1,0:T(8,128)S(1)}, u32[]{:S(2)}, u32[]{:S(2)}) collective-permute-start(f32[192,256]{1,0:T(8,128)S(1)} %get-tuple-element.47), channel_id=1, source_target_pairs={{0,2},{1,3},{2,0},{3,1},{4,6},{5,7},{6,4},{7,5},{8,10},{9,11},{10,... | collective-permute-start | bytes 589832 | tf_op jit(solution)/shard_map/ppermute | solution.py:20
  15.8 9.6 %collective-permute-start.4 = (f32[192,256]{1,0:T(8,128)S(1)}, f32[192,256]{1,0:T(8,128)S(1)}, u32[]{:S(2)}, u32[]{:S(2)}) collective-permute-start(f32[192,256]{1,0:T(8,128)S(1)} %get-tuple-element.48), channel_id=1, source_target_pairs={{0,3},{1,2},{2,1},{3,0},{4,7},{5,6},{6,5},{7,4},{8,11},{9,10},{10,... | collective-permute-start | bytes 589832 | tf_op jit(solution)/shard_map/ppermute | solution.py:20
  15.8 12.8 %collective-permute-start.5 = (bf16[32,32,128]{2,1,0:T(8,128)(2,1)S(1)}, bf16[32,32,128]{2,1,0:T(8,128)(2,1)S(1)}, u32[]{:S(2)}, u32[]{:S(2)}) collective-permute-start(bf16[32,32,128]{2,1,0:T(8,128)(2,1)S(1)} %get-tuple-element.51), channel_id=1, source_target_pairs={{0,4},{4,0},{8,12},{12,8},{16,20},{20,16},{24,28},{28,24},{1,5},{5... | collective-permute-start | bytes 786440 | tf_op jit(solution)/shard_map/ppermute | solution.py:20
  20.2 9.2 %slice-start.2 = ((s8[10354688]{0:T(1024)(128)(4,1)}), s8[4194304]{0:T(1024)(128)(4,1)S(1)}, s32[]{:S(2)}) async-start(s8[10354688]{0:T(1024)(128)(4,1)} %bitcast.54), calls=%async_computation.2 | async-start | bytes 8388608
  20.3 6.0 %copy-start.1 = (f32[8,32,256]{2,1,0:T(8,128)S(1)}, f32[8,32,256]{2,1,0:T(8,128)}, u32[]{:S(2)}) copy-start(f32[8,32,256]{2,1,0:T(8,128)} %refs_4_.1) | copy-start | bytes 786436
  20.3 6.0 %copy-start.2 = (bf16[2,128,128]{2,1,0:T(8,128)(2,1)S(1)}, bf16[2,128,128]{2,1,0:T(8,128)(2,1)}, u32[]{:S(2)}) copy-start(bf16[2,128,128]{2,1,0:T(8,128)(2,1)} %refs_5_.1) | copy-start | bytes 196612
  20.3 6.0 %copy-start.3 = (bf16[64,128]{1,0:T(8,128)(2,1)S(1)}, bf16[64,128]{1,0:T(8,128)(2,1)}, u32[]{:S(2)}) copy-start(bf16[64,128]{1,0:T(8,128)(2,1)} %refs_6_.1) | copy-start | bytes 49156
  20.4 6.0 %copy-start.4 = (bf16[64,64]{1,0:T(8,128)(2,1)S(1)}, bf16[64,64]{1,0:T(8,128)(2,1)}, u32[]{:S(2)}) copy-start(bf16[64,64]{1,0:T(8,128)(2,1)} %refs_7_.1) | copy-start | bytes 24580
  20.4 9.1 %slice-start.3 = ((s8[10354688]{0:T(1024)(128)(4,1)}), s8[4194304]{0:T(1024)(128)(4,1)S(1)}, s32[]{:S(2)}) async-start(s8[10354688]{0:T(1024)(128)(4,1)} %bitcast.54), calls=%async_computation.3 | async-start | bytes 8388608
  20.4 9.1 %slice-start.4 = ((s8[10354688]{0:T(1024)(128)(4,1)}), s8[1966080]{0:T(1024)(128)(4,1)S(1)}, s32[]{:S(2)}) async-start(s8[10354688]{0:T(1024)(128)(4,1)} %bitcast.54), calls=%async_computation.4 | async-start | bytes 3932160
  20.4 9.1 %copy-start.5 = (bf16[16,2,32,256]{3,2,1,0:T(8,128)(2,1)S(1)}, bf16[16,2,32,256]{3,2,1,0:T(8,128)(2,1)}, u32[]{:S(2)}) copy-start(bf16[16,2,32,256]{3,2,1,0:T(8,128)(2,1)} %own.1) | copy-start | bytes 1572868
  20.4 9.1 %copy-start.10 = (bf16[128,256]{1,0:T(8,128)(2,1)S(1)}, bf16[128,256]{1,0:T(8,128)(2,1)}, u32[]{:S(2)}) copy-start(bf16[128,256]{1,0:T(8,128)(2,1)} %phi.1) | copy-start | bytes 196612
  20.4 9.1 %copy-start.11 = (s32[16,16]{1,0:T(8,128)S(1)}, s32[16,16]{1,0:T(8,128)}, u32[]{:S(2)}) copy-start(s32[16,16]{1,0:T(8,128)} %ids.1) | copy-start | bytes 3076
  20.4 9.1 %copy-start.12 = (s32[16,16]{1,0:T(8,128)S(1)}, s32[16,16]{1,0:T(8,128)}, u32[]{:S(2)}) copy-start(s32[16,16]{1,0:T(8,128)} %offsets.1) | copy-start | bytes 3076
  23.9 2.4 %collective-permute-start.2 = (f32[192,256]{1,0:T(8,128)S(1)}, f32[192,256]{1,0:T(8,128)S(1)}, u32[]{:S(2)}, u32[]{:S(2)}) collective-permute-start(f32[192,256]{1,0:T(8,128)S(1)} %get-tuple-element.46), channel_id=1, source_target_pairs={{0,1},{1,0},{2,3},{3,2},{4,5},{5,4},{6,7},{7,6},{8,9},{9,8},{10,11... | collective-permute-start | bytes 589832 | tf_op jit(solution)/shard_map/ppermute | solution.py:20
  24.4 14.0 %collective-permute-start.9 = (bf16[64,32,128]{2,1,0:T(8,128)(2,1)S(1)}, bf16[64,32,128]{2,1,0:T(8,128)(2,1)S(1)}, u32[]{:S(2)}, u32[]{:S(2)}) collective-permute-start(bf16[64,32,128]{2,1,0:T(8,128)(2,1)S(1)} %sums_second.1), channel_id=1, source_target_pairs={{0,4},{4,0},{8,12},{12,8},{16,20},{20,16},{24,28},{28,24},{1,5},{5... | collective-permute-start | bytes 1572872 | tf_op jit(solution)/shard_map/ppermute | solution.py:20
  25.4 13.7 %collective-permute-start.11 = (bf16[32,32,128]{2,1,0:T(8,128)(2,1)S(1)}, bf16[32,32,128]{2,1,0:T(8,128)(2,1)S(1)}, u32[]{:S(2)}, u32[]{:S(2)}) collective-permute-start(bf16[32,32,128]{2,1,0:T(8,128)(2,1)S(1)} %join.3), channel_id=1, source_target_pairs={{0,3},{1,2},{2,1},{3,0},{4,7},{5,6},{6,5},{7,4},{8,11},{9,10},{10,... | collective-permute-start | bytes 786440 | tf_op jit(solution)/shard_map/ppermute | solution.py:20
  28.6 11.1 %collective-permute-start.12 = (bf16[32,32,128]{2,1,0:T(8,128)(2,1)S(1)}, bf16[32,32,128]{2,1,0:T(8,128)(2,1)S(1)}, u32[]{:S(2)}, u32[]{:S(2)}) collective-permute-start(bf16[32,32,128]{2,1,0:T(8,128)(2,1)S(1)} %join.4), channel_id=1, source_target_pairs={{0,2},{1,3},{2,0},{3,1},{4,6},{5,7},{6,4},{7,5},{8,10},{9,11},{10,... | collective-permute-start | bytes 786440 | tf_op jit(solution)/shard_map/ppermute | solution.py:20
  34.7 7.2 %collective-permute-start.7 = (bf16[4,64,128]{2,1,0:T(8,128)(2,1)S(1)}, bf16[4,64,128]{2,1,0:T(8,128)(2,1)S(1)}, u32[]{:S(2)}, u32[]{:S(2)}) collective-permute-start(bf16[4,64,128]{2,1,0:T(8,128)(2,1)S(1)} %get-tuple-element.54), channel_id=1, source_target_pairs={{0,2},{1,3},{2,0},{3,1},{4,6},{5,7},{6,4},{7,5},{8,10},{9,11},{10,... | collective-permute-start | bytes 196616 | tf_op jit(solution)/shard_map/ppermute | solution.py:20
  36.2 6.1 %collective-permute-start.8 = (bf16[4,64,128]{2,1,0:T(8,128)(2,1)S(1)}, bf16[4,64,128]{2,1,0:T(8,128)(2,1)S(1)}, u32[]{:S(2)}, u32[]{:S(2)}) collective-permute-start(bf16[4,64,128]{2,1,0:T(8,128)(2,1)S(1)} %get-tuple-element.55), channel_id=1, source_target_pairs={{0,3},{1,2},{2,1},{3,0},{4,7},{5,6},{6,5},{7,4},{8,11},{9,10},{10,... | collective-permute-start | bytes 196616 | tf_op jit(solution)/shard_map/ppermute | solution.py:20
  38.4 3.9 %collective-permute-start.10 = (bf16[40,32,128]{2,1,0:T(8,128)(2,1)S(1)}, bf16[40,32,128]{2,1,0:T(8,128)(2,1)S(1)}, u32[]{:S(2)}, u32[]{:S(2)}) collective-permute-start(bf16[40,32,128]{2,1,0:T(8,128)(2,1)S(1)} %join.5), channel_id=1, source_target_pairs={{0,1},{1,0},{2,3},{3,2},{4,5},{5,4},{6,7},{7,6},{8,9},{9,8},{10,11... | collective-permute-start | bytes 983048 | tf_op jit(solution)/shard_map/ppermute | solution.py:20

commit v11 on v10

--- a/solution.py
+++ b/solution.py
@@ -401,7 +401,7 @@
     for mask, own, got in list(zip(outer, own_outer, got_outer, strict=True))[: len(outer) // 2]:
         (lows[mask],) = join([own], got)
     (second,) = sums([(tuple(inner), 0)], [far_shape], [far_code], after(me, lows[outer[0]]), "sums_second")
-    got_inner = swap(second, "box", 1)
+    got_inner = swap(after(second, *parts[len(inner) :]), "box", 1)
     late = after(parts[1], second)
     parts = [parts[0]] + [swap(late if mask == 1 else parts[mask], "angle", mask) for mask in inner[-2::-1]] + [*parts[len(inner) :]]
     orders = switch_theta.shape[0]

time: 45.2 us -> 45.1 us (level)
  transfers between devices with their start and end apart: 13 -> 13, of which waited for: 3 -> 1; matrix products, arithmetic and copies ran while one was open for 0% -> 0% of each run, Pallas kernels for 56% -> 57%
where the time goes in v11:
time: 45.1 us; the launch traced here: 44.8 us
  Pallas kernels  27.9 us (62%)
  starting transfers between devices  14.2 us (31%)
  waiting for transfers between devices  1.5 us (3%)
  other arithmetic  0.73 us (2%)
    pallas_call x13, Pallas kernels, kernel_call(): pl.pallas_call(body, out_shape=outs, in_specs=[SM] * len(scalars) + [VM]...  27.9 us
    ppermute x13, starting transfers between devices, swap(): return lax.ppermute(value, axis, pairs)  14.2 us
    ppermute x13, waiting for transfers between devices, swap(): return lax.ppermute(value, axis, pairs)  1.5 us
  transfers between devices with their start and end apart: 13, of which 1 were waited for; matrix products, arithmetic and copies ran while one was open for 0% of the time, Pallas kernels for 57%

profile of v11, /device:TPU:0, one launch (start us, length us, event | category | flops | bytes accessed | tf_op | source)
XLA Modules:
  0.0 44.8 jit_solution(11943876493953296620)
XLA Ops:
  0.0 0.7 %bitcast_add_fusion = (s32[16,128]{1,0:T(8,128)S(1)}, s32[16,128]{1,0:T(8,128)S(1)}) fusion(s32[128,16]{0,1:T(8,128)} %param.31, s32[128,16]{0,1:T(8,128)} %param.30, s32[]{:T(128)} %axis_index.25), kind=kLoop, calls=%fused_computation.6 | loop fusion | flops 53248 | bytes 32772 | tf_op jit(solution)/shard_map/add | solution.py:331
  0.7 3.0 %collective-permute-start = (s32[16,128]{1,0:T(8,128)S(1)}, s32[16,128]{1,0:T(8,128)S(1)}, u32[]{:S(2)}, u32[]{:S(2)}) collective-permute-start(s32[16,128]{1,0:T(8,128)S(1)} %get-tuple-element.68), channel_id=1, source_target_pairs={{0,4},{4,0},{8,12},{12,8},{16,20},{20,16},{24,28},{28,24},{1,5},{5... | collective-permute-start | bytes 24584 | tf_op jit(solution)/shard_map/ppermute | solution.py:20
  3.7 2.6 %collective-permute-start.6 = (bf16[16,2,32,256]{3,2,1,0:T(8,128)(2,1)}, bf16[16,2,32,256]{3,2,1,0:T(8,128)(2,1)S(1)}, u32[]{:S(2)}, u32[]{:S(2)}) collective-permute-start(bf16[16,2,32,256]{3,2,1,0:T(8,128)(2,1)} %own.1), channel_id=1, source_target_pairs={{0,16},{4,20},{8,24},{12,28},{16,0},{20,4},{24,8},{28,12},{1,17},{... | collective-permute-start | bytes 1572872 | tf_op jit(solution)/shard_map/ppermute | solution.py:20
  6.3 0.0 collective-permute-done.code.refs_0_
  6.3 0.0 copy-start.9
  6.4 5.7 %sums_first.1 = (bf16[32,32,128]{2,1,0:T(8,128)(2,1)S(1)}, bf16[32,32,128]{2,1,0:T(8,128)(2,1)S(1)}, f32[316,32,128]{2,1,0:T(8,128)}, f32[129,32,128]{2,1,0:T(8,128)}) custom-call(s32[1]{0:T(128)} %bitcast.me, s32[16,128]{1,0:T(8,128)S(1)} %collective-permute-done.code.refs_0_, bf16[316,32,128]{2,1,0:T(8,128)(2,1)} %bitcast.58, bf16[128,32,128]{2,1,0:T(8,128)(2,1)} %bitcast.59), custom_call_target="tpu_custom_call" | custom-call | flops 4294967296 | bytes 1 | tf_op jit(solution)/shard_map/sums_first/pallas_call | solution.py:32
  12.0 1.1 %collective-permute-start.1 = (bf16[32,32,128]{2,1,0:T(8,128)(2,1)S(1)}, bf16[32,32,128]{2,1,0:T(8,128)(2,1)S(1)}, u32[]{:S(2)}, u32[]{:S(2)}) collective-permute-start(bf16[32,32,128]{2,1,0:T(8,128)(2,1)S(1)} %get-tuple-element.36), channel_id=1, source_target_pairs={{0,4},{4,0},{8,12},{12,8},{16,20},{20,16},{24,28},{28,24},{1,5},{5... | collective-permute-start | bytes 786440 | tf_op jit(solution)/shard_map/ppermute | solution.py:20
  13.2 0.0 copy-done.6
  13.2 0.0 copy-done.7
  13.2 0.0 copy-done.8
  13.2 0.0 copy-done.9
  13.2 0.0 slice-start.1
  13.2 0.0 copy-start
  13.2 1.0 %early.1 = (f32[192,256]{1,0:T(8,128)S(1)}, f32[192,256]{1,0:T(8,128)S(1)}, f32[192,256]{1,0:T(8,128)S(1)}, f32[192,256]{1,0:T(8,128)S(1)}) custom-call(s32[1]{0:T(128)} %bitcast.me, bf16[256,512]{1,0:T(8,128)(2,1)S(1)} %bitcast.57, bf16[128,256]{1,0:T(8,128)(2,1)S(1)} %copy-done.8, bf16[256,512]{1,0:T(8,128)(2,1)S(1)} %copy-done.7, f32[8,16,128]{2,1,0:T(8,128)S(1)} %copy-done.9), custom_call_target="tpu_custom_call" | custom-call | flops 4294967296 | bytes 1 | tf_op jit(solution)/shard_map/early/pallas_call | solution.py:32
  14.2 1.6 %collective-permute-start.3 = (f32[192,256]{1,0:T(8,128)S(1)}, f32[192,256]{1,0:T(8,128)S(1)}, u32[]{:S(2)}, u32[]{:S(2)}) collective-permute-start(f32[192,256]{1,0:T(8,128)S(1)} %get-tuple-element.48), channel_id=1, source_target_pairs={{0,2},{1,3},{2,0},{3,1},{4,6},{5,7},{6,4},{7,5},{8,10},{9,11},{10,... | collective-permute-start | bytes 589832 | tf_op jit(solution)/shard_map/ppermute | solution.py:20
  15.8 0.0 collective-permute-start.4
  15.8 1.0 %collective-permute-start.5 = (bf16[32,32,128]{2,1,0:T(8,128)(2,1)S(1)}, bf16[32,32,128]{2,1,0:T(8,128)(2,1)S(1)}, u32[]{:S(2)}, u32[]{:S(2)}) collective-permute-start(bf16[32,32,128]{2,1,0:T(8,128)(2,1)S(1)} %get-tuple-element.52), channel_id=1, source_target_pairs={{0,4},{4,0},{8,12},{12,8},{16,20},{20,16},{24,28},{28,24},{1,5},{5... | collective-permute-start | bytes 786440 | tf_op jit(solution)/shard_map/ppermute | solution.py:20
  16.8 0.0 slice-done
  16.8 0.0 slice-done.1
  16.8 0.0 copy-done
  16.8 3.4 %sums_third.1 = (f32[32,32,128]{2,1,0:T(8,128)S(1)}, f32[32,32,128]{2,1,0:T(8,128)S(1)}) custom-call(s32[1]{0:T(128)} %bitcast.me, s32[16,128]{1,0:T(8,128)S(1)} %get-tuple-element.67.refs_0_.code, f32[316,32,128]{2,1,0:T(8,128)S(1)} %bitcast.51, f32[129,32,128]{2,1,0:T(8,128)S(1)} %copy-done), custom_call_target="tpu_custom_call" | custom-call | bytes 1 | tf_op jit(solution)/shard_map/sums_third/pallas_call | solution.py:32
  20.2 0.0 collective-permute-done.1.refs_1_
  20.2 0.0 slice-start.2
  20.3 0.1 join.3
  20.3 0.0 copy-start.1
  20.3 0.0 copy-start.2
  20.3 0.0 copy-start.3
  20.4 0.0 copy-start.4
  20.4 0.0 slice-start.3
  20.4 0.0 slice-start.4
  20.4 0.0 copy-start.5
  20.4 0.0 copy-start.10
  20.4 0.0 copy-start.11
  20.4 0.0 copy-start.12
  20.4 3.5 %sums_second.1 = bf16[64,32,128]{2,1,0:T(8,128)(2,1)S(1)} custom-call(s32[1]{0:T(128)} %bitcast.me, s32[16,128]{1,0:T(8,128)S(1)} %collective-permute-done.code.refs_0_, f32[316,32,128]{2,1,0:T(8,128)S(1)} %bitcast.51, f32[129,32,128]{2,1,0:T(8,128)S(1)} %copy-done), custom_call_target="tpu_custom_call" | custom-call | flops 4294967296 | bytes 1 | tf_op jit(solution)/shard_map/sums_second/pallas_call | solution.py:32
  23.9 0.4 collective-permute-start.2
  24.3 0.0 collective-permute-done.3.refs_2_
  24.4 1.2 %collective-permute-start.11 = (bf16[32,32,128]{2,1,0:T(8,128)(2,1)S(1)}, bf16[32,32,128]{2,1,0:T(8,128)(2,1)S(1)}, u32[]{:S(2)}, u32[]{:S(2)}) collective-permute-start(bf16[32,32,128]{2,1,0:T(8,128)(2,1)S(1)} %join.3), channel_id=1, source_target_pairs={{0,3},{1,2},{2,1},{3,0},{4,7},{5,6},{6,5},{7,4},{8,11},{9,10},{10,... | collective-permute-start | bytes 786440 | tf_op jit(solution)/shard_map/ppermute | solution.py:20
  25.6 0.0 collective-permute-done.4.refs_3_
  25.6 1.0 %collective-permute-start.9 = (bf16[64,32,128]{2,1,0:T(8,128)(2,1)S(1)}, bf16[64,32,128]{2,1,0:T(8,128)(2,1)S(1)}, u32[]{:S(2)}, u32[]{:S(2)}) collective-permute-start(bf16[64,32,128]{2,1,0:T(8,128)(2,1)S(1)} %sums_second.1), channel_id=1, source_target_pairs={{0,4},{4,0},{8,12},{12,8},{16,20},{20,16},{24,28},{28,24},{1,5},{5... | collective-permute-start | bytes 1572872 | tf_op jit(solution)/shard_map/ppermute | solution.py:20
  26.6 0.0 collective-permute-done.2.refs_1_
  26.6 0.0 copy-done.1
  26.6 0.0 copy-done.2
  26.6 0.0 copy-done.3
  26.6 0.0 copy-done.4
  26.6 2.2 %shift.1 = (f32[16,2,32,256]{3,2,1,0:T(8,128)S(1)}, f32[2,8,4,16,128]{4,3,2,1,0:T(8,128)S(1)}, bf16[256,256]{1,0:T(8,128)(2,1)S(1)}, bf16[64,128]{1,0:T(8,128)(2,1)S(1)}, bf16[64,64]{1,0:T(8,128)(2,1)S(1)}) custom-call(s32[1]{0:T(128)} %bitcast.me, f32[192,256]{1,0:T(8,128)S(1)} %get-tuple-element.38.refs_0_, f32[192,256]{1,0:T(8,128)S(1)} %collective-permute-done.2.refs_1_, ...), custom_call_target="tpu_custom_call" | custom-call | bytes 1 | tf_op jit(solution)/shard_map/shift/pallas_call | solution.py:32
  28.9 0.0 collective-permute-done.5.refs_1_
  28.9 0.7 %collective-permute-start.12 = (bf16[32,32,128]{2,1,0:T(8,128)(2,1)S(1)}, bf16[32,32,128]{2,1,0:T(8,128)(2,1)S(1)}, u32[]{:S(2)}, u32[]{:S(2)}) collective-permute-start(bf16[32,32,128]{2,1,0:T(8,128)(2,1)S(1)} %join.4), channel_id=1, source_target_pairs={{0,2},{1,3},{2,0},{3,1},{4,6},{5,7},{6,4},{7,5},{8,10},{9,11},{10,... | collective-permute-start | bytes 786440 | tf_op jit(solution)/shard_map/ppermute | solution.py:20
  29.6 0.0 collective-permute-done.6.far
  29.7 5.1 %upper.1 = (bf16[4,64,128]{2,1,0:T(8,128)(2,1)S(1)}, bf16[4,64,128]{2,1,0:T(8,128)(2,1)S(1)}, bf16[4,64,128]{2,1,0:T(8,128)(2,1)S(1)}, bf16[4,64,128]{2,1,0:T(8,128)(2,1)S(1)}) custom-call(s32[1]{0:T(128)} %bitcast.me, s32[1]{0:T(128)} %bitcast.6.home, s32[16,16]{1,0:T(8,128)S(1)} %copy-done.11, s32[16,16]{1,0:T(8,128)S(1)} %copy-done.12, ...), custom_call_target="tpu_custom_call" | custom-call | flops 4294967296 | bytes 1 | tf_op jit(solution)/shard_map/upper/pallas_call | solution.py:32
  34.8 1.5 %collective-permute-start.7 = (bf16[4,64,128]{2,1,0:T(8,128)(2,1)S(1)}, bf16[4,64,128]{2,1,0:T(8,128)(2,1)S(1)}, u32[]{:S(2)}, u32[]{:S(2)}) collective-permute-start(bf16[4,64,128]{2,1,0:T(8,128)(2,1)S(1)} %get-tuple-element.55), channel_id=1, source_target_pairs={{0,2},{1,3},{2,0},{3,1},{4,6},{5,7},{6,4},{7,5},{8,10},{9,11},{10,... | collective-permute-start | bytes 196616 | tf_op jit(solution)/shard_map/ppermute | solution.py:20
  36.3 0.0 collective-permute-start.8
  36.3 2.1 %sums_fourth.1.refs_0_ = f32[32,32,128]{2,1,0:T(8,128)S(1)} custom-call(s32[1]{0:T(128)} %bitcast.me, s32[16,128]{1,0:T(8,128)S(1)} %get-tuple-element.67.refs_0_.code, f32[316,32,128]{2,1,0:T(8,128)S(1)} %bitcast.51, f32[129,32,128]{2,1,0:T(8,128)S(1)} %copy-done), custom_call_target="tpu_custom_call" | custom-call | flops 4294967296 | bytes 1 | tf_op jit(solution)/shard_map/sums_fourth/pallas_call | solution.py:32
  38.4 1.5 %collective-permute-done.9.refs_1_.got = bf16[64,32,128]{2,1,0:T(8,128)(2,1)S(1)} collective-permute-done((bf16[64,32,128]{2,1,0:T(8,128)(2,1)S(1)}, bf16[64,32,128]{2,1,0:T(8,128)(2,1)S(1)}, u32[]{:S(2)}, u32[]{:S(2)}) %collective-permute-start.9) | collective-permute-done | bytes 524320 | tf_op jit(solution)/shard_map/ppermute | solution.py:20
  39.8 0.1 join.5
  39.9 0.1 collective-permute-start.10
  40.0 0.0 collective-permute-done.11.refs_0_
  40.0 0.0 collective-permute-done.12.refs_1_
  40.0 0.1 place.1
  40.1 2.1 %close_self.1.refs_2_ = bf16[40,32,128]{2,1,0:T(8,128)(2,1)S(1)} custom-call(s32[1]{0:T(128)} %bitcast.me, s32[16,128]{1,0:T(8,128)S(1)} %get-tuple-element.67.refs_0_.code, f32[316,32,128]{2,1,0:T(8,128)S(1)} %bitcast.51, f32[129,32,128]{2,1,0:T(8,128)S(1)} %copy-done, bf16[64,32,128]{2,1,0:T(8,128)(2,1)S(1)} %collective-permute-done.9.refs_1_.got, ...), custom_call_target="tpu_custom_call" | custom-call | bytes 1 | tf_op jit(solution)/shard_map/close_self/pallas_call | solution.py:32
  42.2 0.0 collective-permute-done.7.refs_0_
  42.2 0.0 collective-permute-done.8.refs_1_
  42.2 0.0 collective-permute-done.10.refs_3_
  42.2 2.6 %expand.1 = f32[4096,128]{1,0:T(8,128)} custom-call(s32[1]{0:T(128)} %bitcast.me, bf16[4,64,128]{2,1,0:T(8,128)(2,1)S(1)} %collective-permute-done.7.refs_0_, bf16[4,64,128]{2,1,0:T(8,128)(2,1)S(1)} %collective-permute-done.8.refs_1_, bf16[40,32,128]{2,1,0:T(8,128)(2,1)S(1)} %close_self.1.refs_2_, bf16[40,32,128]{2,1,0:T(8,128)(2,1)S(1)} %collective-permute-done.10.refs_3_, ...), custom_call_target="tpu_custom_call" | custom-call | flops 4294967296 | bytes 1 | tf_op jit(solution)/shard_map/expand/pallas_call | solution.py:32
  (14 shorter events, 0.1 us)
Async XLA Ops:
  0.7 5.6 %collective-permute-start = (s32[16,128]{1,0:T(8,128)S(1)}, s32[16,128]{1,0:T(8,128)S(1)}, u32[]{:S(2)}, u32[]{:S(2)}) collective-permute-start(s32[16,128]{1,0:T(8,128)S(1)} %get-tuple-element.68), channel_id=1, source_target_pairs={{0,4},{4,0},{8,12},{12,8},{16,20},{20,16},{24,28},{28,24},{1,5},{5... | collective-permute-start | bytes 24584 | tf_op jit(solution)/shard_map/ppermute | solution.py:20
  3.7 25.9 %collective-permute-start.6 = (bf16[16,2,32,256]{3,2,1,0:T(8,128)(2,1)}, bf16[16,2,32,256]{3,2,1,0:T(8,128)(2,1)S(1)}, u32[]{:S(2)}, u32[]{:S(2)}) collective-permute-start(bf16[16,2,32,256]{3,2,1,0:T(8,128)(2,1)} %own.1), channel_id=1, source_target_pairs={{0,16},{4,20},{8,24},{12,28},{16,0},{20,4},{24,8},{28,12},{1,17},{... | collective-permute-start | bytes 1572872 | tf_op jit(solution)/shard_map/ppermute | solution.py:20
  6.3 6.8 %copy-start.6 = (bf16[2,2,64,512]{3,2,1,0:T(8,128)(2,1)S(1)}, bf16[2,2,64,512]{3,2,1,0:T(8,128)(2,1)}, u32[]{:S(2)}) copy-start(bf16[2,2,64,512]{3,2,1,0:T(8,128)(2,1)} %param.17) | copy-start | bytes 786436
  6.3 6.8 %copy-start.7 = (bf16[256,512]{1,0:T(8,128)(2,1)S(1)}, bf16[256,512]{1,0:T(8,128)(2,1)}, u32[]{:S(2)}) copy-start(bf16[256,512]{1,0:T(8,128)(2,1)} %refs_2_.1) | copy-start | bytes 786436
  6.3 6.8 %copy-start.8 = (bf16[128,256]{1,0:T(8,128)(2,1)S(1)}, bf16[128,256]{1,0:T(8,128)(2,1)}, u32[]{:S(2)}) copy-start(bf16[128,256]{1,0:T(8,128)(2,1)} %refs_1_.1) | copy-start | bytes 196612
  6.3 6.8 %copy-start.9 = (f32[8,16,128]{2,1,0:T(8,128)S(1)}, f32[8,16,128]{2,1,0:T(8,128)}, u32[]{:S(2)}) copy-start(f32[8,16,128]{2,1,0:T(8,128)} %refs_3_.1) | copy-start | bytes 196612
  12.0 8.2 %collective-permute-start.1 = (bf16[32,32,128]{2,1,0:T(8,128)(2,1)S(1)}, bf16[32,32,128]{2,1,0:T(8,128)(2,1)S(1)}, u32[]{:S(2)}, u32[]{:S(2)}) collective-permute-start(bf16[32,32,128]{2,1,0:T(8,128)(2,1)S(1)} %get-tuple-element.36), channel_id=1, source_target_pairs={{0,4},{4,0},{8,12},{12,8},{16,20},{20,16},{24,28},{28,24},{1,5},{5... | collective-permute-start | bytes 786440 | tf_op jit(solution)/shard_map/ppermute | solution.py:20
  13.2 3.6 %slice-start = ((s8[5177344]{0:T(1024)(128)(4,1)}), s8[4194304]{0:T(1024)(128)(4,1)S(1)}, s32[]{:S(2)}) async-start(s8[5177344]{0:T(1024)(128)(4,1)} %bitcast.50), calls=%async_computation | async-start | bytes 8388608
  13.2 3.6 %slice-start.1 = ((s8[5177344]{0:T(1024)(128)(4,1)}), s8[983040]{0:T(1024)(128)(4,1)S(1)}, s32[]{:S(2)}) async-start(s8[5177344]{0:T(1024)(128)(4,1)} %bitcast.50), calls=%async_computation.1 | async-start | bytes 1966080
  13.2 3.6 %copy-start = (f32[129,32,128]{2,1,0:T(8,128)S(1)}, f32[129,32,128]{2,1,0:T(8,128)}, u32[]{:S(2)}) copy-start(f32[129,32,128]{2,1,0:T(8,128)} %get-tuple-element.41.refs_2_.source) | copy-start | bytes 6340612
  14.2 10.1 %collective-permute-start.3 = (f32[192,256]{1,0:T(8,128)S(1)}, f32[192,256]{1,0:T(8,128)S(1)}, u32[]{:S(2)}, u32[]{:S(2)}) collective-permute-start(f32[192,256]{1,0:T(8,128)S(1)} %get-tuple-element.48), channel_id=1, source_target_pairs={{0,2},{1,3},{2,0},{3,1},{4,6},{5,7},{6,4},{7,5},{8,10},{9,11},{10,... | collective-permute-start | bytes 589832 | tf_op jit(solution)/shard_map/ppermute | solution.py:20
  15.8 9.8 %collective-permute-start.4 = (f32[192,256]{1,0:T(8,128)S(1)}, f32[192,256]{1,0:T(8,128)S(1)}, u32[]{:S(2)}, u32[]{:S(2)}) collective-permute-start(f32[192,256]{1,0:T(8,128)S(1)} %get-tuple-element.49), channel_id=1, source_target_pairs={{0,3},{1,2},{2,1},{3,0},{4,7},{5,6},{6,5},{7,4},{8,11},{9,10},{10,... | collective-permute-start | bytes 589832 | tf_op jit(solution)/shard_map/ppermute | solution.py:20
  15.8 13.1 %collective-permute-start.5 = (bf16[32,32,128]{2,1,0:T(8,128)(2,1)S(1)}, bf16[32,32,128]{2,1,0:T(8,128)(2,1)S(1)}, u32[]{:S(2)}, u32[]{:S(2)}) collective-permute-start(bf16[32,32,128]{2,1,0:T(8,128)(2,1)S(1)} %get-tuple-element.52), channel_id=1, source_target_pairs={{0,4},{4,0},{8,12},{12,8},{16,20},{20,16},{24,28},{28,24},{1,5},{5... | collective-permute-start | bytes 786440 | tf_op jit(solution)/shard_map/ppermute | solution.py:20
  20.2 9.4 %slice-start.2 = ((s8[10354688]{0:T(1024)(128)(4,1)}), s8[4194304]{0:T(1024)(128)(4,1)S(1)}, s32[]{:S(2)}) async-start(s8[10354688]{0:T(1024)(128)(4,1)} %bitcast.54), calls=%async_computation.2 | async-start | bytes 8388608
  20.3 6.3 %copy-start.1 = (f32[8,32,256]{2,1,0:T(8,128)S(1)}, f32[8,32,256]{2,1,0:T(8,128)}, u32[]{:S(2)}) copy-start(f32[8,32,256]{2,1,0:T(8,128)} %refs_4_.1) | copy-start | bytes 786436
  20.3 6.3 %copy-start.2 = (bf16[2,128,128]{2,1,0:T(8,128)(2,1)S(1)}, bf16[2,128,128]{2,1,0:T(8,128)(2,1)}, u32[]{:S(2)}) copy-start(bf16[2,128,128]{2,1,0:T(8,128)(2,1)} %refs_5_.1) | copy-start | bytes 196612
  20.3 6.3 %copy-start.3 = (bf16[64,128]{1,0:T(8,128)(2,1)S(1)}, bf16[64,128]{1,0:T(8,128)(2,1)}, u32[]{:S(2)}) copy-start(bf16[64,128]{1,0:T(8,128)(2,1)} %refs_6_.1) | copy-start | bytes 49156
  20.4 6.3 %copy-start.4 = (bf16[64,64]{1,0:T(8,128)(2,1)S(1)}, bf16[64,64]{1,0:T(8,128)(2,1)}, u32[]{:S(2)}) copy-start(bf16[64,64]{1,0:T(8,128)(2,1)} %refs_7_.1) | copy-start | bytes 24580
  20.4 9.2 %slice-start.3 = ((s8[10354688]{0:T(1024)(128)(4,1)}), s8[4194304]{0:T(1024)(128)(4,1)S(1)}, s32[]{:S(2)}) async-start(s8[10354688]{0:T(1024)(128)(4,1)} %bitcast.54), calls=%async_computation.3 | async-start | bytes 8388608
  20.4 9.2 %slice-start.4 = ((s8[10354688]{0:T(1024)(128)(4,1)}), s8[1966080]{0:T(1024)(128)(4,1)S(1)}, s32[]{:S(2)}) async-start(s8[10354688]{0:T(1024)(128)(4,1)} %bitcast.54), calls=%async_computation.4 | async-start | bytes 3932160
  20.4 9.2 %copy-start.5 = (bf16[16,2,32,256]{3,2,1,0:T(8,128)(2,1)S(1)}, bf16[16,2,32,256]{3,2,1,0:T(8,128)(2,1)}, u32[]{:S(2)}) copy-start(bf16[16,2,32,256]{3,2,1,0:T(8,128)(2,1)} %own.1) | copy-start | bytes 1572868
  20.4 9.2 %copy-start.10 = (bf16[128,256]{1,0:T(8,128)(2,1)S(1)}, bf16[128,256]{1,0:T(8,128)(2,1)}, u32[]{:S(2)}) copy-start(bf16[128,256]{1,0:T(8,128)(2,1)} %phi.1) | copy-start | bytes 196612
  20.4 9.2 %copy-start.11 = (s32[16,16]{1,0:T(8,128)S(1)}, s32[16,16]{1,0:T(8,128)}, u32[]{:S(2)}) copy-start(s32[16,16]{1,0:T(8,128)} %ids.1) | copy-start | bytes 3076
  20.4 9.2 %copy-start.12 = (s32[16,16]{1,0:T(8,128)S(1)}, s32[16,16]{1,0:T(8,128)}, u32[]{:S(2)}) copy-start(s32[16,16]{1,0:T(8,128)} %offsets.1) | copy-start | bytes 3076
  23.9 2.7 %collective-permute-start.2 = (f32[192,256]{1,0:T(8,128)S(1)}, f32[192,256]{1,0:T(8,128)S(1)}, u32[]{:S(2)}, u32[]{:S(2)}) collective-permute-start(f32[192,256]{1,0:T(8,128)S(1)} %get-tuple-element.47), channel_id=1, source_target_pairs={{0,1},{1,0},{2,3},{3,2},{4,5},{5,4},{6,7},{7,6},{8,9},{9,8},{10,11... | collective-permute-start | bytes 589832 | tf_op jit(solution)/shard_map/ppermute | solution.py:20
  24.4 15.6 %collective-permute-start.11 = (bf16[32,32,128]{2,1,0:T(8,128)(2,1)S(1)}, bf16[32,32,128]{2,1,0:T(8,128)(2,1)S(1)}, u32[]{:S(2)}, u32[]{:S(2)}) collective-permute-start(bf16[32,32,128]{2,1,0:T(8,128)(2,1)S(1)} %join.3), channel_id=1, source_target_pairs={{0,3},{1,2},{2,1},{3,0},{4,7},{5,6},{6,5},{7,4},{8,11},{9,10},{10,... | collective-permute-start | bytes 786440 | tf_op jit(solution)/shard_map/ppermute | solution.py:20
  25.6 14.3 %collective-permute-start.9 = (bf16[64,32,128]{2,1,0:T(8,128)(2,1)S(1)}, bf16[64,32,128]{2,1,0:T(8,128)(2,1)S(1)}, u32[]{:S(2)}, u32[]{:S(2)}) collective-permute-start(bf16[64,32,128]{2,1,0:T(8,128)(2,1)S(1)} %sums_second.1), channel_id=1, source_target_pairs={{0,4},{4,0},{8,12},{12,8},{16,20},{20,16},{24,28},{28,24},{1,5},{5... | collective-permute-start | bytes 1572872 | tf_op jit(solution)/shard_map/ppermute | solution.py:20
  28.9 11.1 %collective-permute-start.12 = (bf16[32,32,128]{2,1,0:T(8,128)(2,1)S(1)}, bf16[32,32,128]{2,1,0:T(8,128)(2,1)S(1)}, u32[]{:S(2)}, u32[]{:S(2)}) collective-permute-start(bf16[32,32,128]{2,1,0:T(8,128)(2,1)S(1)} %join.4), channel_id=1, source_target_pairs={{0,2},{1,3},{2,0},{3,1},{4,6},{5,7},{6,4},{7,5},{8,10},{9,11},{10,... | collective-permute-start | bytes 786440 | tf_op jit(solution)/shard_map/ppermute | solution.py:20
  34.8 7.4 %collective-permute-start.7 = (bf16[4,64,128]{2,1,0:T(8,128)(2,1)S(1)}, bf16[4,64,128]{2,1,0:T(8,128)(2,1)S(1)}, u32[]{:S(2)}, u32[]{:S(2)}) collective-permute-start(bf16[4,64,128]{2,1,0:T(8,128)(2,1)S(1)} %get-tuple-element.55), channel_id=1, source_target_pairs={{0,2},{1,3},{2,0},{3,1},{4,6},{5,7},{6,4},{7,5},{8,10},{9,11},{10,... | collective-permute-start | bytes 196616 | tf_op jit(solution)/shard_map/ppermute | solution.py:20
  36.3 5.9 %collective-permute-start.8 = (bf16[4,64,128]{2,1,0:T(8,128)(2,1)S(1)}, bf16[4,64,128]{2,1,0:T(8,128)(2,1)S(1)}, u32[]{:S(2)}, u32[]{:S(2)}) collective-permute-start(bf16[4,64,128]{2,1,0:T(8,128)(2,1)S(1)} %get-tuple-element.56), channel_id=1, source_target_pairs={{0,3},{1,2},{2,1},{3,0},{4,7},{5,6},{6,5},{7,4},{8,11},{9,10},{10,... | collective-permute-start | bytes 196616 | tf_op jit(solution)/shard_map/ppermute | solution.py:20
  39.9 2.3 %collective-permute-start.10 = (bf16[40,32,128]{2,1,0:T(8,128)(2,1)S(1)}, bf16[40,32,128]{2,1,0:T(8,128)(2,1)S(1)}, u32[]{:S(2)}, u32[]{:S(2)}) collective-permute-start(bf16[40,32,128]{2,1,0:T(8,128)(2,1)S(1)} %join.5), channel_id=1, source_target_pairs={{0,1},{1,0},{2,3},{3,2},{4,5},{5,4},{6,7},{7,6},{8,9},{9,8},{10,11... | collective-permute-start | bytes 983048 | tf_op jit(solution)/shard_map/ppermute | solution.py:20

commit v12 on v11

--- a/solution.py
+++ b/solution.py
@@ -20,7 +20,7 @@
     return lax.ppermute(value, axis, pairs)
 
 
-COSTS = {"join": 0, "sums_third": 0, "shift": 0, "close_self": 0}
+COSTS = {"join": 0, "sums_third": 0, "shift": 0}
 
 
 def after(value, *others):
@@ -182,24 +182,6 @@
 
     shapes = [struct((a.shape[0] + n, *a.shape[1:]), BF16) for a, n in zip(owns, behind, strict=True)]
     return kernel_call(body, shapes, [], [*owns, got, *extras], "join")
-
-
-def close_body(masks, firsts, per, entries, me, code, table, source, got, *refs):
-    count = len(masks)
-    rows = table.shape[1] // 2
-    for mask, begin, piece, out in zip(masks, firsts, refs[:count], refs[count:], strict=True):
-        first = jnp.bitwise_xor(me[0], mask) * per
-
-        def one(i, carry, first=first, begin=begin, out=out):
-            real, imag = box_sum(first + i, entries, code, table, source)
-            real = real + got[begin + i, 0:rows].astype(F32)
-            imag = imag + got[begin + i, rows:].astype(F32)
-            out[i, 0:rows] = real.astype(BF16)
-            out[i, rows:] = imag.astype(BF16)
-            return carry
-
-        lax.fori_loop(0, per, one, 0, unroll=2)
-        out[per:] = piece[...]
 
 
 def upper_body(masks, peers, entries, me, home, ids, offsets, own, far, table, shifted, phi, *refs):
@@ -442,21 +424,14 @@
     order = after(me, ups[0])
     behind = {mask: ups.pop(mask).reshape(-1, 2 * low, lanes) for mask in inner}
     own_inner = sums(
-        [((mask,), 0) for mask in inner[:-1]],
-        [own_shape] * (len(inner) - 1),
+        [((mask,), 0) for mask in inner],
+        [own_shape] * len(inner),
         [own_code],
         order,
         "sums_fourth",
     )
-    close = join(own_inner, got_inner, [behind[mask] for mask in inner[:-1]])
-    lows.update(zip(inner[:-1], close, strict=True))
-    (lows[0],) = kernel_call(
-        functools.partial(close_body, [0], [per * inner.index(0)], per, entries),
-        [struct((per + behind[0].shape[0], 2 * low, lanes), BF16)],
-        [after(me, close[0]), own_code],
-        [table, source, got_inner, behind[0]],
-        "close_self",
-    )
+    close = join(own_inner, got_inner, [behind[mask] for mask in inner])
+    lows.update(zip(inner, close, strict=True))
     ups = [swap(ups[mask], "angle", mask) for mask in reversed(outer)]
     lows = [swap(lows[mask], "angle", mask) if mask else lows[mask] for mask in range(peers)]
 

time: 45.1 us -> 44.7 us (level)
  Pallas kernels: 27.9 us -> 27.2 us
  starting transfers between devices: 14.2 us -> 14.8 us
    pallas_call x13 -> x12, Pallas kernels: 27.9 us -> 27.2 us  [kernel_call(): pl.pallas_call(body, out_shape=outs, in_specs=[SM] * len(scalars) + [VM]...]
    ppermute x13, starting transfers between devices: 14.2 us -> 14.8 us  [swap(): return lax.ppermute(value, axis, pairs)]
  transfers between devices with their start and end apart: 13 -> 13, of which waited for: 1 -> 3; matrix products, arithmetic and copies ran while one was open for 0% -> 0% of each run, Pallas kernels for 57% -> 55%
where the time goes in v12:
time: 44.7 us; the launch traced here: 44.5 us
  Pallas kernels  27.2 us (61%)
  starting transfers between devices  14.8 us (33%)
  waiting for transfers between devices  1.28 us (3%)
  other arithmetic  0.73 us (2%)
    pallas_call x12, Pallas kernels, kernel_call(): pl.pallas_call(body, out_shape=outs, in_specs=[SM] * len(scalars) + [VM]...  27.2 us
    ppermute x13, starting transfers between devices, swap(): return lax.ppermute(value, axis, pairs)  14.8 us
    ppermute x13, waiting for transfers between devices, swap(): return lax.ppermute(value, axis, pairs)  1.28 us
  transfers between devices with their start and end apart: 13, of which 3 were waited for; matrix products, arithmetic and copies ran while one was open for 0% of the time, Pallas kernels for 55%

profile of v12, /device:TPU:0, one launch (start us, length us, event | category | flops | bytes accessed | tf_op | source)
XLA Modules:
  0.0 44.5 jit_solution(10789620604811688189)
XLA Ops:
  0.0 0.7 %bitcast_add_fusion = (s32[16,128]{1,0:T(8,128)S(1)}, s32[16,128]{1,0:T(8,128)S(1)}) fusion(s32[128,16]{0,1:T(8,128)} %param.31, s32[128,16]{0,1:T(8,128)} %param.30, s32[]{:T(128)} %axis_index.25), kind=kLoop, calls=%fused_computation.6 | loop fusion | flops 53248 | bytes 32772 | tf_op jit(solution)/shard_map/add | solution.py:313
  0.7 3.0 %collective-permute-start = (s32[16,128]{1,0:T(8,128)S(1)}, s32[16,128]{1,0:T(8,128)S(1)}, u32[]{:S(2)}, u32[]{:S(2)}) collective-permute-start(s32[16,128]{1,0:T(8,128)S(1)} %get-tuple-element.74), channel_id=1, source_target_pairs={{0,4},{4,0},{8,12},{12,8},{16,20},{20,16},{24,28},{28,24},{1,5},{5... | collective-permute-start | bytes 24584 | tf_op jit(solution)/shard_map/ppermute | solution.py:20
  3.7 2.6 %collective-permute-start.6 = (bf16[16,2,32,256]{3,2,1,0:T(8,128)(2,1)}, bf16[16,2,32,256]{3,2,1,0:T(8,128)(2,1)S(1)}, u32[]{:S(2)}, u32[]{:S(2)}) collective-permute-start(bf16[16,2,32,256]{3,2,1,0:T(8,128)(2,1)} %own.1), channel_id=1, source_target_pairs={{0,16},{4,20},{8,24},{12,28},{16,0},{20,4},{24,8},{28,12},{1,17},{... | collective-permute-start | bytes 1572872 | tf_op jit(solution)/shard_map/ppermute | solution.py:20
  6.3 0.0 collective-permute-done.code.refs_0_
  6.3 0.0 copy-start.9
  6.4 5.7 %sums_first.1 = (bf16[32,32,128]{2,1,0:T(8,128)(2,1)S(1)}, bf16[32,32,128]{2,1,0:T(8,128)(2,1)S(1)}, f32[316,32,128]{2,1,0:T(8,128)}, f32[129,32,128]{2,1,0:T(8,128)}) custom-call(s32[1]{0:T(128)} %bitcast.me, s32[16,128]{1,0:T(8,128)S(1)} %collective-permute-done.code.refs_0_, bf16[316,32,128]{2,1,0:T(8,128)(2,1)} %bitcast.58, bf16[128,32,128]{2,1,0:T(8,128)(2,1)} %bitcast.59), custom_call_target="tpu_custom_call" | custom-call | flops 4294967296 | bytes 1 | tf_op jit(solution)/shard_map/sums_first/pallas_call | solution.py:32
  12.0 1.1 %collective-permute-start.1 = (bf16[32,32,128]{2,1,0:T(8,128)(2,1)S(1)}, bf16[32,32,128]{2,1,0:T(8,128)(2,1)S(1)}, u32[]{:S(2)}, u32[]{:S(2)}) collective-permute-start(bf16[32,32,128]{2,1,0:T(8,128)(2,1)S(1)} %get-tuple-element.39), channel_id=1, source_target_pairs={{0,4},{4,0},{8,12},{12,8},{16,20},{20,16},{24,28},{28,24},{1,5},{5... | collective-permute-start | bytes 786440 | tf_op jit(solution)/shard_map/ppermute | solution.py:20
  13.2 0.0 copy-done.6
  13.2 0.0 copy-done.7
  13.2 0.0 copy-done.8
  13.2 0.0 copy-done.9
  13.2 0.0 slice-start.1
  13.2 0.0 copy-start
  13.2 1.0 %early.1 = (f32[192,256]{1,0:T(8,128)S(1)}, f32[192,256]{1,0:T(8,128)S(1)}, f32[192,256]{1,0:T(8,128)S(1)}, f32[192,256]{1,0:T(8,128)S(1)}) custom-call(s32[1]{0:T(128)} %bitcast.me, bf16[256,512]{1,0:T(8,128)(2,1)S(1)} %bitcast.57, bf16[128,256]{1,0:T(8,128)(2,1)S(1)} %copy-done.8, bf16[256,512]{1,0:T(8,128)(2,1)S(1)} %copy-done.7, f32[8,16,128]{2,1,0:T(8,128)S(1)} %copy-done.9), custom_call_target="tpu_custom_call" | custom-call | flops 4294967296 | bytes 1 | tf_op jit(solution)/shard_map/early/pallas_call | solution.py:32
  14.2 1.6 %collective-permute-start.3 = (f32[192,256]{1,0:T(8,128)S(1)}, f32[192,256]{1,0:T(8,128)S(1)}, u32[]{:S(2)}, u32[]{:S(2)}) collective-permute-start(f32[192,256]{1,0:T(8,128)S(1)} %get-tuple-element.51), channel_id=1, source_target_pairs={{0,2},{1,3},{2,0},{3,1},{4,6},{5,7},{6,4},{7,5},{8,10},{9,11},{10,... | collective-permute-start | bytes 589832 | tf_op jit(solution)/shard_map/ppermute | solution.py:20
  15.8 0.0 collective-permute-start.4
  15.8 1.0 %collective-permute-start.5 = (bf16[32,32,128]{2,1,0:T(8,128)(2,1)S(1)}, bf16[32,32,128]{2,1,0:T(8,128)(2,1)S(1)}, u32[]{:S(2)}, u32[]{:S(2)}) collective-permute-start(bf16[32,32,128]{2,1,0:T(8,128)(2,1)S(1)} %get-tuple-element.55), channel_id=1, source_target_pairs={{0,4},{4,0},{8,12},{12,8},{16,20},{20,16},{24,28},{28,24},{1,5},{5... | collective-permute-start | bytes 786440 | tf_op jit(solution)/shard_map/ppermute | solution.py:20
  16.8 0.0 slice-done
  16.8 3.4 %sums_third.1 = (f32[32,32,128]{2,1,0:T(8,128)S(1)}, f32[32,32,128]{2,1,0:T(8,128)S(1)}) custom-call(s32[1]{0:T(128)} %bitcast.me, s32[16,128]{1,0:T(8,128)S(1)} %get-tuple-element.73.refs_0_, f32[316,32,128]{2,1,0:T(8,128)S(1)} %bitcast.51, f32[129,32,128]{2,1,0:T(8,128)S(1)} %copy-done), custom_call_target="tpu_custom_call" | custom-call | bytes 1 | tf_op jit(solution)/shard_map/sums_third/pallas_call | solution.py:32
  20.2 0.0 collective-permute-done.1.refs_1_
  20.2 0.0 slice-start.2
  20.2 0.1 join.3
  20.3 0.0 copy-start.1
  20.3 0.0 copy-start.2
  20.3 0.0 copy-start.3
  20.3 0.0 copy-start.4
  20.4 0.0 slice-start.3
  20.4 0.0 slice-start.4
  20.4 0.0 copy-start.5
  20.4 0.0 copy-start.10
  20.4 0.0 copy-start.11
  20.4 0.0 copy-start.12
  20.4 3.5 %sums_second.1 = bf16[64,32,128]{2,1,0:T(8,128)(2,1)S(1)} custom-call(s32[1]{0:T(128)} %bitcast.me, s32[16,128]{1,0:T(8,128)S(1)} %collective-permute-done.code.refs_0_, f32[316,32,128]{2,1,0:T(8,128)S(1)} %bitcast.51, f32[129,32,128]{2,1,0:T(8,128)S(1)} %copy-done), custom_call_target="tpu_custom_call" | custom-call | flops 4294967296 | bytes 1 | tf_op jit(solution)/shard_map/sums_second/pallas_call | solution.py:32
  23.9 0.4 collective-permute-start.2
  24.3 0.0 collective-permute-done.3.refs_2_
  24.3 1.2 %collective-permute-start.11 = (bf16[32,32,128]{2,1,0:T(8,128)(2,1)S(1)}, bf16[32,32,128]{2,1,0:T(8,128)(2,1)S(1)}, u32[]{:S(2)}, u32[]{:S(2)}) collective-permute-start(bf16[32,32,128]{2,1,0:T(8,128)(2,1)S(1)} %join.3), channel_id=1, source_target_pairs={{0,3},{1,2},{2,1},{3,0},{4,7},{5,6},{6,5},{7,4},{8,11},{9,10},{10,... | collective-permute-start | bytes 786440 | tf_op jit(solution)/shard_map/ppermute | solution.py:20
  25.6 0.0 collective-permute-done.4.refs_3_
  25.6 1.0 %collective-permute-start.9 = (bf16[64,32,128]{2,1,0:T(8,128)(2,1)S(1)}, bf16[64,32,128]{2,1,0:T(8,128)(2,1)S(1)}, u32[]{:S(2)}, u32[]{:S(2)}) collective-permute-start(bf16[64,32,128]{2,1,0:T(8,128)(2,1)S(1)} %sums_second.1), channel_id=1, source_target_pairs={{0,4},{4,0},{8,12},{12,8},{16,20},{20,16},{24,28},{28,24},{1,5},{5... | collective-permute-start | bytes 1572872 | tf_op jit(solution)/shard_map/ppermute | solution.py:20
  26.6 0.0 collective-permute-done.2.refs_1_
  26.6 0.0 copy-done.3
  26.6 0.0 copy-done.4
  26.6 2.2 %shift.1 = (f32[16,2,32,256]{3,2,1,0:T(8,128)S(1)}, f32[2,8,4,16,128]{4,3,2,1,0:T(8,128)S(1)}, bf16[256,256]{1,0:T(8,128)(2,1)S(1)}, bf16[64,128]{1,0:T(8,128)(2,1)S(1)}, bf16[64,64]{1,0:T(8,128)(2,1)S(1)}) custom-call(s32[1]{0:T(128)} %bitcast.me, f32[192,256]{1,0:T(8,128)S(1)} %get-tuple-element.41.refs_0_, f32[192,256]{1,0:T(8,128)S(1)} %collective-permute-done.2.refs_1_, ...), custom_call_target="tpu_custom_call" | custom-call | bytes 1 | tf_op jit(solution)/shard_map/shift/pallas_call | solution.py:32
  28.9 0.0 collective-permute-done.5.refs_1_
  28.9 0.7 %collective-permute-start.12 = (bf16[32,32,128]{2,1,0:T(8,128)(2,1)S(1)}, bf16[32,32,128]{2,1,0:T(8,128)(2,1)S(1)}, u32[]{:S(2)}, u32[]{:S(2)}) collective-permute-start(bf16[32,32,128]{2,1,0:T(8,128)(2,1)S(1)} %join.4), channel_id=1, source_target_pairs={{0,2},{1,3},{2,0},{3,1},{4,6},{5,7},{6,4},{7,5},{8,10},{9,11},{10,... | collective-permute-start | bytes 786440 | tf_op jit(solution)/shard_map/ppermute | solution.py:20
  29.6 0.0 collective-permute-done.6.far
  29.6 0.0 slice-done.4
  29.6 0.0 copy-done.5
  29.6 0.0 copy-done.10
  29.6 0.0 copy-done.11
  29.6 0.0 copy-done.12
  29.6 5.1 %upper.1 = (bf16[4,64,128]{2,1,0:T(8,128)(2,1)S(1)}, bf16[4,64,128]{2,1,0:T(8,128)(2,1)S(1)}, bf16[4,64,128]{2,1,0:T(8,128)(2,1)S(1)}, bf16[4,64,128]{2,1,0:T(8,128)(2,1)S(1)}) custom-call(s32[1]{0:T(128)} %bitcast.me, s32[1]{0:T(128)} %bitcast.6.home, s32[16,16]{1,0:T(8,128)S(1)} %copy-done.11, s32[16,16]{1,0:T(8,128)S(1)} %copy-done.12, ...), custom_call_target="tpu_custom_call" | custom-call | flops 4294967296 | bytes 1 | tf_op jit(solution)/shard_map/upper/pallas_call | solution.py:32
  34.8 1.5 %collective-permute-start.7 = (bf16[4,64,128]{2,1,0:T(8,128)(2,1)S(1)}, bf16[4,64,128]{2,1,0:T(8,128)(2,1)S(1)}, u32[]{:S(2)}, u32[]{:S(2)}) collective-permute-start(bf16[4,64,128]{2,1,0:T(8,128)(2,1)S(1)} %get-tuple-element.58), channel_id=1, source_target_pairs={{0,2},{1,3},{2,0},{3,1},{4,6},{5,7},{6,4},{7,5},{8,10},{9,11},{10,... | collective-permute-start | bytes 196616 | tf_op jit(solution)/shard_map/ppermute | solution.py:20
  36.3 0.0 collective-permute-start.8
  36.3 3.4 %sums_fourth.1 = (f32[32,32,128]{2,1,0:T(8,128)S(1)}, f32[32,32,128]{2,1,0:T(8,128)S(1)}) custom-call(s32[1]{0:T(128)} %bitcast.me, s32[16,128]{1,0:T(8,128)S(1)} %get-tuple-element.73.refs_0_, f32[316,32,128]{2,1,0:T(8,128)S(1)} %bitcast.51, f32[129,32,128]{2,1,0:T(8,128)S(1)} %copy-done), custom_call_target="tpu_custom_call" | custom-call | flops 4294967296 | bytes 1 | tf_op jit(solution)/shard_map/sums_fourth/pallas_call | solution.py:32
  39.7 0.1 collective-permute-done.9.refs_2_
  39.8 0.1 join.5
  40.0 0.7 %collective-permute-start.10 = (bf16[40,32,128]{2,1,0:T(8,128)(2,1)S(1)}, bf16[40,32,128]{2,1,0:T(8,128)(2,1)S(1)}, u32[]{:S(2)}, u32[]{:S(2)}) collective-permute-start(bf16[40,32,128]{2,1,0:T(8,128)(2,1)S(1)} %get-tuple-element.67), channel_id=1, source_target_pairs={{0,1},{1,0},{2,3},{3,2},{4,5},{5,4},{6,7},{7,6},{8,9},{9,8},{10,11... | collective-permute-start | bytes 983048 | tf_op jit(solution)/shard_map/ppermute | solution.py:20
  40.6 0.0 collective-permute-done.11.refs_0_
  40.6 0.0 collective-permute-done.12.refs_1_
  40.7 0.1 place.1
  40.7 0.0 collective-permute-done.7.refs_0_
  40.7 0.4 collective-permute-done.8.refs_1_
  41.1 0.8 %collective-permute-done.10.refs_3_ = bf16[40,32,128]{2,1,0:T(8,128)(2,1)S(1)} collective-permute-done((bf16[40,32,128]{2,1,0:T(8,128)(2,1)S(1)}, bf16[40,32,128]{2,1,0:T(8,128)(2,1)S(1)}, u32[]{:S(2)}, u32[]{:S(2)}) %collective-permute-start.10) | collective-permute-done | bytes 327712 | tf_op jit(solution)/shard_map/ppermute | solution.py:20
  41.9 2.6 %expand.1 = f32[4096,128]{1,0:T(8,128)} custom-call(s32[1]{0:T(128)} %bitcast.me, bf16[4,64,128]{2,1,0:T(8,128)(2,1)S(1)} %collective-permute-done.7.refs_0_, bf16[4,64,128]{2,1,0:T(8,128)(2,1)S(1)} %collective-permute-done.8.refs_1_, bf16[40,32,128]{2,1,0:T(8,128)(2,1)S(1)} %get-tuple-element.66.refs_2_, ...), custom_call_target="tpu_custom_call" | custom-call | flops 4294967296 | bytes 1 | tf_op jit(solution)/shard_map/expand/pallas_call | solution.py:32
  (13 shorter events, 0.1 us)
Async XLA Ops:
  0.7 5.6 %collective-permute-start = (s32[16,128]{1,0:T(8,128)S(1)}, s32[16,128]{1,0:T(8,128)S(1)}, u32[]{:S(2)}, u32[]{:S(2)}) collective-permute-start(s32[16,128]{1,0:T(8,128)S(1)} %get-tuple-element.74), channel_id=1, source_target_pairs={{0,4},{4,0},{8,12},{12,8},{16,20},{20,16},{24,28},{28,24},{1,5},{5... | collective-permute-start | bytes 24584 | tf_op jit(solution)/shard_map/ppermute | solution.py:20
  3.7 25.8 %collective-permute-start.6 = (bf16[16,2,32,256]{3,2,1,0:T(8,128)(2,1)}, bf16[16,2,32,256]{3,2,1,0:T(8,128)(2,1)S(1)}, u32[]{:S(2)}, u32[]{:S(2)}) collective-permute-start(bf16[16,2,32,256]{3,2,1,0:T(8,128)(2,1)} %own.1), channel_id=1, source_target_pairs={{0,16},{4,20},{8,24},{12,28},{16,0},{20,4},{24,8},{28,12},{1,17},{... | collective-permute-start | bytes 1572872 | tf_op jit(solution)/shard_map/ppermute | solution.py:20
  6.3 6.8 %copy-start.6 = (bf16[2,2,64,512]{3,2,1,0:T(8,128)(2,1)S(1)}, bf16[2,2,64,512]{3,2,1,0:T(8,128)(2,1)}, u32[]{:S(2)}) copy-start(bf16[2,2,64,512]{3,2,1,0:T(8,128)(2,1)} %param.17) | copy-start | bytes 786436
  6.3 6.8 %copy-start.7 = (bf16[256,512]{1,0:T(8,128)(2,1)S(1)}, bf16[256,512]{1,0:T(8,128)(2,1)}, u32[]{:S(2)}) copy-start(bf16[256,512]{1,0:T(8,128)(2,1)} %refs_2_.1) | copy-start | bytes 786436
  6.3 6.8 %copy-start.8 = (bf16[128,256]{1,0:T(8,128)(2,1)S(1)}, bf16[128,256]{1,0:T(8,128)(2,1)}, u32[]{:S(2)}) copy-start(bf16[128,256]{1,0:T(8,128)(2,1)} %refs_1_.1) | copy-start | bytes 196612
  6.3 6.8 %copy-start.9 = (f32[8,16,128]{2,1,0:T(8,128)S(1)}, f32[8,16,128]{2,1,0:T(8,128)}, u32[]{:S(2)}) copy-start(f32[8,16,128]{2,1,0:T(8,128)} %refs_3_.1) | copy-start | bytes 196612
  12.0 8.2 %collective-permute-start.1 = (bf16[32,32,128]{2,1,0:T(8,128)(2,1)S(1)}, bf16[32,32,128]{2,1,0:T(8,128)(2,1)S(1)}, u32[]{:S(2)}, u32[]{:S(2)}) collective-permute-start(bf16[32,32,128]{2,1,0:T(8,128)(2,1)S(1)} %get-tuple-element.39), channel_id=1, source_target_pairs={{0,4},{4,0},{8,12},{12,8},{16,20},{20,16},{24,28},{28,24},{1,5},{5... | collective-permute-start | bytes 786440 | tf_op jit(solution)/shard_map/ppermute | solution.py:20
  13.1 3.6 %slice-start = ((s8[5177344]{0:T(1024)(128)(4,1)}), s8[4194304]{0:T(1024)(128)(4,1)S(1)}, s32[]{:S(2)}) async-start(s8[5177344]{0:T(1024)(128)(4,1)} %bitcast.50), calls=%async_computation | async-start | bytes 8388608
  13.2 3.6 %slice-start.1 = ((s8[5177344]{0:T(1024)(128)(4,1)}), s8[983040]{0:T(1024)(128)(4,1)S(1)}, s32[]{:S(2)}) async-start(s8[5177344]{0:T(1024)(128)(4,1)} %bitcast.50), calls=%async_computation.1 | async-start | bytes 1966080
  13.2 3.6 %copy-start = (f32[129,32,128]{2,1,0:T(8,128)S(1)}, f32[129,32,128]{2,1,0:T(8,128)}, u32[]{:S(2)}) copy-start(f32[129,32,128]{2,1,0:T(8,128)} %get-tuple-element.44.refs_2_) | copy-start | bytes 6340612
  14.2 10.1 %collective-permute-start.3 = (f32[192,256]{1,0:T(8,128)S(1)}, f32[192,256]{1,0:T(8,128)S(1)}, u32[]{:S(2)}, u32[]{:S(2)}) collective-permute-start(f32[192,256]{1,0:T(8,128)S(1)} %get-tuple-element.51), channel_id=1, source_target_pairs={{0,2},{1,3},{2,0},{3,1},{4,6},{5,7},{6,4},{7,5},{8,10},{9,11},{10,... | collective-permute-start | bytes 589832 | tf_op jit(solution)/shard_map/ppermute | solution.py:20
  15.8 9.8 %collective-permute-start.4 = (f32[192,256]{1,0:T(8,128)S(1)}, f32[192,256]{1,0:T(8,128)S(1)}, u32[]{:S(2)}, u32[]{:S(2)}) collective-permute-start(f32[192,256]{1,0:T(8,128)S(1)} %get-tuple-element.52), channel_id=1, source_target_pairs={{0,3},{1,2},{2,1},{3,0},{4,7},{5,6},{6,5},{7,4},{8,11},{9,10},{10,... | collective-permute-start | bytes 589832 | tf_op jit(solution)/shard_map/ppermute | solution.py:20
  15.8 13.1 %collective-permute-start.5 = (bf16[32,32,128]{2,1,0:T(8,128)(2,1)S(1)}, bf16[32,32,128]{2,1,0:T(8,128)(2,1)S(1)}, u32[]{:S(2)}, u32[]{:S(2)}) collective-permute-start(bf16[32,32,128]{2,1,0:T(8,128)(2,1)S(1)} %get-tuple-element.55), channel_id=1, source_target_pairs={{0,4},{4,0},{8,12},{12,8},{16,20},{20,16},{24,28},{28,24},{1,5},{5... | collective-permute-start | bytes 786440 | tf_op jit(solution)/shard_map/ppermute | solution.py:20
  20.2 9.4 %slice-start.2 = ((s8[10354688]{0:T(1024)(128)(4,1)}), s8[4194304]{0:T(1024)(128)(4,1)S(1)}, s32[]{:S(2)}) async-start(s8[10354688]{0:T(1024)(128)(4,1)} %bitcast.54), calls=%async_computation.2 | async-start | bytes 8388608
  20.3 6.3 %copy-start.1 = (f32[8,32,256]{2,1,0:T(8,128)S(1)}, f32[8,32,256]{2,1,0:T(8,128)}, u32[]{:S(2)}) copy-start(f32[8,32,256]{2,1,0:T(8,128)} %refs_4_.1) | copy-start | bytes 786436
  20.3 6.3 %copy-start.2 = (bf16[2,128,128]{2,1,0:T(8,128)(2,1)S(1)}, bf16[2,128,128]{2,1,0:T(8,128)(2,1)}, u32[]{:S(2)}) copy-start(bf16[2,128,128]{2,1,0:T(8,128)(2,1)} %refs_5_.1) | copy-start | bytes 196612
  20.3 6.3 %copy-start.3 = (bf16[64,128]{1,0:T(8,128)(2,1)S(1)}, bf16[64,128]{1,0:T(8,128)(2,1)}, u32[]{:S(2)}) copy-start(bf16[64,128]{1,0:T(8,128)(2,1)} %refs_6_.1) | copy-start | bytes 49156
  20.3 6.3 %copy-start.4 = (bf16[64,64]{1,0:T(8,128)(2,1)S(1)}, bf16[64,64]{1,0:T(8,128)(2,1)}, u32[]{:S(2)}) copy-start(bf16[64,64]{1,0:T(8,128)(2,1)} %refs_7_.1) | copy-start | bytes 24580
  20.4 9.2 %slice-start.3 = ((s8[10354688]{0:T(1024)(128)(4,1)}), s8[4194304]{0:T(1024)(128)(4,1)S(1)}, s32[]{:S(2)}) async-start(s8[10354688]{0:T(1024)(128)(4,1)} %bitcast.54), calls=%async_computation.3 | async-start | bytes 8388608
  20.4 9.2 %slice-start.4 = ((s8[10354688]{0:T(1024)(128)(4,1)}), s8[1966080]{0:T(1024)(128)(4,1)S(1)}, s32[]{:S(2)}) async-start(s8[10354688]{0:T(1024)(128)(4,1)} %bitcast.54), calls=%async_computation.4 | async-start | bytes 3932160
  20.4 9.2 %copy-start.5 = (bf16[16,2,32,256]{3,2,1,0:T(8,128)(2,1)S(1)}, bf16[16,2,32,256]{3,2,1,0:T(8,128)(2,1)}, u32[]{:S(2)}) copy-start(bf16[16,2,32,256]{3,2,1,0:T(8,128)(2,1)} %own.1) | copy-start | bytes 1572868
  20.4 9.2 %copy-start.10 = (bf16[128,256]{1,0:T(8,128)(2,1)S(1)}, bf16[128,256]{1,0:T(8,128)(2,1)}, u32[]{:S(2)}) copy-start(bf16[128,256]{1,0:T(8,128)(2,1)} %phi.1) | copy-start | bytes 196612
  20.4 9.2 %copy-start.11 = (s32[16,16]{1,0:T(8,128)S(1)}, s32[16,16]{1,0:T(8,128)}, u32[]{:S(2)}) copy-start(s32[16,16]{1,0:T(8,128)} %ids.1) | copy-start | bytes 3076
  20.4 9.2 %copy-start.12 = (s32[16,16]{1,0:T(8,128)S(1)}, s32[16,16]{1,0:T(8,128)}, u32[]{:S(2)}) copy-start(s32[16,16]{1,0:T(8,128)} %offsets.1) | copy-start | bytes 3076
  23.9 2.7 %collective-permute-start.2 = (f32[192,256]{1,0:T(8,128)S(1)}, f32[192,256]{1,0:T(8,128)S(1)}, u32[]{:S(2)}, u32[]{:S(2)}) collective-permute-start(f32[192,256]{1,0:T(8,128)S(1)} %get-tuple-element.50), channel_id=1, source_target_pairs={{0,1},{1,0},{2,3},{3,2},{4,5},{5,4},{6,7},{7,6},{8,9},{9,8},{10,11... | collective-permute-start | bytes 589832 | tf_op jit(solution)/shard_map/ppermute | solution.py:20
  24.3 16.3 %collective-permute-start.11 = (bf16[32,32,128]{2,1,0:T(8,128)(2,1)S(1)}, bf16[32,32,128]{2,1,0:T(8,128)(2,1)S(1)}, u32[]{:S(2)}, u32[]{:S(2)}) collective-permute-start(bf16[32,32,128]{2,1,0:T(8,128)(2,1)S(1)} %join.3), channel_id=1, source_target_pairs={{0,3},{1,2},{2,1},{3,0},{4,7},{5,6},{6,5},{7,4},{8,11},{9,10},{10,... | collective-permute-start | bytes 786440 | tf_op jit(solution)/shard_map/ppermute | solution.py:20
  25.6 14.3 %collective-permute-start.9 = (bf16[64,32,128]{2,1,0:T(8,128)(2,1)S(1)}, bf16[64,32,128]{2,1,0:T(8,128)(2,1)S(1)}, u32[]{:S(2)}, u32[]{:S(2)}) collective-permute-start(bf16[64,32,128]{2,1,0:T(8,128)(2,1)S(1)} %sums_second.1), channel_id=1, source_target_pairs={{0,4},{4,0},{8,12},{12,8},{16,20},{20,16},{24,28},{28,24},{1,5},{5... | collective-permute-start | bytes 1572872 | tf_op jit(solution)/shard_map/ppermute | solution.py:20
  28.9 11.7 %collective-permute-start.12 = (bf16[32,32,128]{2,1,0:T(8,128)(2,1)S(1)}, bf16[32,32,128]{2,1,0:T(8,128)(2,1)S(1)}, u32[]{:S(2)}, u32[]{:S(2)}) collective-permute-start(bf16[32,32,128]{2,1,0:T(8,128)(2,1)S(1)} %join.4), channel_id=1, source_target_pairs={{0,2},{1,3},{2,0},{3,1},{4,6},{5,7},{6,4},{7,5},{8,10},{9,11},{10,... | collective-permute-start | bytes 786440 | tf_op jit(solution)/shard_map/ppermute | solution.py:20
  34.8 5.9 %collective-permute-start.7 = (bf16[4,64,128]{2,1,0:T(8,128)(2,1)S(1)}, bf16[4,64,128]{2,1,0:T(8,128)(2,1)S(1)}, u32[]{:S(2)}, u32[]{:S(2)}) collective-permute-start(bf16[4,64,128]{2,1,0:T(8,128)(2,1)S(1)} %get-tuple-element.58), channel_id=1, source_target_pairs={{0,2},{1,3},{2,0},{3,1},{4,6},{5,7},{6,4},{7,5},{8,10},{9,11},{10,... | collective-permute-start | bytes 196616 | tf_op jit(solution)/shard_map/ppermute | solution.py:20
  36.3 4.8 %collective-permute-start.8 = (bf16[4,64,128]{2,1,0:T(8,128)(2,1)S(1)}, bf16[4,64,128]{2,1,0:T(8,128)(2,1)S(1)}, u32[]{:S(2)}, u32[]{:S(2)}) collective-permute-start(bf16[4,64,128]{2,1,0:T(8,128)(2,1)S(1)} %get-tuple-element.59), channel_id=1, source_target_pairs={{0,3},{1,2},{2,1},{3,0},{4,7},{5,6},{6,5},{7,4},{8,11},{9,10},{10,... | collective-permute-start | bytes 196616 | tf_op jit(solution)/shard_map/ppermute | solution.py:20
  40.0 2.0 %collective-permute-start.10 = (bf16[40,32,128]{2,1,0:T(8,128)(2,1)S(1)}, bf16[40,32,128]{2,1,0:T(8,128)(2,1)S(1)}, u32[]{:S(2)}, u32[]{:S(2)}) collective-permute-start(bf16[40,32,128]{2,1,0:T(8,128)(2,1)S(1)} %get-tuple-element.67), channel_id=1, source_target_pairs={{0,1},{1,0},{2,3},{3,2},{4,5},{5,4},{6,7},{7,6},{8,9},{9,8},{10,11... | collective-permute-start | bytes 983048 | tf_op jit(solution)/shard_map/ppermute | solution.py:20
